TPU v7x, 256 devices: a whole 4x4x8 slice. The times are simulated.
256 devices in a mesh: vid: 128 (over z, y, x_lo, core), aud: 2 (over x_hi).
Axes of the slice: x: 4 (x_hi: 2, x_lo: 2; x = x_hi * 2 + x_lo), y: 4, z: 8, core: 2. Of those that a mesh axis runs over, the one named last changes fastest.
Arguments:
- q_video: bfloat16 [32768, 1536], P('vid', 'aud'), may hold values from -240 to 240
- video_key_rows: bfloat16 [32768, 1536], P('vid', 'aud'), may hold values from -6 to 6
- video_value_rows: bfloat16 [32768, 1536], P('vid', 'aud'), may hold values from -6 to 6
- g_video: bfloat16 [32768, 1536], P('vid', 'aud'), may hold values from -6 to 6
- q_audio: bfloat16 [8192, 1536], P(('vid', 'aud')), may hold values from -240 to 240
- k_audio: bfloat16 [8192, 1536], P(('vid', 'aud')), may hold values from -6 to 6
- v_audio: bfloat16 [8192, 1536], P(('vid', 'aud')), may hold values from -6 to 6
- g_audio: bfloat16 [8192, 1536], P(('vid', 'aud')), may hold values from -6 to 6
- window: int32 [512, 2], replicated, may hold values from 0 to 127, as said below
- audio_len: int32 [128], replicated, may hold values from 1 to 64
Outputs:
- out_video: bfloat16 [32768, 1536], P('vid', 'aud')
- out_audio: bfloat16 [8192, 1536], P(('vid', 'aud'))
- dq_video: bfloat16 [32768, 1536], P('vid', 'aud')
- dk_video: bfloat16 [32768, 1536], P('vid', 'aud')
- dv_video: bfloat16 [32768, 1536], P('vid', 'aud')
- dq_audio: bfloat16 [8192, 1536], P(('vid', 'aud'))
- dk_audio: bfloat16 [8192, 1536], P(('vid', 'aud'))
- dv_audio: bfloat16 [8192, 1536], P(('vid', 'aud'))
Inputs may be any that keep to these rules, and one draw needn't show every extreme that they name: window[i] = (start, count) with 1 <= count <= 3 (3 is reached in every draw), start <= i // 4 < start + count, and start + count <= 128.
All inputs are finite; a program needn't handle non-finite values.
Results may differ from a plain program's by a relative error of at most 0.0095.
Values may be sent and summed in bfloat16 or wider, within the bound.
No kernel may reach another device: no remote copies, remote signals or barrier semaphores. Data moves between devices by JAX's collectives and lax.ppermute only.
A program may use at most 64 MiB of HBM per device.

v0:
```python
import jax
import jax.numpy as jnp
from jax import lax
from jax.sharding import PartitionSpec as P

HD = 64
BLK = 64
WMAX = 3


NEG_FILL = -1e30


def from_behind(value, axis, steps):
    count = lax.axis_size(axis)
    leading, last = (max(0, -steps), min(count, count - steps))
    return lax.ppermute(value, axis, [(source, source + steps) for source in range(leading, last)])


def split_heads(matrix):
    return matrix.reshape(matrix.shape[0], matrix.shape[1] // HD, HD)


def join_heads(tensor):
    return tensor.reshape(tensor.shape[0], -1)


def masked_scores(queries, key_rows, allowed):
    scores = jnp.einsum(
        "rhd,khd->hrk",
        split_heads(queries),
        split_heads(key_rows),
        preferred_element_type=jnp.float32,
    )
    return jnp.where(allowed[None], scores * HD ** (-0.5), NEG_FILL)


def head_delta(cotangent, out_rows):
    return jnp.sum(
        split_heads(cotangent).astype(jnp.float32) * split_heads(out_rows).astype(jnp.float32),
        axis=2,
    )


def gradient_terms(queries, key_rows, value_rows, cotangent, attention_probs, weights_b, deltas):
    scale = HD ** (-0.5)
    g_heads = split_heads(cotangent)
    grad_p = jnp.einsum(
        "rhd,khd->hrk", g_heads, split_heads(value_rows), preferred_element_type=jnp.float32
    )
    grad_s = (attention_probs * (grad_p - deltas.T[:, :, None])).astype(jnp.bfloat16)
    grad_q = (
        jnp.einsum(
            "hrk,khd->rhd", grad_s, split_heads(key_rows), preferred_element_type=jnp.float32
        )
        * scale
    )
    grad_k = (
        jnp.einsum("hrk,rhd->khd", grad_s, split_heads(queries), preferred_element_type=jnp.float32)
        * scale
    )
    grad_v = jnp.einsum("hrk,rhd->khd", weights_b, g_heads, preferred_element_type=jnp.float32)
    return (join_heads(grad_q), join_heads(grad_k), join_heads(grad_v))


def full_attention(queries, key_rows, value_rows, cotangent, allowed, query_valid):
    scores = masked_scores(queries, key_rows, allowed)
    row_max = jnp.max(scores, axis=2, keepdims=True)
    row_sum = jnp.sum(
        jnp.where(allowed[None], jnp.exp(scores - row_max), 0.0), axis=2, keepdims=True
    )
    attention_probs = jnp.where(allowed[None], jnp.exp(scores - (row_max + jnp.log(row_sum))), 0.0)
    weights_b = attention_probs.astype(jnp.bfloat16)
    mixed = jnp.einsum(
        "hrk,khd->rhd", weights_b, split_heads(value_rows), preferred_element_type=jnp.float32
    )
    out_rows = join_heads(mixed * query_valid[:, None, None]).astype(jnp.bfloat16)
    deltas = head_delta(cotangent, out_rows)
    grad_q, grad_k, grad_v = gradient_terms(
        queries, key_rows, value_rows, cotangent, attention_probs, weights_b, deltas
    )
    return (out_rows, grad_q, grad_k, grad_v)


def body(
    q_video,
    video_key_rows,
    video_value_rows,
    g_video,
    q_audio,
    k_audio,
    v_audio,
    g_audio,
    window,
    audio_len,
):
    q_aud, k_aud, v_aud, g_aud = (
        lax.all_to_all(q_audio, "aud", split_axis=1, concat_axis=0, tiled=True),
        lax.all_to_all(k_audio, "aud", split_axis=1, concat_axis=0, tiled=True),
        lax.all_to_all(v_audio, "aud", split_axis=1, concat_axis=0, tiled=True),
        lax.all_to_all(g_audio, "aud", split_axis=1, concat_axis=0, tiled=True),
    )
    video_rows = q_video.shape[0]
    audio_rows = q_aud.shape[0]
    video_blocks = video_rows // BLK
    audio_blocks = audio_rows // BLK
    reach_dev = (WMAX - 2 + audio_blocks) // audio_blocks
    near_count = 2 * reach_dev + 1
    offsets = [
        window_shift for window_shift in range(-reach_dev, reach_dev + 1) if window_shift != 0
    ]
    device = lax.axis_index("vid")
    audio_total = audio_len.shape[0]
    video_total = window.shape[0]

    def nearby_row_span(pieces, axis):
        return jnp.concatenate(
            [pieces[window_shift] for window_shift in range(-reach_dev, reach_dev + 1)], axis=axis
        )

    def rows_of(tensor, window_shift, size, axis):
        return lax.slice_in_dim(
            tensor,
            (window_shift + reach_dev) * size,
            (window_shift + reach_dev + 1) * size,
            axis=axis,
        )

    own_lens = lax.dynamic_slice_in_dim(audio_len, device * audio_blocks, audio_blocks, 0)
    audio_valid = (jnp.arange(audio_rows) % BLK < jnp.repeat(own_lens, BLK)).astype(jnp.float32)
    g_masked = g_aud * audio_valid[:, None].astype(jnp.bfloat16)
    own_window = lax.dynamic_slice_in_dim(window, device * video_blocks, video_blocks, 0)
    near_ablk = (device - reach_dev) * audio_blocks + jnp.arange(near_count * audio_blocks)
    block_ok = (near_ablk[None] >= own_window[:, 0:1]) & (
        near_ablk[None] < own_window[:, 0:1] + own_window[:, 1:2]
    )
    window_tok = jnp.repeat(jnp.repeat(block_ok, BLK, 0), BLK, 1)
    near_lens = jnp.sum(
        jnp.where(near_ablk[:, None] == jnp.arange(audio_total)[None], audio_len[None], 0), axis=1
    )
    key_ok = jnp.arange(near_count * audio_rows) % BLK < jnp.repeat(near_lens, BLK)
    allowed_va = window_tok & key_ok[None]
    video_ones = jnp.ones((video_rows,), jnp.float32)
    key_pieces = {0: k_aud}
    value_pieces = {0: v_aud}
    for window_shift in offsets:
        key_pieces[window_shift], value_pieces[window_shift] = from_behind(
            (k_aud, v_aud), "vid", -window_shift
        )
    out_video, dq_video, dk_near, dv_near = full_attention(
        q_video,
        nearby_row_span(key_pieces, 0),
        nearby_row_span(value_pieces, 0),
        g_video,
        allowed_va,
        video_ones,
    )
    dk_aud = rows_of(dk_near, 0, audio_rows, 0)
    dv_aud = rows_of(dv_near, 0, audio_rows, 0)
    for window_shift in offsets:
        dk_in, dv_in = (
            from_behind(
                rows_of(dk_near, window_shift, audio_rows, 0).astype(jnp.bfloat16),
                "vid",
                window_shift,
            ).astype(jnp.float32),
            from_behind(
                rows_of(dv_near, window_shift, audio_rows, 0).astype(jnp.bfloat16),
                "vid",
                window_shift,
            ).astype(jnp.float32),
        )
        dk_aud = dk_aud + dk_in
        dv_aud = dv_aud + dv_in
    near_vblk = (device - reach_dev) * video_blocks + jnp.arange(near_count * video_blocks)
    matched = near_vblk[:, None] == jnp.arange(video_total)[None]
    near_start = jnp.sum(jnp.where(matched, window[None, :, 0], 0), axis=1)
    near_span = jnp.sum(jnp.where(matched, window[None, :, 1], 0), axis=1)
    own_ablk = device * audio_blocks + jnp.arange(audio_blocks)
    pair_ok = (own_ablk[:, None] >= near_start[None]) & (
        own_ablk[:, None] < near_start[None] + near_span[None]
    )
    allowed_av = jnp.repeat(jnp.repeat(pair_ok, BLK, 0), BLK, 1)
    video_key_parts = {0: video_key_rows}
    video_value_parts = {0: video_value_rows}
    for window_shift in offsets:
        video_key_parts[window_shift], video_value_parts[window_shift] = from_behind(
            (video_key_rows, video_value_rows), "vid", -window_shift
        )
    out_aud, dq_aud, nearby_key_value_grads, dvv_near = full_attention(
        q_aud,
        nearby_row_span(video_key_parts, 0),
        nearby_row_span(video_value_parts, 0),
        g_masked,
        allowed_av,
        audio_valid,
    )
    dk_video = rows_of(nearby_key_value_grads, 0, video_rows, 0)
    dv_video = rows_of(dvv_near, 0, video_rows, 0)
    for window_shift in offsets:
        dk_in, dv_in = from_behind(
            (
                rows_of(nearby_key_value_grads, window_shift, video_rows, 0),
                rows_of(dvv_near, window_shift, video_rows, 0),
            ),
            "vid",
            window_shift,
        )
        dk_video = dk_video + dk_in
        dv_video = dv_video + dv_in
    results = (
        lax.all_to_all(out_aud, "aud", split_axis=0, concat_axis=1, tiled=True),
        lax.all_to_all(dq_aud.astype(jnp.bfloat16), "aud", split_axis=0, concat_axis=1, tiled=True),
        lax.all_to_all(dk_aud.astype(jnp.bfloat16), "aud", split_axis=0, concat_axis=1, tiled=True),
        lax.all_to_all(dv_aud.astype(jnp.bfloat16), "aud", split_axis=0, concat_axis=1, tiled=True),
    )
    return (
        out_video,
        results[0],
        dq_video.astype(jnp.bfloat16),
        dk_video.astype(jnp.bfloat16),
        dv_video.astype(jnp.bfloat16),
        results[1],
        results[2],
        results[3],
    )


def solution(mesh):
    in_specs = (
        P("vid", "aud"),
        P("vid", "aud"),
        P("vid", "aud"),
        P("vid", "aud"),
        P(("vid", "aud"), None),
        P(("vid", "aud"), None),
        P(("vid", "aud"), None),
        P(("vid", "aud"), None),
        P(),
        P(),
    )
    out_specs = (
        P("vid", "aud"),
        P(("vid", "aud"), None),
        P("vid", "aud"),
        P("vid", "aud"),
        P("vid", "aud"),
        P(("vid", "aud"), None),
        P(("vid", "aud"), None),
        P(("vid", "aud"), None),
    )
    return jax.shard_map(body, mesh=mesh, in_specs=in_specs, out_specs=out_specs, check_vma=False)
```

profile of v0, /device:TPU:141, one launch (start us, length us, event | category | flops | bytes accessed | tf_op | source)
XLA Modules:
  0.0 347.1 jit_solution(1796188709967460185)
XLA Ops:
  2.2 4.2 %all-to-all-start.1 = ((bf16[32,2,768]{2,0,1:T(8,128)(2,1)}), bf16[32,2,768]{2,0,1:T(8,128)(2,1)S(1)}, u32[]{:S(2)}, u32[]{:S(2)}) async-start(bf16[32,2,768]{2,0,1:T(8,128)(2,1)} %bitcast.160), calls=%async_computation.1 | async-start | bytes 196608 | tf_op jit(solution)/shard_map/all_to_all | solution.py:99
  12.1 4.2 %all-to-all-start = ((bf16[32,2,768]{2,0,1:T(8,128)(2,1)}), bf16[32,2,768]{2,0,1:T(8,128)(2,1)S(1)}, u32[]{:S(2)}, u32[]{:S(2)}) async-start(bf16[32,2,768]{2,0,1:T(8,128)(2,1)} %bitcast.161), calls=%async_computation | async-start | bytes 196608 | tf_op jit(solution)/shard_map/all_to_all | solution.py:100
  16.3 2.9 collective-permute-start.7
  19.2 3.8 %collective-permute-start.6 = (bf16[64,768]{1,0:T(8,128)(2,1)S(1)}, bf16[64,768]{1,0:T(8,128)(2,1)S(1)}, u32[]{:S(2)}, u32[]{:S(2)}) collective-permute-start(bf16[64,768]{1,0:T(8,128)(2,1)S(1)} %bitcast.205), channel_id=1, source_target_pairs={{2,0},{4,2},{6,4},{8,6},{10,8},{12,10},{14,12},{16,14},{18,16},{20... | collective-permute-start | bytes 294920 | tf_op jit(solution)/shard_map/ppermute | solution.py:17
  23.0 2.5 collective-permute-start.5
  25.5 3.7 %collective-permute-start.4 = (bf16[64,768]{1,0:T(8,128)(2,1)S(1)}, bf16[64,768]{1,0:T(8,128)(2,1)S(1)}, u32[]{:S(2)}, u32[]{:S(2)}) collective-permute-start(bf16[64,768]{1,0:T(8,128)(2,1)S(1)} %bitcast.207), channel_id=1, source_target_pairs={{0,4},{2,6},{4,8},{6,10},{8,12},{10,14},{12,16},{14,18},{16,20},{1... | collective-permute-start | bytes 294920 | tf_op jit(solution)/shard_map/ppermute | solution.py:17
  35.6 4.2 %all-to-all-start.4 = ((bf16[32,2,768]{2,0,1:T(8,128)(2,1)}), bf16[32,2,768]{2,0,1:T(8,128)(2,1)}, u32[]{:S(2)}, u32[]{:S(2)}) async-start(bf16[32,2,768]{2,0,1:T(8,128)(2,1)} %bitcast.158), calls=%async_computation.4 | async-start | bytes 196608 | tf_op jit(solution)/shard_map/all_to_all | solution.py:101
  39.9 2.5 collective-permute-start.3
  43.2 2.9 collective-permute-start.2
  46.3 2.6 collective-permute-start.1
  49.1 3.7 %collective-permute-start = (bf16[64,768]{1,0:T(8,128)(2,1)S(1)}, bf16[64,768]{1,0:T(8,128)(2,1)S(1)}, u32[]{:S(2)}, u32[]{:S(2)}) collective-permute-start(bf16[64,768]{1,0:T(8,128)(2,1)S(1)} %bitcast.213), channel_id=1, source_target_pairs={{0,4},{2,6},{4,8},{6,10},{8,12},{10,14},{12,16},{14,18},{16,20},{1... | collective-permute-start | bytes 294920 | tf_op jit(solution)/shard_map/ppermute | solution.py:17
  55.4 2.4 fusion.40
  59.0 4.2 %multiply_reduce_fusion = (f32[256,12]{0,1:T(8,128)S(1)}, bf16[12,64,256]{2,1,0:T(8,128)(2,1)}) fusion(bf16[256,12,64]{0,2,1:T(8,128)(2,1)S(1)} %bitcast.199, bf16[320,12,64]{0,2,1:T(8,128)(2,1)S(1)} %concatenate.39, f32[12,320,256]{2,1,0:T(8,128)} %copy-done.2, f32[12,256]{1,0:T(8,128)S(1)} %log_add_fusion, pred[256,320]{0,1:T(8,128)(4,1)S(1)} %bitcast_and_fusion), kind=kOutput, calls=%fused_computation.38 | convolution fusion | flops 131724288 | bytes 5316608 | tf_op jit(solution)/shard_map/hrk,khd->rhd/dot_general | solution.py:74
  63.3 2.5 fusion.2
  73.4 2.3 collective-permute-start.29
  75.7 3.2 collective-permute-start.30
  78.9 3.5 %collective-permute-start.31 = (bf16[64,768]{1,0:T(8,128)(2,1)}, bf16[64,768]{1,0:T(8,128)(2,1)}, u32[]{:S(2)}, u32[]{:S(2)}) collective-permute-start(bf16[64,768]{1,0:T(8,128)(2,1)} %copy.236), channel_id=1, source_target_pairs={{0,4},{2,6},{4,8},{6,10},{8,12},{10,14},{12,16},{14,18},{16,20},{1... | collective-permute-start | bytes 294920 | tf_op jit(solution)/shard_map/ppermute | solution.py:17
  82.5 2.9 collective-permute-start.28
  87.1 5.3 %collective-permute-start.25 = (bf16[64,768]{1,0:T(8,128)(2,1)}, bf16[64,768]{1,0:T(8,128)(2,1)}, u32[]{:S(2)}, u32[]{:S(2)}) collective-permute-start(bf16[64,768]{1,0:T(8,128)(2,1)} %copy.228), channel_id=1, source_target_pairs={{2,0},{4,2},{6,4},{8,6},{10,8},{12,10},{14,12},{16,14},{18,16},{20... | collective-permute-start | bytes 294920 | tf_op jit(solution)/shard_map/ppermute | solution.py:17
  92.5 4.2 %all-to-all-start.2 = ((bf16[32,2,768]{2,0,1:T(8,128)(2,1)}), bf16[32,2,768]{2,0,1:T(8,128)(2,1)S(1)}, u32[]{:S(2)}, u32[]{:S(2)}) async-start(bf16[32,2,768]{2,0,1:T(8,128)(2,1)} %bitcast.201), calls=%async_computation.2 | async-start | bytes 196608 | tf_op jit(solution)/shard_map/all_to_all | solution.py:98
  114.5 4.9 %collective-permute-start.27 = (bf16[64,768]{1,0:T(8,128)(2,1)}, bf16[64,768]{1,0:T(8,128)(2,1)}, u32[]{:S(2)}, u32[]{:S(2)}) collective-permute-start(bf16[64,768]{1,0:T(8,128)(2,1)} %copy.230), channel_id=1, source_target_pairs={{0,4},{2,6},{4,8},{6,10},{8,12},{10,14},{12,16},{14,18},{16,20},{1... | collective-permute-start | bytes 294920 | tf_op jit(solution)/shard_map/ppermute | solution.py:17
  119.4 2.6 collective-permute-start.24
  123.9 6.7 %all-to-all-start.7 = ((bf16[2,32,768]{2,1,0:T(8,128)(2,1)}), bf16[2,32,768]{2,1,0:T(8,128)(2,1)}, u32[]{:S(2)}, u32[]{:S(2)}) async-start(bf16[2,32,768]{2,1,0:T(8,128)(2,1)} %bitcast.215), calls=%async_computation.7 | async-start | bytes 196608 | tf_op jit(solution)/shard_map/all_to_all | solution.py:215
  130.6 6.9 %collective-permute-start.14 = (bf16[256,768]{1,0:T(8,128)(2,1)}, bf16[256,768]{1,0:T(8,128)(2,1)}, u32[]{:S(2)}, u32[]{:S(2)}) collective-permute-start(bf16[256,768]{1,0:T(8,128)(2,1)} %param.11), channel_id=1, source_target_pairs={{2,0},{4,2},{6,4},{8,6},{10,8},{12,10},{14,12},{16,14},{18,16},{20... | collective-permute-start | bytes 1179656 | tf_op jit(solution)/shard_map/ppermute | solution.py:17
  139.4 2.5 collective-permute-start.12
  143.7 3.1 collective-permute-start.10
  148.6 7.6 %collective-permute-start.11 = (bf16[256,768]{1,0:T(8,128)(2,1)}, bf16[256,768]{1,0:T(8,128)(2,1)S(1)}, u32[]{:S(2)}, u32[]{:S(2)}) collective-permute-start(bf16[256,768]{1,0:T(8,128)(2,1)} %param.12), channel_id=1, source_target_pairs={{4,0},{6,2},{8,4},{10,6},{12,8},{14,10},{16,12},{18,14},{20,16},{2... | collective-permute-start | bytes 1179656 | tf_op jit(solution)/shard_map/ppermute | solution.py:17
  160.1 25.7 %collective-permute-start.15 = (bf16[256,768]{1,0:T(8,128)(2,1)S(1)}, bf16[256,768]{1,0:T(8,128)(2,1)}, u32[]{:S(2)}, u32[]{:S(2)}) collective-permute-start(bf16[256,768]{1,0:T(8,128)(2,1)S(1)} %copy-done.9), channel_id=1, source_target_pairs={{4,0},{6,2},{8,4},{10,6},{12,8},{14,10},{16,12},{18,14},{20,16},{2... | collective-permute-start | bytes 1179656 | tf_op jit(solution)/shard_map/ppermute | solution.py:17
  188.2 4.0 %copy.203 = bf16[1280,768]{0,1:T(8,128)(2,1)} copy(bf16[1280,768]{1,0:T(8,128)(2,1)} %constant_dynamic-update-slice_fusion) | data formatting | bytes 3932160 | tf_op jit(solution)/shard_map/concatenate | solution.py:117
  198.2 4.0 %copy.204 = bf16[1280,768]{0,1:T(8,128)(2,1)} copy(bf16[1280,768]{1,0:T(8,128)(2,1)} %constant_dynamic-update-slice_fusion.5) | data formatting | bytes 3932160 | tf_op jit(solution)/shard_map/concatenate | solution.py:117
  202.2 2.3 bitcast_reduce_fusion
  209.3 2.3 copy.223
  211.6 2.4 copy.222
  218.6 3.5 %collective-permute-start.22 = (f32[256,768]{1,0:T(8,128)}, f32[256,768]{1,0:T(8,128)}, u32[]{:S(2)}, u32[]{:S(2)}) collective-permute-start(f32[256,768]{1,0:T(8,128)} %copy.222), channel_id=1, source_target_pairs={{0,2},{2,4},{4,6},{6,8},{8,10},{10,12},{12,14},{14,16},{16,18},{18... | collective-permute-start | bytes 2359304 | tf_op jit(solution)/shard_map/ppermute | solution.py:17
  224.1 4.2 %multiply_reduce_fusion.1 = (f32[64,12]{0,1:T(8,128)S(1)}, bf16[64,12,64]{0,2,1:T(8,128)(2,1)}) fusion(bf16[64,12,64]{0,2,1:T(8,128)(2,1)} %copy-done.5, bf16[64]{0:T(256)(128)(2,1)S(1)} %fusion.31, f32[64]{0:T(128)} %compare_convert_fusion, bf16[1280,12,64]{0,2,1:T(8,128)(2,1)} %bitcast.162, f32[12,1280,64]{1,2,0:T(8,128)} %copy-done, ...), kind=kOutput, calls=%fused_computation.39 | convolution fusion | flops 129121536 | bytes 6102656 | tf_op jit(solution)/shard_map/hrk,khd->rhd/dot_general | solution.py:74
  228.3 2.6 fusion.9
  230.9 2.4 copy.219
  233.3 4.3 %collective-permute-start.20 = (f32[256,768]{1,0:T(8,128)}, f32[256,768]{1,0:T(8,128)}, u32[]{:S(2)}, u32[]{:S(2)}) collective-permute-start(f32[256,768]{1,0:T(8,128)} %copy.219), channel_id=1, source_target_pairs={{4,0},{6,2},{8,4},{10,6},{12,8},{14,10},{16,12},{18,14},{20,16},{2... | collective-permute-start | bytes 2359304 | tf_op jit(solution)/shard_map/ppermute | solution.py:17
  246.2 2.4 copy.217
  252.8 4.2 %all-to-all-start.6 = ((bf16[2,32,768]{2,1,0:T(8,128)(2,1)}), bf16[2,32,768]{2,1,0:T(8,128)(2,1)S(1)}, u32[]{:S(2)}, u32[]{:S(2)}) async-start(bf16[2,32,768]{2,1,0:T(8,128)(2,1)} %bitcast.57), calls=%async_computation.6 | async-start | bytes 196608 | tf_op jit(solution)/shard_map/all_to_all | solution.py:214
  257.1 4.2 %collective-permute-start.18 = (f32[256,768]{1,0:T(8,128)}, f32[256,768]{1,0:T(8,128)}, u32[]{:S(2)}, u32[]{:S(2)}) collective-permute-start(f32[256,768]{1,0:T(8,128)} %copy.217), channel_id=1, source_target_pairs={{0,2},{2,4},{4,6},{6,8},{8,10},{10,12},{12,14},{14,16},{16,18},{18... | collective-permute-start | bytes 2359304 | tf_op jit(solution)/shard_map/ppermute | solution.py:17
  263.2 34.2 %collective-permute-start.16 = (f32[256,768]{1,0:T(8,128)}, f32[256,768]{1,0:T(8,128)}, u32[]{:S(2)}, u32[]{:S(2)}) collective-permute-start(f32[256,768]{1,0:T(8,128)} %copy.214), channel_id=1, source_target_pairs={{4,0},{6,2},{8,4},{10,6},{12,8},{14,10},{16,12},{18,14},{20,16},{2... | collective-permute-start | bytes 2359304 | tf_op jit(solution)/shard_map/ppermute | solution.py:17
  297.4 3.5 fusion.17
  304.5 4.2 %all-to-all-start.5 = ((bf16[2,32,768]{2,1,0:T(8,128)(2,1)}), bf16[2,32,768]{2,1,0:T(8,128)(2,1)S(1)}, u32[]{:S(2)}, u32[]{:S(2)}) async-start(bf16[2,32,768]{2,1,0:T(8,128)(2,1)} %convert_element_type.178), calls=%async_computation.5 | async-start | bytes 196608 | tf_op jit(solution)/shard_map/all_to_all | solution.py:213
  312.4 10.7 %all-to-all-done.5 = bf16[2,32,768]{2,1,0:T(8,128)(2,1)S(1)} async-done(((bf16[2,32,768]{2,1,0:T(8,128)(2,1)}), bf16[2,32,768]{2,1,0:T(8,128)(2,1)S(1)}, u32[]{:S(2)}, u32[]{:S(2)}) %all-to-all-start.5) | async-done | bytes 98336 | tf_op jit(solution)/shard_map/all_to_all | solution.py:213
  323.1 7.3 %all-to-all-start.3 = ((bf16[2,32,768]{2,1,0:T(8,128)(2,1)}), bf16[2,32,768]{2,1,0:T(8,128)(2,1)}, u32[]{:S(2)}, u32[]{:S(2)}) async-start(bf16[2,32,768]{2,1,0:T(8,128)(2,1)} %convert_element_type.163), calls=%async_computation.3 | async-start | bytes 196608 | tf_op jit(solution)/shard_map/all_to_all | solution.py:212
  341.5 2.8 add_convert_fusion
  344.3 2.8 add_convert_fusion.1
  (164 shorter events, 109.5 us)
Async XLA Ops:
  2.2 9.9 %all-to-all-start.1 = ((bf16[32,2,768]{2,0,1:T(8,128)(2,1)}), bf16[32,2,768]{2,0,1:T(8,128)(2,1)S(1)}, u32[]{:S(2)}, u32[]{:S(2)}) async-start(bf16[32,2,768]{2,0,1:T(8,128)(2,1)} %bitcast.160), calls=%async_computation.1 | async-start | bytes 196608 | tf_op jit(solution)/shard_map/all_to_all | solution.py:99
  12.1 23.5 %all-to-all-start = ((bf16[32,2,768]{2,0,1:T(8,128)(2,1)}), bf16[32,2,768]{2,0,1:T(8,128)(2,1)S(1)}, u32[]{:S(2)}, u32[]{:S(2)}) async-start(bf16[32,2,768]{2,0,1:T(8,128)(2,1)} %bitcast.161), calls=%async_computation | async-start | bytes 196608 | tf_op jit(solution)/shard_map/all_to_all | solution.py:100
  16.3 26.9 %collective-permute-start.7 = (bf16[64,768]{1,0:T(8,128)(2,1)S(1)}, bf16[64,768]{1,0:T(8,128)(2,1)S(1)}, u32[]{:S(2)}, u32[]{:S(2)}) collective-permute-start(bf16[64,768]{1,0:T(8,128)(2,1)S(1)} %bitcast.204), channel_id=1, source_target_pairs={{4,0},{6,2},{8,4},{10,6},{12,8},{14,10},{16,12},{18,14},{20,16},{2... | collective-permute-start | bytes 294920 | tf_op jit(solution)/shard_map/ppermute | solution.py:17
  19.2 27.1 %collective-permute-start.6 = (bf16[64,768]{1,0:T(8,128)(2,1)S(1)}, bf16[64,768]{1,0:T(8,128)(2,1)S(1)}, u32[]{:S(2)}, u32[]{:S(2)}) collective-permute-start(bf16[64,768]{1,0:T(8,128)(2,1)S(1)} %bitcast.205), channel_id=1, source_target_pairs={{2,0},{4,2},{6,4},{8,6},{10,8},{12,10},{14,12},{16,14},{18,16},{20... | collective-permute-start | bytes 294920 | tf_op jit(solution)/shard_map/ppermute | solution.py:17
  23.0 26.1 %collective-permute-start.5 = (bf16[64,768]{1,0:T(8,128)(2,1)S(1)}, bf16[64,768]{1,0:T(8,128)(2,1)S(1)}, u32[]{:S(2)}, u32[]{:S(2)}) collective-permute-start(bf16[64,768]{1,0:T(8,128)(2,1)S(1)} %bitcast.206), channel_id=1, source_target_pairs={{0,2},{2,4},{4,6},{6,8},{8,10},{10,12},{12,14},{14,16},{16,18},{18... | collective-permute-start | bytes 294920 | tf_op jit(solution)/shard_map/ppermute | solution.py:17
  25.5 27.5 %collective-permute-start.4 = (bf16[64,768]{1,0:T(8,128)(2,1)S(1)}, bf16[64,768]{1,0:T(8,128)(2,1)S(1)}, u32[]{:S(2)}, u32[]{:S(2)}) collective-permute-start(bf16[64,768]{1,0:T(8,128)(2,1)S(1)} %bitcast.207), channel_id=1, source_target_pairs={{0,4},{2,6},{4,8},{6,10},{8,12},{10,14},{12,16},{14,18},{16,20},{1... | collective-permute-start | bytes 294920 | tf_op jit(solution)/shard_map/ppermute | solution.py:17
  35.6 56.8 %all-to-all-start.4 = ((bf16[32,2,768]{2,0,1:T(8,128)(2,1)}), bf16[32,2,768]{2,0,1:T(8,128)(2,1)}, u32[]{:S(2)}, u32[]{:S(2)}) async-start(bf16[32,2,768]{2,0,1:T(8,128)(2,1)} %bitcast.158), calls=%async_computation.4 | async-start | bytes 196608 | tf_op jit(solution)/shard_map/all_to_all | solution.py:101
  39.9 18.0 %collective-permute-start.3 = (bf16[64,768]{1,0:T(8,128)(2,1)S(1)}, bf16[64,768]{1,0:T(8,128)(2,1)S(1)}, u32[]{:S(2)}, u32[]{:S(2)}) collective-permute-start(bf16[64,768]{1,0:T(8,128)(2,1)S(1)} %bitcast.209), channel_id=1, source_target_pairs={{4,0},{6,2},{8,4},{10,6},{12,8},{14,10},{16,12},{18,14},{20,16},{2... | collective-permute-start | bytes 294920 | tf_op jit(solution)/shard_map/ppermute | solution.py:17
  43.2 14.8 %collective-permute-start.2 = (bf16[64,768]{1,0:T(8,128)(2,1)S(1)}, bf16[64,768]{1,0:T(8,128)(2,1)S(1)}, u32[]{:S(2)}, u32[]{:S(2)}) collective-permute-start(bf16[64,768]{1,0:T(8,128)(2,1)S(1)} %bitcast.211), channel_id=1, source_target_pairs={{2,0},{4,2},{6,4},{8,6},{10,8},{12,10},{14,12},{16,14},{18,16},{20... | collective-permute-start | bytes 294920 | tf_op jit(solution)/shard_map/ppermute | solution.py:17
  46.3 11.8 %collective-permute-start.1 = (bf16[64,768]{1,0:T(8,128)(2,1)S(1)}, bf16[64,768]{1,0:T(8,128)(2,1)S(1)}, u32[]{:S(2)}, u32[]{:S(2)}) collective-permute-start(bf16[64,768]{1,0:T(8,128)(2,1)S(1)} %bitcast.212), channel_id=1, source_target_pairs={{0,2},{2,4},{4,6},{6,8},{8,10},{10,12},{12,14},{14,16},{16,18},{18... | collective-permute-start | bytes 294920 | tf_op jit(solution)/shard_map/ppermute | solution.py:17
  49.1 9.2 %collective-permute-start = (bf16[64,768]{1,0:T(8,128)(2,1)S(1)}, bf16[64,768]{1,0:T(8,128)(2,1)S(1)}, u32[]{:S(2)}, u32[]{:S(2)}) collective-permute-start(bf16[64,768]{1,0:T(8,128)(2,1)S(1)} %bitcast.213), channel_id=1, source_target_pairs={{0,4},{2,6},{4,8},{6,10},{8,12},{10,14},{12,16},{14,18},{16,20},{1... | collective-permute-start | bytes 294920 | tf_op jit(solution)/shard_map/ppermute | solution.py:17
  54.5 3.4 copy-start.2
  59.0 4.3 %copy-start.8 = (bf16[320,12,64]{0,2,1:T(8,128)(2,1)}, bf16[320,12,64]{0,2,1:T(8,128)(2,1)S(1)}, u32[]{:S(2)}) copy-start(bf16[320,12,64]{0,2,1:T(8,128)(2,1)S(1)} %concatenate.39) | copy-start | bytes 1474564
  59.0 4.2 %copy-start.3 = (f32[12,320,256]{2,1,0:T(8,128)S(1)}, f32[12,320,256]{2,1,0:T(8,128)}, u32[]{:S(2)}) copy-start(f32[12,320,256]{2,1,0:T(8,128)} %copy-done.2) | copy-start | bytes 11796484
  73.4 34.7 %collective-permute-start.29 = (bf16[64,768]{1,0:T(8,128)(2,1)}, bf16[64,768]{1,0:T(8,128)(2,1)}, u32[]{:S(2)}, u32[]{:S(2)}) collective-permute-start(bf16[64,768]{1,0:T(8,128)(2,1)} %copy.234), channel_id=1, source_target_pairs={{2,0},{4,2},{6,4},{8,6},{10,8},{12,10},{14,12},{16,14},{18,16},{20... | collective-permute-start | bytes 294920 | tf_op jit(solution)/shard_map/ppermute | solution.py:17
  75.7 34.4 %collective-permute-start.30 = (bf16[64,768]{1,0:T(8,128)(2,1)}, bf16[64,768]{1,0:T(8,128)(2,1)}, u32[]{:S(2)}, u32[]{:S(2)}) collective-permute-start(bf16[64,768]{1,0:T(8,128)(2,1)} %copy.235), channel_id=1, source_target_pairs={{0,2},{2,4},{4,6},{6,8},{8,10},{10,12},{12,14},{14,16},{16,18},{18... | collective-permute-start | bytes 294920 | tf_op jit(solution)/shard_map/ppermute | solution.py:17
  78.9 33.3 %collective-permute-start.31 = (bf16[64,768]{1,0:T(8,128)(2,1)}, bf16[64,768]{1,0:T(8,128)(2,1)}, u32[]{:S(2)}, u32[]{:S(2)}) collective-permute-start(bf16[64,768]{1,0:T(8,128)(2,1)} %copy.236), channel_id=1, source_target_pairs={{0,4},{2,6},{4,8},{6,10},{8,12},{10,14},{12,16},{14,18},{16,20},{1... | collective-permute-start | bytes 294920 | tf_op jit(solution)/shard_map/ppermute | solution.py:17
  82.5 32.0 %collective-permute-start.28 = (bf16[64,768]{1,0:T(8,128)(2,1)}, bf16[64,768]{1,0:T(8,128)(2,1)}, u32[]{:S(2)}, u32[]{:S(2)}) collective-permute-start(bf16[64,768]{1,0:T(8,128)(2,1)} %copy.232), channel_id=1, source_target_pairs={{4,0},{6,2},{8,4},{10,6},{12,8},{14,10},{16,12},{18,14},{20,16},{2... | collective-permute-start | bytes 294920 | tf_op jit(solution)/shard_map/ppermute | solution.py:17
  87.1 32.3 %collective-permute-start.25 = (bf16[64,768]{1,0:T(8,128)(2,1)}, bf16[64,768]{1,0:T(8,128)(2,1)}, u32[]{:S(2)}, u32[]{:S(2)}) collective-permute-start(bf16[64,768]{1,0:T(8,128)(2,1)} %copy.228), channel_id=1, source_target_pairs={{2,0},{4,2},{6,4},{8,6},{10,8},{12,10},{14,12},{16,14},{18,16},{20... | collective-permute-start | bytes 294920 | tf_op jit(solution)/shard_map/ppermute | solution.py:17
  92.5 7.0 %all-to-all-start.2 = ((bf16[32,2,768]{2,0,1:T(8,128)(2,1)}), bf16[32,2,768]{2,0,1:T(8,128)(2,1)S(1)}, u32[]{:S(2)}, u32[]{:S(2)}) async-start(bf16[32,2,768]{2,0,1:T(8,128)(2,1)} %bitcast.201), calls=%async_computation.2 | async-start | bytes 196608 | tf_op jit(solution)/shard_map/all_to_all | solution.py:98
  99.5 105.9 %copy-start.5 = (bf16[64,12,64]{0,2,1:T(8,128)(2,1)}, bf16[64,12,64]{0,2,1:T(8,128)(2,1)S(1)}, u32[]{:S(2)}) copy-start(bf16[64,12,64]{0,2,1:T(8,128)(2,1)S(1)} %copy.211) | copy-start | bytes 294916
  108.0 52.1 %copy-start.9 = (bf16[256,768]{1,0:T(8,128)(2,1)S(1)}, bf16[256,768]{1,0:T(8,128)(2,1)}, u32[]{:S(2)}) copy-start(bf16[256,768]{1,0:T(8,128)(2,1)} %param.11) | copy-start | bytes 1179652
  108.0 40.5 %collective-permute-start.9 = (bf16[256,768]{1,0:T(8,128)(2,1)}, bf16[256,768]{1,0:T(8,128)(2,1)}, u32[]{:S(2)}, u32[]{:S(2)}) collective-permute-start(bf16[256,768]{1,0:T(8,128)(2,1)} %param.12), channel_id=1, source_target_pairs={{0,2},{2,4},{4,6},{6,8},{8,10},{10,12},{12,14},{14,16},{16,18},{18... | collective-permute-start | bytes 1179656 | tf_op jit(solution)/shard_map/ppermute | solution.py:17
  110.1 33.6 %collective-permute-start.8 = (bf16[256,768]{1,0:T(8,128)(2,1)}, bf16[256,768]{1,0:T(8,128)(2,1)}, u32[]{:S(2)}, u32[]{:S(2)}) collective-permute-start(bf16[256,768]{1,0:T(8,128)(2,1)} %param.12), channel_id=1, source_target_pairs={{0,4},{2,6},{4,8},{6,10},{8,12},{10,14},{12,16},{14,18},{16,20},{1... | collective-permute-start | bytes 1179656 | tf_op jit(solution)/shard_map/ppermute | solution.py:17
  112.3 18.3 %collective-permute-start.26 = (bf16[64,768]{1,0:T(8,128)(2,1)}, bf16[64,768]{1,0:T(8,128)(2,1)}, u32[]{:S(2)}, u32[]{:S(2)}) collective-permute-start(bf16[64,768]{1,0:T(8,128)(2,1)} %copy.229), channel_id=1, source_target_pairs={{0,2},{2,4},{4,6},{6,8},{8,10},{10,12},{12,14},{14,16},{16,18},{18... | collective-permute-start | bytes 294920 | tf_op jit(solution)/shard_map/ppermute | solution.py:17
  114.5 23.0 %collective-permute-start.27 = (bf16[64,768]{1,0:T(8,128)(2,1)}, bf16[64,768]{1,0:T(8,128)(2,1)}, u32[]{:S(2)}, u32[]{:S(2)}) collective-permute-start(bf16[64,768]{1,0:T(8,128)(2,1)} %copy.230), channel_id=1, source_target_pairs={{0,4},{2,6},{4,8},{6,10},{8,12},{10,14},{12,16},{14,18},{16,20},{1... | collective-permute-start | bytes 294920 | tf_op jit(solution)/shard_map/ppermute | solution.py:17
  119.4 20.0 %collective-permute-start.24 = (bf16[64,768]{1,0:T(8,128)(2,1)}, bf16[64,768]{1,0:T(8,128)(2,1)}, u32[]{:S(2)}, u32[]{:S(2)}) collective-permute-start(bf16[64,768]{1,0:T(8,128)(2,1)} %copy.226), channel_id=1, source_target_pairs={{4,0},{6,2},{8,4},{10,6},{12,8},{14,10},{16,12},{18,14},{20,16},{2... | collective-permute-start | bytes 294920 | tf_op jit(solution)/shard_map/ppermute | solution.py:17
  123.9 128.9 %all-to-all-start.7 = ((bf16[2,32,768]{2,1,0:T(8,128)(2,1)}), bf16[2,32,768]{2,1,0:T(8,128)(2,1)}, u32[]{:S(2)}, u32[]{:S(2)}) async-start(bf16[2,32,768]{2,1,0:T(8,128)(2,1)} %bitcast.215), calls=%async_computation.7 | async-start | bytes 196608 | tf_op jit(solution)/shard_map/all_to_all | solution.py:215
  130.6 64.1 %collective-permute-start.14 = (bf16[256,768]{1,0:T(8,128)(2,1)}, bf16[256,768]{1,0:T(8,128)(2,1)}, u32[]{:S(2)}, u32[]{:S(2)}) collective-permute-start(bf16[256,768]{1,0:T(8,128)(2,1)} %param.11), channel_id=1, source_target_pairs={{2,0},{4,2},{6,4},{8,6},{10,8},{12,10},{14,12},{16,14},{18,16},{20... | collective-permute-start | bytes 1179656 | tf_op jit(solution)/shard_map/ppermute | solution.py:17
  137.5 54.6 %collective-permute-start.13 = (bf16[256,768]{1,0:T(8,128)(2,1)}, bf16[256,768]{1,0:T(8,128)(2,1)}, u32[]{:S(2)}, u32[]{:S(2)}) collective-permute-start(bf16[256,768]{1,0:T(8,128)(2,1)} %param.11), channel_id=1, source_target_pairs={{0,2},{2,4},{4,6},{6,8},{8,10},{10,12},{12,14},{14,16},{16,18},{18... | collective-permute-start | bytes 1179656 | tf_op jit(solution)/shard_map/ppermute | solution.py:17
  139.4 20.6 %collective-permute-start.12 = (bf16[256,768]{1,0:T(8,128)(2,1)}, bf16[256,768]{1,0:T(8,128)(2,1)S(1)}, u32[]{:S(2)}, u32[]{:S(2)}) collective-permute-start(bf16[256,768]{1,0:T(8,128)(2,1)} %param.11), channel_id=1, source_target_pairs={{0,4},{2,6},{4,8},{6,10},{8,12},{10,14},{12,16},{14,18},{16,20},{1... | collective-permute-start | bytes 1179656 | tf_op jit(solution)/shard_map/ppermute | solution.py:17
  143.7 42.9 %collective-permute-start.10 = (bf16[256,768]{1,0:T(8,128)(2,1)}, bf16[256,768]{1,0:T(8,128)(2,1)S(1)}, u32[]{:S(2)}, u32[]{:S(2)}) collective-permute-start(bf16[256,768]{1,0:T(8,128)(2,1)} %param.12), channel_id=1, source_target_pairs={{2,0},{4,2},{6,4},{8,6},{10,8},{12,10},{14,12},{16,14},{18,16},{20... | collective-permute-start | bytes 1179656 | tf_op jit(solution)/shard_map/ppermute | solution.py:17
  148.6 38.8 %collective-permute-start.11 = (bf16[256,768]{1,0:T(8,128)(2,1)}, bf16[256,768]{1,0:T(8,128)(2,1)S(1)}, u32[]{:S(2)}, u32[]{:S(2)}) collective-permute-start(bf16[256,768]{1,0:T(8,128)(2,1)} %param.12), channel_id=1, source_target_pairs={{4,0},{6,2},{8,4},{10,6},{12,8},{14,10},{16,12},{18,14},{20,16},{2... | collective-permute-start | bytes 1179656 | tf_op jit(solution)/shard_map/ppermute | solution.py:17
  160.1 36.4 %collective-permute-start.15 = (bf16[256,768]{1,0:T(8,128)(2,1)S(1)}, bf16[256,768]{1,0:T(8,128)(2,1)}, u32[]{:S(2)}, u32[]{:S(2)}) collective-permute-start(bf16[256,768]{1,0:T(8,128)(2,1)S(1)} %copy-done.9), channel_id=1, source_target_pairs={{4,0},{6,2},{8,4},{10,6},{12,8},{14,10},{16,12},{18,14},{20,16},{2... | collective-permute-start | bytes 1179656 | tf_op jit(solution)/shard_map/ppermute | solution.py:17
  216.3 12.0 %copy-start.1 = (f32[12,1280,64]{1,2,0:T(8,128)S(1)}, f32[12,1280,64]{1,2,0:T(8,128)}, u32[]{:S(2)}) copy-start(f32[12,1280,64]{1,2,0:T(8,128)} %copy-done) | copy-start | bytes 11796484
  216.3 12.0 %copy-start.4 = (bf16[1280,768]{0,1:T(8,128)(2,1)S(1)}, bf16[1280,768]{0,1:T(8,128)(2,1)}, u32[]{:S(2)}) copy-start(bf16[1280,768]{0,1:T(8,128)(2,1)} %copy.203) | copy-start | bytes 5898244
  216.3 12.0 %copy-start.6 = (bf16[64,12,64]{0,2,1:T(8,128)(2,1)S(1)}, bf16[64,12,64]{0,2,1:T(8,128)(2,1)}, u32[]{:S(2)}) copy-start(bf16[64,12,64]{0,2,1:T(8,128)(2,1)} %copy-done.5) | copy-start | bytes 294916
  216.3 40.8 %collective-permute-start.21 = (f32[256,768]{1,0:T(8,128)}, f32[256,768]{1,0:T(8,128)}, u32[]{:S(2)}, u32[]{:S(2)}) collective-permute-start(f32[256,768]{1,0:T(8,128)} %copy.221), channel_id=1, source_target_pairs={{2,0},{4,2},{6,4},{8,6},{10,8},{12,10},{14,12},{16,14},{18,16},{20... | collective-permute-start | bytes 2359304 | tf_op jit(solution)/shard_map/ppermute | solution.py:17
  218.6 42.7 %collective-permute-start.22 = (f32[256,768]{1,0:T(8,128)}, f32[256,768]{1,0:T(8,128)}, u32[]{:S(2)}, u32[]{:S(2)}) collective-permute-start(f32[256,768]{1,0:T(8,128)} %copy.222), channel_id=1, source_target_pairs={{0,2},{2,4},{4,6},{6,8},{8,10},{10,12},{12,14},{14,16},{16,18},{18... | collective-permute-start | bytes 2359304 | tf_op jit(solution)/shard_map/ppermute | solution.py:17
  222.1 41.1 %collective-permute-start.23 = (f32[256,768]{1,0:T(8,128)}, f32[256,768]{1,0:T(8,128)}, u32[]{:S(2)}, u32[]{:S(2)}) collective-permute-start(f32[256,768]{1,0:T(8,128)} %copy.223), channel_id=1, source_target_pairs={{0,4},{2,6},{4,8},{6,10},{8,12},{10,14},{12,16},{14,18},{16,20},{1... | collective-permute-start | bytes 2359304 | tf_op jit(solution)/shard_map/ppermute | solution.py:17
  233.3 108.2 %collective-permute-start.20 = (f32[256,768]{1,0:T(8,128)}, f32[256,768]{1,0:T(8,128)}, u32[]{:S(2)}, u32[]{:S(2)}) collective-permute-start(f32[256,768]{1,0:T(8,128)} %copy.219), channel_id=1, source_target_pairs={{4,0},{6,2},{8,4},{10,6},{12,8},{14,10},{16,12},{18,14},{20,16},{2... | collective-permute-start | bytes 2359304 | tf_op jit(solution)/shard_map/ppermute | solution.py:17
  250.9 93.4 %collective-permute-start.17 = (f32[256,768]{1,0:T(8,128)}, f32[256,768]{1,0:T(8,128)}, u32[]{:S(2)}, u32[]{:S(2)}) collective-permute-start(f32[256,768]{1,0:T(8,128)} %copy.216), channel_id=1, source_target_pairs={{2,0},{4,2},{6,4},{8,6},{10,8},{12,10},{14,12},{16,14},{18,16},{20... | collective-permute-start | bytes 2359304 | tf_op jit(solution)/shard_map/ppermute | solution.py:17
  252.8 51.7 %all-to-all-start.6 = ((bf16[2,32,768]{2,1,0:T(8,128)(2,1)}), bf16[2,32,768]{2,1,0:T(8,128)(2,1)S(1)}, u32[]{:S(2)}, u32[]{:S(2)}) async-start(bf16[2,32,768]{2,1,0:T(8,128)(2,1)} %bitcast.57), calls=%async_computation.6 | async-start | bytes 196608 | tf_op jit(solution)/shard_map/all_to_all | solution.py:214
  257.1 87.2 %collective-permute-start.18 = (f32[256,768]{1,0:T(8,128)}, f32[256,768]{1,0:T(8,128)}, u32[]{:S(2)}, u32[]{:S(2)}) collective-permute-start(f32[256,768]{1,0:T(8,128)} %copy.217), channel_id=1, source_target_pairs={{0,2},{2,4},{4,6},{6,8},{8,10},{10,12},{12,14},{14,16},{16,18},{18... | collective-permute-start | bytes 2359304 | tf_op jit(solution)/shard_map/ppermute | solution.py:17
  261.3 83.0 %collective-permute-start.19 = (f32[256,768]{1,0:T(8,128)}, f32[256,768]{1,0:T(8,128)}, u32[]{:S(2)}, u32[]{:S(2)}) collective-permute-start(f32[256,768]{1,0:T(8,128)} %copy.218), channel_id=1, source_target_pairs={{0,4},{2,6},{4,8},{6,10},{8,12},{10,14},{12,16},{14,18},{16,20},{1... | collective-permute-start | bytes 2359304 | tf_op jit(solution)/shard_map/ppermute | solution.py:17
  263.2 81.1 %collective-permute-start.16 = (f32[256,768]{1,0:T(8,128)}, f32[256,768]{1,0:T(8,128)}, u32[]{:S(2)}, u32[]{:S(2)}) collective-permute-start(f32[256,768]{1,0:T(8,128)} %copy.214), channel_id=1, source_target_pairs={{4,0},{6,2},{8,4},{10,6},{12,8},{14,10},{16,12},{18,14},{20,16},{2... | collective-permute-start | bytes 2359304 | tf_op jit(solution)/shard_map/ppermute | solution.py:17
  304.5 18.6 %all-to-all-start.5 = ((bf16[2,32,768]{2,1,0:T(8,128)(2,1)}), bf16[2,32,768]{2,1,0:T(8,128)(2,1)S(1)}, u32[]{:S(2)}, u32[]{:S(2)}) async-start(bf16[2,32,768]{2,1,0:T(8,128)(2,1)} %convert_element_type.178), calls=%async_computation.5 | async-start | bytes 196608 | tf_op jit(solution)/shard_map/all_to_all | solution.py:213
  323.1 16.9 %all-to-all-start.3 = ((bf16[2,32,768]{2,1,0:T(8,128)(2,1)}), bf16[2,32,768]{2,1,0:T(8,128)(2,1)}, u32[]{:S(2)}, u32[]{:S(2)}) async-start(bf16[2,32,768]{2,1,0:T(8,128)(2,1)} %convert_element_type.163), calls=%async_computation.3 | async-start | bytes 196608 | tf_op jit(solution)/shard_map/all_to_all | solution.py:212
  (2 other events, 3.7 us)
where the time goes:
time: 351 us; the launch traced here: 347 us
  starting transfers between devices  197 us (56%)
  local copies, waits for them, and re-layouts  94.9 us (27%)
  matrix products  28.5 us (8%)
  other arithmetic  14 us (4%)
  waiting for transfers between devices  11.1 us (3%)
    ppermute x32, starting transfers between devices, from_behind(): lax.ppermute(value, axis, [(source, source + steps) for source in range(l...  158 us
    slice x18, local copies, waits for them, and re-layouts, rows_of(): lax.slice_in_dim(tensor, (window_shift + reach_dev) * size, (window_shift...  29.1 us
    unnamed x32, local copies, waits for them, and re-layouts  18.7 us
    concatenate x10, local copies, waits for them, and re-layouts, nearby_row_span(): jnp.concatenate([pieces[window_shift] for window_shift in range(-reach_de...  12.2 us
    all_to_all x1, waiting for transfers between devices, body(): lax.all_to_all(dq_aud.astype(jnp.bfloat16), 'aud', split_axis=0, concat_a...  10.7 us
    dot_general x2, matrix products, full_attention(): jnp.einsum('hrk,khd->rhd', weights_b, split_heads(value_rows), preferred_...  8.44 us
    all_to_all x1, starting transfers between devices, body(): lax.all_to_all(out_aud, 'aud', split_axis=0, concat_axis=1, tiled=True)  7.25 us
  transfers between devices with their start and end apart: 40, of which 2 were waited for; matrix products, arithmetic and copies ran while one was open for 38% of the time, Pallas kernels for 0%

commit v1 on v0

v1 whole, which is shorter than its diff:
```python
import jax
import jax.numpy as jnp
from jax import lax
from jax.experimental import pallas as pl
from jax.experimental.pallas import tpu as pltpu
from jax.sharding import PartitionSpec as P

HD = 64
BLK = 64
WMAX = 3
PAIR = 2 * HD
NEG = -1e30
BF = jnp.bfloat16
F32 = jnp.float32

NPOS = 6
KEYS = NPOS * BLK


def nt(x, y):
    return lax.dot_general(x, y, (((1,), (1,)), ((), ())), preferred_element_type=F32)


def nn(x, y):
    return lax.dot_general(x, y, (((1,), (0,)), ((), ())), preferred_element_type=F32)


def coords(idx_ref):
    idx = idx_ref[0]
    return idx >> 2, (idx >> 1) & 1, idx & 1


def head_part(x, e):
    lane = lax.broadcasted_iota(jnp.int32, x.shape, 1)
    return jnp.where((lane < HD) if e == 0 else (lane >= HD), x, jnp.zeros_like(x))


def pack_kernel(idx_ref, len_ref, *refs):
    mine, other, keep, send = refs[:4], refs[4:8], refs[8], refs[9]
    c, r, a = coords(idx_ref)
    half, quarter = keep.shape[2], keep.shape[3]
    row = lax.broadcasted_iota(jnp.int32, (half, quarter), 0) + a * half
    for slot, arrays in ((r, mine), (1 - r, other)):
        valid = row < len_ref[2 * c + slot]
        for n, ref in enumerate(arrays):
            for part, out in ((a, keep), (1 - a, send)):
                col = pl.multiple_of((2 * part + r) * quarter, 128)
                x = ref[:, pl.ds(col, quarter)]
                if n == 0:
                    x = x * jnp.asarray(HD**-0.5, BF)
                if n == 1:
                    x = jnp.where(valid, x, jnp.zeros_like(x))
                out[n, slot] = x


def piece_rows(idx_ref):
    c, _, a = coords(idx_ref)
    half = BLK // 2
    side = 2 - 2 * (c & 1)
    starts = []
    for place, part in ((1, a), (1, 1 - a), (side, a), (side, 1 - a), (2 - side, a), (2 - side, 1 - a)):
        first = place * 2 * BLK + part * half
        starts.append([pl.multiple_of(first + core * BLK, half) for core in range(2)])
    return starts


def gather_audio(idx_ref, pieces, dst):
    half = BLK // 2
    for ref, firsts in zip(pieces, piece_rows(idx_ref)):
        for core, first in enumerate(firsts):
            for n in range(2):
                dst[n, pl.ds(first, half), :] = ref[n, core]


def scatter_audio(idx_ref, src, pieces):
    half = BLK // 2
    for ref, firsts in zip(pieces, piece_rows(idx_ref)):
        for core, first in enumerate(firsts):
            for n in range(2):
                ref[n, core] = src[n, pl.ds(first, half), :].astype(ref.dtype)


def window_bounds(win_ref, c, stretch, shape, axis):
    block = lax.broadcasted_iota(jnp.int32, shape, axis) // BLK
    lo = jnp.zeros(shape, jnp.int32)
    hi = jnp.zeros(shape, jnp.int32)
    for b in range(4):
        start = win_ref[4 * stretch + b, 0] - (2 * c - 2)
        count = win_ref[4 * stretch + b, 1]
        lo = jnp.where(block == b, start, lo)
        hi = jnp.where(block == b, start + count, hi)
    return lo, hi


def av_bias(idx_ref, win_ref, bias):
    c, r, _ = coords(idx_ref)
    for i, stretch in enumerate((r, 1 - r)):
        shape = bias.shape[1:]
        lo, hi = window_bounds(win_ref, c, stretch, shape, 0)
        place = lax.broadcasted_iota(jnp.int32, shape, 1) // BLK
        bias[i] = jnp.where((place >= lo) & (place < hi), 0.0, NEG)


def va_bias(idx_ref, win_ref, len_ref, bias):
    c, r, _ = coords(idx_ref)
    shape = bias.shape[1:]
    row = lax.broadcasted_iota(jnp.int32, shape, 0)
    place = row // BLK
    length = jnp.zeros(shape, jnp.int32)
    for j in range(NPOS):
        block = jnp.clip(2 * c - 2 + j, 0, len_ref.shape[0] - 1)
        length = jnp.where(place == j, len_ref[block], length)
    valid = (row % BLK) < length
    for i, stretch in enumerate((r, 1 - r)):
        lo, hi = window_bounds(win_ref, c, stretch, shape, 1)
        bias[i] = jnp.where((place >= lo) & (place < hi) & valid, 0.0, NEG)


def stats_kernel(idx_ref, win_ref, *refs):
    pieces = refs[:6]
    video = ((refs[6], refs[7]), (refs[8], refs[9]))
    stat_ref, audio, bias = refs[10:]

    @pl.when(pl.program_id(0) == 0)
    def _():
        av_bias(idx_ref, win_ref, bias)

    gather_audio(idx_ref, pieces, audio)
    queries, cot = audio[0], audio[1]
    lses, deltas = [], []
    for e in range(2):
        parts = []
        for i, (k_ref, v_ref) in enumerate(video):
            s = nt(head_part(k_ref[...], e), queries) + bias[i]
            m = jnp.max(s, axis=0, keepdims=True)
            ex = jnp.exp(s - m)
            dp = nt(head_part(v_ref[...], e), cot)
            parts.append((m, jnp.sum(ex, axis=0, keepdims=True), jnp.sum(ex * dp, axis=0, keepdims=True)))
        m = jnp.maximum(parts[0][0], parts[1][0])
        w0, w1 = jnp.exp(parts[0][0] - m), jnp.exp(parts[1][0] - m)
        total = parts[0][1] * w0 + parts[1][1] * w1
        lses.append(m + jnp.log(total))
        deltas.append((parts[0][2] * w0 + parts[1][2] * w1) / total)
    stat_ref[0] = jnp.concatenate(lses + deltas + lses + deltas, axis=0)


def merge_stats(idx_ref, chips, own, by_a, by_b, before2, after2):
    c, _, _ = coords(idx_ref)
    even = (c & 1) == 0
    before = jnp.where(even, by_b, by_a)
    after = jnp.where(even, by_a, by_b)
    w = 2 * BLK

    def part(x, k, there):
        x = x[:, k * w : (k + 1) * w]
        return jnp.where(there, x[0:2], NEG), x[2:4]

    one, two = c >= 1, c >= 2
    nxt, nxt2 = c + 1 < chips, c + 2 < chips
    always = c >= 0
    groups = (
        (part(own, 0, always), part(before, 1, one), part(before2, 2, two)),
        (part(own, 1, always), part(before, 2, one), part(after, 0, nxt)),
        (part(own, 2, always), part(after, 1, nxt), part(after2, 0, nxt2)),
    )
    lses, deltas = [], []
    for group in groups:
        m = jnp.maximum(jnp.maximum(group[0][0], group[1][0]), group[2][0])
        ws = [jnp.exp(lse - m) for lse, _ in group]
        total = ws[0] + ws[1] + ws[2]
        lses.append(m + jnp.log(total))
        deltas.append(sum(wt * d for wt, (_, d) in zip(ws, group)) / total)
    return jnp.concatenate(lses, axis=1), jnp.concatenate(deltas, axis=1)


def va_kernel(idx_ref, win_ref, len_ref, *refs):
    pieces = refs[:6]
    video = ((refs[6], refs[7]), (refs[8], refs[9]))
    outs = ((refs[10], refs[11]), (refs[12], refs[13]))
    back = refs[14:20]
    audio, bias, grads = refs[20:]

    @pl.when(pl.program_id(0) == 0)
    def _():
        va_bias(idx_ref, win_ref, len_ref, bias)

    gather_audio(idx_ref, pieces, audio)
    keys, values = audio[0], audio[1]
    keys_t, values_t = keys.T, values.T
    k_heads = [head_part(keys, e) for e in range(2)]
    v_heads = [head_part(values, e) for e in range(2)]
    dk, dv = None, None
    for i, ((q_ref, g_ref), (out_ref, dq_ref)) in enumerate(zip(video, outs)):
        q = q_ref[...] * jnp.asarray(HD**-0.5, BF)
        g = g_ref[...]
        out_t, dq_t = [], []
        for e in range(2):
            s = nt(k_heads[e], q) + bias[i]
            m = jnp.max(s, axis=0, keepdims=True)
            ex = jnp.exp(s - m)
            p = ex * (1.0 / jnp.sum(ex, axis=0, keepdims=True))
            pb = p.astype(BF)
            dp = nt(v_heads[e], g)
            delta = jnp.sum(p * dp, axis=0, keepdims=True)
            ds = (p * (dp - delta)).astype(BF)
            dk_e, dv_e = nn(ds, head_part(q, e)), nn(pb, head_part(g, e))
            dk = dk_e if dk is None else dk + dk_e
            dv = dv_e if dv is None else dv + dv_e
            out_t.append(nn(values_t[e * HD : (e + 1) * HD], pb))
            dq_t.append(nn(keys_t[e * HD : (e + 1) * HD], ds))
        out_ref[...] = jnp.concatenate(out_t, axis=0).T.astype(BF)
        dq_ref[...] = (jnp.concatenate(dq_t, axis=0).T * HD**-0.5).astype(BF)
    grads[0] = dk
    grads[1] = dv
    scatter_audio(idx_ref, grads, back)


def av_kernel(chips, idx_ref, win_ref, *refs):
    pieces = refs[:6]
    video = ((refs[6], refs[7]), (refs[8], refs[9]))
    stats = [ref[0] for ref in refs[10:15]]
    outs = ((refs[21], refs[22]), (refs[23], refs[24]))
    back = refs[25:31]
    audio, bias, grads = refs[31:]

    @pl.when(pl.program_id(0) == 0)
    def _():
        av_bias(idx_ref, win_ref, bias)

    gather_audio(idx_ref, pieces, audio)
    queries, cot = audio[0], audio[1]
    q_heads = [head_part(queries, e) for e in range(2)]
    g_heads = [head_part(cot, e) for e in range(2)]
    lse, delta = merge_stats(idx_ref, chips, *stats)
    dq_t, out_t = [None, None], [None, None]
    for i, ((k_ref, v_ref), (dk_ref, dv_ref)) in enumerate(zip(video, outs)):
        keys, values = k_ref[...], v_ref[...]
        keys_t, values_t = keys.T, values.T
        dk, dv = None, None
        for e in range(2):
            s = nt(head_part(keys, e), queries) + bias[i]
            p = jnp.exp(s - lse[e : e + 1])
            pb = p.astype(BF)
            dp = nt(head_part(values, e), cot)
            ds = (p * (dp - delta[e : e + 1])).astype(BF)
            dk_e, dv_e = nn(ds, q_heads[e]), nn(pb, g_heads[e])
            dk = dk_e if dk is None else dk + dk_e
            dv = dv_e if dv is None else dv + dv_e
            dq_e = nn(keys_t[e * HD : (e + 1) * HD], ds)
            out_e = nn(values_t[e * HD : (e + 1) * HD], pb)
            dq_t[e] = dq_e if i == 0 else dq_t[e] + dq_e
            out_t[e] = out_e if i == 0 else out_t[e] + out_e
        dk_ref[...] = dk.astype(BF)
        dv_ref[...] = dv.astype(BF)
    grads[0] = jnp.concatenate(dq_t, axis=0).T * HD**-0.5
    grads[1] = jnp.concatenate(out_t, axis=0).T
    scatter_audio(idx_ref, grads, back)


def sum_kernel(idx_ref, len_ref, keep, by_aud, by_a, by_ax, by_b, by_bx, mine, other):
    c, r, a = coords(idx_ref)
    half, quarter = keep.shape[2], keep.shape[3]
    row = lax.broadcasted_iota(jnp.int32, (half, quarter), 0) + a * half
    for slot, out in ((r, mine), (1 - r, other)):
        valid = row < len_ref[2 * c + slot]
        for part, parts in ((a, (keep, by_a, by_b)), (1 - a, (by_aud, by_ax, by_bx))):
            for n in range(4):
                x = sum(ref[n, slot].astype(F32) for ref in parts)
                if n == 3:
                    x = jnp.where(valid, x, 0.0)
                out[n, part] = x.astype(BF)


def join_audio_kernel(idx_ref, mine, other, *outs):
    _, r, _ = coords(idx_ref)
    quarter = mine.shape[3]
    for n, out in enumerate(outs):
        for part in range(2):
            for core, ref in ((r, mine), (1 - r, other)):
                col = pl.multiple_of((2 * part + core) * quarter, 128)
                out[:, pl.ds(col, quarter)] = ref[n, part]


def join_video_kernel(idx_ref, *refs):
    for src, out in zip(refs[4:8], refs[8:12]):
        out[...] = src[...]


def cost(flops, transcendentals, nbytes):
    return pl.CostEstimate(flops=flops, transcendentals=transcendentals, bytes_accessed=nbytes)


def make_body(mesh):
    nv = mesh.shape["vid"]
    chips = nv // 2
    everyone = [(v, a) for v in range(nv) for a in range(2)]

    def perm(move):
        pairs = []
        for v, a in everyone:
            w, b = move(v, a)
            if 0 <= w < nv:
                pairs.append((2 * v + a, 2 * w + b))
        return pairs

    def diagonal(v):
        return 2 * ((((v >> 1) + 1) ^ 1) - 1) + (v & 1)

    moves = {
        "core": perm(lambda v, a: (v ^ 1, a)),
        "aud": perm(lambda v, a: (v, 1 - a)),
        "A": perm(lambda v, a: (v ^ 2, a)),
        "Ax": perm(lambda v, a: (v ^ 2, 1 - a)),
        "B": perm(lambda v, a: (diagonal(v), a)),
        "Bx": perm(lambda v, a: (diagonal(v), 1 - a)),
        "p2": perm(lambda v, a: (v + 4, a)),
        "m2": perm(lambda v, a: (v - 4, a)),
    }

    def move(x, name):
        return lax.ppermute(x, ("vid", "aud"), moves[name])

    def body(q_v, k_v, v_v, g_v, q_a, k_a, v_a, g_a, window, audio_len):
        rows, width = q_v.shape
        quarter = width // 2
        half = q_a.shape[0]
        steps = quarter // PAIR
        idx = jnp.reshape(2 * lax.axis_index("vid") + lax.axis_index("aud"), (1,)).astype(jnp.int32)
        shape = jax.ShapeDtypeStruct

        smem = pl.BlockSpec(memory_space=pltpu.SMEM)
        win_spec = pl.BlockSpec((8, 2), lambda h, i: (i[0] >> 2, 0), memory_space=pltpu.SMEM)
        len_spec = pl.BlockSpec(memory_space=pltpu.SMEM)

        def piece_spec(n):
            return pl.BlockSpec((2, 2, half, PAIR), lambda h, i: (n, 0, 0, h))

        own_spec = pl.BlockSpec((rows, PAIR), lambda h, i: (0, ((i[0] >> 1) & 1) * steps + h))
        far_spec = pl.BlockSpec((rows, PAIR), lambda h, i: (0, h))
        join_spec = pl.BlockSpec((rows, PAIR), lambda h, i: (0, (1 - ((i[0] >> 1) & 1)) * steps + h))
        stat_spec = pl.BlockSpec((1, 8, KEYS), lambda h, i: (h, 0, 0))
        any_spec = pl.BlockSpec(memory_space=pl.ANY)

        def call(kernel, name, ins, outs, args, grid=(steps,), scratch=(), aliases=None, est=None):
            return pl.pallas_call(
                kernel,
                name=name,
                grid_spec=pltpu.PrefetchScalarGridSpec(
                    num_scalar_prefetch=1,
                    grid=grid,
                    in_specs=ins,
                    out_specs=[s for s, _ in outs],
                    scratch_shapes=list(scratch),
                ),
                out_shape=[o for _, o in outs],
                input_output_aliases=aliases or {},
                cost_estimate=est,
            )(idx, *args)

        audio = (q_a, g_a, k_a, v_a)
        audio_other = [move(x, "core") for x in audio]
        piece = shape((4, 2, half, quarter), BF)
        whole = pl.BlockSpec(memory_space=pltpu.VMEM)
        keep, send = call(
            pack_kernel, "pack", [smem] + [whole] * 8, [(whole, piece)] * 2, (audio_len, *audio, *audio_other), grid=(),
            est=cost(0, 0, 1200000),
        )
        pieces = [
            keep,
            move(send, "aud"),
            move(keep, "A"),
            move(send, "Ax"),
            move(keep, "B"),
            move(send, "Bx"),
        ]
        q_f, k_f, v_f, g_f = [move(x, "core") for x in (q_v, k_v, v_v, g_v)]

        audio_scratch = pltpu.VMEM((2, KEYS, PAIR), BF)
        grad_scratch = pltpu.VMEM((2, KEYS, PAIR), F32)
        pairs = 2 * steps * 2 * rows * KEYS

        stat = shape((steps, 8, KEYS), F32)
        (stats,) = call(
            stats_kernel,
            "stats",
            [win_spec] + [piece_spec(0)] * 6 + [own_spec] * 4,
            [(stat_spec, stat)],
            (window, *pieces, k_v, v_v, k_f, v_f),
            scratch=(audio_scratch, pltpu.VMEM((2, rows, KEYS), F32)),
            est=cost(4 * HD * pairs, pairs, 3000000),
        )
        others = [move(stats, name) for name in ("A", "B", "p2", "m2")]

        full, far = shape((rows, width), BF), shape((rows, quarter), BF)
        va = call(
            va_kernel,
            "va",
            [win_spec, len_spec] + [piece_spec(1)] * 6 + [own_spec] * 4,
            [(own_spec, full)] * 2 + [(far_spec, far)] * 2 + [(piece_spec(0), piece)] * 6,
            (window, audio_len, *pieces, q_v, g_v, q_f, g_f),
            scratch=(audio_scratch, pltpu.VMEM((2, KEYS, rows), F32), grad_scratch),
            est=cost(10 * HD * pairs, pairs, 5000000),
        )
        out_video, dq_video, out_far, dq_far = va[:4]
        av = call(
            lambda *refs: av_kernel(chips, *refs),
            "av",
            [win_spec] + [piece_spec(0)] * 6 + [own_spec] * 4 + [stat_spec] * 5 + [any_spec] * 6,
            [(own_spec, full)] * 2 + [(far_spec, far)] * 2 + [(piece_spec(1), piece)] * 6,
            (window, *pieces, k_v, v_v, k_f, v_f, stats, *others, *va[4:]),
            scratch=(audio_scratch, pltpu.VMEM((2, rows, KEYS), F32), grad_scratch),
            aliases={17 + i: 4 + i for i in range(6)},
            est=cost(12 * HD * pairs, pairs, 5000000),
        )
        dk_video, dv_video, dk_far, dv_far = av[:4]
        back = av[4:]
        parts = [back[0]] + [move(x, name) for x, name in zip(back[1:], ("aud", "A", "Ax", "B", "Bx"))]

        fars = [move(x, "core") for x in (out_far, dq_far, dk_far, dv_far)]
        out_video, dq_video, dk_video, dv_video = call(
            join_video_kernel,
            "join_video",
            [any_spec] * 4 + [far_spec] * 4,
            [(join_spec, full)] * 4,
            (out_video, dq_video, dk_video, dv_video, *fars),
            aliases={1 + i: i for i in range(4)},
            est=cost(0, 0, 1600000),
        )
        mine, other = call(
            sum_kernel, "sum_audio", [smem] + [whole] * 6, [(whole, piece_q(piece))] * 2, (audio_len, *parts), grid=(),
            est=cost(1000000, 0, 1600000),
        )
        other = move(other, "core")
        dk_audio, dv_audio, dq_audio, out_audio = call(
            join_audio_kernel,
            "join_audio",
            [whole] * 2,
            [(whole, shape((half, 2 * width), BF))] * 4,
            (mine, other),
            grid=(),
            est=cost(0, 0, 800000),
        )
        return (out_video, out_audio, dq_video, dk_video, dv_video, dq_audio, dk_audio, dv_audio)

    return body


def piece_q(piece):
    return jax.ShapeDtypeStruct((4, 2) + piece.shape[2:], piece.dtype)


def solution(mesh):
    video, audio = P("vid", "aud"), P(("vid", "aud"), None)
    return jax.shard_map(
        make_body(mesh),
        mesh=mesh,
        in_specs=(video,) * 4 + (audio,) * 4 + (P(), P()),
        out_specs=(video, audio, video, video, video, audio, audio, audio),
        check_vma=False,
    )
```

time: 351 us -> 106 us (0.30)
  the two profiles are of different devices: /device:TPU:141 before, /device:TPU:127 now
where the time goes in v1:
time: 106 us; the launch traced here: 105 us
  starting transfers between devices  50.7 us (48%)
  Pallas kernels  30.4 us (29%)
  waiting for transfers between devices  16.1 us (15%)
  local copies, waits for them, and re-layouts  7.06 us (7%)
    ppermute x27, starting transfers between devices, move(): return lax.ppermute(x, ('vid', 'aud'), moves[name])  50.7 us
    pallas_call x7, Pallas kernels, call(): pl.pallas_call(kernel, name=name, grid_spec=pltpu.PrefetchScalarGridSpec(...  30.4 us
    ppermute x27, waiting for transfers between devices, move(): return lax.ppermute(x, ('vid', 'aud'), moves[name])  16.1 us
    unnamed x65, local copies, waits for them, and re-layouts  7.06 us
  transfers between devices with their start and end apart: 27, of which 9 were waited for; matrix products, arithmetic and copies ran while one was open for 1% of the time, Pallas kernels for 18%

profile of v1, /device:TPU:127, one launch (start us, length us, event | category | flops | bytes accessed | tf_op | source)
XLA Modules:
  0.0 105.3 jit_solution(2771816972699077238)
XLA Ops:
  0.6 0.8 collective-permute-start
  1.5 0.4 collective-permute-start.3
  2.0 0.5 collective-permute-done.refs_4_
  2.6 0.4 collective-permute-done.2.refs_6_
  3.1 0.4 collective-permute-done.1.refs_5_
  3.5 0.2 copy-done.23
  3.7 0.4 copy-done.24
  4.1 2.1 %pack.1 = (bf16[4,2,32,384]{3,2,1,0:T(8,128)(2,1)}, bf16[4,2,32,384]{3,2,1,0:T(8,128)(2,1)}) custom-call(s32[1]{0:T(128)} %bitcast.idx_ref.refs_0_, s32[128]{0:T(128)} %len_ref.5, bf16[32,1536]{1,0:T(8,128)(2,1)} %refs_0_.1, bf16[32,1536]{1,0:T(8,128)(2,1)} %refs_1_.2, bf16[32,1536]{1,0:T(8,128)(2,1)} %refs_2_.1, bf16[32,1536]{1,0:T(8,128)(2,1)} %refs_3_.1, ...), custom_call_target="tpu_custom_call" | custom-call | bytes 1200000 | tf_op jit(solution)/shard_map/pack/pallas_call | solution.py:345
  6.1 4.3 %collective-permute-start.8 = (bf16[4,2,32,384]{3,2,1,0:T(8,128)(2,1)}, bf16[4,2,32,384]{3,2,1,0:T(8,128)(2,1)S(1)}, u32[]{:S(2)}, u32[]{:S(2)}) collective-permute-start(bf16[4,2,32,384]{3,2,1,0:T(8,128)(2,1)} %get-tuple-element.41), channel_id=1, source_target_pairs={{4,9},{5,8},{6,11},{7,10},{8,5},{9,4},{10,7},{11,6},{12,17},{13,16... | collective-permute-start | bytes 589832 | tf_op jit(solution)/shard_map/ppermute | solution.py:321
  10.5 0.5 collective-permute-start.6
  11.0 1.8 %collective-permute-start.4 = (bf16[4,2,32,384]{3,2,1,0:T(8,128)(2,1)}, bf16[4,2,32,384]{3,2,1,0:T(8,128)(2,1)S(1)}, u32[]{:S(2)}, u32[]{:S(2)}) collective-permute-start(bf16[4,2,32,384]{3,2,1,0:T(8,128)(2,1)} %get-tuple-element.41), channel_id=1, source_target_pairs={{0,1},{1,0},{2,3},{3,2},{4,5},{5,4},{6,7},{7,6},{8,9},{9,8},{10,11... | collective-permute-start | bytes 589832 | tf_op jit(solution)/shard_map/ppermute | solution.py:321
  12.8 0.7 collective-permute-start.11
  13.5 4.8 %collective-permute-start.7 = (bf16[4,2,32,384]{3,2,1,0:T(8,128)(2,1)}, bf16[4,2,32,384]{3,2,1,0:T(8,128)(2,1)S(1)}, u32[]{:S(2)}, u32[]{:S(2)}) collective-permute-start(bf16[4,2,32,384]{3,2,1,0:T(8,128)(2,1)} %get-tuple-element.40.refs_0_.refs_2_), channel_id=1, source_target_pairs={{4,8},{5,9},{6,10},{7,11},{8,4},{9,5},{10,6},{11,7},{12,16},{13,17... | collective-permute-start | bytes 589832 | tf_op jit(solution)/shard_map/ppermute | solution.py:321
  18.3 3.7 %collective-permute-done.8.refs_5_.refs_7_ = bf16[4,2,32,384]{3,2,1,0:T(8,128)(2,1)S(1)} collective-permute-done((bf16[4,2,32,384]{3,2,1,0:T(8,128)(2,1)}, bf16[4,2,32,384]{3,2,1,0:T(8,128)(2,1)S(1)}, u32[]{:S(2)}, u32[]{:S(2)}) %collective-permute-start.8) | collective-permute-done | bytes 196640 | tf_op jit(solution)/shard_map/ppermute | solution.py:321
  22.1 1.7 %collective-permute-start.12 = (bf16[256,768]{1,0:T(8,128)(2,1)S(1)}, bf16[256,768]{1,0:T(8,128)(2,1)S(1)}, u32[]{:S(2)}, u32[]{:S(2)}) collective-permute-start(bf16[256,768]{1,0:T(8,128)(2,1)S(1)} %copy-done.6), channel_id=1, source_target_pairs={{0,2},{1,3},{2,0},{3,1},{4,6},{5,7},{6,4},{7,5},{8,10},{9,11},{10,... | collective-permute-start | bytes 1179656 | tf_op jit(solution)/shard_map/ppermute | solution.py:321
  23.7 0.6 collective-permute-done.6.refs_3_.refs_5_
  24.4 1.0 collective-permute-start.9
  25.5 1.2 %collective-permute-done.7.refs_4_.refs_6_ = bf16[4,2,32,384]{3,2,1,0:T(8,128)(2,1)S(1)} collective-permute-done((bf16[4,2,32,384]{3,2,1,0:T(8,128)(2,1)}, bf16[4,2,32,384]{3,2,1,0:T(8,128)(2,1)S(1)}, u32[]{:S(2)}, u32[]{:S(2)}) %collective-permute-start.7) | collective-permute-done | bytes 196640 | tf_op jit(solution)/shard_map/ppermute | solution.py:321
  26.7 0.9 copy.28.win_ref.refs_1_
  27.5 4.8 %collective-permute-done.5.refs_2_.refs_4_ = bf16[4,2,32,384]{3,2,1,0:T(8,128)(2,1)S(1)} collective-permute-done((bf16[4,2,32,384]{3,2,1,0:T(8,128)(2,1)}, bf16[4,2,32,384]{3,2,1,0:T(8,128)(2,1)S(1)}, u32[]{:S(2)}, u32[]{:S(2)}) %collective-permute-start.5) | collective-permute-done | bytes 196640 | tf_op jit(solution)/shard_map/ppermute | solution.py:321
  32.4 0.6 copy-done.4
  33.2 0.8 copy-done.8
  34.0 4.4 %stats.1.refs_12_ = f32[3,8,384]{2,1,0:T(8,128)} custom-call(s32[1]{0:T(128)} %bitcast.idx_ref.refs_0_, s32[512,2]{1,0:T(8,128)} %copy.28.win_ref.refs_1_, bf16[4,2,32,384]{3,2,1,0:T(8,128)(2,1)} %get-tuple-element.40.refs_0_.refs_2_, bf16[4,2,32,384]{3,2,1,0:T(8,128)(2,1)} %copy-done.2, bf16[4,2,32,384]{3,2,1,0:T(8,128)(2,1)} %copy-done.4, ...), custom_call_target="tpu_custom_call" | custom-call | flops 301989888 | bytes 3000000 | tf_op jit(solution)/shard_map/stats/pallas_call | solution.py:345
  38.4 1.9 %collective-permute-start.16 = (f32[3,8,384]{2,1,0:T(8,128)}, f32[3,8,384]{2,1,0:T(8,128)S(1)}, u32[]{:S(2)}, u32[]{:S(2)}) collective-permute-start(f32[3,8,384]{2,1,0:T(8,128)} %stats.1.refs_12_), channel_id=1, source_target_pairs={{8,0},{9,1},{10,2},{11,3},{12,4},{13,5},{14,6},{15,7},{16,8},{17,9... | collective-permute-start | bytes 110600 | tf_op jit(solution)/shard_map/ppermute | solution.py:321
  40.3 6.7 %collective-permute-start.15 = (f32[3,8,384]{2,1,0:T(8,128)}, f32[3,8,384]{2,1,0:T(8,128)S(1)}, u32[]{:S(2)}, u32[]{:S(2)}) collective-permute-start(f32[3,8,384]{2,1,0:T(8,128)} %stats.1.refs_12_), channel_id=1, source_target_pairs={{0,8},{1,9},{2,10},{3,11},{4,12},{5,13},{6,14},{7,15},{8,16},{9,17... | collective-permute-start | bytes 110600 | tf_op jit(solution)/shard_map/ppermute | solution.py:321
  47.0 2.1 %collective-permute-start.14 = (f32[3,8,384]{2,1,0:T(8,128)}, f32[3,8,384]{2,1,0:T(8,128)S(1)}, u32[]{:S(2)}, u32[]{:S(2)}) collective-permute-start(f32[3,8,384]{2,1,0:T(8,128)} %stats.1.refs_12_), channel_id=1, source_target_pairs={{4,8},{5,9},{6,10},{7,11},{8,4},{9,5},{10,6},{11,7},{12,16},{13,17... | collective-permute-start | bytes 110600 | tf_op jit(solution)/shard_map/ppermute | solution.py:321
  49.1 0.3 collective-permute-start.13
  49.5 0.4 copy-done.9
  49.9 0.7 copy-done.10
  50.6 9.8 %va.1 = (bf16[256,768]{1,0:T(8,128)(2,1)}, bf16[256,768]{1,0:T(8,128)(2,1)}, bf16[256,384]{1,0:T(8,128)(2,1)}, bf16[256,384]{1,0:T(8,128)(2,1)}, bf16[4,2,32,384...) custom-call(s32[1]{0:T(128)} %bitcast.idx_ref.refs_0_, ...), custom_call_target="tpu_custom_call" | custom-call | flops 754974720 | bytes 5000000 | tf_op jit(solution)/shard_map/va/pallas_call | solution.py:345
  60.5 0.5 copy-done.25
  61.1 7.4 %av.1 = (bf16[256,768]{1,0:T(8,128)(2,1)}, bf16[256,768]{1,0:T(8,128)(2,1)}, bf16[256,384]{1,0:T(8,128)(2,1)}, bf16[256,384]{1,0:T(8,128)(2,1)}, bf16[4,2,32,384...) custom-call(s32[1]{0:T(128)} %bitcast.idx_ref.refs_0_, ...), custom_call_target="tpu_custom_call", output_to_operand_aliasing={{4}: (17, {}), {5}: (18, {}), {6}: (19, {}), {7}: (20, {}),... | custom-call | flops 905969664 | bytes 5000000 | tf_op jit(solution)/shard_map/av/pallas_call | solution.py:345
  68.5 1.0 collective-permute-start.21
  69.4 0.5 collective-permute-start.22
  69.9 2.1 %collective-permute-start.23 = (bf16[4,2,32,384]{3,2,1,0:T(8,128)(2,1)}, bf16[4,2,32,384]{3,2,1,0:T(8,128)(2,1)S(1)}, u32[]{:S(2)}, u32[]{:S(2)}) collective-permute-start(bf16[4,2,32,384]{3,2,1,0:T(8,128)(2,1)} %get-tuple-element.60), channel_id=1, source_target_pairs={{0,5},{1,4},{2,7},{3,6},{4,1},{5,0},{6,3},{7,2},{8,13},{9,12},{10,... | collective-permute-start | bytes 589832 | tf_op jit(solution)/shard_map/ppermute | solution.py:321
  72.0 7.2 %collective-permute-start.24 = (bf16[4,2,32,384]{3,2,1,0:T(8,128)(2,1)}, bf16[4,2,32,384]{3,2,1,0:T(8,128)(2,1)S(1)}, u32[]{:S(2)}, u32[]{:S(2)}) collective-permute-start(bf16[4,2,32,384]{3,2,1,0:T(8,128)(2,1)} %get-tuple-element.61), channel_id=1, source_target_pairs={{4,8},{5,9},{6,10},{7,11},{8,4},{9,5},{10,6},{11,7},{12,16},{13,17... | collective-permute-start | bytes 589832 | tf_op jit(solution)/shard_map/ppermute | solution.py:321
  79.2 2.3 %collective-permute-start.25 = (bf16[4,2,32,384]{3,2,1,0:T(8,128)(2,1)}, bf16[4,2,32,384]{3,2,1,0:T(8,128)(2,1)S(1)}, u32[]{:S(2)}, u32[]{:S(2)}) collective-permute-start(bf16[4,2,32,384]{3,2,1,0:T(8,128)(2,1)} %get-tuple-element.62), channel_id=1, source_target_pairs={{4,9},{5,8},{6,11},{7,10},{8,5},{9,4},{10,7},{11,6},{12,17},{13,16... | collective-permute-start | bytes 589832 | tf_op jit(solution)/shard_map/ppermute | solution.py:321
  81.6 3.6 %collective-permute-start.17 = (bf16[256,384]{1,0:T(8,128)(2,1)S(1)}, bf16[256,384]{1,0:T(8,128)(2,1)S(1)}, u32[]{:S(2)}, u32[]{:S(2)}) collective-permute-start(bf16[256,384]{1,0:T(8,128)(2,1)S(1)} %copy-done.31), channel_id=1, source_target_pairs={{0,2},{1,3},{2,0},{3,1},{4,6},{5,7},{6,4},{7,5},{8,10},{9,11},{10,... | collective-permute-start | bytes 589832 | tf_op jit(solution)/shard_map/ppermute | solution.py:321
  85.3 0.5 collective-permute-start.19
  85.8 1.2 %collective-permute-start.20 = (bf16[256,384]{1,0:T(8,128)(2,1)}, bf16[256,384]{1,0:T(8,128)(2,1)S(1)}, u32[]{:S(2)}, u32[]{:S(2)}) collective-permute-start(bf16[256,384]{1,0:T(8,128)(2,1)} %get-tuple-element.55), channel_id=1, source_target_pairs={{0,2},{1,3},{2,0},{3,1},{4,6},{5,7},{6,4},{7,5},{8,10},{9,11},{10,... | collective-permute-start | bytes 589832 | tf_op jit(solution)/shard_map/ppermute | solution.py:321
  87.0 4.3 %collective-permute-done.25.by_bx = bf16[4,2,32,384]{3,2,1,0:T(8,128)(2,1)S(1)} collective-permute-done((bf16[4,2,32,384]{3,2,1,0:T(8,128)(2,1)}, bf16[4,2,32,384]{3,2,1,0:T(8,128)(2,1)S(1)}, u32[]{:S(2)}, u32[]{:S(2)}) %collective-permute-start.25) | collective-permute-done | bytes 196640 | tf_op jit(solution)/shard_map/ppermute | solution.py:321
  91.3 0.7 copy-done.20
  91.9 2.2 %sum_audio.1 = (bf16[4,2,32,384]{3,2,1,0:T(8,128)(2,1)}, bf16[4,2,32,384]{3,2,1,0:T(8,128)(2,1)}) custom-call(s32[1]{0:T(128)} %bitcast.idx_ref.refs_0_, s32[128]{0:T(128)} %len_ref.5, bf16[4,2,32,384]{3,2,1,0:T(8,128)(2,1)} %get-tuple-element.57.keep, bf16[4,2,32,384]{3,2,1,0:T(8,128)(2,1)} %copy-done.16, bf16[4,2,32,384]{3,2,1,0:T(8,128)(2,1)} %copy-done.17, ...), custom_call_target="tpu_custom_call" | custom-call | flops 1000000 | bytes 1600000 | tf_op jit(solution)/shard_map/sum_audio/pallas_call | solution.py:345
  94.2 4.9 %collective-permute-start.26 = (bf16[4,2,32,384]{3,2,1,0:T(8,128)(2,1)}, bf16[4,2,32,384]{3,2,1,0:T(8,128)(2,1)S(1)}, u32[]{:S(2)}, u32[]{:S(2)}) collective-permute-start(bf16[4,2,32,384]{3,2,1,0:T(8,128)(2,1)} %get-tuple-element.64), channel_id=1, source_target_pairs={{0,2},{1,3},{2,0},{3,1},{4,6},{5,7},{6,4},{7,5},{8,10},{9,11},{10,... | collective-permute-start | bytes 589832 | tf_op jit(solution)/shard_map/ppermute | solution.py:321
  99.2 0.6 copy-done.11
  100.0 2.8 %join_video.1 = (bf16[256,768]{1,0:T(8,128)(2,1)}, bf16[256,768]{1,0:T(8,128)(2,1)}, bf16[256,768]{1,0:T(8,128)(2,1)}, bf16[256,768]{1,0:T(8,128)(2,1)}) custom-call(s32[1]{0:T(128)} %bitcast.idx_ref.refs_0_, bf16[256,768]{1,0:T(8,128)(2,1)} %get-tuple-element.42.refs_0_, ...), custom_call_target="tpu_custom_call", output_to_operand_aliasing={{0}: (1, {}), {1}: (2, {}), {2}: (3, {}), {3}: (4, {})} | custom-call | bytes 1600000 | tf_op jit(solution)/shard_map/join_video/pallas_call | solution.py:345
  102.8 0.7 copy-done.15
  103.5 1.8 %join_audio.1 = (bf16[32,1536]{1,0:T(8,128)(2,1)}, bf16[32,1536]{1,0:T(8,128)(2,1)}, bf16[32,1536]{1,0:T(8,128)(2,1)}, bf16[32,1536]{1,0:T(8,128)(2,1)}) custom-call(s32[1]{0:T(128)} %bitcast.idx_ref.refs_0_, bf16[4,2,32,384]{3,2,1,0:T(8,128)(2,1)} %get-tuple-element.63.mine, bf16[4,2,32,384]{3,2,1,0:T(8,128)(2,1)} %copy-done.15), custom_call_target="tpu_custom_call" | custom-call | bytes 800000 | tf_op jit(solution)/shard_map/join_audio/pallas_call | solution.py:345
  (78 shorter events, 1.3 us)
Async XLA Ops:
  0.6 1.9 %collective-permute-start = (bf16[32,1536]{1,0:T(8,128)(2,1)}, bf16[32,1536]{1,0:T(8,128)(2,1)S(1)}, u32[]{:S(2)}, u32[]{:S(2)}) collective-permute-start(bf16[32,1536]{1,0:T(8,128)(2,1)} %refs_0_.1), channel_id=1, source_target_pairs={{0,2},{1,3},{2,0},{3,1},{4,6},{5,7},{6,4},{7,5},{8,10},{9,11},{10,... | collective-permute-start | bytes 294920 | tf_op jit(solution)/shard_map/ppermute | solution.py:321
  1.4 1.5 %collective-permute-start.2 = (bf16[32,1536]{1,0:T(8,128)(2,1)}, bf16[32,1536]{1,0:T(8,128)(2,1)S(1)}, u32[]{:S(2)}, u32[]{:S(2)}) collective-permute-start(bf16[32,1536]{1,0:T(8,128)(2,1)} %refs_2_.1), channel_id=1, source_target_pairs={{0,2},{1,3},{2,0},{3,1},{4,6},{5,7},{6,4},{7,5},{8,10},{9,11},{10,... | collective-permute-start | bytes 294920 | tf_op jit(solution)/shard_map/ppermute | solution.py:321
  1.5 1.6 %collective-permute-start.3 = (bf16[32,1536]{1,0:T(8,128)(2,1)}, bf16[32,1536]{1,0:T(8,128)(2,1)S(1)}, u32[]{:S(2)}, u32[]{:S(2)}) collective-permute-start(bf16[32,1536]{1,0:T(8,128)(2,1)} %refs_3_.1), channel_id=1, source_target_pairs={{0,2},{1,3},{2,0},{3,1},{4,6},{5,7},{6,4},{7,5},{8,10},{9,11},{10,... | collective-permute-start | bytes 294920 | tf_op jit(solution)/shard_map/ppermute | solution.py:321
  1.9 1.5 %collective-permute-start.1 = (bf16[32,1536]{1,0:T(8,128)(2,1)}, bf16[32,1536]{1,0:T(8,128)(2,1)S(1)}, u32[]{:S(2)}, u32[]{:S(2)}) collective-permute-start(bf16[32,1536]{1,0:T(8,128)(2,1)} %refs_1_.2), channel_id=1, source_target_pairs={{0,2},{1,3},{2,0},{3,1},{4,6},{5,7},{6,4},{7,5},{8,10},{9,11},{10,... | collective-permute-start | bytes 294920 | tf_op jit(solution)/shard_map/ppermute | solution.py:321
  2.6 0.9 copy-start.21
  4.1 8.7 %copy-start.5 = (bf16[256,768]{1,0:T(8,128)(2,1)S(1)}, bf16[256,768]{1,0:T(8,128)(2,1)}, u32[]{:S(2)}) copy-start(bf16[256,768]{1,0:T(8,128)(2,1)} %refs_8_.1) | copy-start | bytes 1179652
  4.1 18.0 %copy-start.6 = (bf16[256,768]{1,0:T(8,128)(2,1)S(1)}, bf16[256,768]{1,0:T(8,128)(2,1)}, u32[]{:S(2)}) copy-start(bf16[256,768]{1,0:T(8,128)(2,1)} %refs_9_.1) | copy-start | bytes 1179652
  4.1 22.6 %copy-start.29 = (s32[512,2]{0,1:T(2,128)S(1)}, s32[512,2]{0,1:T(2,128)}, u32[]{:S(2)}) copy-start(s32[512,2]{0,1:T(2,128)} %param.18) | copy-start | bytes 12292
  6.1 15.9 %collective-permute-start.8 = (bf16[4,2,32,384]{3,2,1,0:T(8,128)(2,1)}, bf16[4,2,32,384]{3,2,1,0:T(8,128)(2,1)S(1)}, u32[]{:S(2)}, u32[]{:S(2)}) collective-permute-start(bf16[4,2,32,384]{3,2,1,0:T(8,128)(2,1)} %get-tuple-element.41), channel_id=1, source_target_pairs={{4,9},{5,8},{6,11},{7,10},{8,5},{9,4},{10,7},{11,6},{12,17},{13,16... | collective-permute-start | bytes 589832 | tf_op jit(solution)/shard_map/ppermute | solution.py:321
  10.5 13.9 %collective-permute-start.6 = (bf16[4,2,32,384]{3,2,1,0:T(8,128)(2,1)}, bf16[4,2,32,384]{3,2,1,0:T(8,128)(2,1)S(1)}, u32[]{:S(2)}, u32[]{:S(2)}) collective-permute-start(bf16[4,2,32,384]{3,2,1,0:T(8,128)(2,1)} %get-tuple-element.41), channel_id=1, source_target_pairs={{0,5},{1,4},{2,7},{3,6},{4,1},{5,0},{6,3},{7,2},{8,13},{9,12},{10,... | collective-permute-start | bytes 589832 | tf_op jit(solution)/shard_map/ppermute | solution.py:321
  11.0 14.4 %collective-permute-start.4 = (bf16[4,2,32,384]{3,2,1,0:T(8,128)(2,1)}, bf16[4,2,32,384]{3,2,1,0:T(8,128)(2,1)S(1)}, u32[]{:S(2)}, u32[]{:S(2)}) collective-permute-start(bf16[4,2,32,384]{3,2,1,0:T(8,128)(2,1)} %get-tuple-element.41), channel_id=1, source_target_pairs={{0,1},{1,0},{2,3},{3,2},{4,5},{5,4},{6,7},{7,6},{8,9},{9,8},{10,11... | collective-permute-start | bytes 589832 | tf_op jit(solution)/shard_map/ppermute | solution.py:321
  12.8 19.6 %collective-permute-start.11 = (bf16[256,768]{1,0:T(8,128)(2,1)S(1)}, bf16[256,768]{1,0:T(8,128)(2,1)S(1)}, u32[]{:S(2)}, u32[]{:S(2)}) collective-permute-start(bf16[256,768]{1,0:T(8,128)(2,1)S(1)} %copy-done.5), channel_id=1, source_target_pairs={{0,2},{1,3},{2,0},{3,1},{4,6},{5,7},{6,4},{7,5},{8,10},{9,11},{10,... | collective-permute-start | bytes 1179656 | tf_op jit(solution)/shard_map/ppermute | solution.py:321
  13.5 13.2 %collective-permute-start.7 = (bf16[4,2,32,384]{3,2,1,0:T(8,128)(2,1)}, bf16[4,2,32,384]{3,2,1,0:T(8,128)(2,1)S(1)}, u32[]{:S(2)}, u32[]{:S(2)}) collective-permute-start(bf16[4,2,32,384]{3,2,1,0:T(8,128)(2,1)} %get-tuple-element.40.refs_0_.refs_2_), channel_id=1, source_target_pairs={{4,8},{5,9},{6,10},{7,11},{8,4},{9,5},{10,6},{11,7},{12,16},{13,17... | collective-permute-start | bytes 589832 | tf_op jit(solution)/shard_map/ppermute | solution.py:321
  22.1 10.3 %copy-start = (bf16[4,2,32,384]{3,2,1,0:T(8,128)(2,1)}, bf16[4,2,32,384]{3,2,1,0:T(8,128)(2,1)S(1)}, u32[]{:S(2)}) copy-start(bf16[4,2,32,384]{3,2,1,0:T(8,128)(2,1)S(1)} %collective-permute-done.8.refs_5_.refs_7_) | copy-start | bytes 589828
  22.1 10.3 %collective-permute-start.12 = (bf16[256,768]{1,0:T(8,128)(2,1)S(1)}, bf16[256,768]{1,0:T(8,128)(2,1)S(1)}, u32[]{:S(2)}, u32[]{:S(2)}) collective-permute-start(bf16[256,768]{1,0:T(8,128)(2,1)S(1)} %copy-done.6), channel_id=1, source_target_pairs={{0,2},{1,3},{2,0},{3,1},{4,6},{5,7},{6,4},{7,5},{8,10},{9,11},{10,... | collective-permute-start | bytes 1179656 | tf_op jit(solution)/shard_map/ppermute | solution.py:321
  24.4 8.0 %copy-start.1 = (bf16[4,2,32,384]{3,2,1,0:T(8,128)(2,1)}, bf16[4,2,32,384]{3,2,1,0:T(8,128)(2,1)S(1)}, u32[]{:S(2)}) copy-start(bf16[4,2,32,384]{3,2,1,0:T(8,128)(2,1)S(1)} %collective-permute-done.6.refs_3_.refs_5_) | copy-start | bytes 589828
  24.4 24.8 %collective-permute-start.9 = (bf16[256,768]{1,0:T(8,128)(2,1)}, bf16[256,768]{1,0:T(8,128)(2,1)S(1)}, u32[]{:S(2)}, u32[]{:S(2)}) collective-permute-start(bf16[256,768]{1,0:T(8,128)(2,1)} %refs_6_.2), channel_id=1, source_target_pairs={{0,2},{1,3},{2,0},{3,1},{4,6},{5,7},{6,4},{7,5},{8,10},{9,11},{10,... | collective-permute-start | bytes 1179656 | tf_op jit(solution)/shard_map/ppermute | solution.py:321
  25.4 7.0 %copy-start.2 = (bf16[4,2,32,384]{3,2,1,0:T(8,128)(2,1)}, bf16[4,2,32,384]{3,2,1,0:T(8,128)(2,1)S(1)}, u32[]{:S(2)}) copy-start(bf16[4,2,32,384]{3,2,1,0:T(8,128)(2,1)S(1)} %collective-permute-done.4.refs_1_.refs_3_) | copy-start | bytes 589828
  25.4 24.1 %collective-permute-start.10 = (bf16[256,768]{1,0:T(8,128)(2,1)}, bf16[256,768]{1,0:T(8,128)(2,1)S(1)}, u32[]{:S(2)}, u32[]{:S(2)}) collective-permute-start(bf16[256,768]{1,0:T(8,128)(2,1)} %refs_7_.2), channel_id=1, source_target_pairs={{0,2},{1,3},{2,0},{3,1},{4,6},{5,7},{6,4},{7,5},{8,10},{9,11},{10,... | collective-permute-start | bytes 1179656 | tf_op jit(solution)/shard_map/ppermute | solution.py:321
  26.7 5.7 %copy-start.3 = (bf16[4,2,32,384]{3,2,1,0:T(8,128)(2,1)}, bf16[4,2,32,384]{3,2,1,0:T(8,128)(2,1)S(1)}, u32[]{:S(2)}) copy-start(bf16[4,2,32,384]{3,2,1,0:T(8,128)(2,1)S(1)} %collective-permute-done.7.refs_4_.refs_6_) | copy-start | bytes 589828
  26.7 5.7 %collective-permute-start.5 = (bf16[4,2,32,384]{3,2,1,0:T(8,128)(2,1)}, bf16[4,2,32,384]{3,2,1,0:T(8,128)(2,1)S(1)}, u32[]{:S(2)}, u32[]{:S(2)}) collective-permute-start(bf16[4,2,32,384]{3,2,1,0:T(8,128)(2,1)} %get-tuple-element.40.refs_0_.refs_2_), channel_id=1, source_target_pairs={{0,4},{1,5},{2,6},{3,7},{4,0},{5,1},{6,2},{7,3},{8,12},{9,13},{10,... | collective-permute-start | bytes 589832 | tf_op jit(solution)/shard_map/ppermute | solution.py:321
  32.4 0.8 copy-start.7
  33.2 0.8 copy-start.8
  38.4 22.0 %collective-permute-start.16 = (f32[3,8,384]{2,1,0:T(8,128)}, f32[3,8,384]{2,1,0:T(8,128)S(1)}, u32[]{:S(2)}, u32[]{:S(2)}) collective-permute-start(f32[3,8,384]{2,1,0:T(8,128)} %stats.1.refs_12_), channel_id=1, source_target_pairs={{8,0},{9,1},{10,2},{11,3},{12,4},{13,5},{14,6},{15,7},{16,8},{17,9... | collective-permute-start | bytes 110600 | tf_op jit(solution)/shard_map/ppermute | solution.py:321
  40.3 20.2 %collective-permute-start.15 = (f32[3,8,384]{2,1,0:T(8,128)}, f32[3,8,384]{2,1,0:T(8,128)S(1)}, u32[]{:S(2)}, u32[]{:S(2)}) collective-permute-start(f32[3,8,384]{2,1,0:T(8,128)} %stats.1.refs_12_), channel_id=1, source_target_pairs={{0,8},{1,9},{2,10},{3,11},{4,12},{5,13},{6,14},{7,15},{8,16},{9,17... | collective-permute-start | bytes 110600 | tf_op jit(solution)/shard_map/ppermute | solution.py:321
  47.0 13.5 %collective-permute-start.14 = (f32[3,8,384]{2,1,0:T(8,128)}, f32[3,8,384]{2,1,0:T(8,128)S(1)}, u32[]{:S(2)}, u32[]{:S(2)}) collective-permute-start(f32[3,8,384]{2,1,0:T(8,128)} %stats.1.refs_12_), channel_id=1, source_target_pairs={{4,8},{5,9},{6,10},{7,11},{8,4},{9,5},{10,6},{11,7},{12,16},{13,17... | collective-permute-start | bytes 110600 | tf_op jit(solution)/shard_map/ppermute | solution.py:321
  49.1 0.7 copy-start.9
  49.1 11.3 %collective-permute-start.13 = (f32[3,8,384]{2,1,0:T(8,128)}, f32[3,8,384]{2,1,0:T(8,128)S(1)}, u32[]{:S(2)}, u32[]{:S(2)}) collective-permute-start(f32[3,8,384]{2,1,0:T(8,128)} %stats.1.refs_12_), channel_id=1, source_target_pairs={{0,4},{1,5},{2,6},{3,7},{4,0},{5,1},{6,2},{7,3},{8,12},{9,13},{10,... | collective-permute-start | bytes 110600 | tf_op jit(solution)/shard_map/ppermute | solution.py:321
  49.9 0.7 copy-start.10
  61.1 20.5 %copy-start.31 = (bf16[256,384]{1,0:T(8,128)(2,1)S(1)}, bf16[256,384]{1,0:T(8,128)(2,1)}, u32[]{:S(2)}) copy-start(bf16[256,384]{1,0:T(8,128)(2,1)} %get-tuple-element.52) | copy-start | bytes 589828
  61.1 24.1 %copy-start.30 = (bf16[256,384]{1,0:T(8,128)(2,1)S(1)}, bf16[256,384]{1,0:T(8,128)(2,1)}, u32[]{:S(2)}) copy-start(bf16[256,384]{1,0:T(8,128)(2,1)} %get-tuple-element.53) | copy-start | bytes 589828
  68.5 13.1 %collective-permute-start.21 = (bf16[4,2,32,384]{3,2,1,0:T(8,128)(2,1)}, bf16[4,2,32,384]{3,2,1,0:T(8,128)(2,1)S(1)}, u32[]{:S(2)}, u32[]{:S(2)}) collective-permute-start(bf16[4,2,32,384]{3,2,1,0:T(8,128)(2,1)} %get-tuple-element.58), channel_id=1, source_target_pairs={{0,1},{1,0},{2,3},{3,2},{4,5},{5,4},{6,7},{7,6},{8,9},{9,8},{10,11... | collective-permute-start | bytes 589832 | tf_op jit(solution)/shard_map/ppermute | solution.py:321
  69.4 15.7 %collective-permute-start.22 = (bf16[4,2,32,384]{3,2,1,0:T(8,128)(2,1)}, bf16[4,2,32,384]{3,2,1,0:T(8,128)(2,1)S(1)}, u32[]{:S(2)}, u32[]{:S(2)}) collective-permute-start(bf16[4,2,32,384]{3,2,1,0:T(8,128)(2,1)} %get-tuple-element.59), channel_id=1, source_target_pairs={{0,4},{1,5},{2,6},{3,7},{4,0},{5,1},{6,2},{7,3},{8,12},{9,13},{10,... | collective-permute-start | bytes 589832 | tf_op jit(solution)/shard_map/ppermute | solution.py:321
  69.9 15.4 %collective-permute-start.23 = (bf16[4,2,32,384]{3,2,1,0:T(8,128)(2,1)}, bf16[4,2,32,384]{3,2,1,0:T(8,128)(2,1)S(1)}, u32[]{:S(2)}, u32[]{:S(2)}) collective-permute-start(bf16[4,2,32,384]{3,2,1,0:T(8,128)(2,1)} %get-tuple-element.60), channel_id=1, source_target_pairs={{0,5},{1,4},{2,7},{3,6},{4,1},{5,0},{6,3},{7,2},{8,13},{9,12},{10,... | collective-permute-start | bytes 589832 | tf_op jit(solution)/shard_map/ppermute | solution.py:321
  72.0 13.8 %collective-permute-start.24 = (bf16[4,2,32,384]{3,2,1,0:T(8,128)(2,1)}, bf16[4,2,32,384]{3,2,1,0:T(8,128)(2,1)S(1)}, u32[]{:S(2)}, u32[]{:S(2)}) collective-permute-start(bf16[4,2,32,384]{3,2,1,0:T(8,128)(2,1)} %get-tuple-element.61), channel_id=1, source_target_pairs={{4,8},{5,9},{6,10},{7,11},{8,4},{9,5},{10,6},{11,7},{12,16},{13,17... | collective-permute-start | bytes 589832 | tf_op jit(solution)/shard_map/ppermute | solution.py:321
  79.2 12.1 %collective-permute-start.25 = (bf16[4,2,32,384]{3,2,1,0:T(8,128)(2,1)}, bf16[4,2,32,384]{3,2,1,0:T(8,128)(2,1)S(1)}, u32[]{:S(2)}, u32[]{:S(2)}) collective-permute-start(bf16[4,2,32,384]{3,2,1,0:T(8,128)(2,1)} %get-tuple-element.62), channel_id=1, source_target_pairs={{4,9},{5,8},{6,11},{7,10},{8,5},{9,4},{10,7},{11,6},{12,17},{13,16... | collective-permute-start | bytes 589832 | tf_op jit(solution)/shard_map/ppermute | solution.py:321
  81.5 9.7 %copy-start.16 = (bf16[4,2,32,384]{3,2,1,0:T(8,128)(2,1)}, bf16[4,2,32,384]{3,2,1,0:T(8,128)(2,1)S(1)}, u32[]{:S(2)}) copy-start(bf16[4,2,32,384]{3,2,1,0:T(8,128)(2,1)S(1)} %collective-permute-done.21.by_aud) | copy-start | bytes 589828
  81.6 17.5 %collective-permute-start.17 = (bf16[256,384]{1,0:T(8,128)(2,1)S(1)}, bf16[256,384]{1,0:T(8,128)(2,1)S(1)}, u32[]{:S(2)}, u32[]{:S(2)}) collective-permute-start(bf16[256,384]{1,0:T(8,128)(2,1)S(1)} %copy-done.31), channel_id=1, source_target_pairs={{0,2},{1,3},{2,0},{3,1},{4,6},{5,7},{6,4},{7,5},{8,10},{9,11},{10,... | collective-permute-start | bytes 589832 | tf_op jit(solution)/shard_map/ppermute | solution.py:321
  85.2 6.1 %copy-start.17 = (bf16[4,2,32,384]{3,2,1,0:T(8,128)(2,1)}, bf16[4,2,32,384]{3,2,1,0:T(8,128)(2,1)S(1)}, u32[]{:S(2)}) copy-start(bf16[4,2,32,384]{3,2,1,0:T(8,128)(2,1)S(1)} %collective-permute-done.22.by_a) | copy-start | bytes 589828
  85.2 13.9 %collective-permute-start.18 = (bf16[256,384]{1,0:T(8,128)(2,1)S(1)}, bf16[256,384]{1,0:T(8,128)(2,1)S(1)}, u32[]{:S(2)}, u32[]{:S(2)}) collective-permute-start(bf16[256,384]{1,0:T(8,128)(2,1)S(1)} %copy-done.30), channel_id=1, source_target_pairs={{0,2},{1,3},{2,0},{3,1},{4,6},{5,7},{6,4},{7,5},{8,10},{9,11},{10,... | collective-permute-start | bytes 589832 | tf_op jit(solution)/shard_map/ppermute | solution.py:321
  85.3 5.9 %copy-start.18 = (bf16[4,2,32,384]{3,2,1,0:T(8,128)(2,1)}, bf16[4,2,32,384]{3,2,1,0:T(8,128)(2,1)S(1)}, u32[]{:S(2)}) copy-start(bf16[4,2,32,384]{3,2,1,0:T(8,128)(2,1)S(1)} %collective-permute-done.23.by_ax) | copy-start | bytes 589828
  85.3 13.8 %collective-permute-start.19 = (bf16[256,384]{1,0:T(8,128)(2,1)}, bf16[256,384]{1,0:T(8,128)(2,1)S(1)}, u32[]{:S(2)}, u32[]{:S(2)}) collective-permute-start(bf16[256,384]{1,0:T(8,128)(2,1)} %get-tuple-element.54), channel_id=1, source_target_pairs={{0,2},{1,3},{2,0},{3,1},{4,6},{5,7},{6,4},{7,5},{8,10},{9,11},{10,... | collective-permute-start | bytes 589832 | tf_op jit(solution)/shard_map/ppermute | solution.py:321
  85.8 5.5 %copy-start.19 = (bf16[4,2,32,384]{3,2,1,0:T(8,128)(2,1)}, bf16[4,2,32,384]{3,2,1,0:T(8,128)(2,1)S(1)}, u32[]{:S(2)}) copy-start(bf16[4,2,32,384]{3,2,1,0:T(8,128)(2,1)S(1)} %collective-permute-done.24.by_b) | copy-start | bytes 589828
  85.8 13.4 %collective-permute-start.20 = (bf16[256,384]{1,0:T(8,128)(2,1)}, bf16[256,384]{1,0:T(8,128)(2,1)S(1)}, u32[]{:S(2)}, u32[]{:S(2)}) collective-permute-start(bf16[256,384]{1,0:T(8,128)(2,1)} %get-tuple-element.55), channel_id=1, source_target_pairs={{0,2},{1,3},{2,0},{3,1},{4,6},{5,7},{6,4},{7,5},{8,10},{9,11},{10,... | collective-permute-start | bytes 589832 | tf_op jit(solution)/shard_map/ppermute | solution.py:321
  94.2 8.7 %collective-permute-start.26 = (bf16[4,2,32,384]{3,2,1,0:T(8,128)(2,1)}, bf16[4,2,32,384]{3,2,1,0:T(8,128)(2,1)S(1)}, u32[]{:S(2)}, u32[]{:S(2)}) collective-permute-start(bf16[4,2,32,384]{3,2,1,0:T(8,128)(2,1)} %get-tuple-element.64), channel_id=1, source_target_pairs={{0,2},{1,3},{2,0},{3,1},{4,6},{5,7},{6,4},{7,5},{8,10},{9,11},{10,... | collective-permute-start | bytes 589832 | tf_op jit(solution)/shard_map/ppermute | solution.py:321
  99.1 0.8 copy-start.12
  99.1 0.8 copy-start.13
  99.1 0.9 copy-start.14
  (11 other events, 7.1 us)

commit v2 on v1

--- a/solution.py
+++ b/solution.py
@@ -5,14 +5,15 @@
 from jax.experimental.pallas import tpu as pltpu
 from jax.sharding import PartitionSpec as P
 
+
 HD = 64
 BLK = 64
-WMAX = 3
 PAIR = 2 * HD
 NEG = -1e30
 BF = jnp.bfloat16
 F32 = jnp.float32
 
+
 NPOS = 6
 KEYS = NPOS * BLK
 
@@ -36,8 +37,14 @@
 
 
 def pack_kernel(idx_ref, len_ref, *refs):
-    mine, other, keep, send = refs[:4], refs[4:8], refs[8], refs[9]
+    mine, other, keep, send, local, sems = refs[:4], refs[4:8], refs[8], refs[9], refs[10], refs[11]
     c, r, a = coords(idx_ref)
+    copies = [pltpu.make_async_copy(src, local.at[n], sems.at[n]) for n, src in enumerate(mine)]
+    for copy in copies:
+        copy.start()
+    for copy in copies:
+        copy.wait()
+    mine = [local.at[n] for n in range(4)]
     half, quarter = keep.shape[2], keep.shape[3]
     row = lax.broadcasted_iota(jnp.int32, (half, quarter), 0) + a * half
     for slot, arrays in ((r, mine), (1 - r, other)):
@@ -257,7 +264,7 @@
     scatter_audio(idx_ref, grads, back)
 
 
-def sum_kernel(idx_ref, len_ref, keep, by_aud, by_a, by_ax, by_b, by_bx, mine, other):
+def sum_kernel(idx_ref, len_ref, keep, by_aud, by_a, by_ax, by_b, by_bx, after, mine, other):
     c, r, a = coords(idx_ref)
     half, quarter = keep.shape[2], keep.shape[3]
     row = lax.broadcasted_iota(jnp.int32, (half, quarter), 0) + a * half
@@ -284,6 +291,7 @@
 def join_video_kernel(idx_ref, *refs):
     for src, out in zip(refs[4:8], refs[8:12]):
         out[...] = src[...]
+    refs[12][0] = 0
 
 
 def cost(flops, transcendentals, nbytes):
@@ -320,7 +328,7 @@
     def move(x, name):
         return lax.ppermute(x, ("vid", "aud"), moves[name])
 
-    def body(q_v, k_v, v_v, g_v, q_a, k_a, v_a, g_a, window, audio_len):
+    def step(q_v, k_v, v_v, g_v, q_a, k_a, v_a, g_a, window, audio_len):
         rows, width = q_v.shape
         quarter = width // 2
         half = q_a.shape[0]
@@ -340,11 +348,11 @@
         join_spec = pl.BlockSpec((rows, PAIR), lambda h, i: (0, (1 - ((i[0] >> 1) & 1)) * steps + h))
         stat_spec = pl.BlockSpec((1, 8, KEYS), lambda h, i: (h, 0, 0))
         any_spec = pl.BlockSpec(memory_space=pl.ANY)
-
-        def call(kernel, name, ins, outs, args, grid=(steps,), scratch=(), aliases=None, est=None):
+        hbm = pl.BlockSpec(memory_space=pltpu.HBM)
+
+        def call(kernel, ins, outs, args, grid=(steps,), scratch=(), aliases=None, est=None):
             return pl.pallas_call(
                 kernel,
-                name=name,
                 grid_spec=pltpu.PrefetchScalarGridSpec(
                     num_scalar_prefetch=1,
                     grid=grid,
@@ -355,6 +363,7 @@
                 out_shape=[o for _, o in outs],
                 input_output_aliases=aliases or {},
                 cost_estimate=est,
+                compiler_params=pltpu.CompilerParams(vmem_limit_bytes=24 << 20),
             )(idx, *args)
 
         audio = (q_a, g_a, k_a, v_a)
@@ -362,18 +371,12 @@
         piece = shape((4, 2, half, quarter), BF)
         whole = pl.BlockSpec(memory_space=pltpu.VMEM)
         keep, send = call(
-            pack_kernel, "pack", [smem] + [whole] * 8, [(whole, piece)] * 2, (audio_len, *audio, *audio_other), grid=(),
+            pack_kernel, [smem] + [hbm] * 4 + [whole] * 4, [(whole, piece)] * 2, (audio_len, *[pltpu.with_memory_space_constraint(x, pltpu.HBM) for x in audio], *audio_other), grid=(),
+            scratch=(pltpu.VMEM((4, half, 2 * width), BF), pltpu.SemaphoreType.DMA((4,))),
             est=cost(0, 0, 1200000),
         )
-        pieces = [
-            keep,
-            move(send, "aud"),
-            move(keep, "A"),
-            move(send, "Ax"),
-            move(keep, "B"),
-            move(send, "Bx"),
-        ]
-        q_f, k_f, v_f, g_f = [move(x, "core") for x in (q_v, k_v, v_v, g_v)]
+        pieces = [keep, move(send, "aud"), move(keep, "A"), move(send, "Ax"), move(keep, "B"), move(send, "Bx")]
+        k_f, v_f, q_f, g_f = [move(x, "core") for x in (k_v, v_v, q_v, g_v)]
 
         audio_scratch = pltpu.VMEM((2, KEYS, PAIR), BF)
         grad_scratch = pltpu.VMEM((2, KEYS, PAIR), F32)
@@ -382,7 +385,6 @@
         stat = shape((steps, 8, KEYS), F32)
         (stats,) = call(
             stats_kernel,
-            "stats",
             [win_spec] + [piece_spec(0)] * 6 + [own_spec] * 4,
             [(stat_spec, stat)],
             (window, *pieces, k_v, v_v, k_f, v_f),
@@ -394,7 +396,6 @@
         full, far = shape((rows, width), BF), shape((rows, quarter), BF)
         va = call(
             va_kernel,
-            "va",
             [win_spec, len_spec] + [piece_spec(1)] * 6 + [own_spec] * 4,
             [(own_spec, full)] * 2 + [(far_spec, far)] * 2 + [(piece_spec(0), piece)] * 6,
             (window, audio_len, *pieces, q_v, g_v, q_f, g_f),
@@ -404,7 +405,6 @@
         out_video, dq_video, out_far, dq_far = va[:4]
         av = call(
             lambda *refs: av_kernel(chips, *refs),
-            "av",
             [win_spec] + [piece_spec(0)] * 6 + [own_spec] * 4 + [stat_spec] * 5 + [any_spec] * 6,
             [(own_spec, full)] * 2 + [(far_spec, far)] * 2 + [(piece_spec(1), piece)] * 6,
             (window, *pieces, k_v, v_v, k_f, v_f, stats, *others, *va[4:]),
@@ -417,23 +417,21 @@
         parts = [back[0]] + [move(x, name) for x, name in zip(back[1:], ("aud", "A", "Ax", "B", "Bx"))]
 
         fars = [move(x, "core") for x in (out_far, dq_far, dk_far, dv_far)]
-        out_video, dq_video, dk_video, dv_video = call(
+        out_video, dq_video, dk_video, dv_video, joined = call(
             join_video_kernel,
-            "join_video",
             [any_spec] * 4 + [far_spec] * 4,
-            [(join_spec, full)] * 4,
+            [(join_spec, full)] * 4 + [(smem, shape((1,), jnp.int32))],
             (out_video, dq_video, dk_video, dv_video, *fars),
             aliases={1 + i: i for i in range(4)},
             est=cost(0, 0, 1600000),
         )
         mine, other = call(
-            sum_kernel, "sum_audio", [smem] + [whole] * 6, [(whole, piece_q(piece))] * 2, (audio_len, *parts), grid=(),
+            sum_kernel, [smem] + [whole] * 6 + [smem], [(whole, piece)] * 2, (audio_len, *parts, joined), grid=(),
             est=cost(1000000, 0, 1600000),
         )
         other = move(other, "core")
         dk_audio, dv_audio, dq_audio, out_audio = call(
             join_audio_kernel,
-            "join_audio",
             [whole] * 2,
             [(whole, shape((half, 2 * width), BF))] * 4,
             (mine, other),
@@ -442,11 +440,7 @@
         )
         return (out_video, out_audio, dq_video, dk_video, dv_video, dq_audio, dk_audio, dv_audio)
 
-    return body
-
-
-def piece_q(piece):
-    return jax.ShapeDtypeStruct((4, 2) + piece.shape[2:], piece.dtype)
+    return step
 
 
 def solution(mesh):

time: 106 us -> 94.2 us (0.89)
  local copies, waits for them, and re-layouts: 7.06 us -> 0.17 us
  waiting for transfers between devices: 16.1 us -> 21.4 us
  Pallas kernels: 30.4 us -> 25.3 us
  starting transfers between devices: 50.7 us -> 46.2 us
    unnamed x65 -> x13, local copies, waits for them, and re-layouts: 7.06 us -> 0.17 us
    ppermute x27, waiting for transfers between devices: 16.1 us -> 21.4 us  [move(): return lax.ppermute(x, ('vid', 'aud'), moves[name])]
    pallas_call x7, Pallas kernels: 30.4 us -> 25.3 us  [call(): pl.pallas_call(kernel, grid_spec=pltpu.PrefetchScalarGridSpec(num_scalar_...]
    ppermute x27, starting transfers between devices: 50.7 us -> 46.2 us  [move(): return lax.ppermute(x, ('vid', 'aud'), moves[name])]
  transfers between devices with their start and end apart: 27 -> 27, of which waited for: 9 -> 11; matrix products, arithmetic and copies ran while one was open for 1% -> 0% of each run, Pallas kernels for 18% -> 23%
where the time goes in v2:
time: 94.2 us; the launch traced here: 93.8 us
  starting transfers between devices  46.2 us (49%)
  Pallas kernels  25.3 us (27%)
  waiting for transfers between devices  21.4 us (23%)
    ppermute x27, starting transfers between devices, move(): return lax.ppermute(x, ('vid', 'aud'), moves[name])  46.2 us
    pallas_call x7, Pallas kernels, call(): pl.pallas_call(kernel, grid_spec=pltpu.PrefetchScalarGridSpec(num_scalar_...  25.3 us
    ppermute x27, waiting for transfers between devices, move(): return lax.ppermute(x, ('vid', 'aud'), moves[name])  21.4 us
  transfers between devices with their start and end apart: 27, of which 11 were waited for; matrix products, arithmetic and copies ran while one was open for 0% of the time, Pallas kernels for 23%

profile of v2, /device:TPU:127, one launch (start us, length us, event | category | flops | bytes accessed | tf_op | source)
XLA Modules:
  0.0 93.8 jit_solution(6446154458038996304)
XLA Ops:
  0.6 0.8 collective-permute-start
  1.4 0.1 collective-permute-start.2
  1.5 0.4 collective-permute-start.3
  1.9 0.1 collective-permute-start.1
  2.0 0.5 collective-permute-done.refs_4_
  2.6 0.4 collective-permute-done.2.refs_6_
  2.9 0.2 collective-permute-done.3.refs_7_
  3.1 0.4 collective-permute-done.1.refs_5_
  3.4 1.7 %shard_map.161 = (bf16[4,2,32,384]{3,2,1,0:T(8,128)(2,1)S(1)}, bf16[4,2,32,384]{3,2,1,0:T(8,128)(2,1)S(1)}) custom-call(s32[1]{0:T(128)} %bitcast.idx_ref.refs_0_, s32[128]{0:T(128)S(1)} %copy-done.4, bf16[32,1536]{1,0:T(8,128)(2,1)} %refs_0_.1, bf16[32,1536]{1,0:T(8,128)(2,1)} %refs_1_.2, bf16[32,1536]{1,0:T(8,128)(2,1)} %refs_2_.1, ...), custom_call_target="tpu_custom_call" | custom-call | bytes 1200000 | tf_op jit(solution)/shard_map/pallas_call | solution.py:354
  5.1 4.3 %collective-permute-start.8 = (bf16[4,2,32,384]{3,2,1,0:T(8,128)(2,1)S(1)}, bf16[4,2,32,384]{3,2,1,0:T(8,128)(2,1)S(1)}, u32[]{:S(2)}, u32[]{:S(2)}) collective-permute-start(bf16[4,2,32,384]{3,2,1,0:T(8,128)(2,1)S(1)} %get-tuple-element.42), channel_id=1, source_target_pairs={{4,9},{5,8},{6,11},{7,10},{8,5},{9,4},{10,7},{11,6},{12,17},{13,16... | collective-permute-start | bytes 589832 | tf_op jit(solution)/shard_map/ppermute | solution.py:329
  9.4 0.5 collective-permute-start.6
  10.0 1.8 %collective-permute-start.4 = (bf16[4,2,32,384]{3,2,1,0:T(8,128)(2,1)S(1)}, bf16[4,2,32,384]{3,2,1,0:T(8,128)(2,1)S(1)}, u32[]{:S(2)}, u32[]{:S(2)}) collective-permute-start(bf16[4,2,32,384]{3,2,1,0:T(8,128)(2,1)S(1)} %get-tuple-element.42), channel_id=1, source_target_pairs={{0,1},{1,0},{2,3},{3,2},{4,5},{5,4},{6,7},{7,6},{8,9},{9,8},{10,11... | collective-permute-start | bytes 589832 | tf_op jit(solution)/shard_map/ppermute | solution.py:329
  11.8 0.7 collective-permute-start.11
  12.5 4.8 %collective-permute-start.7 = (bf16[4,2,32,384]{3,2,1,0:T(8,128)(2,1)S(1)}, bf16[4,2,32,384]{3,2,1,0:T(8,128)(2,1)S(1)}, u32[]{:S(2)}, u32[]{:S(2)}) collective-permute-start(bf16[4,2,32,384]{3,2,1,0:T(8,128)(2,1)S(1)} %get-tuple-element.41.refs_0_.refs_2_), channel_id=1, source_target_pairs={{4,8},{5,9},{6,10},{7,11},{8,4},{9,5},{10,6},{11,7},{12,16},{13,17... | collective-permute-start | bytes 589832 | tf_op jit(solution)/shard_map/ppermute | solution.py:329
  17.3 3.5 %collective-permute-done.8.refs_5_.refs_7_ = bf16[4,2,32,384]{3,2,1,0:T(8,128)(2,1)S(1)} collective-permute-done((bf16[4,2,32,384]{3,2,1,0:T(8,128)(2,1)S(1)}, bf16[4,2,32,384]{3,2,1,0:T(8,128)(2,1)S(1)}, u32[]{:S(2)}, u32[]{:S(2)}) %collective-permute-start.8) | collective-permute-done | bytes 196640 | tf_op jit(solution)/shard_map/ppermute | solution.py:329
  20.8 1.7 %collective-permute-start.12 = (bf16[256,768]{1,0:T(8,128)(2,1)S(1)}, bf16[256,768]{1,0:T(8,128)(2,1)S(1)}, u32[]{:S(2)}, u32[]{:S(2)}) collective-permute-start(bf16[256,768]{1,0:T(8,128)(2,1)S(1)} %copy-done.1), channel_id=1, source_target_pairs={{0,2},{1,3},{2,0},{3,1},{4,6},{5,7},{6,4},{7,5},{8,10},{9,11},{10,... | collective-permute-start | bytes 1179656 | tf_op jit(solution)/shard_map/ppermute | solution.py:329
  22.5 0.6 collective-permute-done.6.refs_3_.refs_5_
  23.1 1.0 %collective-permute-start.9 = (bf16[256,768]{1,0:T(8,128)(2,1)}, bf16[256,768]{1,0:T(8,128)(2,1)S(1)}, u32[]{:S(2)}, u32[]{:S(2)}) collective-permute-start(bf16[256,768]{1,0:T(8,128)(2,1)} %refs_6_.2), channel_id=1, source_target_pairs={{0,2},{1,3},{2,0},{3,1},{4,6},{5,7},{6,4},{7,5},{8,10},{9,11},{10,... | collective-permute-start | bytes 1179656 | tf_op jit(solution)/shard_map/ppermute | solution.py:329
  24.1 0.0 collective-permute-start.10
  24.1 1.3 %collective-permute-done.7.refs_4_.refs_6_ = bf16[4,2,32,384]{3,2,1,0:T(8,128)(2,1)S(1)} collective-permute-done((bf16[4,2,32,384]{3,2,1,0:T(8,128)(2,1)S(1)}, bf16[4,2,32,384]{3,2,1,0:T(8,128)(2,1)S(1)}, u32[]{:S(2)}, u32[]{:S(2)}) %collective-permute-start.7) | collective-permute-done | bytes 196640 | tf_op jit(solution)/shard_map/ppermute | solution.py:329
  25.4 0.0 collective-permute-start.5
  25.4 0.1 copy.28.win_ref.refs_1_
  25.6 0.0 copy-start.2
  25.6 0.0 copy-start.3
  25.6 5.3 %collective-permute-done.5.refs_2_.refs_4_ = bf16[4,2,32,384]{3,2,1,0:T(8,128)(2,1)S(1)} collective-permute-done((bf16[4,2,32,384]{3,2,1,0:T(8,128)(2,1)S(1)}, bf16[4,2,32,384]{3,2,1,0:T(8,128)(2,1)S(1)}, u32[]{:S(2)}, u32[]{:S(2)}) %collective-permute-start.5) | collective-permute-done | bytes 196640 | tf_op jit(solution)/shard_map/ppermute | solution.py:329
  30.9 3.4 %shard_map.163.refs_12_ = f32[3,8,384]{2,1,0:T(8,128)S(1)} custom-call(s32[1]{0:T(128)} %bitcast.idx_ref.refs_0_, s32[512,2]{1,0:T(8,128)S(1)} %copy.28.win_ref.refs_1_, bf16[4,2,32,384]{3,2,1,0:T(8,128)(2,1)S(1)} %get-tuple-element.41.refs_0_.refs_2_, bf16[4,2,32,384]{3,2,1,0:T(8,128)(2,1)S(1)} %collective-permute-done.4.refs_1_.refs_3_, ...), custom_call_target="tpu_custom_call" | custom-call | flops 301989888 | bytes 3000000 | tf_op jit(solution)/shard_map/pallas_call | solution.py:354
  34.3 1.9 %collective-permute-start.16 = (f32[3,8,384]{2,1,0:T(8,128)S(1)}, f32[3,8,384]{2,1,0:T(8,128)S(1)}, u32[]{:S(2)}, u32[]{:S(2)}) collective-permute-start(f32[3,8,384]{2,1,0:T(8,128)S(1)} %shard_map.163.refs_12_), channel_id=1, source_target_pairs={{8,0},{9,1},{10,2},{11,3},{12,4},{13,5},{14,6},{15,7},{16,8},{17,9... | collective-permute-start | bytes 110600 | tf_op jit(solution)/shard_map/ppermute | solution.py:329
  36.3 6.7 %collective-permute-start.15 = (f32[3,8,384]{2,1,0:T(8,128)S(1)}, f32[3,8,384]{2,1,0:T(8,128)S(1)}, u32[]{:S(2)}, u32[]{:S(2)}) collective-permute-start(f32[3,8,384]{2,1,0:T(8,128)S(1)} %shard_map.163.refs_12_), channel_id=1, source_target_pairs={{0,8},{1,9},{2,10},{3,11},{4,12},{5,13},{6,14},{7,15},{8,16},{9,17... | collective-permute-start | bytes 110600 | tf_op jit(solution)/shard_map/ppermute | solution.py:329
  43.0 2.1 %collective-permute-start.14 = (f32[3,8,384]{2,1,0:T(8,128)S(1)}, f32[3,8,384]{2,1,0:T(8,128)S(1)}, u32[]{:S(2)}, u32[]{:S(2)}) collective-permute-start(f32[3,8,384]{2,1,0:T(8,128)S(1)} %shard_map.163.refs_12_), channel_id=1, source_target_pairs={{4,8},{5,9},{6,10},{7,11},{8,4},{9,5},{10,6},{11,7},{12,16},{13,17... | collective-permute-start | bytes 110600 | tf_op jit(solution)/shard_map/ppermute | solution.py:329
  45.1 0.2 collective-permute-start.13
  45.3 9.8 %shard_map.162 = (bf16[256,768]{1,0:T(8,128)(2,1)}, bf16[256,768]{1,0:T(8,128)(2,1)}, bf16[256,384]{1,0:T(8,128)(2,1)S(1)}, bf16[256,384]{1,0:T(8,128)(2,1)S(1)}...) custom-call(s32[1]{0:T(128)} %bitcast.idx_ref.refs_0_, ...), custom_call_target="tpu_custom_call" | custom-call | flops 754974720 | bytes 5000000 | tf_op jit(solution)/shard_map/pallas_call | solution.py:354
  55.0 2.4 %collective-permute-start.17 = (bf16[256,384]{1,0:T(8,128)(2,1)S(1)}, bf16[256,384]{1,0:T(8,128)(2,1)S(1)}, u32[]{:S(2)}, u32[]{:S(2)}) collective-permute-start(bf16[256,384]{1,0:T(8,128)(2,1)S(1)} %get-tuple-element.53), channel_id=1, source_target_pairs={{0,2},{1,3},{2,0},{3,1},{4,6},{5,7},{6,4},{7,5},{8,10},{9,11},{10,... | collective-permute-start | bytes 589832 | tf_op jit(solution)/shard_map/ppermute | solution.py:329
  57.4 0.3 collective-permute-start.18
  57.7 6.7 %shard_map.164 = (bf16[256,768]{1,0:T(8,128)(2,1)}, bf16[256,768]{1,0:T(8,128)(2,1)}, bf16[256,384]{1,0:T(8,128)(2,1)S(1)}, bf16[256,384]{1,0:T(8,128)(2,1)S(1)}...) custom-call(s32[1]{0:T(128)} %bitcast.idx_ref.refs_0_, ...), custom_call_target="tpu_custom_call", output_to_operand_aliasing={{4}: (17, {}), {5}: (18, {}), {6}: (19, {}), {7}: (20, {}),... | custom-call | flops 905969664 | bytes 5000000 | tf_op jit(solution)/shard_map/pallas_call | solution.py:354
  64.4 0.3 collective-permute-start.19
  64.7 0.3 collective-permute-start.20
  65.0 1.0 %collective-permute-start.21 = (bf16[4,2,32,384]{3,2,1,0:T(8,128)(2,1)S(1)}, bf16[4,2,32,384]{3,2,1,0:T(8,128)(2,1)S(1)}, u32[]{:S(2)}, u32[]{:S(2)}) collective-permute-start(bf16[4,2,32,384]{3,2,1,0:T(8,128)(2,1)S(1)} %get-tuple-element.59), channel_id=1, source_target_pairs={{0,1},{1,0},{2,3},{3,2},{4,5},{5,4},{6,7},{7,6},{8,9},{9,8},{10,11... | collective-permute-start | bytes 589832 | tf_op jit(solution)/shard_map/ppermute | solution.py:329
  66.0 0.9 collective-permute-start.22
  66.9 2.1 %collective-permute-start.23 = (bf16[4,2,32,384]{3,2,1,0:T(8,128)(2,1)S(1)}, bf16[4,2,32,384]{3,2,1,0:T(8,128)(2,1)S(1)}, u32[]{:S(2)}, u32[]{:S(2)}) collective-permute-start(bf16[4,2,32,384]{3,2,1,0:T(8,128)(2,1)S(1)} %get-tuple-element.61), channel_id=1, source_target_pairs={{0,5},{1,4},{2,7},{3,6},{4,1},{5,0},{6,3},{7,2},{8,13},{9,12},{10,... | collective-permute-start | bytes 589832 | tf_op jit(solution)/shard_map/ppermute | solution.py:329
  68.9 6.9 %collective-permute-start.24 = (bf16[4,2,32,384]{3,2,1,0:T(8,128)(2,1)S(1)}, bf16[4,2,32,384]{3,2,1,0:T(8,128)(2,1)S(1)}, u32[]{:S(2)}, u32[]{:S(2)}) collective-permute-start(bf16[4,2,32,384]{3,2,1,0:T(8,128)(2,1)S(1)} %get-tuple-element.62), channel_id=1, source_target_pairs={{4,8},{5,9},{6,10},{7,11},{8,4},{9,5},{10,6},{11,7},{12,16},{13,17... | collective-permute-start | bytes 589832 | tf_op jit(solution)/shard_map/ppermute | solution.py:329
  75.9 2.7 %collective-permute-start.25 = (bf16[4,2,32,384]{3,2,1,0:T(8,128)(2,1)S(1)}, bf16[4,2,32,384]{3,2,1,0:T(8,128)(2,1)S(1)}, u32[]{:S(2)}, u32[]{:S(2)}) collective-permute-start(bf16[4,2,32,384]{3,2,1,0:T(8,128)(2,1)S(1)} %get-tuple-element.63), channel_id=1, source_target_pairs={{4,9},{5,8},{6,11},{7,10},{8,5},{9,4},{10,7},{11,6},{12,17},{13,16... | collective-permute-start | bytes 589832 | tf_op jit(solution)/shard_map/ppermute | solution.py:329
  78.5 1.6 %shard_map.165 = (bf16[256,768]{1,0:T(8,128)(2,1)}, bf16[256,768]{1,0:T(8,128)(2,1)}, bf16[256,768]{1,0:T(8,128)(2,1)}, bf16[256,768]{1,0:T(8,128)(2,1)}, s32[1]{0:T(128)}) custom-call(s32[1]{0:T(128)} %bitcast.idx_ref.refs_0_, bf16[256,768]{1,0:T(8,128)(2,1)} %get-tuple-element.43.refs_0_, ...), custom_call_target="tpu_custom_call", output_to_operand_aliasing={{0}: (1, {}), {1}: (2, {}), {2}: (3, {}), {3}: (4, {})} | custom-call | bytes 1600000 | tf_op jit(solution)/shard_map/pallas_call | solution.py:354
  80.2 0.5 collective-permute-done.24.by_b
  80.7 7.6 %collective-permute-done.25.by_bx = bf16[4,2,32,384]{3,2,1,0:T(8,128)(2,1)S(1)} collective-permute-done((bf16[4,2,32,384]{3,2,1,0:T(8,128)(2,1)S(1)}, bf16[4,2,32,384]{3,2,1,0:T(8,128)(2,1)S(1)}, u32[]{:S(2)}, u32[]{:S(2)}) %collective-permute-start.25) | collective-permute-done | bytes 196640 | tf_op jit(solution)/shard_map/ppermute | solution.py:329
  88.3 1.4 %shard_map.166 = (bf16[4,2,32,384]{3,2,1,0:T(8,128)(2,1)S(1)}, bf16[4,2,32,384]{3,2,1,0:T(8,128)(2,1)S(1)}) custom-call(s32[1]{0:T(128)} %bitcast.idx_ref.refs_0_, s32[128]{0:T(128)S(1)} %copy-done.4, bf16[4,2,32,384]{3,2,1,0:T(8,128)(2,1)S(1)} %get-tuple-element.58.keep, bf16[4,2,32,384]{3,2,1,0:T(8,128)(2,1)S(1)} %collective-permute-done.21.by_aud, ...), custom_call_target="tpu_custom_call" | custom-call | flops 1000000 | bytes 1600000 | tf_op jit(solution)/shard_map/pallas_call | solution.py:354
  89.7 2.3 %collective-permute-start.26 = (bf16[4,2,32,384]{3,2,1,0:T(8,128)(2,1)S(1)}, bf16[4,2,32,384]{3,2,1,0:T(8,128)(2,1)S(1)}, u32[]{:S(2)}, u32[]{:S(2)}) collective-permute-start(bf16[4,2,32,384]{3,2,1,0:T(8,128)(2,1)S(1)} %get-tuple-element.66), channel_id=1, source_target_pairs={{0,2},{1,3},{2,0},{3,1},{4,6},{5,7},{6,4},{7,5},{8,10},{9,11},{10,... | collective-permute-start | bytes 589832 | tf_op jit(solution)/shard_map/ppermute | solution.py:329
  92.0 1.1 %collective-permute-done.26.other = bf16[4,2,32,384]{3,2,1,0:T(8,128)(2,1)S(1)} collective-permute-done((bf16[4,2,32,384]{3,2,1,0:T(8,128)(2,1)S(1)}, bf16[4,2,32,384]{3,2,1,0:T(8,128)(2,1)S(1)}, u32[]{:S(2)}, u32[]{:S(2)}) %collective-permute-start.26) | collective-permute-done | bytes 196640 | tf_op jit(solution)/shard_map/ppermute | solution.py:329
  93.0 0.8 shard_map.167
  (26 shorter events, 0.1 us)
Async XLA Ops:
  0.6 1.9 %collective-permute-start = (bf16[32,1536]{1,0:T(8,128)(2,1)}, bf16[32,1536]{1,0:T(8,128)(2,1)S(1)}, u32[]{:S(2)}, u32[]{:S(2)}) collective-permute-start(bf16[32,1536]{1,0:T(8,128)(2,1)} %refs_0_.1), channel_id=1, source_target_pairs={{0,2},{1,3},{2,0},{3,1},{4,6},{5,7},{6,4},{7,5},{8,10},{9,11},{10,... | collective-permute-start | bytes 294920 | tf_op jit(solution)/shard_map/ppermute | solution.py:329
  1.4 1.5 %collective-permute-start.2 = (bf16[32,1536]{1,0:T(8,128)(2,1)}, bf16[32,1536]{1,0:T(8,128)(2,1)S(1)}, u32[]{:S(2)}, u32[]{:S(2)}) collective-permute-start(bf16[32,1536]{1,0:T(8,128)(2,1)} %refs_2_.1), channel_id=1, source_target_pairs={{0,2},{1,3},{2,0},{3,1},{4,6},{5,7},{6,4},{7,5},{8,10},{9,11},{10,... | collective-permute-start | bytes 294920 | tf_op jit(solution)/shard_map/ppermute | solution.py:329
  1.5 1.6 %collective-permute-start.3 = (bf16[32,1536]{1,0:T(8,128)(2,1)}, bf16[32,1536]{1,0:T(8,128)(2,1)S(1)}, u32[]{:S(2)}, u32[]{:S(2)}) collective-permute-start(bf16[32,1536]{1,0:T(8,128)(2,1)} %refs_3_.1), channel_id=1, source_target_pairs={{0,2},{1,3},{2,0},{3,1},{4,6},{5,7},{6,4},{7,5},{8,10},{9,11},{10,... | collective-permute-start | bytes 294920 | tf_op jit(solution)/shard_map/ppermute | solution.py:329
  1.9 1.5 %collective-permute-start.1 = (bf16[32,1536]{1,0:T(8,128)(2,1)}, bf16[32,1536]{1,0:T(8,128)(2,1)S(1)}, u32[]{:S(2)}, u32[]{:S(2)}) collective-permute-start(bf16[32,1536]{1,0:T(8,128)(2,1)} %refs_1_.2), channel_id=1, source_target_pairs={{0,2},{1,3},{2,0},{3,1},{4,6},{5,7},{6,4},{7,5},{8,10},{9,11},{10,... | collective-permute-start | bytes 294920 | tf_op jit(solution)/shard_map/ppermute | solution.py:329
  2.0 1.4 %copy-start.4 = (s32[128]{0:T(128)S(1)}, s32[128]{0:T(128)}, u32[]{:S(2)}) copy-start(s32[128]{0:T(128)} %len_ref.5) | copy-start | bytes 1540
  3.4 8.3 %copy-start = (bf16[256,768]{1,0:T(8,128)(2,1)S(1)}, bf16[256,768]{1,0:T(8,128)(2,1)}, u32[]{:S(2)}) copy-start(bf16[256,768]{1,0:T(8,128)(2,1)} %refs_8_.1) | copy-start | bytes 1179652
  3.4 17.4 %copy-start.1 = (bf16[256,768]{1,0:T(8,128)(2,1)S(1)}, bf16[256,768]{1,0:T(8,128)(2,1)}, u32[]{:S(2)}) copy-start(bf16[256,768]{1,0:T(8,128)(2,1)} %refs_9_.1) | copy-start | bytes 1179652
  3.4 22.0 %copy-start.5 = (s32[512,2]{0,1:T(2,128)S(1)}, s32[512,2]{0,1:T(2,128)}, u32[]{:S(2)}) copy-start(s32[512,2]{0,1:T(2,128)} %param.18) | copy-start | bytes 12292
  5.1 15.7 %collective-permute-start.8 = (bf16[4,2,32,384]{3,2,1,0:T(8,128)(2,1)S(1)}, bf16[4,2,32,384]{3,2,1,0:T(8,128)(2,1)S(1)}, u32[]{:S(2)}, u32[]{:S(2)}) collective-permute-start(bf16[4,2,32,384]{3,2,1,0:T(8,128)(2,1)S(1)} %get-tuple-element.42), channel_id=1, source_target_pairs={{4,9},{5,8},{6,11},{7,10},{8,5},{9,4},{10,7},{11,6},{12,17},{13,16... | collective-permute-start | bytes 589832 | tf_op jit(solution)/shard_map/ppermute | solution.py:329
  9.4 13.7 %collective-permute-start.6 = (bf16[4,2,32,384]{3,2,1,0:T(8,128)(2,1)S(1)}, bf16[4,2,32,384]{3,2,1,0:T(8,128)(2,1)S(1)}, u32[]{:S(2)}, u32[]{:S(2)}) collective-permute-start(bf16[4,2,32,384]{3,2,1,0:T(8,128)(2,1)S(1)} %get-tuple-element.42), channel_id=1, source_target_pairs={{0,5},{1,4},{2,7},{3,6},{4,1},{5,0},{6,3},{7,2},{8,13},{9,12},{10,... | collective-permute-start | bytes 589832 | tf_op jit(solution)/shard_map/ppermute | solution.py:329
  10.0 14.2 %collective-permute-start.4 = (bf16[4,2,32,384]{3,2,1,0:T(8,128)(2,1)S(1)}, bf16[4,2,32,384]{3,2,1,0:T(8,128)(2,1)S(1)}, u32[]{:S(2)}, u32[]{:S(2)}) collective-permute-start(bf16[4,2,32,384]{3,2,1,0:T(8,128)(2,1)S(1)} %get-tuple-element.42), channel_id=1, source_target_pairs={{0,1},{1,0},{2,3},{3,2},{4,5},{5,4},{6,7},{7,6},{8,9},{9,8},{10,11... | collective-permute-start | bytes 589832 | tf_op jit(solution)/shard_map/ppermute | solution.py:329
  11.8 19.1 %collective-permute-start.11 = (bf16[256,768]{1,0:T(8,128)(2,1)S(1)}, bf16[256,768]{1,0:T(8,128)(2,1)S(1)}, u32[]{:S(2)}, u32[]{:S(2)}) collective-permute-start(bf16[256,768]{1,0:T(8,128)(2,1)S(1)} %copy-done), channel_id=1, source_target_pairs={{0,2},{1,3},{2,0},{3,1},{4,6},{5,7},{6,4},{7,5},{8,10},{9,11},{10,... | collective-permute-start | bytes 1179656 | tf_op jit(solution)/shard_map/ppermute | solution.py:329
  12.5 12.9 %collective-permute-start.7 = (bf16[4,2,32,384]{3,2,1,0:T(8,128)(2,1)S(1)}, bf16[4,2,32,384]{3,2,1,0:T(8,128)(2,1)S(1)}, u32[]{:S(2)}, u32[]{:S(2)}) collective-permute-start(bf16[4,2,32,384]{3,2,1,0:T(8,128)(2,1)S(1)} %get-tuple-element.41.refs_0_.refs_2_), channel_id=1, source_target_pairs={{4,8},{5,9},{6,10},{7,11},{8,4},{9,5},{10,6},{11,7},{12,16},{13,17... | collective-permute-start | bytes 589832 | tf_op jit(solution)/shard_map/ppermute | solution.py:329
  20.8 10.1 %collective-permute-start.12 = (bf16[256,768]{1,0:T(8,128)(2,1)S(1)}, bf16[256,768]{1,0:T(8,128)(2,1)S(1)}, u32[]{:S(2)}, u32[]{:S(2)}) collective-permute-start(bf16[256,768]{1,0:T(8,128)(2,1)S(1)} %copy-done.1), channel_id=1, source_target_pairs={{0,2},{1,3},{2,0},{3,1},{4,6},{5,7},{6,4},{7,5},{8,10},{9,11},{10,... | collective-permute-start | bytes 1179656 | tf_op jit(solution)/shard_map/ppermute | solution.py:329
  23.1 22.0 %collective-permute-start.9 = (bf16[256,768]{1,0:T(8,128)(2,1)}, bf16[256,768]{1,0:T(8,128)(2,1)S(1)}, u32[]{:S(2)}, u32[]{:S(2)}) collective-permute-start(bf16[256,768]{1,0:T(8,128)(2,1)} %refs_6_.2), channel_id=1, source_target_pairs={{0,2},{1,3},{2,0},{3,1},{4,6},{5,7},{6,4},{7,5},{8,10},{9,11},{10,... | collective-permute-start | bytes 1179656 | tf_op jit(solution)/shard_map/ppermute | solution.py:329
  24.1 21.1 %collective-permute-start.10 = (bf16[256,768]{1,0:T(8,128)(2,1)}, bf16[256,768]{1,0:T(8,128)(2,1)}, u32[]{:S(2)}, u32[]{:S(2)}) collective-permute-start(bf16[256,768]{1,0:T(8,128)(2,1)} %refs_7_.2), channel_id=1, source_target_pairs={{0,2},{1,3},{2,0},{3,1},{4,6},{5,7},{6,4},{7,5},{8,10},{9,11},{10,... | collective-permute-start | bytes 1179656 | tf_op jit(solution)/shard_map/ppermute | solution.py:329
  25.4 5.5 %collective-permute-start.5 = (bf16[4,2,32,384]{3,2,1,0:T(8,128)(2,1)S(1)}, bf16[4,2,32,384]{3,2,1,0:T(8,128)(2,1)S(1)}, u32[]{:S(2)}, u32[]{:S(2)}) collective-permute-start(bf16[4,2,32,384]{3,2,1,0:T(8,128)(2,1)S(1)} %get-tuple-element.41.refs_0_.refs_2_), channel_id=1, source_target_pairs={{0,4},{1,5},{2,6},{3,7},{4,0},{5,1},{6,2},{7,3},{8,12},{9,13},{10,... | collective-permute-start | bytes 589832 | tf_op jit(solution)/shard_map/ppermute | solution.py:329
  25.6 19.7 %copy-start.2 = (bf16[256,768]{1,0:T(8,128)(2,1)S(1)}, bf16[256,768]{1,0:T(8,128)(2,1)}, u32[]{:S(2)}) copy-start(bf16[256,768]{1,0:T(8,128)(2,1)} %refs_6_.2) | copy-start | bytes 1179652
  25.6 19.7 %copy-start.3 = (bf16[256,768]{1,0:T(8,128)(2,1)S(1)}, bf16[256,768]{1,0:T(8,128)(2,1)}, u32[]{:S(2)}) copy-start(bf16[256,768]{1,0:T(8,128)(2,1)} %refs_7_.2) | copy-start | bytes 1179652
  34.3 23.1 %collective-permute-start.16 = (f32[3,8,384]{2,1,0:T(8,128)S(1)}, f32[3,8,384]{2,1,0:T(8,128)S(1)}, u32[]{:S(2)}, u32[]{:S(2)}) collective-permute-start(f32[3,8,384]{2,1,0:T(8,128)S(1)} %shard_map.163.refs_12_), channel_id=1, source_target_pairs={{8,0},{9,1},{10,2},{11,3},{12,4},{13,5},{14,6},{15,7},{16,8},{17,9... | collective-permute-start | bytes 110600 | tf_op jit(solution)/shard_map/ppermute | solution.py:329
  36.3 21.4 %collective-permute-start.15 = (f32[3,8,384]{2,1,0:T(8,128)S(1)}, f32[3,8,384]{2,1,0:T(8,128)S(1)}, u32[]{:S(2)}, u32[]{:S(2)}) collective-permute-start(f32[3,8,384]{2,1,0:T(8,128)S(1)} %shard_map.163.refs_12_), channel_id=1, source_target_pairs={{0,8},{1,9},{2,10},{3,11},{4,12},{5,13},{6,14},{7,15},{8,16},{9,17... | collective-permute-start | bytes 110600 | tf_op jit(solution)/shard_map/ppermute | solution.py:329
  43.0 14.7 %collective-permute-start.14 = (f32[3,8,384]{2,1,0:T(8,128)S(1)}, f32[3,8,384]{2,1,0:T(8,128)S(1)}, u32[]{:S(2)}, u32[]{:S(2)}) collective-permute-start(f32[3,8,384]{2,1,0:T(8,128)S(1)} %shard_map.163.refs_12_), channel_id=1, source_target_pairs={{4,8},{5,9},{6,10},{7,11},{8,4},{9,5},{10,6},{11,7},{12,16},{13,17... | collective-permute-start | bytes 110600 | tf_op jit(solution)/shard_map/ppermute | solution.py:329
  45.1 12.6 %collective-permute-start.13 = (f32[3,8,384]{2,1,0:T(8,128)S(1)}, f32[3,8,384]{2,1,0:T(8,128)S(1)}, u32[]{:S(2)}, u32[]{:S(2)}) collective-permute-start(f32[3,8,384]{2,1,0:T(8,128)S(1)} %shard_map.163.refs_12_), channel_id=1, source_target_pairs={{0,4},{1,5},{2,6},{3,7},{4,0},{5,1},{6,2},{7,3},{8,12},{9,13},{10,... | collective-permute-start | bytes 110600 | tf_op jit(solution)/shard_map/ppermute | solution.py:329
  55.0 10.9 %collective-permute-start.17 = (bf16[256,384]{1,0:T(8,128)(2,1)S(1)}, bf16[256,384]{1,0:T(8,128)(2,1)S(1)}, u32[]{:S(2)}, u32[]{:S(2)}) collective-permute-start(bf16[256,384]{1,0:T(8,128)(2,1)S(1)} %get-tuple-element.53), channel_id=1, source_target_pairs={{0,2},{1,3},{2,0},{3,1},{4,6},{5,7},{6,4},{7,5},{8,10},{9,11},{10,... | collective-permute-start | bytes 589832 | tf_op jit(solution)/shard_map/ppermute | solution.py:329
  57.4 9.5 %collective-permute-start.18 = (bf16[256,384]{1,0:T(8,128)(2,1)S(1)}, bf16[256,384]{1,0:T(8,128)(2,1)S(1)}, u32[]{:S(2)}, u32[]{:S(2)}) collective-permute-start(bf16[256,384]{1,0:T(8,128)(2,1)S(1)} %get-tuple-element.54), channel_id=1, source_target_pairs={{0,2},{1,3},{2,0},{3,1},{4,6},{5,7},{6,4},{7,5},{8,10},{9,11},{10,... | collective-permute-start | bytes 589832 | tf_op jit(solution)/shard_map/ppermute | solution.py:329
  64.4 4.6 %collective-permute-start.19 = (bf16[256,384]{1,0:T(8,128)(2,1)S(1)}, bf16[256,384]{1,0:T(8,128)(2,1)S(1)}, u32[]{:S(2)}, u32[]{:S(2)}) collective-permute-start(bf16[256,384]{1,0:T(8,128)(2,1)S(1)} %get-tuple-element.55), channel_id=1, source_target_pairs={{0,2},{1,3},{2,0},{3,1},{4,6},{5,7},{6,4},{7,5},{8,10},{9,11},{10,... | collective-permute-start | bytes 589832 | tf_op jit(solution)/shard_map/ppermute | solution.py:329
  64.7 11.2 %collective-permute-start.20 = (bf16[256,384]{1,0:T(8,128)(2,1)S(1)}, bf16[256,384]{1,0:T(8,128)(2,1)S(1)}, u32[]{:S(2)}, u32[]{:S(2)}) collective-permute-start(bf16[256,384]{1,0:T(8,128)(2,1)S(1)} %get-tuple-element.56), channel_id=1, source_target_pairs={{0,2},{1,3},{2,0},{3,1},{4,6},{5,7},{6,4},{7,5},{8,10},{9,11},{10,... | collective-permute-start | bytes 589832 | tf_op jit(solution)/shard_map/ppermute | solution.py:329
  65.0 15.2 %collective-permute-start.21 = (bf16[4,2,32,384]{3,2,1,0:T(8,128)(2,1)S(1)}, bf16[4,2,32,384]{3,2,1,0:T(8,128)(2,1)S(1)}, u32[]{:S(2)}, u32[]{:S(2)}) collective-permute-start(bf16[4,2,32,384]{3,2,1,0:T(8,128)(2,1)S(1)} %get-tuple-element.59), channel_id=1, source_target_pairs={{0,1},{1,0},{2,3},{3,2},{4,5},{5,4},{6,7},{7,6},{8,9},{9,8},{10,11... | collective-permute-start | bytes 589832 | tf_op jit(solution)/shard_map/ppermute | solution.py:329
  66.0 14.2 %collective-permute-start.22 = (bf16[4,2,32,384]{3,2,1,0:T(8,128)(2,1)S(1)}, bf16[4,2,32,384]{3,2,1,0:T(8,128)(2,1)S(1)}, u32[]{:S(2)}, u32[]{:S(2)}) collective-permute-start(bf16[4,2,32,384]{3,2,1,0:T(8,128)(2,1)S(1)} %get-tuple-element.60), channel_id=1, source_target_pairs={{0,4},{1,5},{2,6},{3,7},{4,0},{5,1},{6,2},{7,3},{8,12},{9,13},{10,... | collective-permute-start | bytes 589832 | tf_op jit(solution)/shard_map/ppermute | solution.py:329
  66.9 13.3 %collective-permute-start.23 = (bf16[4,2,32,384]{3,2,1,0:T(8,128)(2,1)S(1)}, bf16[4,2,32,384]{3,2,1,0:T(8,128)(2,1)S(1)}, u32[]{:S(2)}, u32[]{:S(2)}) collective-permute-start(bf16[4,2,32,384]{3,2,1,0:T(8,128)(2,1)S(1)} %get-tuple-element.61), channel_id=1, source_target_pairs={{0,5},{1,4},{2,7},{3,6},{4,1},{5,0},{6,3},{7,2},{8,13},{9,12},{10,... | collective-permute-start | bytes 589832 | tf_op jit(solution)/shard_map/ppermute | solution.py:329
  68.9 11.8 %collective-permute-start.24 = (bf16[4,2,32,384]{3,2,1,0:T(8,128)(2,1)S(1)}, bf16[4,2,32,384]{3,2,1,0:T(8,128)(2,1)S(1)}, u32[]{:S(2)}, u32[]{:S(2)}) collective-permute-start(bf16[4,2,32,384]{3,2,1,0:T(8,128)(2,1)S(1)} %get-tuple-element.62), channel_id=1, source_target_pairs={{4,8},{5,9},{6,10},{7,11},{8,4},{9,5},{10,6},{11,7},{12,16},{13,17... | collective-permute-start | bytes 589832 | tf_op jit(solution)/shard_map/ppermute | solution.py:329
  75.9 12.4 %collective-permute-start.25 = (bf16[4,2,32,384]{3,2,1,0:T(8,128)(2,1)S(1)}, bf16[4,2,32,384]{3,2,1,0:T(8,128)(2,1)S(1)}, u32[]{:S(2)}, u32[]{:S(2)}) collective-permute-start(bf16[4,2,32,384]{3,2,1,0:T(8,128)(2,1)S(1)} %get-tuple-element.63), channel_id=1, source_target_pairs={{4,9},{5,8},{6,11},{7,10},{8,5},{9,4},{10,7},{11,6},{12,17},{13,16... | collective-permute-start | bytes 589832 | tf_op jit(solution)/shard_map/ppermute | solution.py:329
  89.7 3.4 %collective-permute-start.26 = (bf16[4,2,32,384]{3,2,1,0:T(8,128)(2,1)S(1)}, bf16[4,2,32,384]{3,2,1,0:T(8,128)(2,1)S(1)}, u32[]{:S(2)}, u32[]{:S(2)}) collective-permute-start(bf16[4,2,32,384]{3,2,1,0:T(8,128)(2,1)S(1)} %get-tuple-element.66), channel_id=1, source_target_pairs={{0,2},{1,3},{2,0},{3,1},{4,6},{5,7},{6,4},{7,5},{8,10},{9,11},{10,... | collective-permute-start | bytes 589832 | tf_op jit(solution)/shard_map/ppermute | solution.py:329

commit v3 on v2

--- a/solution.py
+++ b/solution.py
@@ -8,6 +8,7 @@
 
 HD = 64
 BLK = 64
+WMAX = 3
 PAIR = 2 * HD
 NEG = -1e30
 BF = jnp.bfloat16
@@ -16,6 +17,7 @@
 
 NPOS = 6
 KEYS = NPOS * BLK
+GROUP = 8
 
 
 def nt(x, y):
@@ -108,19 +110,43 @@
         bias[i] = jnp.where((place >= lo) & (place < hi), 0.0, NEG)
 
 
-def va_bias(idx_ref, win_ref, len_ref, bias):
+def window_of(idx_ref, win_ref, stretch, b):
+    c, _, _ = coords(idx_ref)
+    return win_ref[4 * stretch + b, 0] - (2 * c - 2), win_ref[4 * stretch + b, 1]
+
+
+def block_bias(idx_ref, win_ref, len_ref, bias):
     c, r, _ = coords(idx_ref)
-    shape = bias.shape[1:]
-    row = lax.broadcasted_iota(jnp.int32, shape, 0)
-    place = row // BLK
-    length = jnp.zeros(shape, jnp.int32)
-    for j in range(NPOS):
-        block = jnp.clip(2 * c - 2 + j, 0, len_ref.shape[0] - 1)
-        length = jnp.where(place == j, len_ref[block], length)
-    valid = (row % BLK) < length
+    row = lax.broadcasted_iota(jnp.int32, bias.shape[1:], 0)
     for i, stretch in enumerate((r, 1 - r)):
-        lo, hi = window_bounds(win_ref, c, stretch, shape, 1)
-        bias[i] = jnp.where((place >= lo) & (place < hi) & valid, 0.0, NEG)
+        for b in range(4):
+            start, count = window_of(idx_ref, win_ref, stretch, b)
+            keep = row < count * BLK
+            if len_ref is not None:
+                length = jnp.zeros(row.shape, jnp.int32)
+                for j in range(WMAX):
+                    block = jnp.clip(2 * c - 2 + start + j, 0, len_ref.shape[0] - 1)
+                    length = jnp.where(row // BLK == j, len_ref[block], length)
+                keep = keep & (row % BLK < length)
+            bias[4 * i + b] = jnp.where(keep, 0.0, NEG)
+
+
+def both_heads(x):
+    return jnp.concatenate([head_part(x, 0), head_part(x, 1)], axis=0)
+
+
+def own_heads(x):
+    lane = lax.broadcasted_iota(jnp.int32, (BLK, PAIR), 1)
+    return jnp.where(lane < HD, x[:BLK], x[BLK:])
+
+
+def block_groups(r):
+    blocks = [(i, stretch, b) for b in range(4) for i, stretch in enumerate((r, 1 - r))]
+    return [blocks[n : n + GROUP] for n in range(0, 8, GROUP)]
+
+
+def tn(x, y):
+    return lax.dot_general(x, y, (((0,), (0,)), ((), ())), preferred_element_type=F32)
 
 
 def stats_kernel(idx_ref, win_ref, *refs):
@@ -186,39 +212,41 @@
     outs = ((refs[10], refs[11]), (refs[12], refs[13]))
     back = refs[14:20]
     audio, bias, grads = refs[20:]
+    _, r, _ = coords(idx_ref)
 
     @pl.when(pl.program_id(0) == 0)
     def _():
-        va_bias(idx_ref, win_ref, len_ref, bias)
+        block_bias(idx_ref, win_ref, len_ref, bias)
 
     gather_audio(idx_ref, pieces, audio)
-    keys, values = audio[0], audio[1]
-    keys_t, values_t = keys.T, values.T
-    k_heads = [head_part(keys, e) for e in range(2)]
-    v_heads = [head_part(values, e) for e in range(2)]
-    dk, dv = None, None
-    for i, ((q_ref, g_ref), (out_ref, dq_ref)) in enumerate(zip(video, outs)):
-        q = q_ref[...] * jnp.asarray(HD**-0.5, BF)
-        g = g_ref[...]
-        out_t, dq_t = [], []
-        for e in range(2):
-            s = nt(k_heads[e], q) + bias[i]
-            m = jnp.max(s, axis=0, keepdims=True)
-            ex = jnp.exp(s - m)
-            p = ex * (1.0 / jnp.sum(ex, axis=0, keepdims=True))
+    grads[...] = jnp.zeros(grads.shape, F32)
+    scale = jnp.asarray(HD**-0.5, BF)
+    for group in block_groups(r):
+        work = []
+        for i, stretch, b in group:
+            start, _ = window_of(idx_ref, win_ref, stretch, b)
+            span = pl.ds(pl.multiple_of(start * BLK, BLK), WMAX * BLK)
+            rows = slice(b * BLK, (b + 1) * BLK)
+            q = both_heads(video[i][0][rows, :] * scale)
+            g = both_heads(video[i][1][rows, :])
+            keys, values = audio[0, span, :], audio[1, span, :]
+            s = nt(keys, q) + bias[4 * i + b]
+            dp = nt(values, g)
+            work.append((i, rows, span, q, g, keys, values, s, dp))
+        done = []
+        for i, rows, span, q, g, keys, values, s, dp in work:
+            ex = jnp.exp(s - jnp.max(s, axis=0, keepdims=True))
+            inv = 1.0 / jnp.sum(ex, axis=0, keepdims=True)
+            delta = jnp.sum(ex * dp, axis=0, keepdims=True) * inv
+            p = ex * inv
             pb = p.astype(BF)
-            dp = nt(v_heads[e], g)
-            delta = jnp.sum(p * dp, axis=0, keepdims=True)
             ds = (p * (dp - delta)).astype(BF)
-            dk_e, dv_e = nn(ds, head_part(q, e)), nn(pb, head_part(g, e))
-            dk = dk_e if dk is None else dk + dk_e
-            dv = dv_e if dv is None else dv + dv_e
-            out_t.append(nn(values_t[e * HD : (e + 1) * HD], pb))
-            dq_t.append(nn(keys_t[e * HD : (e + 1) * HD], ds))
-        out_ref[...] = jnp.concatenate(out_t, axis=0).T.astype(BF)
-        dq_ref[...] = (jnp.concatenate(dq_t, axis=0).T * HD**-0.5).astype(BF)
-    grads[0] = dk
-    grads[1] = dv
+            done.append((i, rows, span, nn(ds, q), nn(pb, g), tn(pb, values), tn(ds, keys)))
+        for i, rows, span, dk, dv, out, dq in done:
+            grads[0, span, :] += dk
+            grads[1, span, :] += dv
+            outs[i][0][rows, :] = own_heads(out).astype(BF)
+            outs[i][1][rows, :] = (own_heads(dq) * HD**-0.5).astype(BF)
     scatter_audio(idx_ref, grads, back)
 
 
@@ -228,39 +256,42 @@
     stats = [ref[0] for ref in refs[10:15]]
     outs = ((refs[21], refs[22]), (refs[23], refs[24]))
     back = refs[25:31]
-    audio, bias, grads = refs[31:]
+    audio, bias, grads, rowstat = refs[31:]
+    _, r, _ = coords(idx_ref)
 
     @pl.when(pl.program_id(0) == 0)
     def _():
-        av_bias(idx_ref, win_ref, bias)
+        block_bias(idx_ref, win_ref, None, bias)
 
     gather_audio(idx_ref, pieces, audio)
-    queries, cot = audio[0], audio[1]
-    q_heads = [head_part(queries, e) for e in range(2)]
-    g_heads = [head_part(cot, e) for e in range(2)]
-    lse, delta = merge_stats(idx_ref, chips, *stats)
-    dq_t, out_t = [None, None], [None, None]
-    for i, ((k_ref, v_ref), (dk_ref, dv_ref)) in enumerate(zip(video, outs)):
-        keys, values = k_ref[...], v_ref[...]
-        keys_t, values_t = keys.T, values.T
-        dk, dv = None, None
-        for e in range(2):
-            s = nt(head_part(keys, e), queries) + bias[i]
-            p = jnp.exp(s - lse[e : e + 1])
+    for n, x in enumerate(merge_stats(idx_ref, chips, *stats)):
+        wide = [jnp.broadcast_to(x[e : e + 1], (HD, KEYS)) for e in range(2)]
+        rowstat[n] = jnp.concatenate(wide, axis=0).T
+    grads[...] = jnp.zeros(grads.shape, F32)
+    for group in block_groups(r):
+        work = []
+        for i, stretch, b in group:
+            start, _ = window_of(idx_ref, win_ref, stretch, b)
+            span = pl.ds(pl.multiple_of(start * BLK, BLK), WMAX * BLK)
+            rows = slice(b * BLK, (b + 1) * BLK)
+            keys = both_heads(video[i][0][rows, :])
+            values = both_heads(video[i][1][rows, :])
+            q, g = audio[0, span, :], audio[1, span, :]
+            s = nt(q, keys) + bias[4 * i + b]
+            dp = nt(g, values)
+            work.append((i, rows, span, keys, values, q, g, s, dp))
+        done = []
+        for i, rows, span, keys, values, q, g, s, dp in work:
+            p = jnp.exp(s - rowstat[0, span, :])
             pb = p.astype(BF)
-            dp = nt(head_part(values, e), cot)
-            ds = (p * (dp - delta[e : e + 1])).astype(BF)
-            dk_e, dv_e = nn(ds, q_heads[e]), nn(pb, g_heads[e])
-            dk = dk_e if dk is None else dk + dk_e
-            dv = dv_e if dv is None else dv + dv_e
-            dq_e = nn(keys_t[e * HD : (e + 1) * HD], ds)
-            out_e = nn(values_t[e * HD : (e + 1) * HD], pb)
-            dq_t[e] = dq_e if i == 0 else dq_t[e] + dq_e
-            out_t[e] = out_e if i == 0 else out_t[e] + out_e
-        dk_ref[...] = dk.astype(BF)
-        dv_ref[...] = dv.astype(BF)
-    grads[0] = jnp.concatenate(dq_t, axis=0).T * HD**-0.5
-    grads[1] = jnp.concatenate(out_t, axis=0).T
+            ds = (p * (dp - rowstat[1, span, :])).astype(BF)
+            done.append((i, rows, span, nn(ds, keys), nn(pb, values), tn(ds, q), tn(pb, g)))
+        for i, rows, span, dq, out, dk, dv in done:
+            grads[0, span, :] += dq
+            grads[1, span, :] += out
+            outs[i][0][rows, :] = own_heads(dk).astype(BF)
+            outs[i][1][rows, :] = own_heads(dv).astype(BF)
+    grads[0] = grads[0] * HD**-0.5
     scatter_audio(idx_ref, grads, back)
 
 
@@ -380,6 +411,7 @@
 
         audio_scratch = pltpu.VMEM((2, KEYS, PAIR), BF)
         grad_scratch = pltpu.VMEM((2, KEYS, PAIR), F32)
+        bias_scratch = pltpu.VMEM((8, WMAX * BLK, PAIR), F32)
         pairs = 2 * steps * 2 * rows * KEYS
 
         stat = shape((steps, 8, KEYS), F32)
@@ -399,7 +431,7 @@
             [win_spec, len_spec] + [piece_spec(1)] * 6 + [own_spec] * 4,
             [(own_spec, full)] * 2 + [(far_spec, far)] * 2 + [(piece_spec(0), piece)] * 6,
             (window, audio_len, *pieces, q_v, g_v, q_f, g_f),
-            scratch=(audio_scratch, pltpu.VMEM((2, KEYS, rows), F32), grad_scratch),
+            scratch=(audio_scratch, bias_scratch, grad_scratch),
             est=cost(10 * HD * pairs, pairs, 5000000),
         )
         out_video, dq_video, out_far, dq_far = va[:4]
@@ -408,7 +440,7 @@
             [win_spec] + [piece_spec(0)] * 6 + [own_spec] * 4 + [stat_spec] * 5 + [any_spec] * 6,
             [(own_spec, full)] * 2 + [(far_spec, far)] * 2 + [(piece_spec(1), piece)] * 6,
             (window, *pieces, k_v, v_v, k_f, v_f, stats, *others, *va[4:]),
-            scratch=(audio_scratch, pltpu.VMEM((2, rows, KEYS), F32), grad_scratch),
+            scratch=(audio_scratch, bias_scratch, grad_scratch, grad_scratch),
             aliases={17 + i: 4 + i for i in range(6)},
             est=cost(12 * HD * pairs, pairs, 5000000),
         )

time: 94.2 us -> 88.6 us (0.941)
  Pallas kernels: 25.3 us -> 19.8 us
    pallas_call x7, Pallas kernels: 25.3 us -> 19.8 us  [call(): pl.pallas_call(kernel, grid_spec=pltpu.PrefetchScalarGridSpec(num_scalar_...]
  transfers between devices with their start and end apart: 27 -> 27, of which waited for: 11 -> 11; matrix products, arithmetic and copies ran while one was open for 0% -> 0% of each run, Pallas kernels for 23% -> 18%
where the time goes in v3:
time: 88.6 us; the launch traced here: 88.2 us
  starting transfers between devices  46.4 us (52%)
  waiting for transfers between devices  21.1 us (24%)
  Pallas kernels  19.8 us (22%)
    ppermute x27, starting transfers between devices, move(): return lax.ppermute(x, ('vid', 'aud'), moves[name])  46.4 us
    ppermute x27, waiting for transfers between devices, move(): return lax.ppermute(x, ('vid', 'aud'), moves[name])  21.1 us
    pallas_call x7, Pallas kernels, call(): pl.pallas_call(kernel, grid_spec=pltpu.PrefetchScalarGridSpec(num_scalar_...  19.8 us
  transfers between devices with their start and end apart: 27, of which 11 were waited for; matrix products, arithmetic and copies ran while one was open for 0% of the time, Pallas kernels for 18%

profile of v3, /device:TPU:127, one launch (start us, length us, event | category | flops | bytes accessed | tf_op | source)
XLA Modules:
  0.0 88.2 jit_solution(11412233086007778605)
XLA Ops:
  0.6 0.8 collective-permute-start
  1.4 0.1 collective-permute-start.2
  1.5 0.4 collective-permute-start.3
  1.9 0.1 collective-permute-start.1
  2.0 0.5 collective-permute-done.refs_4_
  2.6 0.4 collective-permute-done.2.refs_6_
  2.9 0.2 collective-permute-done.3.refs_7_
  3.1 0.4 collective-permute-done.1.refs_5_
  3.4 1.7 %shard_map.161 = (bf16[4,2,32,384]{3,2,1,0:T(8,128)(2,1)S(1)}, bf16[4,2,32,384]{3,2,1,0:T(8,128)(2,1)S(1)}) custom-call(s32[1]{0:T(128)} %bitcast.idx_ref.refs_0_, s32[128]{0:T(128)S(1)} %copy-done.4, bf16[32,1536]{1,0:T(8,128)(2,1)} %refs_0_.1, bf16[32,1536]{1,0:T(8,128)(2,1)} %refs_1_.2, bf16[32,1536]{1,0:T(8,128)(2,1)} %refs_2_.1, ...), custom_call_target="tpu_custom_call" | custom-call | bytes 1200000 | tf_op jit(solution)/shard_map/pallas_call | solution.py:385
  5.1 4.3 %collective-permute-start.8 = (bf16[4,2,32,384]{3,2,1,0:T(8,128)(2,1)S(1)}, bf16[4,2,32,384]{3,2,1,0:T(8,128)(2,1)S(1)}, u32[]{:S(2)}, u32[]{:S(2)}) collective-permute-start(bf16[4,2,32,384]{3,2,1,0:T(8,128)(2,1)S(1)} %get-tuple-element.42), channel_id=1, source_target_pairs={{4,9},{5,8},{6,11},{7,10},{8,5},{9,4},{10,7},{11,6},{12,17},{13,16... | collective-permute-start | bytes 589832 | tf_op jit(solution)/shard_map/ppermute | solution.py:360
  9.4 0.5 collective-permute-start.6
  10.0 1.8 %collective-permute-start.4 = (bf16[4,2,32,384]{3,2,1,0:T(8,128)(2,1)S(1)}, bf16[4,2,32,384]{3,2,1,0:T(8,128)(2,1)S(1)}, u32[]{:S(2)}, u32[]{:S(2)}) collective-permute-start(bf16[4,2,32,384]{3,2,1,0:T(8,128)(2,1)S(1)} %get-tuple-element.42), channel_id=1, source_target_pairs={{0,1},{1,0},{2,3},{3,2},{4,5},{5,4},{6,7},{7,6},{8,9},{9,8},{10,11... | collective-permute-start | bytes 589832 | tf_op jit(solution)/shard_map/ppermute | solution.py:360
  11.8 0.7 collective-permute-start.11
  12.5 4.8 %collective-permute-start.7 = (bf16[4,2,32,384]{3,2,1,0:T(8,128)(2,1)S(1)}, bf16[4,2,32,384]{3,2,1,0:T(8,128)(2,1)S(1)}, u32[]{:S(2)}, u32[]{:S(2)}) collective-permute-start(bf16[4,2,32,384]{3,2,1,0:T(8,128)(2,1)S(1)} %get-tuple-element.41.refs_0_.refs_2_), channel_id=1, source_target_pairs={{4,8},{5,9},{6,10},{7,11},{8,4},{9,5},{10,6},{11,7},{12,16},{13,17... | collective-permute-start | bytes 589832 | tf_op jit(solution)/shard_map/ppermute | solution.py:360
  17.3 3.5 %collective-permute-done.8.refs_5_.refs_7_ = bf16[4,2,32,384]{3,2,1,0:T(8,128)(2,1)S(1)} collective-permute-done((bf16[4,2,32,384]{3,2,1,0:T(8,128)(2,1)S(1)}, bf16[4,2,32,384]{3,2,1,0:T(8,128)(2,1)S(1)}, u32[]{:S(2)}, u32[]{:S(2)}) %collective-permute-start.8) | collective-permute-done | bytes 196640 | tf_op jit(solution)/shard_map/ppermute | solution.py:360
  20.8 1.7 %collective-permute-start.12 = (bf16[256,768]{1,0:T(8,128)(2,1)S(1)}, bf16[256,768]{1,0:T(8,128)(2,1)S(1)}, u32[]{:S(2)}, u32[]{:S(2)}) collective-permute-start(bf16[256,768]{1,0:T(8,128)(2,1)S(1)} %copy-done.1), channel_id=1, source_target_pairs={{0,2},{1,3},{2,0},{3,1},{4,6},{5,7},{6,4},{7,5},{8,10},{9,11},{10,... | collective-permute-start | bytes 1179656 | tf_op jit(solution)/shard_map/ppermute | solution.py:360
  22.5 0.6 collective-permute-done.6.refs_3_.refs_5_
  23.1 1.0 %collective-permute-start.9 = (bf16[256,768]{1,0:T(8,128)(2,1)}, bf16[256,768]{1,0:T(8,128)(2,1)S(1)}, u32[]{:S(2)}, u32[]{:S(2)}) collective-permute-start(bf16[256,768]{1,0:T(8,128)(2,1)} %refs_6_.2), channel_id=1, source_target_pairs={{0,2},{1,3},{2,0},{3,1},{4,6},{5,7},{6,4},{7,5},{8,10},{9,11},{10,... | collective-permute-start | bytes 1179656 | tf_op jit(solution)/shard_map/ppermute | solution.py:360
  24.1 0.0 collective-permute-start.10
  24.1 1.3 %collective-permute-done.7.refs_4_.refs_6_ = bf16[4,2,32,384]{3,2,1,0:T(8,128)(2,1)S(1)} collective-permute-done((bf16[4,2,32,384]{3,2,1,0:T(8,128)(2,1)S(1)}, bf16[4,2,32,384]{3,2,1,0:T(8,128)(2,1)S(1)}, u32[]{:S(2)}, u32[]{:S(2)}) %collective-permute-start.7) | collective-permute-done | bytes 196640 | tf_op jit(solution)/shard_map/ppermute | solution.py:360
  25.4 0.0 collective-permute-start.5
  25.4 0.1 copy.28.win_ref.refs_1_
  25.6 0.0 copy-start.2
  25.6 0.0 copy-start.3
  25.6 5.3 %collective-permute-done.5.refs_2_.refs_4_ = bf16[4,2,32,384]{3,2,1,0:T(8,128)(2,1)S(1)} collective-permute-done((bf16[4,2,32,384]{3,2,1,0:T(8,128)(2,1)S(1)}, bf16[4,2,32,384]{3,2,1,0:T(8,128)(2,1)S(1)}, u32[]{:S(2)}, u32[]{:S(2)}) %collective-permute-start.5) | collective-permute-done | bytes 196640 | tf_op jit(solution)/shard_map/ppermute | solution.py:360
  30.9 0.0 collective-permute-done.11.refs_8_.refs_10_
  30.9 0.0 collective-permute-done.12.refs_9_.refs_11_
  30.9 3.4 %shard_map.163.refs_12_ = f32[3,8,384]{2,1,0:T(8,128)S(1)} custom-call(s32[1]{0:T(128)} %bitcast.idx_ref.refs_0_, s32[512,2]{1,0:T(8,128)S(1)} %copy.28.win_ref.refs_1_, bf16[4,2,32,384]{3,2,1,0:T(8,128)(2,1)S(1)} %get-tuple-element.41.refs_0_.refs_2_, bf16[4,2,32,384]{3,2,1,0:T(8,128)(2,1)S(1)} %collective-permute-done.4.refs_1_.refs_3_, ...), custom_call_target="tpu_custom_call" | custom-call | flops 301989888 | bytes 3000000 | tf_op jit(solution)/shard_map/pallas_call | solution.py:385
  34.3 1.9 %collective-permute-start.16 = (f32[3,8,384]{2,1,0:T(8,128)S(1)}, f32[3,8,384]{2,1,0:T(8,128)S(1)}, u32[]{:S(2)}, u32[]{:S(2)}) collective-permute-start(f32[3,8,384]{2,1,0:T(8,128)S(1)} %shard_map.163.refs_12_), channel_id=1, source_target_pairs={{8,0},{9,1},{10,2},{11,3},{12,4},{13,5},{14,6},{15,7},{16,8},{17,9... | collective-permute-start | bytes 110600 | tf_op jit(solution)/shard_map/ppermute | solution.py:360
  36.3 6.7 %collective-permute-start.15 = (f32[3,8,384]{2,1,0:T(8,128)S(1)}, f32[3,8,384]{2,1,0:T(8,128)S(1)}, u32[]{:S(2)}, u32[]{:S(2)}) collective-permute-start(f32[3,8,384]{2,1,0:T(8,128)S(1)} %shard_map.163.refs_12_), channel_id=1, source_target_pairs={{0,8},{1,9},{2,10},{3,11},{4,12},{5,13},{6,14},{7,15},{8,16},{9,17... | collective-permute-start | bytes 110600 | tf_op jit(solution)/shard_map/ppermute | solution.py:360
  43.0 2.1 %collective-permute-start.14 = (f32[3,8,384]{2,1,0:T(8,128)S(1)}, f32[3,8,384]{2,1,0:T(8,128)S(1)}, u32[]{:S(2)}, u32[]{:S(2)}) collective-permute-start(f32[3,8,384]{2,1,0:T(8,128)S(1)} %shard_map.163.refs_12_), channel_id=1, source_target_pairs={{4,8},{5,9},{6,10},{7,11},{8,4},{9,5},{10,6},{11,7},{12,16},{13,17... | collective-permute-start | bytes 110600 | tf_op jit(solution)/shard_map/ppermute | solution.py:360
  45.1 0.2 collective-permute-start.13
  45.3 5.6 %shard_map.162 = (bf16[256,768]{1,0:T(8,128)(2,1)}, bf16[256,768]{1,0:T(8,128)(2,1)}, bf16[256,384]{1,0:T(8,128)(2,1)S(1)}, bf16[256,384]{1,0:T(8,128)(2,1)S(1)}...) custom-call(s32[1]{0:T(128)} %bitcast.idx_ref.refs_0_, ...), custom_call_target="tpu_custom_call" | custom-call | flops 754974720 | bytes 5000000 | tf_op jit(solution)/shard_map/pallas_call | solution.py:385
  50.9 2.4 %collective-permute-start.17 = (bf16[256,384]{1,0:T(8,128)(2,1)S(1)}, bf16[256,384]{1,0:T(8,128)(2,1)S(1)}, u32[]{:S(2)}, u32[]{:S(2)}) collective-permute-start(bf16[256,384]{1,0:T(8,128)(2,1)S(1)} %get-tuple-element.53), channel_id=1, source_target_pairs={{0,2},{1,3},{2,0},{3,1},{4,6},{5,7},{6,4},{7,5},{8,10},{9,11},{10,... | collective-permute-start | bytes 589832 | tf_op jit(solution)/shard_map/ppermute | solution.py:360
  53.3 0.3 collective-permute-start.18
  53.6 5.3 %shard_map.164 = (bf16[256,768]{1,0:T(8,128)(2,1)}, bf16[256,768]{1,0:T(8,128)(2,1)}, bf16[256,384]{1,0:T(8,128)(2,1)S(1)}, bf16[256,384]{1,0:T(8,128)(2,1)S(1)}...) custom-call(s32[1]{0:T(128)} %bitcast.idx_ref.refs_0_, ...), custom_call_target="tpu_custom_call", output_to_operand_aliasing={{4}: (17, {}), {5}: (18, {}), {6}: (19, {}), {7}: (20, {}),... | custom-call | flops 905969664 | bytes 5000000 | tf_op jit(solution)/shard_map/pallas_call | solution.py:385
  58.9 1.7 %collective-permute-start.19 = (bf16[256,384]{1,0:T(8,128)(2,1)S(1)}, bf16[256,384]{1,0:T(8,128)(2,1)S(1)}, u32[]{:S(2)}, u32[]{:S(2)}) collective-permute-start(bf16[256,384]{1,0:T(8,128)(2,1)S(1)} %get-tuple-element.55), channel_id=1, source_target_pairs={{0,2},{1,3},{2,0},{3,1},{4,6},{5,7},{6,4},{7,5},{8,10},{9,11},{10,... | collective-permute-start | bytes 589832 | tf_op jit(solution)/shard_map/ppermute | solution.py:360
  60.6 1.0 %collective-permute-start.21 = (bf16[4,2,32,384]{3,2,1,0:T(8,128)(2,1)S(1)}, bf16[4,2,32,384]{3,2,1,0:T(8,128)(2,1)S(1)}, u32[]{:S(2)}, u32[]{:S(2)}) collective-permute-start(bf16[4,2,32,384]{3,2,1,0:T(8,128)(2,1)S(1)} %get-tuple-element.59), channel_id=1, source_target_pairs={{0,1},{1,0},{2,3},{3,2},{4,5},{5,4},{6,7},{7,6},{8,9},{9,8},{10,11... | collective-permute-start | bytes 589832 | tf_op jit(solution)/shard_map/ppermute | solution.py:360
  61.7 2.2 %collective-permute-start.23 = (bf16[4,2,32,384]{3,2,1,0:T(8,128)(2,1)S(1)}, bf16[4,2,32,384]{3,2,1,0:T(8,128)(2,1)S(1)}, u32[]{:S(2)}, u32[]{:S(2)}) collective-permute-start(bf16[4,2,32,384]{3,2,1,0:T(8,128)(2,1)S(1)} %get-tuple-element.61), channel_id=1, source_target_pairs={{0,5},{1,4},{2,7},{3,6},{4,1},{5,0},{6,3},{7,2},{8,13},{9,12},{10,... | collective-permute-start | bytes 589832 | tf_op jit(solution)/shard_map/ppermute | solution.py:360
  63.9 6.4 %collective-permute-start.24 = (bf16[4,2,32,384]{3,2,1,0:T(8,128)(2,1)S(1)}, bf16[4,2,32,384]{3,2,1,0:T(8,128)(2,1)S(1)}, u32[]{:S(2)}, u32[]{:S(2)}) collective-permute-start(bf16[4,2,32,384]{3,2,1,0:T(8,128)(2,1)S(1)} %get-tuple-element.62), channel_id=1, source_target_pairs={{4,8},{5,9},{6,10},{7,11},{8,4},{9,5},{10,6},{11,7},{12,16},{13,17... | collective-permute-start | bytes 589832 | tf_op jit(solution)/shard_map/ppermute | solution.py:360
  70.3 3.0 %collective-permute-start.25 = (bf16[4,2,32,384]{3,2,1,0:T(8,128)(2,1)S(1)}, bf16[4,2,32,384]{3,2,1,0:T(8,128)(2,1)S(1)}, u32[]{:S(2)}, u32[]{:S(2)}) collective-permute-start(bf16[4,2,32,384]{3,2,1,0:T(8,128)(2,1)S(1)} %get-tuple-element.63), channel_id=1, source_target_pairs={{4,9},{5,8},{6,11},{7,10},{8,5},{9,4},{10,7},{11,6},{12,17},{13,16... | collective-permute-start | bytes 589832 | tf_op jit(solution)/shard_map/ppermute | solution.py:360
  73.3 1.6 %shard_map.165 = (bf16[256,768]{1,0:T(8,128)(2,1)}, bf16[256,768]{1,0:T(8,128)(2,1)}, bf16[256,768]{1,0:T(8,128)(2,1)}, bf16[256,768]{1,0:T(8,128)(2,1)}, s32[1]{0:T(128)}) custom-call(s32[1]{0:T(128)} %bitcast.idx_ref.refs_0_, bf16[256,768]{1,0:T(8,128)(2,1)} %get-tuple-element.43.refs_0_, ...), custom_call_target="tpu_custom_call", output_to_operand_aliasing={{0}: (1, {}), {1}: (2, {}), {2}: (3, {}), {3}: (4, {})} | custom-call | bytes 1600000 | tf_op jit(solution)/shard_map/pallas_call | solution.py:385
  74.9 0.2 collective-permute-done.24.by_b
  75.1 7.6 %collective-permute-done.25.by_bx = bf16[4,2,32,384]{3,2,1,0:T(8,128)(2,1)S(1)} collective-permute-done((bf16[4,2,32,384]{3,2,1,0:T(8,128)(2,1)S(1)}, bf16[4,2,32,384]{3,2,1,0:T(8,128)(2,1)S(1)}, u32[]{:S(2)}, u32[]{:S(2)}) %collective-permute-start.25) | collective-permute-done | bytes 196640 | tf_op jit(solution)/shard_map/ppermute | solution.py:360
  82.7 1.4 %shard_map.166 = (bf16[4,2,32,384]{3,2,1,0:T(8,128)(2,1)S(1)}, bf16[4,2,32,384]{3,2,1,0:T(8,128)(2,1)S(1)}) custom-call(s32[1]{0:T(128)} %bitcast.idx_ref.refs_0_, s32[128]{0:T(128)S(1)} %copy-done.4, bf16[4,2,32,384]{3,2,1,0:T(8,128)(2,1)S(1)} %get-tuple-element.58.keep, bf16[4,2,32,384]{3,2,1,0:T(8,128)(2,1)S(1)} %collective-permute-done.21.by_aud, ...), custom_call_target="tpu_custom_call" | custom-call | flops 1000000 | bytes 1600000 | tf_op jit(solution)/shard_map/pallas_call | solution.py:385
  84.1 2.3 %collective-permute-start.26 = (bf16[4,2,32,384]{3,2,1,0:T(8,128)(2,1)S(1)}, bf16[4,2,32,384]{3,2,1,0:T(8,128)(2,1)S(1)}, u32[]{:S(2)}, u32[]{:S(2)}) collective-permute-start(bf16[4,2,32,384]{3,2,1,0:T(8,128)(2,1)S(1)} %get-tuple-element.66), channel_id=1, source_target_pairs={{0,2},{1,3},{2,0},{3,1},{4,6},{5,7},{6,4},{7,5},{8,10},{9,11},{10,... | collective-permute-start | bytes 589832 | tf_op jit(solution)/shard_map/ppermute | solution.py:360
  86.4 1.1 %collective-permute-done.26.other = bf16[4,2,32,384]{3,2,1,0:T(8,128)(2,1)S(1)} collective-permute-done((bf16[4,2,32,384]{3,2,1,0:T(8,128)(2,1)S(1)}, bf16[4,2,32,384]{3,2,1,0:T(8,128)(2,1)S(1)}, u32[]{:S(2)}, u32[]{:S(2)}) %collective-permute-start.26) | collective-permute-done | bytes 196640 | tf_op jit(solution)/shard_map/ppermute | solution.py:360
  87.5 0.8 shard_map.167
  (26 shorter events, 0.1 us)
Async XLA Ops:
  0.6 1.9 %collective-permute-start = (bf16[32,1536]{1,0:T(8,128)(2,1)}, bf16[32,1536]{1,0:T(8,128)(2,1)S(1)}, u32[]{:S(2)}, u32[]{:S(2)}) collective-permute-start(bf16[32,1536]{1,0:T(8,128)(2,1)} %refs_0_.1), channel_id=1, source_target_pairs={{0,2},{1,3},{2,0},{3,1},{4,6},{5,7},{6,4},{7,5},{8,10},{9,11},{10,... | collective-permute-start | bytes 294920 | tf_op jit(solution)/shard_map/ppermute | solution.py:360
  1.4 1.5 %collective-permute-start.2 = (bf16[32,1536]{1,0:T(8,128)(2,1)}, bf16[32,1536]{1,0:T(8,128)(2,1)S(1)}, u32[]{:S(2)}, u32[]{:S(2)}) collective-permute-start(bf16[32,1536]{1,0:T(8,128)(2,1)} %refs_2_.1), channel_id=1, source_target_pairs={{0,2},{1,3},{2,0},{3,1},{4,6},{5,7},{6,4},{7,5},{8,10},{9,11},{10,... | collective-permute-start | bytes 294920 | tf_op jit(solution)/shard_map/ppermute | solution.py:360
  1.5 1.6 %collective-permute-start.3 = (bf16[32,1536]{1,0:T(8,128)(2,1)}, bf16[32,1536]{1,0:T(8,128)(2,1)S(1)}, u32[]{:S(2)}, u32[]{:S(2)}) collective-permute-start(bf16[32,1536]{1,0:T(8,128)(2,1)} %refs_3_.1), channel_id=1, source_target_pairs={{0,2},{1,3},{2,0},{3,1},{4,6},{5,7},{6,4},{7,5},{8,10},{9,11},{10,... | collective-permute-start | bytes 294920 | tf_op jit(solution)/shard_map/ppermute | solution.py:360
  1.9 1.5 %collective-permute-start.1 = (bf16[32,1536]{1,0:T(8,128)(2,1)}, bf16[32,1536]{1,0:T(8,128)(2,1)S(1)}, u32[]{:S(2)}, u32[]{:S(2)}) collective-permute-start(bf16[32,1536]{1,0:T(8,128)(2,1)} %refs_1_.2), channel_id=1, source_target_pairs={{0,2},{1,3},{2,0},{3,1},{4,6},{5,7},{6,4},{7,5},{8,10},{9,11},{10,... | collective-permute-start | bytes 294920 | tf_op jit(solution)/shard_map/ppermute | solution.py:360
  2.0 1.4 %copy-start.4 = (s32[128]{0:T(128)S(1)}, s32[128]{0:T(128)}, u32[]{:S(2)}) copy-start(s32[128]{0:T(128)} %len_ref.5) | copy-start | bytes 1540
  3.4 8.3 %copy-start = (bf16[256,768]{1,0:T(8,128)(2,1)S(1)}, bf16[256,768]{1,0:T(8,128)(2,1)}, u32[]{:S(2)}) copy-start(bf16[256,768]{1,0:T(8,128)(2,1)} %refs_8_.1) | copy-start | bytes 1179652
  3.4 17.4 %copy-start.1 = (bf16[256,768]{1,0:T(8,128)(2,1)S(1)}, bf16[256,768]{1,0:T(8,128)(2,1)}, u32[]{:S(2)}) copy-start(bf16[256,768]{1,0:T(8,128)(2,1)} %refs_9_.1) | copy-start | bytes 1179652
  3.4 22.0 %copy-start.5 = (s32[512,2]{0,1:T(2,128)S(1)}, s32[512,2]{0,1:T(2,128)}, u32[]{:S(2)}) copy-start(s32[512,2]{0,1:T(2,128)} %param.18) | copy-start | bytes 12292
  5.1 15.7 %collective-permute-start.8 = (bf16[4,2,32,384]{3,2,1,0:T(8,128)(2,1)S(1)}, bf16[4,2,32,384]{3,2,1,0:T(8,128)(2,1)S(1)}, u32[]{:S(2)}, u32[]{:S(2)}) collective-permute-start(bf16[4,2,32,384]{3,2,1,0:T(8,128)(2,1)S(1)} %get-tuple-element.42), channel_id=1, source_target_pairs={{4,9},{5,8},{6,11},{7,10},{8,5},{9,4},{10,7},{11,6},{12,17},{13,16... | collective-permute-start | bytes 589832 | tf_op jit(solution)/shard_map/ppermute | solution.py:360
  9.4 13.7 %collective-permute-start.6 = (bf16[4,2,32,384]{3,2,1,0:T(8,128)(2,1)S(1)}, bf16[4,2,32,384]{3,2,1,0:T(8,128)(2,1)S(1)}, u32[]{:S(2)}, u32[]{:S(2)}) collective-permute-start(bf16[4,2,32,384]{3,2,1,0:T(8,128)(2,1)S(1)} %get-tuple-element.42), channel_id=1, source_target_pairs={{0,5},{1,4},{2,7},{3,6},{4,1},{5,0},{6,3},{7,2},{8,13},{9,12},{10,... | collective-permute-start | bytes 589832 | tf_op jit(solution)/shard_map/ppermute | solution.py:360
  10.0 14.2 %collective-permute-start.4 = (bf16[4,2,32,384]{3,2,1,0:T(8,128)(2,1)S(1)}, bf16[4,2,32,384]{3,2,1,0:T(8,128)(2,1)S(1)}, u32[]{:S(2)}, u32[]{:S(2)}) collective-permute-start(bf16[4,2,32,384]{3,2,1,0:T(8,128)(2,1)S(1)} %get-tuple-element.42), channel_id=1, source_target_pairs={{0,1},{1,0},{2,3},{3,2},{4,5},{5,4},{6,7},{7,6},{8,9},{9,8},{10,11... | collective-permute-start | bytes 589832 | tf_op jit(solution)/shard_map/ppermute | solution.py:360
  11.8 19.1 %collective-permute-start.11 = (bf16[256,768]{1,0:T(8,128)(2,1)S(1)}, bf16[256,768]{1,0:T(8,128)(2,1)S(1)}, u32[]{:S(2)}, u32[]{:S(2)}) collective-permute-start(bf16[256,768]{1,0:T(8,128)(2,1)S(1)} %copy-done), channel_id=1, source_target_pairs={{0,2},{1,3},{2,0},{3,1},{4,6},{5,7},{6,4},{7,5},{8,10},{9,11},{10,... | collective-permute-start | bytes 1179656 | tf_op jit(solution)/shard_map/ppermute | solution.py:360
  12.5 12.9 %collective-permute-start.7 = (bf16[4,2,32,384]{3,2,1,0:T(8,128)(2,1)S(1)}, bf16[4,2,32,384]{3,2,1,0:T(8,128)(2,1)S(1)}, u32[]{:S(2)}, u32[]{:S(2)}) collective-permute-start(bf16[4,2,32,384]{3,2,1,0:T(8,128)(2,1)S(1)} %get-tuple-element.41.refs_0_.refs_2_), channel_id=1, source_target_pairs={{4,8},{5,9},{6,10},{7,11},{8,4},{9,5},{10,6},{11,7},{12,16},{13,17... | collective-permute-start | bytes 589832 | tf_op jit(solution)/shard_map/ppermute | solution.py:360
  20.8 10.1 %collective-permute-start.12 = (bf16[256,768]{1,0:T(8,128)(2,1)S(1)}, bf16[256,768]{1,0:T(8,128)(2,1)S(1)}, u32[]{:S(2)}, u32[]{:S(2)}) collective-permute-start(bf16[256,768]{1,0:T(8,128)(2,1)S(1)} %copy-done.1), channel_id=1, source_target_pairs={{0,2},{1,3},{2,0},{3,1},{4,6},{5,7},{6,4},{7,5},{8,10},{9,11},{10,... | collective-permute-start | bytes 1179656 | tf_op jit(solution)/shard_map/ppermute | solution.py:360
  23.1 22.0 %collective-permute-start.9 = (bf16[256,768]{1,0:T(8,128)(2,1)}, bf16[256,768]{1,0:T(8,128)(2,1)S(1)}, u32[]{:S(2)}, u32[]{:S(2)}) collective-permute-start(bf16[256,768]{1,0:T(8,128)(2,1)} %refs_6_.2), channel_id=1, source_target_pairs={{0,2},{1,3},{2,0},{3,1},{4,6},{5,7},{6,4},{7,5},{8,10},{9,11},{10,... | collective-permute-start | bytes 1179656 | tf_op jit(solution)/shard_map/ppermute | solution.py:360
  24.1 21.1 %collective-permute-start.10 = (bf16[256,768]{1,0:T(8,128)(2,1)}, bf16[256,768]{1,0:T(8,128)(2,1)}, u32[]{:S(2)}, u32[]{:S(2)}) collective-permute-start(bf16[256,768]{1,0:T(8,128)(2,1)} %refs_7_.2), channel_id=1, source_target_pairs={{0,2},{1,3},{2,0},{3,1},{4,6},{5,7},{6,4},{7,5},{8,10},{9,11},{10,... | collective-permute-start | bytes 1179656 | tf_op jit(solution)/shard_map/ppermute | solution.py:360
  25.4 5.5 %collective-permute-start.5 = (bf16[4,2,32,384]{3,2,1,0:T(8,128)(2,1)S(1)}, bf16[4,2,32,384]{3,2,1,0:T(8,128)(2,1)S(1)}, u32[]{:S(2)}, u32[]{:S(2)}) collective-permute-start(bf16[4,2,32,384]{3,2,1,0:T(8,128)(2,1)S(1)} %get-tuple-element.41.refs_0_.refs_2_), channel_id=1, source_target_pairs={{0,4},{1,5},{2,6},{3,7},{4,0},{5,1},{6,2},{7,3},{8,12},{9,13},{10,... | collective-permute-start | bytes 589832 | tf_op jit(solution)/shard_map/ppermute | solution.py:360
  25.6 19.7 %copy-start.2 = (bf16[256,768]{1,0:T(8,128)(2,1)S(1)}, bf16[256,768]{1,0:T(8,128)(2,1)}, u32[]{:S(2)}) copy-start(bf16[256,768]{1,0:T(8,128)(2,1)} %refs_6_.2) | copy-start | bytes 1179652
  25.6 19.7 %copy-start.3 = (bf16[256,768]{1,0:T(8,128)(2,1)S(1)}, bf16[256,768]{1,0:T(8,128)(2,1)}, u32[]{:S(2)}) copy-start(bf16[256,768]{1,0:T(8,128)(2,1)} %refs_7_.2) | copy-start | bytes 1179652
  34.3 19.0 %collective-permute-start.16 = (f32[3,8,384]{2,1,0:T(8,128)S(1)}, f32[3,8,384]{2,1,0:T(8,128)S(1)}, u32[]{:S(2)}, u32[]{:S(2)}) collective-permute-start(f32[3,8,384]{2,1,0:T(8,128)S(1)} %shard_map.163.refs_12_), channel_id=1, source_target_pairs={{8,0},{9,1},{10,2},{11,3},{12,4},{13,5},{14,6},{15,7},{16,8},{17,9... | collective-permute-start | bytes 110600 | tf_op jit(solution)/shard_map/ppermute | solution.py:360
  36.3 17.3 %collective-permute-start.15 = (f32[3,8,384]{2,1,0:T(8,128)S(1)}, f32[3,8,384]{2,1,0:T(8,128)S(1)}, u32[]{:S(2)}, u32[]{:S(2)}) collective-permute-start(f32[3,8,384]{2,1,0:T(8,128)S(1)} %shard_map.163.refs_12_), channel_id=1, source_target_pairs={{0,8},{1,9},{2,10},{3,11},{4,12},{5,13},{6,14},{7,15},{8,16},{9,17... | collective-permute-start | bytes 110600 | tf_op jit(solution)/shard_map/ppermute | solution.py:360
  43.0 10.6 %collective-permute-start.14 = (f32[3,8,384]{2,1,0:T(8,128)S(1)}, f32[3,8,384]{2,1,0:T(8,128)S(1)}, u32[]{:S(2)}, u32[]{:S(2)}) collective-permute-start(f32[3,8,384]{2,1,0:T(8,128)S(1)} %shard_map.163.refs_12_), channel_id=1, source_target_pairs={{4,8},{5,9},{6,10},{7,11},{8,4},{9,5},{10,6},{11,7},{12,16},{13,17... | collective-permute-start | bytes 110600 | tf_op jit(solution)/shard_map/ppermute | solution.py:360
  45.1 8.5 %collective-permute-start.13 = (f32[3,8,384]{2,1,0:T(8,128)S(1)}, f32[3,8,384]{2,1,0:T(8,128)S(1)}, u32[]{:S(2)}, u32[]{:S(2)}) collective-permute-start(f32[3,8,384]{2,1,0:T(8,128)S(1)} %shard_map.163.refs_12_), channel_id=1, source_target_pairs={{0,4},{1,5},{2,6},{3,7},{4,0},{5,1},{6,2},{7,3},{8,12},{9,13},{10,... | collective-permute-start | bytes 110600 | tf_op jit(solution)/shard_map/ppermute | solution.py:360
  50.9 10.8 %collective-permute-start.17 = (bf16[256,384]{1,0:T(8,128)(2,1)S(1)}, bf16[256,384]{1,0:T(8,128)(2,1)S(1)}, u32[]{:S(2)}, u32[]{:S(2)}) collective-permute-start(bf16[256,384]{1,0:T(8,128)(2,1)S(1)} %get-tuple-element.53), channel_id=1, source_target_pairs={{0,2},{1,3},{2,0},{3,1},{4,6},{5,7},{6,4},{7,5},{8,10},{9,11},{10,... | collective-permute-start | bytes 589832 | tf_op jit(solution)/shard_map/ppermute | solution.py:360
  53.3 8.4 %collective-permute-start.18 = (bf16[256,384]{1,0:T(8,128)(2,1)S(1)}, bf16[256,384]{1,0:T(8,128)(2,1)S(1)}, u32[]{:S(2)}, u32[]{:S(2)}) collective-permute-start(bf16[256,384]{1,0:T(8,128)(2,1)S(1)} %get-tuple-element.54), channel_id=1, source_target_pairs={{0,2},{1,3},{2,0},{3,1},{4,6},{5,7},{6,4},{7,5},{8,10},{9,11},{10,... | collective-permute-start | bytes 589832 | tf_op jit(solution)/shard_map/ppermute | solution.py:360
  58.9 5.0 %collective-permute-start.19 = (bf16[256,384]{1,0:T(8,128)(2,1)S(1)}, bf16[256,384]{1,0:T(8,128)(2,1)S(1)}, u32[]{:S(2)}, u32[]{:S(2)}) collective-permute-start(bf16[256,384]{1,0:T(8,128)(2,1)S(1)} %get-tuple-element.55), channel_id=1, source_target_pairs={{0,2},{1,3},{2,0},{3,1},{4,6},{5,7},{6,4},{7,5},{8,10},{9,11},{10,... | collective-permute-start | bytes 589832 | tf_op jit(solution)/shard_map/ppermute | solution.py:360
  60.6 9.7 %collective-permute-start.20 = (bf16[256,384]{1,0:T(8,128)(2,1)S(1)}, bf16[256,384]{1,0:T(8,128)(2,1)S(1)}, u32[]{:S(2)}, u32[]{:S(2)}) collective-permute-start(bf16[256,384]{1,0:T(8,128)(2,1)S(1)} %get-tuple-element.56), channel_id=1, source_target_pairs={{0,2},{1,3},{2,0},{3,1},{4,6},{5,7},{6,4},{7,5},{8,10},{9,11},{10,... | collective-permute-start | bytes 589832 | tf_op jit(solution)/shard_map/ppermute | solution.py:360
  60.6 14.3 %collective-permute-start.21 = (bf16[4,2,32,384]{3,2,1,0:T(8,128)(2,1)S(1)}, bf16[4,2,32,384]{3,2,1,0:T(8,128)(2,1)S(1)}, u32[]{:S(2)}, u32[]{:S(2)}) collective-permute-start(bf16[4,2,32,384]{3,2,1,0:T(8,128)(2,1)S(1)} %get-tuple-element.59), channel_id=1, source_target_pairs={{0,1},{1,0},{2,3},{3,2},{4,5},{5,4},{6,7},{7,6},{8,9},{9,8},{10,11... | collective-permute-start | bytes 589832 | tf_op jit(solution)/shard_map/ppermute | solution.py:360
  61.7 13.3 %collective-permute-start.22 = (bf16[4,2,32,384]{3,2,1,0:T(8,128)(2,1)S(1)}, bf16[4,2,32,384]{3,2,1,0:T(8,128)(2,1)S(1)}, u32[]{:S(2)}, u32[]{:S(2)}) collective-permute-start(bf16[4,2,32,384]{3,2,1,0:T(8,128)(2,1)S(1)} %get-tuple-element.60), channel_id=1, source_target_pairs={{0,4},{1,5},{2,6},{3,7},{4,0},{5,1},{6,2},{7,3},{8,12},{9,13},{10,... | collective-permute-start | bytes 589832 | tf_op jit(solution)/shard_map/ppermute | solution.py:360
  61.7 13.2 %collective-permute-start.23 = (bf16[4,2,32,384]{3,2,1,0:T(8,128)(2,1)S(1)}, bf16[4,2,32,384]{3,2,1,0:T(8,128)(2,1)S(1)}, u32[]{:S(2)}, u32[]{:S(2)}) collective-permute-start(bf16[4,2,32,384]{3,2,1,0:T(8,128)(2,1)S(1)} %get-tuple-element.61), channel_id=1, source_target_pairs={{0,5},{1,4},{2,7},{3,6},{4,1},{5,0},{6,3},{7,2},{8,13},{9,12},{10,... | collective-permute-start | bytes 589832 | tf_op jit(solution)/shard_map/ppermute | solution.py:360
  63.9 11.2 %collective-permute-start.24 = (bf16[4,2,32,384]{3,2,1,0:T(8,128)(2,1)S(1)}, bf16[4,2,32,384]{3,2,1,0:T(8,128)(2,1)S(1)}, u32[]{:S(2)}, u32[]{:S(2)}) collective-permute-start(bf16[4,2,32,384]{3,2,1,0:T(8,128)(2,1)S(1)} %get-tuple-element.62), channel_id=1, source_target_pairs={{4,8},{5,9},{6,10},{7,11},{8,4},{9,5},{10,6},{11,7},{12,16},{13,17... | collective-permute-start | bytes 589832 | tf_op jit(solution)/shard_map/ppermute | solution.py:360
  70.3 12.4 %collective-permute-start.25 = (bf16[4,2,32,384]{3,2,1,0:T(8,128)(2,1)S(1)}, bf16[4,2,32,384]{3,2,1,0:T(8,128)(2,1)S(1)}, u32[]{:S(2)}, u32[]{:S(2)}) collective-permute-start(bf16[4,2,32,384]{3,2,1,0:T(8,128)(2,1)S(1)} %get-tuple-element.63), channel_id=1, source_target_pairs={{4,9},{5,8},{6,11},{7,10},{8,5},{9,4},{10,7},{11,6},{12,17},{13,16... | collective-permute-start | bytes 589832 | tf_op jit(solution)/shard_map/ppermute | solution.py:360
  84.1 3.4 %collective-permute-start.26 = (bf16[4,2,32,384]{3,2,1,0:T(8,128)(2,1)S(1)}, bf16[4,2,32,384]{3,2,1,0:T(8,128)(2,1)S(1)}, u32[]{:S(2)}, u32[]{:S(2)}) collective-permute-start(bf16[4,2,32,384]{3,2,1,0:T(8,128)(2,1)S(1)} %get-tuple-element.66), channel_id=1, source_target_pairs={{0,2},{1,3},{2,0},{3,1},{4,6},{5,7},{6,4},{7,5},{8,10},{9,11},{10,... | collective-permute-start | bytes 589832 | tf_op jit(solution)/shard_map/ppermute | solution.py:360

commit v4 on v3

--- a/solution.py
+++ b/solution.py
@@ -101,15 +101,6 @@
     return lo, hi
 
 
-def av_bias(idx_ref, win_ref, bias):
-    c, r, _ = coords(idx_ref)
-    for i, stretch in enumerate((r, 1 - r)):
-        shape = bias.shape[1:]
-        lo, hi = window_bounds(win_ref, c, stretch, shape, 0)
-        place = lax.broadcasted_iota(jnp.int32, shape, 1) // BLK
-        bias[i] = jnp.where((place >= lo) & (place < hi), 0.0, NEG)
-
-
 def window_of(idx_ref, win_ref, stretch, b):
     c, _, _ = coords(idx_ref)
     return win_ref[4 * stretch + b, 0] - (2 * c - 2), win_ref[4 * stretch + b, 1]
@@ -149,16 +140,43 @@
     return lax.dot_general(x, y, (((0,), (0,)), ((), ())), preferred_element_type=F32)
 
 
-def stats_kernel(idx_ref, win_ref, *refs):
-    pieces = refs[:6]
-    video = ((refs[6], refs[7]), (refs[8], refs[9]))
-    stat_ref, audio, bias = refs[10:]
+def group_places(c):
+    side = 2 - 2 * (c & 1)
+    return 1, side, 2 - side
+
+
+def group_bias(idx_ref, win_ref, groups, bias):
+    c, r, _ = coords(idx_ref)
+    places = group_places(c)
+    shape = bias.shape[1:]
+    lane = lax.broadcasted_iota(jnp.int32, shape, 1)
+    place = jnp.zeros(shape, jnp.int32)
+    for n, group in enumerate(groups):
+        place = jnp.where(lane // PAIR == n, 2 * places[group], place)
+    place = place + (lane % PAIR) // BLK
+    for i, stretch in enumerate((r, 1 - r)):
+        lo, hi = window_bounds(win_ref, c, stretch, shape, 0)
+        bias[i] = jnp.where((place >= lo) & (place < hi), 0.0, NEG)
+
+
+def stats_kernel(groups, idx_ref, win_ref, *refs):
+    count = len(groups)
+    pieces, refs = refs[: 2 * count], refs[2 * count :]
+    video, refs = ((refs[0], refs[1]), (refs[2], refs[3])), refs[4:]
+    stat_ref, audio, bias = refs[-3:]
+    _, _, a = coords(idx_ref)
+    half = BLK // 2
 
     @pl.when(pl.program_id(0) == 0)
     def _():
-        av_bias(idx_ref, win_ref, bias)
-
-    gather_audio(idx_ref, pieces, audio)
+        group_bias(idx_ref, win_ref, groups, bias)
+
+    for n in range(count):
+        for ref, part in ((pieces[2 * n], a), (pieces[2 * n + 1], 1 - a)):
+            for core in range(2):
+                first = pl.multiple_of(n * PAIR + core * BLK + part * half, half)
+                for k in range(2):
+                    audio[k, pl.ds(first, half), :] = ref[k, core]
     queries, cot = audio[0], audio[1]
     lses, deltas = [], []
     for e in range(2):
@@ -174,36 +192,33 @@
         total = parts[0][1] * w0 + parts[1][1] * w1
         lses.append(m + jnp.log(total))
         deltas.append((parts[0][2] * w0 + parts[1][2] * w1) / total)
-    stat_ref[0] = jnp.concatenate(lses + deltas + lses + deltas, axis=0)
-
-
-def merge_stats(idx_ref, chips, own, by_a, by_b, before2, after2):
+    rows = jnp.concatenate(lses + deltas + lses + deltas, axis=0)
+    if count == 1:
+        rows = jnp.concatenate([refs[0][0, :, :PAIR], rows], axis=1)
+    stat_ref[0] = rows
+
+
+def merge_stats(idx_ref, chips, own_a, own_b, by_a, by_b, by_q, by_q2):
     c, _, _ = coords(idx_ref)
     even = (c & 1) == 0
-    before = jnp.where(even, by_b, by_a)
-    after = jnp.where(even, by_a, by_b)
-    w = 2 * BLK
-
-    def part(x, k, there):
-        x = x[:, k * w : (k + 1) * w]
-        return jnp.where(there, x[0:2], NEG), x[2:4]
-
-    one, two = c >= 1, c >= 2
-    nxt, nxt2 = c + 1 < chips, c + 2 < chips
-    always = c >= 0
-    groups = (
-        (part(own, 0, always), part(before, 1, one), part(before2, 2, two)),
-        (part(own, 1, always), part(before, 2, one), part(after, 0, nxt)),
-        (part(own, 2, always), part(after, 1, nxt), part(after2, 0, nxt2)),
-    )
-    lses, deltas = [], []
-    for group in groups:
+    has_b = jnp.where(even, c >= 2, c + 2 < chips)
+    has_q2 = jnp.where(even, c + 2 < chips, c >= 2)
+
+    def part(x, k, there=None):
+        x = x[:, k * PAIR : (k + 1) * PAIR]
+        return (x[0:2] if there is None else jnp.where(there, x[0:2], NEG)), x[2:4]
+
+    merged = []
+    for group in (
+        (part(own_a, 0), part(by_a, 1), part(by_b, 1, has_b)),
+        (part(own_a, 1), part(by_a, 0), part(by_q2, 1, has_q2)),
+        (part(own_b, 1), part(by_b, 0, has_b), part(by_q, 1, has_b)),
+    ):
         m = jnp.maximum(jnp.maximum(group[0][0], group[1][0]), group[2][0])
         ws = [jnp.exp(lse - m) for lse, _ in group]
         total = ws[0] + ws[1] + ws[2]
-        lses.append(m + jnp.log(total))
-        deltas.append(sum(wt * d for wt, (_, d) in zip(ws, group)) / total)
-    return jnp.concatenate(lses, axis=1), jnp.concatenate(deltas, axis=1)
+        merged.append((m + jnp.log(total), sum(wt * d for wt, (_, d) in zip(ws, group)) / total))
+    return merged
 
 
 def va_kernel(idx_ref, win_ref, len_ref, *refs):
@@ -253,20 +268,21 @@
 def av_kernel(chips, idx_ref, win_ref, *refs):
     pieces = refs[:6]
     video = ((refs[6], refs[7]), (refs[8], refs[9]))
-    stats = [ref[0] for ref in refs[10:15]]
-    outs = ((refs[21], refs[22]), (refs[23], refs[24]))
-    back = refs[25:31]
-    audio, bias, grads, rowstat = refs[31:]
-    _, r, _ = coords(idx_ref)
+    stats = [ref[0] for ref in refs[10:16]]
+    outs = ((refs[22], refs[23]), (refs[24], refs[25]))
+    back = refs[26:32]
+    audio, bias, grads, rowstat = refs[32:]
+    c, r, _ = coords(idx_ref)
 
     @pl.when(pl.program_id(0) == 0)
     def _():
         block_bias(idx_ref, win_ref, None, bias)
 
     gather_audio(idx_ref, pieces, audio)
-    for n, x in enumerate(merge_stats(idx_ref, chips, *stats)):
-        wide = [jnp.broadcast_to(x[e : e + 1], (HD, KEYS)) for e in range(2)]
-        rowstat[n] = jnp.concatenate(wide, axis=0).T
+    for place, merged in zip(group_places(c), merge_stats(idx_ref, chips, *stats)):
+        for n, x in enumerate(merged):
+            wide = [jnp.broadcast_to(x[e : e + 1], (HD, PAIR)) for e in range(2)]
+            rowstat[n, pl.ds(place * PAIR, PAIR), :] = jnp.concatenate(wide, axis=0).T
     grads[...] = jnp.zeros(grads.shape, F32)
     for group in block_groups(r):
         work = []
@@ -352,8 +368,8 @@
         "Ax": perm(lambda v, a: (v ^ 2, 1 - a)),
         "B": perm(lambda v, a: (diagonal(v), a)),
         "Bx": perm(lambda v, a: (diagonal(v), 1 - a)),
-        "p2": perm(lambda v, a: (v + 4, a)),
-        "m2": perm(lambda v, a: (v - 4, a)),
+        "Q": perm(lambda v, a: (v - 4 if v & 2 else v + 4, a)),
+        "Q2": perm(lambda v, a: (v + 4 if v & 2 else v - 4, a)),
     }
 
     def move(x, name):
@@ -377,7 +393,7 @@
         own_spec = pl.BlockSpec((rows, PAIR), lambda h, i: (0, ((i[0] >> 1) & 1) * steps + h))
         far_spec = pl.BlockSpec((rows, PAIR), lambda h, i: (0, h))
         join_spec = pl.BlockSpec((rows, PAIR), lambda h, i: (0, (1 - ((i[0] >> 1) & 1)) * steps + h))
-        stat_spec = pl.BlockSpec((1, 8, KEYS), lambda h, i: (h, 0, 0))
+        stat_spec = pl.BlockSpec((1, 8, 2 * PAIR), lambda h, i: (h, 0, 0))
         any_spec = pl.BlockSpec(memory_space=pl.ANY)
         hbm = pl.BlockSpec(memory_space=pltpu.HBM)
 
@@ -414,16 +430,24 @@
         bias_scratch = pltpu.VMEM((8, WMAX * BLK, PAIR), F32)
         pairs = 2 * steps * 2 * rows * KEYS
 
-        stat = shape((steps, 8, KEYS), F32)
-        (stats,) = call(
-            stats_kernel,
-            [win_spec] + [piece_spec(0)] * 6 + [own_spec] * 4,
-            [(stat_spec, stat)],
-            (window, *pieces, k_v, v_v, k_f, v_f),
-            scratch=(audio_scratch, pltpu.VMEM((2, rows, KEYS), F32)),
-            est=cost(4 * HD * pairs, pairs, 3000000),
-        )
-        others = [move(stats, name) for name in ("A", "B", "p2", "m2")]
+        stat = shape((steps, 8, 2 * PAIR), F32)
+
+        def find_stats(groups, before):
+            lanes = len(groups) * PAIR
+            (found,) = call(
+                lambda *refs: stats_kernel(groups, *refs),
+                [win_spec] + [piece_spec(0)] * (2 * len(groups)) + [own_spec] * 4 + [stat_spec] * len(before),
+                [(stat_spec, stat)],
+                (window, *[pieces[2 * g + n] for g in groups for n in range(2)], k_v, v_v, k_f, v_f, *before),
+                scratch=(pltpu.VMEM((2, lanes, PAIR), BF), pltpu.VMEM((2, rows, lanes), F32)),
+                est=cost(4 * HD * pairs * lanes // KEYS, pairs * lanes // KEYS, 2000000),
+            )
+            return found
+
+        stats_a = find_stats((0, 1), ())
+        by_a, by_q = move(stats_a, "A"), move(stats_a, "Q")
+        stats_b = find_stats((2,), (stats_a,))
+        by_b, by_q2 = move(stats_b, "B"), move(stats_b, "Q2")
 
         full, far = shape((rows, width), BF), shape((rows, quarter), BF)
         va = call(
@@ -437,11 +461,11 @@
         out_video, dq_video, out_far, dq_far = va[:4]
         av = call(
             lambda *refs: av_kernel(chips, *refs),
-            [win_spec] + [piece_spec(0)] * 6 + [own_spec] * 4 + [stat_spec] * 5 + [any_spec] * 6,
+            [win_spec] + [piece_spec(0)] * 6 + [own_spec] * 4 + [stat_spec] * 6 + [any_spec] * 6,
             [(own_spec, full)] * 2 + [(far_spec, far)] * 2 + [(piece_spec(1), piece)] * 6,
-            (window, *pieces, k_v, v_v, k_f, v_f, stats, *others, *va[4:]),
+            (window, *pieces, k_v, v_v, k_f, v_f, stats_a, stats_b, by_a, by_b, by_q, by_q2, *va[4:]),
             scratch=(audio_scratch, bias_scratch, grad_scratch, grad_scratch),
-            aliases={17 + i: 4 + i for i in range(6)},
+            aliases={18 + i: 4 + i for i in range(6)},
             est=cost(12 * HD * pairs, pairs, 5000000),
         )
         dk_video, dv_video, dk_far, dv_far = av[:4]

time: 88.6 us -> 91.3 us (1.030)
  the two profiles are of different devices: /device:TPU:127 before, /device:TPU:129 now
where the time goes in v4:
time: 91.3 us; the launch traced here: 90.9 us
  starting transfers between devices  46.2 us (51%)
  Pallas kernels  22.2 us (24%)
  waiting for transfers between devices  21.5 us (24%)
    ppermute x27, starting transfers between devices, move(): return lax.ppermute(x, ('vid', 'aud'), moves[name])  46.2 us
    pallas_call x8, Pallas kernels, call(): pl.pallas_call(kernel, grid_spec=pltpu.PrefetchScalarGridSpec(num_scalar_...  22.2 us
    ppermute x27, waiting for transfers between devices, move(): return lax.ppermute(x, ('vid', 'aud'), moves[name])  21.5 us
  transfers between devices with their start and end apart: 27, of which 10 were waited for; matrix products, arithmetic and copies ran while one was open for 0% of the time, Pallas kernels for 22%

profile of v4, /device:TPU:129, one launch (start us, length us, event | category | flops | bytes accessed | tf_op | source)
XLA Modules:
  0.0 90.9 jit_solution(5897824474349561123)
XLA Ops:
  0.6 0.8 collective-permute-start
  1.4 0.1 collective-permute-start.2
  1.5 0.4 collective-permute-start.3
  1.9 0.1 collective-permute-start.1
  2.0 0.4 collective-permute-start.11
  2.4 0.1 collective-permute-done.refs_4_
  2.6 0.4 collective-permute-done.2.refs_6_
  2.9 0.2 collective-permute-done.3.refs_7_
  3.1 0.4 collective-permute-done.1.refs_5_
  3.4 2.3 %shard_map.161 = (bf16[4,2,32,384]{3,2,1,0:T(8,128)(2,1)S(1)}, bf16[4,2,32,384]{3,2,1,0:T(8,128)(2,1)}) custom-call(s32[1]{0:T(128)} %bitcast.idx_ref.refs_0_, s32[128]{0:T(128)S(1)} %copy-done.4, bf16[32,1536]{1,0:T(8,128)(2,1)} %refs_0_.1, bf16[32,1536]{1,0:T(8,128)(2,1)} %refs_1_.4, bf16[32,1536]{1,0:T(8,128)(2,1)} %refs_2_.1, bf16[32,1536]{1,0:T(8,128)(2,1)} %refs_3_.1, ...), custom_call_target="tpu_custom_call" | custom-call | bytes 1200000 | tf_op jit(solution)/shard_map/pallas_call | solution.py:401
  5.8 2.6 %collective-permute-start.6 = (bf16[4,2,32,384]{3,2,1,0:T(8,128)(2,1)}, bf16[4,2,32,384]{3,2,1,0:T(8,128)(2,1)S(1)}, u32[]{:S(2)}, u32[]{:S(2)}) collective-permute-start(bf16[4,2,32,384]{3,2,1,0:T(8,128)(2,1)} %get-tuple-element.42), channel_id=1, source_target_pairs={{0,5},{1,4},{2,7},{3,6},{4,1},{5,0},{6,3},{7,2},{8,13},{9,12},{10,... | collective-permute-start | bytes 589832 | tf_op jit(solution)/shard_map/ppermute | solution.py:376
  8.3 0.5 collective-permute-start.4
  8.9 0.7 collective-permute-start.12
  9.6 0.3 collective-permute-start.5
  9.8 7.9 %collective-permute-done.6.refs_3_.refs_5_ = bf16[4,2,32,384]{3,2,1,0:T(8,128)(2,1)S(1)} collective-permute-done((bf16[4,2,32,384]{3,2,1,0:T(8,128)(2,1)}, bf16[4,2,32,384]{3,2,1,0:T(8,128)(2,1)S(1)}, u32[]{:S(2)}, u32[]{:S(2)}) %collective-permute-start.6) | collective-permute-done | bytes 196640 | tf_op jit(solution)/shard_map/ppermute | solution.py:376
  17.7 1.1 %collective-permute-start.9 = (bf16[256,768]{1,0:T(8,128)(2,1)}, bf16[256,768]{1,0:T(8,128)(2,1)S(1)}, u32[]{:S(2)}, u32[]{:S(2)}) collective-permute-start(bf16[256,768]{1,0:T(8,128)(2,1)} %refs_6_.2), channel_id=1, source_target_pairs={{0,2},{1,3},{2,0},{3,1},{4,6},{5,7},{6,4},{7,5},{8,10},{9,11},{10,... | collective-permute-start | bytes 1179656 | tf_op jit(solution)/shard_map/ppermute | solution.py:376
  18.8 0.0 collective-permute-done.4.refs_1_.refs_3_
  18.8 0.0 collective-permute-start.10
  18.8 6.4 %collective-permute-start.8 = (bf16[4,2,32,384]{3,2,1,0:T(8,128)(2,1)}, bf16[4,2,32,384]{3,2,1,0:T(8,128)(2,1)S(1)}, u32[]{:S(2)}, u32[]{:S(2)}) collective-permute-start(bf16[4,2,32,384]{3,2,1,0:T(8,128)(2,1)} %get-tuple-element.42), channel_id=1, source_target_pairs={{4,9},{5,8},{6,11},{7,10},{8,5},{9,4},{10,7},{11,6},{12,17},{13,16... | collective-permute-start | bytes 589832 | tf_op jit(solution)/shard_map/ppermute | solution.py:376
  25.2 3.4 %collective-permute-start.7 = (bf16[4,2,32,384]{3,2,1,0:T(8,128)(2,1)S(1)}, bf16[4,2,32,384]{3,2,1,0:T(8,128)(2,1)S(1)}, u32[]{:S(2)}, u32[]{:S(2)}) collective-permute-start(bf16[4,2,32,384]{3,2,1,0:T(8,128)(2,1)S(1)} %get-tuple-element.41.refs_0_.refs_2_), channel_id=1, source_target_pairs={{4,8},{5,9},{6,10},{7,11},{8,4},{9,5},{10,6},{11,7},{12,16},{13,17... | collective-permute-start | bytes 589832 | tf_op jit(solution)/shard_map/ppermute | solution.py:376
  28.6 0.1 copy.28.win_ref.refs_1_
  28.8 2.9 %shard_map.163.refs_8_.refs_12_ = f32[3,8,256]{2,1,0:T(8,128)S(1)} custom-call(s32[1]{0:T(128)} %bitcast.idx_ref.refs_0_, s32[512,2]{1,0:T(8,128)S(1)} %copy.28.win_ref.refs_1_, bf16[4,2,32,384]{3,2,1,0:T(8,128)(2,1)S(1)} %get-tuple-element.41.refs_0_.refs_2_, bf16[4,2,32,384]{3,2,1,0:T(8,128)(2,1)S(1)} %collective-permute-done.4.refs_1_.refs_3_, ...), custom_call_target="tpu_custom_call" | custom-call | flops 201326592 | bytes 2000000 | tf_op jit(solution)/shard_map/pallas_call | solution.py:401
  31.8 0.0 copy-start.2
  31.8 0.0 copy-start.3
  31.8 0.4 collective-permute-done.8.refs_5_.refs_3_.refs_7_
  32.2 4.7 %collective-permute-done.7.refs_4_.refs_2_.refs_6_ = bf16[4,2,32,384]{3,2,1,0:T(8,128)(2,1)S(1)} collective-permute-done((bf16[4,2,32,384]{3,2,1,0:T(8,128)(2,1)S(1)}, bf16[4,2,32,384]{3,2,1,0:T(8,128)(2,1)S(1)}, u32[]{:S(2)}, u32[]{:S(2)}) %collective-permute-start.7) | collective-permute-done | bytes 196640 | tf_op jit(solution)/shard_map/ppermute | solution.py:376
  36.9 2.2 %shard_map.164.refs_13_ = f32[3,8,256]{2,1,0:T(8,128)S(1)} custom-call(s32[1]{0:T(128)} %bitcast.idx_ref.refs_0_, s32[512,2]{1,0:T(8,128)S(1)} %copy.28.win_ref.refs_1_, bf16[4,2,32,384]{3,2,1,0:T(8,128)(2,1)S(1)} %collective-permute-done.7.refs_4_.refs_2_.refs_6_, bf16[4,2,32,384]{3,2,1,0:T(8,128)(2,1)S(1)} %collective-permute-done.8.refs_5_.refs_3_.refs_7_, ...), custom_call_target="tpu_custom_call" | custom-call | flops 100663296 | bytes 2000000 | tf_op jit(solution)/shard_map/pallas_call | solution.py:401
  39.1 1.9 %collective-permute-start.16 = (f32[3,8,256]{2,1,0:T(8,128)S(1)}, f32[3,8,256]{2,1,0:T(8,128)S(1)}, u32[]{:S(2)}, u32[]{:S(2)}) collective-permute-start(f32[3,8,256]{2,1,0:T(8,128)S(1)} %shard_map.164.refs_13_), channel_id=1, source_target_pairs={{4,12},{5,13},{6,14},{7,15},{8,0},{9,1},{10,2},{11,3},{12,20},{13,... | collective-permute-start | bytes 73736 | tf_op jit(solution)/shard_map/ppermute | solution.py:376
  41.0 4.7 %collective-permute-start.14 = (f32[3,8,256]{2,1,0:T(8,128)S(1)}, f32[3,8,256]{2,1,0:T(8,128)S(1)}, u32[]{:S(2)}, u32[]{:S(2)}) collective-permute-start(f32[3,8,256]{2,1,0:T(8,128)S(1)} %shard_map.164.refs_13_), channel_id=1, source_target_pairs={{4,8},{5,9},{6,10},{7,11},{8,4},{9,5},{10,6},{11,7},{12,16},{13,17... | collective-permute-start | bytes 73736 | tf_op jit(solution)/shard_map/ppermute | solution.py:376
  45.8 1.9 %collective-permute-start.15 = (f32[3,8,256]{2,1,0:T(8,128)S(1)}, f32[3,8,256]{2,1,0:T(8,128)S(1)}, u32[]{:S(2)}, u32[]{:S(2)}) collective-permute-start(f32[3,8,256]{2,1,0:T(8,128)S(1)} %shard_map.163.refs_8_.refs_12_), channel_id=1, source_target_pairs={{0,8},{1,9},{2,10},{3,11},{8,16},{9,17},{10,18},{11,19},{12,4},{13... | collective-permute-start | bytes 73736 | tf_op jit(solution)/shard_map/ppermute | solution.py:376
  47.7 3.2 %collective-permute-start.13 = (f32[3,8,256]{2,1,0:T(8,128)S(1)}, f32[3,8,256]{2,1,0:T(8,128)S(1)}, u32[]{:S(2)}, u32[]{:S(2)}) collective-permute-start(f32[3,8,256]{2,1,0:T(8,128)S(1)} %shard_map.163.refs_8_.refs_12_), channel_id=1, source_target_pairs={{0,4},{1,5},{2,6},{3,7},{4,0},{5,1},{6,2},{7,3},{8,12},{9,13},{10,... | collective-permute-start | bytes 73736 | tf_op jit(solution)/shard_map/ppermute | solution.py:376
  51.0 5.6 %shard_map.162 = (bf16[256,768]{1,0:T(8,128)(2,1)}, bf16[256,768]{1,0:T(8,128)(2,1)}, bf16[256,384]{1,0:T(8,128)(2,1)S(1)}, bf16[256,384]{1,0:T(8,128)(2,1)S(1)}...) custom-call(s32[1]{0:T(128)} %bitcast.idx_ref.refs_0_, ...), custom_call_target="tpu_custom_call" | custom-call | flops 754974720 | bytes 5000000 | tf_op jit(solution)/shard_map/pallas_call | solution.py:401
  56.6 2.6 %collective-permute-start.17 = (bf16[256,384]{1,0:T(8,128)(2,1)S(1)}, bf16[256,384]{1,0:T(8,128)(2,1)S(1)}, u32[]{:S(2)}, u32[]{:S(2)}) collective-permute-start(bf16[256,384]{1,0:T(8,128)(2,1)S(1)} %get-tuple-element.53), channel_id=1, source_target_pairs={{0,2},{1,3},{2,0},{3,1},{4,6},{5,7},{6,4},{7,5},{8,10},{9,11},{10,... | collective-permute-start | bytes 589832 | tf_op jit(solution)/shard_map/ppermute | solution.py:376
  59.2 0.3 collective-permute-start.18
  59.5 5.3 %shard_map.165 = (bf16[256,768]{1,0:T(8,128)(2,1)}, bf16[256,768]{1,0:T(8,128)(2,1)}, bf16[256,384]{1,0:T(8,128)(2,1)S(1)}, bf16[256,384]{1,0:T(8,128)(2,1)S(1)}...) custom-call(s32[1]{0:T(128)} %bitcast.idx_ref.refs_0_, ...), custom_call_target="tpu_custom_call", output_to_operand_aliasing={{4}: (18, {}), {5}: (19, {}), {6}: (20, {}), {7}: (21, {}),... | custom-call | flops 905969664 | bytes 5000000 | tf_op jit(solution)/shard_map/pallas_call | solution.py:401
  64.8 0.2 collective-permute-start.19
  65.0 0.3 collective-permute-start.20
  65.3 0.4 collective-permute-start.21
  65.7 2.9 %collective-permute-start.23 = (bf16[4,2,32,384]{3,2,1,0:T(8,128)(2,1)S(1)}, bf16[4,2,32,384]{3,2,1,0:T(8,128)(2,1)S(1)}, u32[]{:S(2)}, u32[]{:S(2)}) collective-permute-start(bf16[4,2,32,384]{3,2,1,0:T(8,128)(2,1)S(1)} %get-tuple-element.61), channel_id=1, source_target_pairs={{0,5},{1,4},{2,7},{3,6},{4,1},{5,0},{6,3},{7,2},{8,13},{9,12},{10,... | collective-permute-start | bytes 589832 | tf_op jit(solution)/shard_map/ppermute | solution.py:376
  68.6 4.4 %collective-permute-start.24 = (bf16[4,2,32,384]{3,2,1,0:T(8,128)(2,1)S(1)}, bf16[4,2,32,384]{3,2,1,0:T(8,128)(2,1)S(1)}, u32[]{:S(2)}, u32[]{:S(2)}) collective-permute-start(bf16[4,2,32,384]{3,2,1,0:T(8,128)(2,1)S(1)} %get-tuple-element.62), channel_id=1, source_target_pairs={{4,8},{5,9},{6,10},{7,11},{8,4},{9,5},{10,6},{11,7},{12,16},{13,17... | collective-permute-start | bytes 589832 | tf_op jit(solution)/shard_map/ppermute | solution.py:376
  73.0 4.3 %collective-permute-start.25 = (bf16[4,2,32,384]{3,2,1,0:T(8,128)(2,1)S(1)}, bf16[4,2,32,384]{3,2,1,0:T(8,128)(2,1)S(1)}, u32[]{:S(2)}, u32[]{:S(2)}) collective-permute-start(bf16[4,2,32,384]{3,2,1,0:T(8,128)(2,1)S(1)} %get-tuple-element.63), channel_id=1, source_target_pairs={{4,9},{5,8},{6,11},{7,10},{8,5},{9,4},{10,7},{11,6},{12,17},{13,16... | collective-permute-start | bytes 589832 | tf_op jit(solution)/shard_map/ppermute | solution.py:376
  77.3 1.6 %shard_map.166 = (bf16[256,768]{1,0:T(8,128)(2,1)}, bf16[256,768]{1,0:T(8,128)(2,1)}, bf16[256,768]{1,0:T(8,128)(2,1)}, bf16[256,768]{1,0:T(8,128)(2,1)}, s32[1]{0:T(128)}) custom-call(s32[1]{0:T(128)} %bitcast.idx_ref.refs_0_, bf16[256,768]{1,0:T(8,128)(2,1)} %get-tuple-element.43.refs_0_, ...), custom_call_target="tpu_custom_call", output_to_operand_aliasing={{0}: (1, {}), {1}: (2, {}), {2}: (3, {}), {3}: (4, {})} | custom-call | bytes 1600000 | tf_op jit(solution)/shard_map/pallas_call | solution.py:401
  79.0 1.1 %collective-permute-done.24.by_b = bf16[4,2,32,384]{3,2,1,0:T(8,128)(2,1)S(1)} collective-permute-done((bf16[4,2,32,384]{3,2,1,0:T(8,128)(2,1)S(1)}, bf16[4,2,32,384]{3,2,1,0:T(8,128)(2,1)S(1)}, u32[]{:S(2)}, u32[]{:S(2)}) %collective-permute-start.24) | collective-permute-done | bytes 196640 | tf_op jit(solution)/shard_map/ppermute | solution.py:376
  80.1 5.3 %collective-permute-done.25.by_bx = bf16[4,2,32,384]{3,2,1,0:T(8,128)(2,1)S(1)} collective-permute-done((bf16[4,2,32,384]{3,2,1,0:T(8,128)(2,1)S(1)}, bf16[4,2,32,384]{3,2,1,0:T(8,128)(2,1)S(1)}, u32[]{:S(2)}, u32[]{:S(2)}) %collective-permute-start.25) | collective-permute-done | bytes 196640 | tf_op jit(solution)/shard_map/ppermute | solution.py:376
  85.4 1.4 %shard_map.167 = (bf16[4,2,32,384]{3,2,1,0:T(8,128)(2,1)S(1)}, bf16[4,2,32,384]{3,2,1,0:T(8,128)(2,1)S(1)}) custom-call(s32[1]{0:T(128)} %bitcast.idx_ref.refs_0_, s32[128]{0:T(128)S(1)} %copy-done.4, bf16[4,2,32,384]{3,2,1,0:T(8,128)(2,1)S(1)} %get-tuple-element.58.keep, bf16[4,2,32,384]{3,2,1,0:T(8,128)(2,1)S(1)} %collective-permute-done.21.by_aud, ...), custom_call_target="tpu_custom_call" | custom-call | flops 1000000 | bytes 1600000 | tf_op jit(solution)/shard_map/pallas_call | solution.py:401
  86.8 2.3 %collective-permute-start.26 = (bf16[4,2,32,384]{3,2,1,0:T(8,128)(2,1)S(1)}, bf16[4,2,32,384]{3,2,1,0:T(8,128)(2,1)S(1)}, u32[]{:S(2)}, u32[]{:S(2)}) collective-permute-start(bf16[4,2,32,384]{3,2,1,0:T(8,128)(2,1)S(1)} %get-tuple-element.66), channel_id=1, source_target_pairs={{0,2},{1,3},{2,0},{3,1},{4,6},{5,7},{6,4},{7,5},{8,10},{9,11},{10,... | collective-permute-start | bytes 589832 | tf_op jit(solution)/shard_map/ppermute | solution.py:376
  89.1 1.1 %collective-permute-done.26.other = bf16[4,2,32,384]{3,2,1,0:T(8,128)(2,1)S(1)} collective-permute-done((bf16[4,2,32,384]{3,2,1,0:T(8,128)(2,1)S(1)}, bf16[4,2,32,384]{3,2,1,0:T(8,128)(2,1)S(1)}, u32[]{:S(2)}, u32[]{:S(2)}) %collective-permute-start.26) | collective-permute-done | bytes 196640 | tf_op jit(solution)/shard_map/ppermute | solution.py:376
  90.1 0.8 shard_map.168
  (27 shorter events, 0.1 us)
Async XLA Ops:
  0.6 1.9 %collective-permute-start = (bf16[32,1536]{1,0:T(8,128)(2,1)}, bf16[32,1536]{1,0:T(8,128)(2,1)S(1)}, u32[]{:S(2)}, u32[]{:S(2)}) collective-permute-start(bf16[32,1536]{1,0:T(8,128)(2,1)} %refs_0_.1), channel_id=1, source_target_pairs={{0,2},{1,3},{2,0},{3,1},{4,6},{5,7},{6,4},{7,5},{8,10},{9,11},{10,... | collective-permute-start | bytes 294920 | tf_op jit(solution)/shard_map/ppermute | solution.py:376
  1.4 1.5 %collective-permute-start.2 = (bf16[32,1536]{1,0:T(8,128)(2,1)}, bf16[32,1536]{1,0:T(8,128)(2,1)S(1)}, u32[]{:S(2)}, u32[]{:S(2)}) collective-permute-start(bf16[32,1536]{1,0:T(8,128)(2,1)} %refs_2_.1), channel_id=1, source_target_pairs={{0,2},{1,3},{2,0},{3,1},{4,6},{5,7},{6,4},{7,5},{8,10},{9,11},{10,... | collective-permute-start | bytes 294920 | tf_op jit(solution)/shard_map/ppermute | solution.py:376
  1.5 1.6 %collective-permute-start.3 = (bf16[32,1536]{1,0:T(8,128)(2,1)}, bf16[32,1536]{1,0:T(8,128)(2,1)S(1)}, u32[]{:S(2)}, u32[]{:S(2)}) collective-permute-start(bf16[32,1536]{1,0:T(8,128)(2,1)} %refs_3_.1), channel_id=1, source_target_pairs={{0,2},{1,3},{2,0},{3,1},{4,6},{5,7},{6,4},{7,5},{8,10},{9,11},{10,... | collective-permute-start | bytes 294920 | tf_op jit(solution)/shard_map/ppermute | solution.py:376
  1.9 1.5 %collective-permute-start.1 = (bf16[32,1536]{1,0:T(8,128)(2,1)}, bf16[32,1536]{1,0:T(8,128)(2,1)S(1)}, u32[]{:S(2)}, u32[]{:S(2)}) collective-permute-start(bf16[32,1536]{1,0:T(8,128)(2,1)} %refs_1_.4), channel_id=1, source_target_pairs={{0,2},{1,3},{2,0},{3,1},{4,6},{5,7},{6,4},{7,5},{8,10},{9,11},{10,... | collective-permute-start | bytes 294920 | tf_op jit(solution)/shard_map/ppermute | solution.py:376
  2.0 23.2 %collective-permute-start.11 = (bf16[256,768]{1,0:T(8,128)(2,1)}, bf16[256,768]{1,0:T(8,128)(2,1)S(1)}, u32[]{:S(2)}, u32[]{:S(2)}) collective-permute-start(bf16[256,768]{1,0:T(8,128)(2,1)} %refs_8_.1), channel_id=1, source_target_pairs={{0,2},{1,3},{2,0},{3,1},{4,6},{5,7},{6,4},{7,5},{8,10},{9,11},{10,... | collective-permute-start | bytes 1179656 | tf_op jit(solution)/shard_map/ppermute | solution.py:376
  2.4 1.0 %copy-start.4 = (s32[128]{0:T(128)S(1)}, s32[128]{0:T(128)}, u32[]{:S(2)}) copy-start(s32[128]{0:T(128)} %len_ref.5) | copy-start | bytes 1540
  3.4 5.4 %copy-start.1 = (bf16[256,768]{1,0:T(8,128)(2,1)S(1)}, bf16[256,768]{1,0:T(8,128)(2,1)}, u32[]{:S(2)}) copy-start(bf16[256,768]{1,0:T(8,128)(2,1)} %refs_9_.1) | copy-start | bytes 1179652
  3.4 25.2 %copy-start.5 = (s32[512,2]{0,1:T(2,128)S(1)}, s32[512,2]{0,1:T(2,128)}, u32[]{:S(2)}) copy-start(s32[512,2]{0,1:T(2,128)} %param.18) | copy-start | bytes 12292
  3.4 25.4 %copy-start = (bf16[256,768]{1,0:T(8,128)(2,1)S(1)}, bf16[256,768]{1,0:T(8,128)(2,1)}, u32[]{:S(2)}) copy-start(bf16[256,768]{1,0:T(8,128)(2,1)} %refs_8_.1) | copy-start | bytes 1179652
  5.8 11.9 %collective-permute-start.6 = (bf16[4,2,32,384]{3,2,1,0:T(8,128)(2,1)}, bf16[4,2,32,384]{3,2,1,0:T(8,128)(2,1)S(1)}, u32[]{:S(2)}, u32[]{:S(2)}) collective-permute-start(bf16[4,2,32,384]{3,2,1,0:T(8,128)(2,1)} %get-tuple-element.42), channel_id=1, source_target_pairs={{0,5},{1,4},{2,7},{3,6},{4,1},{5,0},{6,3},{7,2},{8,13},{9,12},{10,... | collective-permute-start | bytes 589832 | tf_op jit(solution)/shard_map/ppermute | solution.py:376
  8.3 10.5 %collective-permute-start.4 = (bf16[4,2,32,384]{3,2,1,0:T(8,128)(2,1)}, bf16[4,2,32,384]{3,2,1,0:T(8,128)(2,1)S(1)}, u32[]{:S(2)}, u32[]{:S(2)}) collective-permute-start(bf16[4,2,32,384]{3,2,1,0:T(8,128)(2,1)} %get-tuple-element.42), channel_id=1, source_target_pairs={{0,1},{1,0},{2,3},{3,2},{4,5},{5,4},{6,7},{7,6},{8,9},{9,8},{10,11... | collective-permute-start | bytes 589832 | tf_op jit(solution)/shard_map/ppermute | solution.py:376
  8.9 19.9 %collective-permute-start.12 = (bf16[256,768]{1,0:T(8,128)(2,1)S(1)}, bf16[256,768]{1,0:T(8,128)(2,1)S(1)}, u32[]{:S(2)}, u32[]{:S(2)}) collective-permute-start(bf16[256,768]{1,0:T(8,128)(2,1)S(1)} %copy-done.1), channel_id=1, source_target_pairs={{0,2},{1,3},{2,0},{3,1},{4,6},{5,7},{6,4},{7,5},{8,10},{9,11},{10,... | collective-permute-start | bytes 1179656 | tf_op jit(solution)/shard_map/ppermute | solution.py:376
  9.6 9.2 %collective-permute-start.5 = (bf16[4,2,32,384]{3,2,1,0:T(8,128)(2,1)S(1)}, bf16[4,2,32,384]{3,2,1,0:T(8,128)(2,1)S(1)}, u32[]{:S(2)}, u32[]{:S(2)}) collective-permute-start(bf16[4,2,32,384]{3,2,1,0:T(8,128)(2,1)S(1)} %get-tuple-element.41.refs_0_.refs_2_), channel_id=1, source_target_pairs={{0,4},{1,5},{2,6},{3,7},{4,0},{5,1},{6,2},{7,3},{8,12},{9,13},{10,... | collective-permute-start | bytes 589832 | tf_op jit(solution)/shard_map/ppermute | solution.py:376
  17.7 30.0 %collective-permute-start.9 = (bf16[256,768]{1,0:T(8,128)(2,1)}, bf16[256,768]{1,0:T(8,128)(2,1)S(1)}, u32[]{:S(2)}, u32[]{:S(2)}) collective-permute-start(bf16[256,768]{1,0:T(8,128)(2,1)} %refs_6_.2), channel_id=1, source_target_pairs={{0,2},{1,3},{2,0},{3,1},{4,6},{5,7},{6,4},{7,5},{8,10},{9,11},{10,... | collective-permute-start | bytes 1179656 | tf_op jit(solution)/shard_map/ppermute | solution.py:376
  18.8 32.1 %collective-permute-start.10 = (bf16[256,768]{1,0:T(8,128)(2,1)}, bf16[256,768]{1,0:T(8,128)(2,1)}, u32[]{:S(2)}, u32[]{:S(2)}) collective-permute-start(bf16[256,768]{1,0:T(8,128)(2,1)} %refs_7_.2), channel_id=1, source_target_pairs={{0,2},{1,3},{2,0},{3,1},{4,6},{5,7},{6,4},{7,5},{8,10},{9,11},{10,... | collective-permute-start | bytes 1179656 | tf_op jit(solution)/shard_map/ppermute | solution.py:376
  18.8 13.4 %collective-permute-start.8 = (bf16[4,2,32,384]{3,2,1,0:T(8,128)(2,1)}, bf16[4,2,32,384]{3,2,1,0:T(8,128)(2,1)S(1)}, u32[]{:S(2)}, u32[]{:S(2)}) collective-permute-start(bf16[4,2,32,384]{3,2,1,0:T(8,128)(2,1)} %get-tuple-element.42), channel_id=1, source_target_pairs={{4,9},{5,8},{6,11},{7,10},{8,5},{9,4},{10,7},{11,6},{12,17},{13,16... | collective-permute-start | bytes 589832 | tf_op jit(solution)/shard_map/ppermute | solution.py:376
  25.2 11.7 %collective-permute-start.7 = (bf16[4,2,32,384]{3,2,1,0:T(8,128)(2,1)S(1)}, bf16[4,2,32,384]{3,2,1,0:T(8,128)(2,1)S(1)}, u32[]{:S(2)}, u32[]{:S(2)}) collective-permute-start(bf16[4,2,32,384]{3,2,1,0:T(8,128)(2,1)S(1)} %get-tuple-element.41.refs_0_.refs_2_), channel_id=1, source_target_pairs={{4,8},{5,9},{6,10},{7,11},{8,4},{9,5},{10,6},{11,7},{12,16},{13,17... | collective-permute-start | bytes 589832 | tf_op jit(solution)/shard_map/ppermute | solution.py:376
  31.8 19.2 %copy-start.2 = (bf16[256,768]{1,0:T(8,128)(2,1)S(1)}, bf16[256,768]{1,0:T(8,128)(2,1)}, u32[]{:S(2)}) copy-start(bf16[256,768]{1,0:T(8,128)(2,1)} %refs_6_.2) | copy-start | bytes 1179652
  31.8 19.2 %copy-start.3 = (bf16[256,768]{1,0:T(8,128)(2,1)S(1)}, bf16[256,768]{1,0:T(8,128)(2,1)}, u32[]{:S(2)}) copy-start(bf16[256,768]{1,0:T(8,128)(2,1)} %refs_7_.2) | copy-start | bytes 1179652
  39.1 20.1 %collective-permute-start.16 = (f32[3,8,256]{2,1,0:T(8,128)S(1)}, f32[3,8,256]{2,1,0:T(8,128)S(1)}, u32[]{:S(2)}, u32[]{:S(2)}) collective-permute-start(f32[3,8,256]{2,1,0:T(8,128)S(1)} %shard_map.164.refs_13_), channel_id=1, source_target_pairs={{4,12},{5,13},{6,14},{7,15},{8,0},{9,1},{10,2},{11,3},{12,20},{13,... | collective-permute-start | bytes 73736 | tf_op jit(solution)/shard_map/ppermute | solution.py:376
  41.0 18.4 %collective-permute-start.14 = (f32[3,8,256]{2,1,0:T(8,128)S(1)}, f32[3,8,256]{2,1,0:T(8,128)S(1)}, u32[]{:S(2)}, u32[]{:S(2)}) collective-permute-start(f32[3,8,256]{2,1,0:T(8,128)S(1)} %shard_map.164.refs_13_), channel_id=1, source_target_pairs={{4,8},{5,9},{6,10},{7,11},{8,4},{9,5},{10,6},{11,7},{12,16},{13,17... | collective-permute-start | bytes 73736 | tf_op jit(solution)/shard_map/ppermute | solution.py:376
  45.8 13.7 %collective-permute-start.15 = (f32[3,8,256]{2,1,0:T(8,128)S(1)}, f32[3,8,256]{2,1,0:T(8,128)S(1)}, u32[]{:S(2)}, u32[]{:S(2)}) collective-permute-start(f32[3,8,256]{2,1,0:T(8,128)S(1)} %shard_map.163.refs_8_.refs_12_), channel_id=1, source_target_pairs={{0,8},{1,9},{2,10},{3,11},{8,16},{9,17},{10,18},{11,19},{12,4},{13... | collective-permute-start | bytes 73736 | tf_op jit(solution)/shard_map/ppermute | solution.py:376
  47.7 11.7 %collective-permute-start.13 = (f32[3,8,256]{2,1,0:T(8,128)S(1)}, f32[3,8,256]{2,1,0:T(8,128)S(1)}, u32[]{:S(2)}, u32[]{:S(2)}) collective-permute-start(f32[3,8,256]{2,1,0:T(8,128)S(1)} %shard_map.163.refs_8_.refs_12_), channel_id=1, source_target_pairs={{0,4},{1,5},{2,6},{3,7},{4,0},{5,1},{6,2},{7,3},{8,12},{9,13},{10,... | collective-permute-start | bytes 73736 | tf_op jit(solution)/shard_map/ppermute | solution.py:376
  56.6 9.1 %collective-permute-start.17 = (bf16[256,384]{1,0:T(8,128)(2,1)S(1)}, bf16[256,384]{1,0:T(8,128)(2,1)S(1)}, u32[]{:S(2)}, u32[]{:S(2)}) collective-permute-start(bf16[256,384]{1,0:T(8,128)(2,1)S(1)} %get-tuple-element.53), channel_id=1, source_target_pairs={{0,2},{1,3},{2,0},{3,1},{4,6},{5,7},{6,4},{7,5},{8,10},{9,11},{10,... | collective-permute-start | bytes 589832 | tf_op jit(solution)/shard_map/ppermute | solution.py:376
  59.2 6.5 %collective-permute-start.18 = (bf16[256,384]{1,0:T(8,128)(2,1)S(1)}, bf16[256,384]{1,0:T(8,128)(2,1)S(1)}, u32[]{:S(2)}, u32[]{:S(2)}) collective-permute-start(bf16[256,384]{1,0:T(8,128)(2,1)S(1)} %get-tuple-element.54), channel_id=1, source_target_pairs={{0,2},{1,3},{2,0},{3,1},{4,6},{5,7},{6,4},{7,5},{8,10},{9,11},{10,... | collective-permute-start | bytes 589832 | tf_op jit(solution)/shard_map/ppermute | solution.py:376
  64.8 3.8 %collective-permute-start.19 = (bf16[256,384]{1,0:T(8,128)(2,1)S(1)}, bf16[256,384]{1,0:T(8,128)(2,1)S(1)}, u32[]{:S(2)}, u32[]{:S(2)}) collective-permute-start(bf16[256,384]{1,0:T(8,128)(2,1)S(1)} %get-tuple-element.55), channel_id=1, source_target_pairs={{0,2},{1,3},{2,0},{3,1},{4,6},{5,7},{6,4},{7,5},{8,10},{9,11},{10,... | collective-permute-start | bytes 589832 | tf_op jit(solution)/shard_map/ppermute | solution.py:376
  65.0 7.9 %collective-permute-start.20 = (bf16[256,384]{1,0:T(8,128)(2,1)S(1)}, bf16[256,384]{1,0:T(8,128)(2,1)S(1)}, u32[]{:S(2)}, u32[]{:S(2)}) collective-permute-start(bf16[256,384]{1,0:T(8,128)(2,1)S(1)} %get-tuple-element.56), channel_id=1, source_target_pairs={{0,2},{1,3},{2,0},{3,1},{4,6},{5,7},{6,4},{7,5},{8,10},{9,11},{10,... | collective-permute-start | bytes 589832 | tf_op jit(solution)/shard_map/ppermute | solution.py:376
  65.3 13.7 %collective-permute-start.21 = (bf16[4,2,32,384]{3,2,1,0:T(8,128)(2,1)S(1)}, bf16[4,2,32,384]{3,2,1,0:T(8,128)(2,1)S(1)}, u32[]{:S(2)}, u32[]{:S(2)}) collective-permute-start(bf16[4,2,32,384]{3,2,1,0:T(8,128)(2,1)S(1)} %get-tuple-element.59), channel_id=1, source_target_pairs={{0,1},{1,0},{2,3},{3,2},{4,5},{5,4},{6,7},{7,6},{8,9},{9,8},{10,11... | collective-permute-start | bytes 589832 | tf_op jit(solution)/shard_map/ppermute | solution.py:376
  65.7 13.3 %collective-permute-start.22 = (bf16[4,2,32,384]{3,2,1,0:T(8,128)(2,1)S(1)}, bf16[4,2,32,384]{3,2,1,0:T(8,128)(2,1)S(1)}, u32[]{:S(2)}, u32[]{:S(2)}) collective-permute-start(bf16[4,2,32,384]{3,2,1,0:T(8,128)(2,1)S(1)} %get-tuple-element.60), channel_id=1, source_target_pairs={{0,4},{1,5},{2,6},{3,7},{4,0},{5,1},{6,2},{7,3},{8,12},{9,13},{10,... | collective-permute-start | bytes 589832 | tf_op jit(solution)/shard_map/ppermute | solution.py:376
  65.7 13.2 %collective-permute-start.23 = (bf16[4,2,32,384]{3,2,1,0:T(8,128)(2,1)S(1)}, bf16[4,2,32,384]{3,2,1,0:T(8,128)(2,1)S(1)}, u32[]{:S(2)}, u32[]{:S(2)}) collective-permute-start(bf16[4,2,32,384]{3,2,1,0:T(8,128)(2,1)S(1)} %get-tuple-element.61), channel_id=1, source_target_pairs={{0,5},{1,4},{2,7},{3,6},{4,1},{5,0},{6,3},{7,2},{8,13},{9,12},{10,... | collective-permute-start | bytes 589832 | tf_op jit(solution)/shard_map/ppermute | solution.py:376
  68.6 11.5 %collective-permute-start.24 = (bf16[4,2,32,384]{3,2,1,0:T(8,128)(2,1)S(1)}, bf16[4,2,32,384]{3,2,1,0:T(8,128)(2,1)S(1)}, u32[]{:S(2)}, u32[]{:S(2)}) collective-permute-start(bf16[4,2,32,384]{3,2,1,0:T(8,128)(2,1)S(1)} %get-tuple-element.62), channel_id=1, source_target_pairs={{4,8},{5,9},{6,10},{7,11},{8,4},{9,5},{10,6},{11,7},{12,16},{13,17... | collective-permute-start | bytes 589832 | tf_op jit(solution)/shard_map/ppermute | solution.py:376
  73.0 12.4 %collective-permute-start.25 = (bf16[4,2,32,384]{3,2,1,0:T(8,128)(2,1)S(1)}, bf16[4,2,32,384]{3,2,1,0:T(8,128)(2,1)S(1)}, u32[]{:S(2)}, u32[]{:S(2)}) collective-permute-start(bf16[4,2,32,384]{3,2,1,0:T(8,128)(2,1)S(1)} %get-tuple-element.63), channel_id=1, source_target_pairs={{4,9},{5,8},{6,11},{7,10},{8,5},{9,4},{10,7},{11,6},{12,17},{13,16... | collective-permute-start | bytes 589832 | tf_op jit(solution)/shard_map/ppermute | solution.py:376
  86.8 3.4 %collective-permute-start.26 = (bf16[4,2,32,384]{3,2,1,0:T(8,128)(2,1)S(1)}, bf16[4,2,32,384]{3,2,1,0:T(8,128)(2,1)S(1)}, u32[]{:S(2)}, u32[]{:S(2)}) collective-permute-start(bf16[4,2,32,384]{3,2,1,0:T(8,128)(2,1)S(1)} %get-tuple-element.66), channel_id=1, source_target_pairs={{0,2},{1,3},{2,0},{3,1},{4,6},{5,7},{6,4},{7,5},{8,10},{9,11},{10,... | collective-permute-start | bytes 589832 | tf_op jit(solution)/shard_map/ppermute | solution.py:376

commit v5 on v4

--- a/solution.py
+++ b/solution.py
@@ -73,20 +73,26 @@
     return starts
 
 
-def gather_audio(idx_ref, pieces, dst):
+def gather_audio(idx_ref, pieces, arrays, dst):
     half = BLK // 2
     for ref, firsts in zip(pieces, piece_rows(idx_ref)):
         for core, first in enumerate(firsts):
-            for n in range(2):
-                dst[n, pl.ds(first, half), :] = ref[n, core]
-
-
-def scatter_audio(idx_ref, src, pieces):
+            for n, k in enumerate(arrays):
+                dst[n, pl.ds(first, half), :] = ref[k, core]
+
+
+def scatter_audio(idx_ref, sources, pieces):
     half = BLK // 2
     for ref, firsts in zip(pieces, piece_rows(idx_ref)):
         for core, first in enumerate(firsts):
-            for n in range(2):
-                ref[n, core] = src[n, pl.ds(first, half), :].astype(ref.dtype)
+            for n, src in enumerate(sources):
+                ref[n, core] = src[n % 2, pl.ds(first, half), :]
+
+
+def pair_cols(idx_ref, h, quarter):
+    _, r, _ = coords(idx_ref)
+    col = pl.multiple_of(h * PAIR, PAIR)
+    return pl.ds(col, PAIR), pl.ds(pl.multiple_of(r * quarter + col, PAIR), PAIR)
 
 
 def window_bounds(win_ref, c, stretch, shape, axis):
@@ -165,37 +171,37 @@
     video, refs = ((refs[0], refs[1]), (refs[2], refs[3])), refs[4:]
     stat_ref, audio, bias = refs[-3:]
     _, _, a = coords(idx_ref)
-    half = BLK // 2
-
-    @pl.when(pl.program_id(0) == 0)
-    def _():
-        group_bias(idx_ref, win_ref, groups, bias)
-
+    half, quarter = BLK // 2, audio.shape[2]
+    group_bias(idx_ref, win_ref, groups, bias)
     for n in range(count):
         for ref, part in ((pieces[2 * n], a), (pieces[2 * n + 1], 1 - a)):
             for core in range(2):
                 first = pl.multiple_of(n * PAIR + core * BLK + part * half, half)
                 for k in range(2):
                     audio[k, pl.ds(first, half), :] = ref[k, core]
-    queries, cot = audio[0], audio[1]
-    lses, deltas = [], []
-    for e in range(2):
-        parts = []
-        for i, (k_ref, v_ref) in enumerate(video):
-            s = nt(head_part(k_ref[...], e), queries) + bias[i]
-            m = jnp.max(s, axis=0, keepdims=True)
-            ex = jnp.exp(s - m)
-            dp = nt(head_part(v_ref[...], e), cot)
-            parts.append((m, jnp.sum(ex, axis=0, keepdims=True), jnp.sum(ex * dp, axis=0, keepdims=True)))
-        m = jnp.maximum(parts[0][0], parts[1][0])
-        w0, w1 = jnp.exp(parts[0][0] - m), jnp.exp(parts[1][0] - m)
-        total = parts[0][1] * w0 + parts[1][1] * w1
-        lses.append(m + jnp.log(total))
-        deltas.append((parts[0][2] * w0 + parts[1][2] * w1) / total)
-    rows = jnp.concatenate(lses + deltas + lses + deltas, axis=0)
-    if count == 1:
-        rows = jnp.concatenate([refs[0][0, :, :PAIR], rows], axis=1)
-    stat_ref[0] = rows
+
+    @pl.loop(0, quarter // PAIR)
+    def _(h):
+        cols, wide_cols = pair_cols(idx_ref, h, quarter)
+        queries, cot = audio[0, :, cols], audio[1, :, cols]
+        lses, deltas = [], []
+        for e in range(2):
+            parts = []
+            for i, (k_ref, v_ref) in enumerate(video):
+                s = nt(head_part(k_ref[:, wide_cols], e), queries) + bias[i]
+                m = jnp.max(s, axis=0, keepdims=True)
+                ex = jnp.exp(s - m)
+                dp = nt(head_part(v_ref[:, wide_cols], e), cot)
+                parts.append((m, jnp.sum(ex, axis=0, keepdims=True), jnp.sum(ex * dp, axis=0, keepdims=True)))
+            m = jnp.maximum(parts[0][0], parts[1][0])
+            w0, w1 = jnp.exp(parts[0][0] - m), jnp.exp(parts[1][0] - m)
+            total = parts[0][1] * w0 + parts[1][1] * w1
+            lses.append(m + jnp.log(total))
+            deltas.append((parts[0][2] * w0 + parts[1][2] * w1) / total)
+        rows = jnp.concatenate(lses + deltas + lses + deltas, axis=0)
+        if count == 1:
+            rows = jnp.concatenate([refs[0][h][:, :PAIR], rows], axis=1)
+        stat_ref[h] = rows
 
 
 def merge_stats(idx_ref, chips, own_a, own_b, by_a, by_b, by_q, by_q2):
@@ -225,90 +231,94 @@
     pieces = refs[:6]
     video = ((refs[6], refs[7]), (refs[8], refs[9]))
     outs = ((refs[10], refs[11]), (refs[12], refs[13]))
-    back = refs[14:20]
-    audio, bias, grads = refs[20:]
+    kv_grads, audio, bias, grads = refs[14:]
     _, r, _ = coords(idx_ref)
-
-    @pl.when(pl.program_id(0) == 0)
-    def _():
-        block_bias(idx_ref, win_ref, len_ref, bias)
-
-    gather_audio(idx_ref, pieces, audio)
-    grads[...] = jnp.zeros(grads.shape, F32)
+    quarter = audio.shape[2]
+    block_bias(idx_ref, win_ref, len_ref, bias)
+    gather_audio(idx_ref, pieces, (2, 3), audio)
     scale = jnp.asarray(HD**-0.5, BF)
-    for group in block_groups(r):
-        work = []
-        for i, stretch, b in group:
-            start, _ = window_of(idx_ref, win_ref, stretch, b)
-            span = pl.ds(pl.multiple_of(start * BLK, BLK), WMAX * BLK)
-            rows = slice(b * BLK, (b + 1) * BLK)
-            q = both_heads(video[i][0][rows, :] * scale)
-            g = both_heads(video[i][1][rows, :])
-            keys, values = audio[0, span, :], audio[1, span, :]
-            s = nt(keys, q) + bias[4 * i + b]
-            dp = nt(values, g)
-            work.append((i, rows, span, q, g, keys, values, s, dp))
-        done = []
-        for i, rows, span, q, g, keys, values, s, dp in work:
-            ex = jnp.exp(s - jnp.max(s, axis=0, keepdims=True))
-            inv = 1.0 / jnp.sum(ex, axis=0, keepdims=True)
-            delta = jnp.sum(ex * dp, axis=0, keepdims=True) * inv
-            p = ex * inv
-            pb = p.astype(BF)
-            ds = (p * (dp - delta)).astype(BF)
-            done.append((i, rows, span, nn(ds, q), nn(pb, g), tn(pb, values), tn(ds, keys)))
-        for i, rows, span, dk, dv, out, dq in done:
-            grads[0, span, :] += dk
-            grads[1, span, :] += dv
-            outs[i][0][rows, :] = own_heads(out).astype(BF)
-            outs[i][1][rows, :] = (own_heads(dq) * HD**-0.5).astype(BF)
-    scatter_audio(idx_ref, grads, back)
+
+    @pl.loop(0, quarter // PAIR)
+    def _(h):
+        cols, wide_cols = pair_cols(idx_ref, h, quarter)
+        grads[...] = jnp.zeros(grads.shape, F32)
+        for group in block_groups(r):
+            work = []
+            for i, stretch, b in group:
+                start, _ = window_of(idx_ref, win_ref, stretch, b)
+                span = pl.ds(pl.multiple_of(start * BLK, BLK), WMAX * BLK)
+                rows = slice(b * BLK, (b + 1) * BLK)
+                q = both_heads(video[i][0][rows, wide_cols] * scale)
+                g = both_heads(video[i][1][rows, wide_cols])
+                keys, values = audio[0, span, cols], audio[1, span, cols]
+                s = nt(keys, q) + bias[4 * i + b]
+                dp = nt(values, g)
+                work.append((i, rows, span, q, g, keys, values, s, dp))
+            done = []
+            for i, rows, span, q, g, keys, values, s, dp in work:
+                ex = jnp.exp(s - jnp.max(s, axis=0, keepdims=True))
+                inv = 1.0 / jnp.sum(ex, axis=0, keepdims=True)
+                delta = jnp.sum(ex * dp, axis=0, keepdims=True) * inv
+                p = ex * inv
+                pb = p.astype(BF)
+                ds = (p * (dp - delta)).astype(BF)
+                done.append((i, rows, span, nn(ds, q), nn(pb, g), tn(pb, values), tn(ds, keys)))
+            for i, rows, span, dk, dv, out, dq in done:
+                grads[0, span, :] += dk
+                grads[1, span, :] += dv
+                outs[i][0][rows, cols] = own_heads(out).astype(BF)
+                outs[i][1][rows, cols] = (own_heads(dq) * HD**-0.5).astype(BF)
+        for n in range(2):
+            kv_grads[n, :, cols] = grads[n].astype(BF)
 
 
 def av_kernel(chips, idx_ref, win_ref, *refs):
     pieces = refs[:6]
     video = ((refs[6], refs[7]), (refs[8], refs[9]))
-    stats = [ref[0] for ref in refs[10:16]]
-    outs = ((refs[22], refs[23]), (refs[24], refs[25]))
-    back = refs[26:32]
-    audio, bias, grads, rowstat = refs[32:]
+    stats, kv_grads = refs[10:16], refs[16]
+    outs = ((refs[17], refs[18]), (refs[19], refs[20]))
+    back = refs[21:27]
+    audio, bias, grads, rowstat, qo_grads = refs[27:]
     c, r, _ = coords(idx_ref)
-
-    @pl.when(pl.program_id(0) == 0)
-    def _():
-        block_bias(idx_ref, win_ref, None, bias)
-
-    gather_audio(idx_ref, pieces, audio)
-    for place, merged in zip(group_places(c), merge_stats(idx_ref, chips, *stats)):
-        for n, x in enumerate(merged):
-            wide = [jnp.broadcast_to(x[e : e + 1], (HD, PAIR)) for e in range(2)]
-            rowstat[n, pl.ds(place * PAIR, PAIR), :] = jnp.concatenate(wide, axis=0).T
-    grads[...] = jnp.zeros(grads.shape, F32)
-    for group in block_groups(r):
-        work = []
-        for i, stretch, b in group:
-            start, _ = window_of(idx_ref, win_ref, stretch, b)
-            span = pl.ds(pl.multiple_of(start * BLK, BLK), WMAX * BLK)
-            rows = slice(b * BLK, (b + 1) * BLK)
-            keys = both_heads(video[i][0][rows, :])
-            values = both_heads(video[i][1][rows, :])
-            q, g = audio[0, span, :], audio[1, span, :]
-            s = nt(q, keys) + bias[4 * i + b]
-            dp = nt(g, values)
-            work.append((i, rows, span, keys, values, q, g, s, dp))
-        done = []
-        for i, rows, span, keys, values, q, g, s, dp in work:
-            p = jnp.exp(s - rowstat[0, span, :])
-            pb = p.astype(BF)
-            ds = (p * (dp - rowstat[1, span, :])).astype(BF)
-            done.append((i, rows, span, nn(ds, keys), nn(pb, values), tn(ds, q), tn(pb, g)))
-        for i, rows, span, dq, out, dk, dv in done:
-            grads[0, span, :] += dq
-            grads[1, span, :] += out
-            outs[i][0][rows, :] = own_heads(dk).astype(BF)
-            outs[i][1][rows, :] = own_heads(dv).astype(BF)
-    grads[0] = grads[0] * HD**-0.5
-    scatter_audio(idx_ref, grads, back)
+    quarter = audio.shape[2]
+    block_bias(idx_ref, win_ref, None, bias)
+    gather_audio(idx_ref, pieces, (0, 1), audio)
+
+    @pl.loop(0, quarter // PAIR)
+    def _(h):
+        cols, wide_cols = pair_cols(idx_ref, h, quarter)
+        for place, merged in zip(group_places(c), merge_stats(idx_ref, chips, *[ref[h] for ref in stats])):
+            for n, x in enumerate(merged):
+                wide = [jnp.broadcast_to(x[e : e + 1], (HD, PAIR)) for e in range(2)]
+                rowstat[n, pl.ds(place * PAIR, PAIR), :] = jnp.concatenate(wide, axis=0).T
+        grads[...] = jnp.zeros(grads.shape, F32)
+        for group in block_groups(r):
+            work = []
+            for i, stretch, b in group:
+                start, _ = window_of(idx_ref, win_ref, stretch, b)
+                span = pl.ds(pl.multiple_of(start * BLK, BLK), WMAX * BLK)
+                rows = slice(b * BLK, (b + 1) * BLK)
+                keys = both_heads(video[i][0][rows, wide_cols])
+                values = both_heads(video[i][1][rows, wide_cols])
+                q, g = audio[0, span, cols], audio[1, span, cols]
+                s = nt(q, keys) + bias[4 * i + b]
+                dp = nt(g, values)
+                work.append((i, rows, span, keys, values, q, g, s, dp))
+            done = []
+            for i, rows, span, keys, values, q, g, s, dp in work:
+                p = jnp.exp(s - rowstat[0, span, :])
+                pb = p.astype(BF)
+                ds = (p * (dp - rowstat[1, span, :])).astype(BF)
+                done.append((i, rows, span, nn(ds, keys), nn(pb, values), tn(ds, q), tn(pb, g)))
+            for i, rows, span, dq, out, dk, dv in done:
+                grads[0, span, :] += dq
+                grads[1, span, :] += out
+                outs[i][0][rows, cols] = own_heads(dk).astype(BF)
+                outs[i][1][rows, cols] = own_heads(dv).astype(BF)
+        qo_grads[0, :, cols] = (grads[0] * HD**-0.5).astype(BF)
+        qo_grads[1, :, cols] = grads[1].astype(BF)
+
+    scatter_audio(idx_ref, (kv_grads, kv_grads, qo_grads, qo_grads), back)
 
 
 def sum_kernel(idx_ref, len_ref, keep, by_aud, by_a, by_ax, by_b, by_bx, after, mine, other):
@@ -336,8 +346,11 @@
 
 
 def join_video_kernel(idx_ref, *refs):
-    for src, out in zip(refs[4:8], refs[8:12]):
-        out[...] = src[...]
+    _, r, _ = coords(idx_ref)
+    quarter = refs[0].shape[1]
+    for own, far, out in zip(refs[:4], refs[4:8], refs[8:12]):
+        for core, src in ((r, own), (1 - r, far)):
+            out[:, pl.ds(pl.multiple_of(core * quarter, PAIR), quarter)] = src[...]
     refs[12][0] = 0
 
 
@@ -384,20 +397,12 @@
         shape = jax.ShapeDtypeStruct
 
         smem = pl.BlockSpec(memory_space=pltpu.SMEM)
-        win_spec = pl.BlockSpec((8, 2), lambda h, i: (i[0] >> 2, 0), memory_space=pltpu.SMEM)
-        len_spec = pl.BlockSpec(memory_space=pltpu.SMEM)
-
-        def piece_spec(n):
-            return pl.BlockSpec((2, 2, half, PAIR), lambda h, i: (n, 0, 0, h))
-
-        own_spec = pl.BlockSpec((rows, PAIR), lambda h, i: (0, ((i[0] >> 1) & 1) * steps + h))
-        far_spec = pl.BlockSpec((rows, PAIR), lambda h, i: (0, h))
-        join_spec = pl.BlockSpec((rows, PAIR), lambda h, i: (0, (1 - ((i[0] >> 1) & 1)) * steps + h))
-        stat_spec = pl.BlockSpec((1, 8, 2 * PAIR), lambda h, i: (h, 0, 0))
-        any_spec = pl.BlockSpec(memory_space=pl.ANY)
+        win_spec = pl.BlockSpec((8, 2), lambda g, i: (i[0] >> 2, 0), memory_space=pltpu.SMEM)
+        len_spec = smem
+        whole = pl.BlockSpec(memory_space=pltpu.VMEM)
         hbm = pl.BlockSpec(memory_space=pltpu.HBM)
 
-        def call(kernel, ins, outs, args, grid=(steps,), scratch=(), aliases=None, est=None):
+        def call(kernel, ins, outs, args, grid=(1,), scratch=(), est=None):
             return pl.pallas_call(
                 kernel,
                 grid_spec=pltpu.PrefetchScalarGridSpec(
@@ -408,7 +413,6 @@
                     scratch_shapes=list(scratch),
                 ),
                 out_shape=[o for _, o in outs],
-                input_output_aliases=aliases or {},
                 cost_estimate=est,
                 compiler_params=pltpu.CompilerParams(vmem_limit_bytes=24 << 20),
             )(idx, *args)
@@ -416,7 +420,6 @@
         audio = (q_a, g_a, k_a, v_a)
         audio_other = [move(x, "core") for x in audio]
         piece = shape((4, 2, half, quarter), BF)
-        whole = pl.BlockSpec(memory_space=pltpu.VMEM)
         keep, send = call(
             pack_kernel, [smem] + [hbm] * 4 + [whole] * 4, [(whole, piece)] * 2, (audio_len, *[pltpu.with_memory_space_constraint(x, pltpu.HBM) for x in audio], *audio_other), grid=(),
             scratch=(pltpu.VMEM((4, half, 2 * width), BF), pltpu.SemaphoreType.DMA((4,))),
@@ -425,7 +428,7 @@
         pieces = [keep, move(send, "aud"), move(keep, "A"), move(send, "Ax"), move(keep, "B"), move(send, "Bx")]
         k_f, v_f, q_f, g_f = [move(x, "core") for x in (k_v, v_v, q_v, g_v)]
 
-        audio_scratch = pltpu.VMEM((2, KEYS, PAIR), BF)
+        audio_scratch = pltpu.VMEM((2, KEYS, quarter), BF)
         grad_scratch = pltpu.VMEM((2, KEYS, PAIR), F32)
         bias_scratch = pltpu.VMEM((8, WMAX * BLK, PAIR), F32)
         pairs = 2 * steps * 2 * rows * KEYS
@@ -436,10 +439,10 @@
             lanes = len(groups) * PAIR
             (found,) = call(
                 lambda *refs: stats_kernel(groups, *refs),
-                [win_spec] + [piece_spec(0)] * (2 * len(groups)) + [own_spec] * 4 + [stat_spec] * len(before),
-                [(stat_spec, stat)],
+                [win_spec] + [whole] * (2 * len(groups) + 4 + len(before)),
+                [(whole, stat)],
                 (window, *[pieces[2 * g + n] for g in groups for n in range(2)], k_v, v_v, k_f, v_f, *before),
-                scratch=(pltpu.VMEM((2, lanes, PAIR), BF), pltpu.VMEM((2, rows, lanes), F32)),
+                scratch=(pltpu.VMEM((2, lanes, quarter), BF), pltpu.VMEM((2, rows, lanes), F32)),
                 est=cost(4 * HD * pairs * lanes // KEYS, pairs * lanes // KEYS, 2000000),
             )
             return found
@@ -449,36 +452,31 @@
         stats_b = find_stats((2,), (stats_a,))
         by_b, by_q2 = move(stats_b, "B"), move(stats_b, "Q2")
 
-        full, far = shape((rows, width), BF), shape((rows, quarter), BF)
-        va = call(
+        full, part = shape((rows, width), BF), shape((rows, quarter), BF)
+        out_own, dq_own, out_far, dq_far, kv_grads = call(
             va_kernel,
-            [win_spec, len_spec] + [piece_spec(1)] * 6 + [own_spec] * 4,
-            [(own_spec, full)] * 2 + [(far_spec, far)] * 2 + [(piece_spec(0), piece)] * 6,
+            [win_spec, len_spec] + [whole] * 10,
+            [(whole, part)] * 4 + [(whole, shape((2, KEYS, quarter), BF))],
             (window, audio_len, *pieces, q_v, g_v, q_f, g_f),
             scratch=(audio_scratch, bias_scratch, grad_scratch),
             est=cost(10 * HD * pairs, pairs, 5000000),
         )
-        out_video, dq_video, out_far, dq_far = va[:4]
-        av = call(
+        dk_own, dv_own, dk_far, dv_far, *back = call(
             lambda *refs: av_kernel(chips, *refs),
-            [win_spec] + [piece_spec(0)] * 6 + [own_spec] * 4 + [stat_spec] * 6 + [any_spec] * 6,
-            [(own_spec, full)] * 2 + [(far_spec, far)] * 2 + [(piece_spec(1), piece)] * 6,
-            (window, *pieces, k_v, v_v, k_f, v_f, stats_a, stats_b, by_a, by_b, by_q, by_q2, *va[4:]),
-            scratch=(audio_scratch, bias_scratch, grad_scratch, grad_scratch),
-            aliases={18 + i: 4 + i for i in range(6)},
+            [win_spec] + [whole] * 17,
+            [(whole, part)] * 4 + [(whole, piece)] * 6,
+            (window, *pieces, k_v, v_v, k_f, v_f, stats_a, stats_b, by_a, by_b, by_q, by_q2, kv_grads),
+            scratch=(audio_scratch, bias_scratch, grad_scratch, grad_scratch, audio_scratch),
             est=cost(12 * HD * pairs, pairs, 5000000),
         )
-        dk_video, dv_video, dk_far, dv_far = av[:4]
-        back = av[4:]
         parts = [back[0]] + [move(x, name) for x, name in zip(back[1:], ("aud", "A", "Ax", "B", "Bx"))]
 
         fars = [move(x, "core") for x in (out_far, dq_far, dk_far, dv_far)]
         out_video, dq_video, dk_video, dv_video, joined = call(
             join_video_kernel,
-            [any_spec] * 4 + [far_spec] * 4,
-            [(join_spec, full)] * 4 + [(smem, shape((1,), jnp.int32))],
-            (out_video, dq_video, dk_video, dv_video, *fars),
-            aliases={1 + i: i for i in range(4)},
+            [whole] * 8,
+            [(whole, full)] * 4 + [(smem, shape((1,), jnp.int32))],
+            (out_own, dq_own, dk_own, dv_own, *fars),
             est=cost(0, 0, 1600000),
         )
         mine, other = call(

time: 91.3 us -> 88.9 us (0.974)
  Pallas kernels: 22.2 us -> 18.9 us
    pallas_call x8, Pallas kernels: 22.2 us -> 18.9 us  [call(): pl.pallas_call(kernel, grid_spec=pltpu.PrefetchScalarGridSpec(num_scalar_...]
  transfers between devices with their start and end apart: 27 -> 27, of which waited for: 10 -> 10; matrix products, arithmetic and copies ran while one was open for 0% -> 0% of each run, Pallas kernels for 22% -> 19%
where the time goes in v5:
time: 88.9 us; the launch traced here: 88.6 us
  starting transfers between devices  46.5 us (52%)
  waiting for transfers between devices  22.1 us (25%)
  Pallas kernels  18.9 us (21%)
    ppermute x27, starting transfers between devices, move(): return lax.ppermute(x, ('vid', 'aud'), moves[name])  46.5 us
    ppermute x27, waiting for transfers between devices, move(): return lax.ppermute(x, ('vid', 'aud'), moves[name])  22.1 us
    pallas_call x8, Pallas kernels, call(): pl.pallas_call(kernel, grid_spec=pltpu.PrefetchScalarGridSpec(num_scalar_...  18.9 us
  transfers between devices with their start and end apart: 27, of which 10 were waited for; matrix products, arithmetic and copies ran while one was open for 0% of the time, Pallas kernels for 19%

profile of v5, /device:TPU:129, one launch (start us, length us, event | category | flops | bytes accessed | tf_op | source)
XLA Modules:
  0.0 88.6 jit_solution(4279297746945286699)
XLA Ops:
  0.6 0.8 collective-permute-start
  1.4 0.1 collective-permute-start.2
  1.5 0.4 collective-permute-start.3
  1.9 0.1 collective-permute-start.1
  2.0 0.4 collective-permute-start.11
  2.4 0.1 collective-permute-done.refs_4_
  2.6 0.4 collective-permute-done.2.refs_6_
  2.9 0.2 collective-permute-done.3.refs_7_
  3.1 0.4 collective-permute-done.1.refs_5_
  3.4 2.3 %shard_map.161 = (bf16[4,2,32,384]{3,2,1,0:T(8,128)(2,1)S(1)}, bf16[4,2,32,384]{3,2,1,0:T(8,128)(2,1)}) custom-call(s32[1]{0:T(128)} %bitcast.idx_ref.refs_0_, s32[128]{0:T(128)S(1)} %copy-done.4, bf16[32,1536]{1,0:T(8,128)(2,1)} %refs_0_.1, bf16[32,1536]{1,0:T(8,128)(2,1)} %refs_1_.4, bf16[32,1536]{1,0:T(8,128)(2,1)} %refs_2_.1, bf16[32,1536]{1,0:T(8,128)(2,1)} %refs_3_.1, ...), custom_call_target="tpu_custom_call" | custom-call | bytes 1200000 | tf_op jit(solution)/shard_map/pallas_call | solution.py:406
  5.8 2.6 %collective-permute-start.6 = (bf16[4,2,32,384]{3,2,1,0:T(8,128)(2,1)}, bf16[4,2,32,384]{3,2,1,0:T(8,128)(2,1)S(1)}, u32[]{:S(2)}, u32[]{:S(2)}) collective-permute-start(bf16[4,2,32,384]{3,2,1,0:T(8,128)(2,1)} %get-tuple-element.37), channel_id=1, source_target_pairs={{0,5},{1,4},{2,7},{3,6},{4,1},{5,0},{6,3},{7,2},{8,13},{9,12},{10,... | collective-permute-start | bytes 589832 | tf_op jit(solution)/shard_map/ppermute | solution.py:389
  8.3 0.5 collective-permute-start.4
  8.9 0.7 collective-permute-start.12
  9.6 0.3 collective-permute-start.5
  9.8 7.9 %collective-permute-done.6.refs_3_.refs_5_ = bf16[4,2,32,384]{3,2,1,0:T(8,128)(2,1)S(1)} collective-permute-done((bf16[4,2,32,384]{3,2,1,0:T(8,128)(2,1)}, bf16[4,2,32,384]{3,2,1,0:T(8,128)(2,1)S(1)}, u32[]{:S(2)}, u32[]{:S(2)}) %collective-permute-start.6) | collective-permute-done | bytes 196640 | tf_op jit(solution)/shard_map/ppermute | solution.py:389
  17.7 1.1 %collective-permute-start.9 = (bf16[256,768]{1,0:T(8,128)(2,1)}, bf16[256,768]{1,0:T(8,128)(2,1)S(1)}, u32[]{:S(2)}, u32[]{:S(2)}) collective-permute-start(bf16[256,768]{1,0:T(8,128)(2,1)} %refs_6_.2), channel_id=1, source_target_pairs={{0,2},{1,3},{2,0},{3,1},{4,6},{5,7},{6,4},{7,5},{8,10},{9,11},{10,... | collective-permute-start | bytes 1179656 | tf_op jit(solution)/shard_map/ppermute | solution.py:389
  18.8 0.0 collective-permute-done.4.refs_1_.refs_3_
  18.8 0.0 collective-permute-start.10
  18.8 6.4 %collective-permute-start.8 = (bf16[4,2,32,384]{3,2,1,0:T(8,128)(2,1)}, bf16[4,2,32,384]{3,2,1,0:T(8,128)(2,1)S(1)}, u32[]{:S(2)}, u32[]{:S(2)}) collective-permute-start(bf16[4,2,32,384]{3,2,1,0:T(8,128)(2,1)} %get-tuple-element.37), channel_id=1, source_target_pairs={{4,9},{5,8},{6,11},{7,10},{8,5},{9,4},{10,7},{11,6},{12,17},{13,16... | collective-permute-start | bytes 589832 | tf_op jit(solution)/shard_map/ppermute | solution.py:389
  25.2 3.4 %collective-permute-start.7 = (bf16[4,2,32,384]{3,2,1,0:T(8,128)(2,1)S(1)}, bf16[4,2,32,384]{3,2,1,0:T(8,128)(2,1)S(1)}, u32[]{:S(2)}, u32[]{:S(2)}) collective-permute-start(bf16[4,2,32,384]{3,2,1,0:T(8,128)(2,1)S(1)} %get-tuple-element.36.refs_0_.refs_2_), channel_id=1, source_target_pairs={{4,8},{5,9},{6,10},{7,11},{8,4},{9,5},{10,6},{11,7},{12,16},{13,17... | collective-permute-start | bytes 589832 | tf_op jit(solution)/shard_map/ppermute | solution.py:389
  28.6 0.1 copy.18.win_ref.refs_1_
  28.8 2.5 %shard_map.163.refs_8_.refs_12_ = f32[3,8,256]{2,1,0:T(8,128)S(1)} custom-call(s32[1]{0:T(128)} %bitcast.idx_ref.refs_0_, s32[512,2]{1,0:T(8,128)S(1)} %copy.18.win_ref.refs_1_, bf16[4,2,32,384]{3,2,1,0:T(8,128)(2,1)S(1)} %get-tuple-element.36.refs_0_.refs_2_, bf16[4,2,32,384]{3,2,1,0:T(8,128)(2,1)S(1)} %collective-permute-done.4.refs_1_.refs_3_, ...), custom_call_target="tpu_custom_call" | custom-call | flops 201326592 | bytes 2000000 | tf_op jit(solution)/shard_map/pallas_call | solution.py:406
  31.4 0.0 copy-start.2
  31.4 0.0 copy-start.3
  31.4 0.8 collective-permute-done.8.refs_5_.refs_3_.refs_7_
  32.2 4.7 %collective-permute-done.7.refs_4_.refs_2_.refs_6_ = bf16[4,2,32,384]{3,2,1,0:T(8,128)(2,1)S(1)} collective-permute-done((bf16[4,2,32,384]{3,2,1,0:T(8,128)(2,1)S(1)}, bf16[4,2,32,384]{3,2,1,0:T(8,128)(2,1)S(1)}, u32[]{:S(2)}, u32[]{:S(2)}) %collective-permute-start.7) | collective-permute-done | bytes 196640 | tf_op jit(solution)/shard_map/ppermute | solution.py:389
  36.9 1.8 %shard_map.164.refs_13_ = f32[3,8,256]{2,1,0:T(8,128)S(1)} custom-call(s32[1]{0:T(128)} %bitcast.idx_ref.refs_0_, s32[512,2]{1,0:T(8,128)S(1)} %copy.18.win_ref.refs_1_, bf16[4,2,32,384]{3,2,1,0:T(8,128)(2,1)S(1)} %collective-permute-done.7.refs_4_.refs_2_.refs_6_, bf16[4,2,32,384]{3,2,1,0:T(8,128)(2,1)S(1)} %collective-permute-done.8.refs_5_.refs_3_.refs_7_, ...), custom_call_target="tpu_custom_call" | custom-call | flops 100663296 | bytes 2000000 | tf_op jit(solution)/shard_map/pallas_call | solution.py:406
  38.8 1.9 %collective-permute-start.16 = (f32[3,8,256]{2,1,0:T(8,128)S(1)}, f32[3,8,256]{2,1,0:T(8,128)S(1)}, u32[]{:S(2)}, u32[]{:S(2)}) collective-permute-start(f32[3,8,256]{2,1,0:T(8,128)S(1)} %shard_map.164.refs_13_), channel_id=1, source_target_pairs={{4,12},{5,13},{6,14},{7,15},{8,0},{9,1},{10,2},{11,3},{12,20},{13,... | collective-permute-start | bytes 73736 | tf_op jit(solution)/shard_map/ppermute | solution.py:389
  40.7 4.7 %collective-permute-start.14 = (f32[3,8,256]{2,1,0:T(8,128)S(1)}, f32[3,8,256]{2,1,0:T(8,128)S(1)}, u32[]{:S(2)}, u32[]{:S(2)}) collective-permute-start(f32[3,8,256]{2,1,0:T(8,128)S(1)} %shard_map.164.refs_13_), channel_id=1, source_target_pairs={{4,8},{5,9},{6,10},{7,11},{8,4},{9,5},{10,6},{11,7},{12,16},{13,17... | collective-permute-start | bytes 73736 | tf_op jit(solution)/shard_map/ppermute | solution.py:389
  45.4 1.9 %collective-permute-start.15 = (f32[3,8,256]{2,1,0:T(8,128)S(1)}, f32[3,8,256]{2,1,0:T(8,128)S(1)}, u32[]{:S(2)}, u32[]{:S(2)}) collective-permute-start(f32[3,8,256]{2,1,0:T(8,128)S(1)} %shard_map.163.refs_8_.refs_12_), channel_id=1, source_target_pairs={{0,8},{1,9},{2,10},{3,11},{8,16},{9,17},{10,18},{11,19},{12,4},{13... | collective-permute-start | bytes 73736 | tf_op jit(solution)/shard_map/ppermute | solution.py:389
  47.4 3.2 %collective-permute-start.13 = (f32[3,8,256]{2,1,0:T(8,128)S(1)}, f32[3,8,256]{2,1,0:T(8,128)S(1)}, u32[]{:S(2)}, u32[]{:S(2)}) collective-permute-start(f32[3,8,256]{2,1,0:T(8,128)S(1)} %shard_map.163.refs_8_.refs_12_), channel_id=1, source_target_pairs={{0,4},{1,5},{2,6},{3,7},{4,0},{5,1},{6,2},{7,3},{8,12},{9,13},{10,... | collective-permute-start | bytes 73736 | tf_op jit(solution)/shard_map/ppermute | solution.py:389
  50.6 4.6 %shard_map.162 = (bf16[256,384]{1,0:T(8,128)(2,1)S(1)}, bf16[256,384]{1,0:T(8,128)(2,1)S(1)}, bf16[256,384]{1,0:T(8,128)(2,1)S(1)}, bf16[256,384]{1,0:T(8,128)(2,1)S(1)}, bf16[2,384,384]{2,1,0:T(8,128)(2,1)S(1)}) custom-call(s32[1]{0:T(128)} %bitcast.idx_ref.refs_0_, s32[512,2]{1,0:T(8,128)S(1)} %copy.18.win_ref.refs_1_, s32[128]{0:T(128)S(1)} %copy-done.4, ...), custom_call_target="tpu_custom_call" | custom-call | flops 754974720 | bytes 5000000 | tf_op jit(solution)/shard_map/pallas_call | solution.py:406
  55.2 2.7 %collective-permute-start.17 = (bf16[256,384]{1,0:T(8,128)(2,1)S(1)}, bf16[256,384]{1,0:T(8,128)(2,1)S(1)}, u32[]{:S(2)}, u32[]{:S(2)}) collective-permute-start(bf16[256,384]{1,0:T(8,128)(2,1)S(1)} %get-tuple-element.43), channel_id=1, source_target_pairs={{0,2},{1,3},{2,0},{3,1},{4,6},{5,7},{6,4},{7,5},{8,10},{9,11},{10,... | collective-permute-start | bytes 589832 | tf_op jit(solution)/shard_map/ppermute | solution.py:389
  57.9 0.1 collective-permute-start.18
  58.0 4.2 %shard_map.165 = (bf16[256,384]{1,0:T(8,128)(2,1)S(1)}, bf16[256,384]{1,0:T(8,128)(2,1)S(1)}, bf16[256,384]{1,0:T(8,128)(2,1)S(1)}, bf16[256,384]{1,0:T(8,128)(2...) custom-call(s32[1]{0:T(128)} %bitcast.idx_ref.refs_0_, ...), custom_call_target="tpu_custom_call" | custom-call | flops 905969664 | bytes 5000000 | tf_op jit(solution)/shard_map/pallas_call | solution.py:406
  62.2 0.7 collective-permute-start.19
  62.9 0.1 collective-permute-start.20
  63.0 0.4 collective-permute-start.21
  63.4 2.8 %collective-permute-start.23 = (bf16[4,2,32,384]{3,2,1,0:T(8,128)(2,1)S(1)}, bf16[4,2,32,384]{3,2,1,0:T(8,128)(2,1)S(1)}, u32[]{:S(2)}, u32[]{:S(2)}) collective-permute-start(bf16[4,2,32,384]{3,2,1,0:T(8,128)(2,1)S(1)} %get-tuple-element.51), channel_id=1, source_target_pairs={{0,5},{1,4},{2,7},{3,6},{4,1},{5,0},{6,3},{7,2},{8,13},{9,12},{10,... | collective-permute-start | bytes 589832 | tf_op jit(solution)/shard_map/ppermute | solution.py:389
  66.3 4.4 %collective-permute-start.24 = (bf16[4,2,32,384]{3,2,1,0:T(8,128)(2,1)S(1)}, bf16[4,2,32,384]{3,2,1,0:T(8,128)(2,1)S(1)}, u32[]{:S(2)}, u32[]{:S(2)}) collective-permute-start(bf16[4,2,32,384]{3,2,1,0:T(8,128)(2,1)S(1)} %get-tuple-element.52), channel_id=1, source_target_pairs={{4,8},{5,9},{6,10},{7,11},{8,4},{9,5},{10,6},{11,7},{12,16},{13,17... | collective-permute-start | bytes 589832 | tf_op jit(solution)/shard_map/ppermute | solution.py:389
  70.7 4.3 %collective-permute-start.25 = (bf16[4,2,32,384]{3,2,1,0:T(8,128)(2,1)S(1)}, bf16[4,2,32,384]{3,2,1,0:T(8,128)(2,1)S(1)}, u32[]{:S(2)}, u32[]{:S(2)}) collective-permute-start(bf16[4,2,32,384]{3,2,1,0:T(8,128)(2,1)S(1)} %get-tuple-element.53), channel_id=1, source_target_pairs={{4,9},{5,8},{6,11},{7,10},{8,5},{9,4},{10,7},{11,6},{12,17},{13,16... | collective-permute-start | bytes 589832 | tf_op jit(solution)/shard_map/ppermute | solution.py:389
  75.0 1.3 %shard_map.166 = (bf16[256,768]{1,0:T(8,128)(2,1)}, bf16[256,768]{1,0:T(8,128)(2,1)}, bf16[256,768]{1,0:T(8,128)(2,1)}, bf16[256,768]{1,0:T(8,128)(2,1)}, s32[1]{0:T(128)}) custom-call(s32[1]{0:T(128)} %bitcast.idx_ref.refs_0_, bf16[256,384]{1,0:T(8,128)(2,1)S(1)} %get-tuple-element.38.refs_0_, bf16[256,384]{1,0:T(8,128)(2,1)S(1)} %get-tuple-element.39.refs_1_, ...), custom_call_target="tpu_custom_call" | custom-call | bytes 1600000 | tf_op jit(solution)/shard_map/pallas_call | solution.py:406
  76.3 1.2 %collective-permute-done.24.by_b = bf16[4,2,32,384]{3,2,1,0:T(8,128)(2,1)S(1)} collective-permute-done((bf16[4,2,32,384]{3,2,1,0:T(8,128)(2,1)S(1)}, bf16[4,2,32,384]{3,2,1,0:T(8,128)(2,1)S(1)}, u32[]{:S(2)}, u32[]{:S(2)}) %collective-permute-start.24) | collective-permute-done | bytes 196640 | tf_op jit(solution)/shard_map/ppermute | solution.py:389
  77.6 5.4 %collective-permute-done.25.by_bx = bf16[4,2,32,384]{3,2,1,0:T(8,128)(2,1)S(1)} collective-permute-done((bf16[4,2,32,384]{3,2,1,0:T(8,128)(2,1)S(1)}, bf16[4,2,32,384]{3,2,1,0:T(8,128)(2,1)S(1)}, u32[]{:S(2)}, u32[]{:S(2)}) %collective-permute-start.25) | collective-permute-done | bytes 196640 | tf_op jit(solution)/shard_map/ppermute | solution.py:389
  82.9 1.3 %shard_map.167 = (bf16[4,2,32,384]{3,2,1,0:T(8,128)(2,1)S(1)}, bf16[4,2,32,384]{3,2,1,0:T(8,128)(2,1)S(1)}) custom-call(s32[1]{0:T(128)} %bitcast.idx_ref.refs_0_, s32[128]{0:T(128)S(1)} %copy-done.4, bf16[4,2,32,384]{3,2,1,0:T(8,128)(2,1)S(1)} %get-tuple-element.48.keep, bf16[4,2,32,384]{3,2,1,0:T(8,128)(2,1)S(1)} %collective-permute-done.21.by_aud, ...), custom_call_target="tpu_custom_call" | custom-call | flops 1000000 | bytes 1600000 | tf_op jit(solution)/shard_map/pallas_call | solution.py:406
  84.3 2.5 %collective-permute-start.26 = (bf16[4,2,32,384]{3,2,1,0:T(8,128)(2,1)S(1)}, bf16[4,2,32,384]{3,2,1,0:T(8,128)(2,1)S(1)}, u32[]{:S(2)}, u32[]{:S(2)}) collective-permute-start(bf16[4,2,32,384]{3,2,1,0:T(8,128)(2,1)S(1)} %get-tuple-element.56), channel_id=1, source_target_pairs={{0,2},{1,3},{2,0},{3,1},{4,6},{5,7},{6,4},{7,5},{8,10},{9,11},{10,... | collective-permute-start | bytes 589832 | tf_op jit(solution)/shard_map/ppermute | solution.py:389
  86.8 1.1 %collective-permute-done.26.other = bf16[4,2,32,384]{3,2,1,0:T(8,128)(2,1)S(1)} collective-permute-done((bf16[4,2,32,384]{3,2,1,0:T(8,128)(2,1)S(1)}, bf16[4,2,32,384]{3,2,1,0:T(8,128)(2,1)S(1)}, u32[]{:S(2)}, u32[]{:S(2)}) %collective-permute-start.26) | collective-permute-done | bytes 196640 | tf_op jit(solution)/shard_map/ppermute | solution.py:389
  87.8 0.8 shard_map.168
  (27 shorter events, 0.1 us)
Async XLA Ops:
  0.6 1.9 %collective-permute-start = (bf16[32,1536]{1,0:T(8,128)(2,1)}, bf16[32,1536]{1,0:T(8,128)(2,1)S(1)}, u32[]{:S(2)}, u32[]{:S(2)}) collective-permute-start(bf16[32,1536]{1,0:T(8,128)(2,1)} %refs_0_.1), channel_id=1, source_target_pairs={{0,2},{1,3},{2,0},{3,1},{4,6},{5,7},{6,4},{7,5},{8,10},{9,11},{10,... | collective-permute-start | bytes 294920 | tf_op jit(solution)/shard_map/ppermute | solution.py:389
  1.4 1.5 %collective-permute-start.2 = (bf16[32,1536]{1,0:T(8,128)(2,1)}, bf16[32,1536]{1,0:T(8,128)(2,1)S(1)}, u32[]{:S(2)}, u32[]{:S(2)}) collective-permute-start(bf16[32,1536]{1,0:T(8,128)(2,1)} %refs_2_.1), channel_id=1, source_target_pairs={{0,2},{1,3},{2,0},{3,1},{4,6},{5,7},{6,4},{7,5},{8,10},{9,11},{10,... | collective-permute-start | bytes 294920 | tf_op jit(solution)/shard_map/ppermute | solution.py:389
  1.5 1.6 %collective-permute-start.3 = (bf16[32,1536]{1,0:T(8,128)(2,1)}, bf16[32,1536]{1,0:T(8,128)(2,1)S(1)}, u32[]{:S(2)}, u32[]{:S(2)}) collective-permute-start(bf16[32,1536]{1,0:T(8,128)(2,1)} %refs_3_.1), channel_id=1, source_target_pairs={{0,2},{1,3},{2,0},{3,1},{4,6},{5,7},{6,4},{7,5},{8,10},{9,11},{10,... | collective-permute-start | bytes 294920 | tf_op jit(solution)/shard_map/ppermute | solution.py:389
  1.9 1.5 %collective-permute-start.1 = (bf16[32,1536]{1,0:T(8,128)(2,1)}, bf16[32,1536]{1,0:T(8,128)(2,1)S(1)}, u32[]{:S(2)}, u32[]{:S(2)}) collective-permute-start(bf16[32,1536]{1,0:T(8,128)(2,1)} %refs_1_.4), channel_id=1, source_target_pairs={{0,2},{1,3},{2,0},{3,1},{4,6},{5,7},{6,4},{7,5},{8,10},{9,11},{10,... | collective-permute-start | bytes 294920 | tf_op jit(solution)/shard_map/ppermute | solution.py:389
  2.0 23.2 %collective-permute-start.11 = (bf16[256,768]{1,0:T(8,128)(2,1)}, bf16[256,768]{1,0:T(8,128)(2,1)S(1)}, u32[]{:S(2)}, u32[]{:S(2)}) collective-permute-start(bf16[256,768]{1,0:T(8,128)(2,1)} %refs_8_.1), channel_id=1, source_target_pairs={{0,2},{1,3},{2,0},{3,1},{4,6},{5,7},{6,4},{7,5},{8,10},{9,11},{10,... | collective-permute-start | bytes 1179656 | tf_op jit(solution)/shard_map/ppermute | solution.py:389
  2.4 1.0 %copy-start.4 = (s32[128]{0:T(128)S(1)}, s32[128]{0:T(128)}, u32[]{:S(2)}) copy-start(s32[128]{0:T(128)} %len_ref.5) | copy-start | bytes 1540
  3.4 5.4 %copy-start.1 = (bf16[256,768]{1,0:T(8,128)(2,1)S(1)}, bf16[256,768]{1,0:T(8,128)(2,1)}, u32[]{:S(2)}) copy-start(bf16[256,768]{1,0:T(8,128)(2,1)} %refs_9_.1) | copy-start | bytes 1179652
  3.4 25.2 %copy-start.5 = (s32[512,2]{0,1:T(2,128)S(1)}, s32[512,2]{0,1:T(2,128)}, u32[]{:S(2)}) copy-start(s32[512,2]{0,1:T(2,128)} %param.18) | copy-start | bytes 12292
  3.4 25.4 %copy-start = (bf16[256,768]{1,0:T(8,128)(2,1)S(1)}, bf16[256,768]{1,0:T(8,128)(2,1)}, u32[]{:S(2)}) copy-start(bf16[256,768]{1,0:T(8,128)(2,1)} %refs_8_.1) | copy-start | bytes 1179652
  5.8 11.9 %collective-permute-start.6 = (bf16[4,2,32,384]{3,2,1,0:T(8,128)(2,1)}, bf16[4,2,32,384]{3,2,1,0:T(8,128)(2,1)S(1)}, u32[]{:S(2)}, u32[]{:S(2)}) collective-permute-start(bf16[4,2,32,384]{3,2,1,0:T(8,128)(2,1)} %get-tuple-element.37), channel_id=1, source_target_pairs={{0,5},{1,4},{2,7},{3,6},{4,1},{5,0},{6,3},{7,2},{8,13},{9,12},{10,... | collective-permute-start | bytes 589832 | tf_op jit(solution)/shard_map/ppermute | solution.py:389
  8.3 10.5 %collective-permute-start.4 = (bf16[4,2,32,384]{3,2,1,0:T(8,128)(2,1)}, bf16[4,2,32,384]{3,2,1,0:T(8,128)(2,1)S(1)}, u32[]{:S(2)}, u32[]{:S(2)}) collective-permute-start(bf16[4,2,32,384]{3,2,1,0:T(8,128)(2,1)} %get-tuple-element.37), channel_id=1, source_target_pairs={{0,1},{1,0},{2,3},{3,2},{4,5},{5,4},{6,7},{7,6},{8,9},{9,8},{10,11... | collective-permute-start | bytes 589832 | tf_op jit(solution)/shard_map/ppermute | solution.py:389
  8.9 19.9 %collective-permute-start.12 = (bf16[256,768]{1,0:T(8,128)(2,1)S(1)}, bf16[256,768]{1,0:T(8,128)(2,1)S(1)}, u32[]{:S(2)}, u32[]{:S(2)}) collective-permute-start(bf16[256,768]{1,0:T(8,128)(2,1)S(1)} %copy-done.1), channel_id=1, source_target_pairs={{0,2},{1,3},{2,0},{3,1},{4,6},{5,7},{6,4},{7,5},{8,10},{9,11},{10,... | collective-permute-start | bytes 1179656 | tf_op jit(solution)/shard_map/ppermute | solution.py:389
  9.6 9.2 %collective-permute-start.5 = (bf16[4,2,32,384]{3,2,1,0:T(8,128)(2,1)S(1)}, bf16[4,2,32,384]{3,2,1,0:T(8,128)(2,1)S(1)}, u32[]{:S(2)}, u32[]{:S(2)}) collective-permute-start(bf16[4,2,32,384]{3,2,1,0:T(8,128)(2,1)S(1)} %get-tuple-element.36.refs_0_.refs_2_), channel_id=1, source_target_pairs={{0,4},{1,5},{2,6},{3,7},{4,0},{5,1},{6,2},{7,3},{8,12},{9,13},{10,... | collective-permute-start | bytes 589832 | tf_op jit(solution)/shard_map/ppermute | solution.py:389
  17.7 29.7 %collective-permute-start.9 = (bf16[256,768]{1,0:T(8,128)(2,1)}, bf16[256,768]{1,0:T(8,128)(2,1)S(1)}, u32[]{:S(2)}, u32[]{:S(2)}) collective-permute-start(bf16[256,768]{1,0:T(8,128)(2,1)} %refs_6_.2), channel_id=1, source_target_pairs={{0,2},{1,3},{2,0},{3,1},{4,6},{5,7},{6,4},{7,5},{8,10},{9,11},{10,... | collective-permute-start | bytes 1179656 | tf_op jit(solution)/shard_map/ppermute | solution.py:389
  18.8 31.8 %collective-permute-start.10 = (bf16[256,768]{1,0:T(8,128)(2,1)}, bf16[256,768]{1,0:T(8,128)(2,1)}, u32[]{:S(2)}, u32[]{:S(2)}) collective-permute-start(bf16[256,768]{1,0:T(8,128)(2,1)} %refs_7_.2), channel_id=1, source_target_pairs={{0,2},{1,3},{2,0},{3,1},{4,6},{5,7},{6,4},{7,5},{8,10},{9,11},{10,... | collective-permute-start | bytes 1179656 | tf_op jit(solution)/shard_map/ppermute | solution.py:389
  18.8 13.4 %collective-permute-start.8 = (bf16[4,2,32,384]{3,2,1,0:T(8,128)(2,1)}, bf16[4,2,32,384]{3,2,1,0:T(8,128)(2,1)S(1)}, u32[]{:S(2)}, u32[]{:S(2)}) collective-permute-start(bf16[4,2,32,384]{3,2,1,0:T(8,128)(2,1)} %get-tuple-element.37), channel_id=1, source_target_pairs={{4,9},{5,8},{6,11},{7,10},{8,5},{9,4},{10,7},{11,6},{12,17},{13,16... | collective-permute-start | bytes 589832 | tf_op jit(solution)/shard_map/ppermute | solution.py:389
  25.2 11.7 %collective-permute-start.7 = (bf16[4,2,32,384]{3,2,1,0:T(8,128)(2,1)S(1)}, bf16[4,2,32,384]{3,2,1,0:T(8,128)(2,1)S(1)}, u32[]{:S(2)}, u32[]{:S(2)}) collective-permute-start(bf16[4,2,32,384]{3,2,1,0:T(8,128)(2,1)S(1)} %get-tuple-element.36.refs_0_.refs_2_), channel_id=1, source_target_pairs={{4,8},{5,9},{6,10},{7,11},{8,4},{9,5},{10,6},{11,7},{12,16},{13,17... | collective-permute-start | bytes 589832 | tf_op jit(solution)/shard_map/ppermute | solution.py:389
  31.4 19.3 %copy-start.2 = (bf16[256,768]{1,0:T(8,128)(2,1)S(1)}, bf16[256,768]{1,0:T(8,128)(2,1)}, u32[]{:S(2)}) copy-start(bf16[256,768]{1,0:T(8,128)(2,1)} %refs_6_.2) | copy-start | bytes 1179652
  31.4 19.2 %copy-start.3 = (bf16[256,768]{1,0:T(8,128)(2,1)S(1)}, bf16[256,768]{1,0:T(8,128)(2,1)}, u32[]{:S(2)}) copy-start(bf16[256,768]{1,0:T(8,128)(2,1)} %refs_7_.2) | copy-start | bytes 1179652
  38.8 19.1 %collective-permute-start.16 = (f32[3,8,256]{2,1,0:T(8,128)S(1)}, f32[3,8,256]{2,1,0:T(8,128)S(1)}, u32[]{:S(2)}, u32[]{:S(2)}) collective-permute-start(f32[3,8,256]{2,1,0:T(8,128)S(1)} %shard_map.164.refs_13_), channel_id=1, source_target_pairs={{4,12},{5,13},{6,14},{7,15},{8,0},{9,1},{10,2},{11,3},{12,20},{13,... | collective-permute-start | bytes 73736 | tf_op jit(solution)/shard_map/ppermute | solution.py:389
  40.7 17.3 %collective-permute-start.14 = (f32[3,8,256]{2,1,0:T(8,128)S(1)}, f32[3,8,256]{2,1,0:T(8,128)S(1)}, u32[]{:S(2)}, u32[]{:S(2)}) collective-permute-start(f32[3,8,256]{2,1,0:T(8,128)S(1)} %shard_map.164.refs_13_), channel_id=1, source_target_pairs={{4,8},{5,9},{6,10},{7,11},{8,4},{9,5},{10,6},{11,7},{12,16},{13,17... | collective-permute-start | bytes 73736 | tf_op jit(solution)/shard_map/ppermute | solution.py:389
  45.4 12.6 %collective-permute-start.15 = (f32[3,8,256]{2,1,0:T(8,128)S(1)}, f32[3,8,256]{2,1,0:T(8,128)S(1)}, u32[]{:S(2)}, u32[]{:S(2)}) collective-permute-start(f32[3,8,256]{2,1,0:T(8,128)S(1)} %shard_map.163.refs_8_.refs_12_), channel_id=1, source_target_pairs={{0,8},{1,9},{2,10},{3,11},{8,16},{9,17},{10,18},{11,19},{12,4},{13... | collective-permute-start | bytes 73736 | tf_op jit(solution)/shard_map/ppermute | solution.py:389
  47.4 10.6 %collective-permute-start.13 = (f32[3,8,256]{2,1,0:T(8,128)S(1)}, f32[3,8,256]{2,1,0:T(8,128)S(1)}, u32[]{:S(2)}, u32[]{:S(2)}) collective-permute-start(f32[3,8,256]{2,1,0:T(8,128)S(1)} %shard_map.163.refs_8_.refs_12_), channel_id=1, source_target_pairs={{0,4},{1,5},{2,6},{3,7},{4,0},{5,1},{6,2},{7,3},{8,12},{9,13},{10,... | collective-permute-start | bytes 73736 | tf_op jit(solution)/shard_map/ppermute | solution.py:389
  55.2 8.2 %collective-permute-start.17 = (bf16[256,384]{1,0:T(8,128)(2,1)S(1)}, bf16[256,384]{1,0:T(8,128)(2,1)S(1)}, u32[]{:S(2)}, u32[]{:S(2)}) collective-permute-start(bf16[256,384]{1,0:T(8,128)(2,1)S(1)} %get-tuple-element.43), channel_id=1, source_target_pairs={{0,2},{1,3},{2,0},{3,1},{4,6},{5,7},{6,4},{7,5},{8,10},{9,11},{10,... | collective-permute-start | bytes 589832 | tf_op jit(solution)/shard_map/ppermute | solution.py:389
  57.9 5.5 %collective-permute-start.18 = (bf16[256,384]{1,0:T(8,128)(2,1)S(1)}, bf16[256,384]{1,0:T(8,128)(2,1)S(1)}, u32[]{:S(2)}, u32[]{:S(2)}) collective-permute-start(bf16[256,384]{1,0:T(8,128)(2,1)S(1)} %get-tuple-element.44), channel_id=1, source_target_pairs={{0,2},{1,3},{2,0},{3,1},{4,6},{5,7},{6,4},{7,5},{8,10},{9,11},{10,... | collective-permute-start | bytes 589832 | tf_op jit(solution)/shard_map/ppermute | solution.py:389
  62.2 4.0 %collective-permute-start.19 = (bf16[256,384]{1,0:T(8,128)(2,1)S(1)}, bf16[256,384]{1,0:T(8,128)(2,1)S(1)}, u32[]{:S(2)}, u32[]{:S(2)}) collective-permute-start(bf16[256,384]{1,0:T(8,128)(2,1)S(1)} %get-tuple-element.45), channel_id=1, source_target_pairs={{0,2},{1,3},{2,0},{3,1},{4,6},{5,7},{6,4},{7,5},{8,10},{9,11},{10,... | collective-permute-start | bytes 589832 | tf_op jit(solution)/shard_map/ppermute | solution.py:389
  62.9 7.8 %collective-permute-start.20 = (bf16[256,384]{1,0:T(8,128)(2,1)S(1)}, bf16[256,384]{1,0:T(8,128)(2,1)S(1)}, u32[]{:S(2)}, u32[]{:S(2)}) collective-permute-start(bf16[256,384]{1,0:T(8,128)(2,1)S(1)} %get-tuple-element.46), channel_id=1, source_target_pairs={{0,2},{1,3},{2,0},{3,1},{4,6},{5,7},{6,4},{7,5},{8,10},{9,11},{10,... | collective-permute-start | bytes 589832 | tf_op jit(solution)/shard_map/ppermute | solution.py:389
  63.0 13.3 %collective-permute-start.21 = (bf16[4,2,32,384]{3,2,1,0:T(8,128)(2,1)S(1)}, bf16[4,2,32,384]{3,2,1,0:T(8,128)(2,1)S(1)}, u32[]{:S(2)}, u32[]{:S(2)}) collective-permute-start(bf16[4,2,32,384]{3,2,1,0:T(8,128)(2,1)S(1)} %get-tuple-element.49), channel_id=1, source_target_pairs={{0,1},{1,0},{2,3},{3,2},{4,5},{5,4},{6,7},{7,6},{8,9},{9,8},{10,11... | collective-permute-start | bytes 589832 | tf_op jit(solution)/shard_map/ppermute | solution.py:389
  63.4 12.9 %collective-permute-start.22 = (bf16[4,2,32,384]{3,2,1,0:T(8,128)(2,1)S(1)}, bf16[4,2,32,384]{3,2,1,0:T(8,128)(2,1)S(1)}, u32[]{:S(2)}, u32[]{:S(2)}) collective-permute-start(bf16[4,2,32,384]{3,2,1,0:T(8,128)(2,1)S(1)} %get-tuple-element.50), channel_id=1, source_target_pairs={{0,4},{1,5},{2,6},{3,7},{4,0},{5,1},{6,2},{7,3},{8,12},{9,13},{10,... | collective-permute-start | bytes 589832 | tf_op jit(solution)/shard_map/ppermute | solution.py:389
  63.4 12.9 %collective-permute-start.23 = (bf16[4,2,32,384]{3,2,1,0:T(8,128)(2,1)S(1)}, bf16[4,2,32,384]{3,2,1,0:T(8,128)(2,1)S(1)}, u32[]{:S(2)}, u32[]{:S(2)}) collective-permute-start(bf16[4,2,32,384]{3,2,1,0:T(8,128)(2,1)S(1)} %get-tuple-element.51), channel_id=1, source_target_pairs={{0,5},{1,4},{2,7},{3,6},{4,1},{5,0},{6,3},{7,2},{8,13},{9,12},{10,... | collective-permute-start | bytes 589832 | tf_op jit(solution)/shard_map/ppermute | solution.py:389
  66.3 11.3 %collective-permute-start.24 = (bf16[4,2,32,384]{3,2,1,0:T(8,128)(2,1)S(1)}, bf16[4,2,32,384]{3,2,1,0:T(8,128)(2,1)S(1)}, u32[]{:S(2)}, u32[]{:S(2)}) collective-permute-start(bf16[4,2,32,384]{3,2,1,0:T(8,128)(2,1)S(1)} %get-tuple-element.52), channel_id=1, source_target_pairs={{4,8},{5,9},{6,10},{7,11},{8,4},{9,5},{10,6},{11,7},{12,16},{13,17... | collective-permute-start | bytes 589832 | tf_op jit(solution)/shard_map/ppermute | solution.py:389
  70.7 12.3 %collective-permute-start.25 = (bf16[4,2,32,384]{3,2,1,0:T(8,128)(2,1)S(1)}, bf16[4,2,32,384]{3,2,1,0:T(8,128)(2,1)S(1)}, u32[]{:S(2)}, u32[]{:S(2)}) collective-permute-start(bf16[4,2,32,384]{3,2,1,0:T(8,128)(2,1)S(1)} %get-tuple-element.53), channel_id=1, source_target_pairs={{4,9},{5,8},{6,11},{7,10},{8,5},{9,4},{10,7},{11,6},{12,17},{13,16... | collective-permute-start | bytes 589832 | tf_op jit(solution)/shard_map/ppermute | solution.py:389
  84.3 3.5 %collective-permute-start.26 = (bf16[4,2,32,384]{3,2,1,0:T(8,128)(2,1)S(1)}, bf16[4,2,32,384]{3,2,1,0:T(8,128)(2,1)S(1)}, u32[]{:S(2)}, u32[]{:S(2)}) collective-permute-start(bf16[4,2,32,384]{3,2,1,0:T(8,128)(2,1)S(1)} %get-tuple-element.56), channel_id=1, source_target_pairs={{0,2},{1,3},{2,0},{3,1},{4,6},{5,7},{6,4},{7,5},{8,10},{9,11},{10,... | collective-permute-start | bytes 589832 | tf_op jit(solution)/shard_map/ppermute | solution.py:389

commit v6 on v5

--- a/solution.py
+++ b/solution.py
@@ -38,44 +38,59 @@
     return jnp.where((lane < HD) if e == 0 else (lane >= HD), x, jnp.zeros_like(x))
 
 
-def pack_kernel(idx_ref, len_ref, *refs):
-    mine, other, keep, send, local, sems = refs[:4], refs[4:8], refs[8], refs[9], refs[10], refs[11]
-    c, r, a = coords(idx_ref)
-    copies = [pltpu.make_async_copy(src, local.at[n], sems.at[n]) for n, src in enumerate(mine)]
+def load_kernel(idx_ref, *refs):
+    srcs, dst, sems = refs[:4], refs[4], refs[5]
+    copies = [pltpu.make_async_copy(src, dst.at[n], sems.at[n]) for n, src in enumerate(srcs)]
     for copy in copies:
         copy.start()
     for copy in copies:
         copy.wait()
-    mine = [local.at[n] for n in range(4)]
+
+
+def pack_kernel(idx_ref, len_ref, mine, *refs):
+    other, (keep, send, carry) = refs[:4], refs[4:]
+    c, r, a = coords(idx_ref)
     half, quarter = keep.shape[2], keep.shape[3]
     row = lax.broadcasted_iota(jnp.int32, (half, quarter), 0) + a * half
-    for slot, arrays in ((r, mine), (1 - r, other)):
+    carried = a ^ r
+    for slot, arrays in ((r, [mine.at[n] for n in range(4)]), (1 - r, other)):
         valid = row < len_ref[2 * c + slot]
         for n, ref in enumerate(arrays):
-            for part, out in ((a, keep), (1 - a, send)):
-                col = pl.multiple_of((2 * part + r) * quarter, 128)
+
+            def part(which, core):
+                col = pl.multiple_of((2 * which + core) * quarter, 128)
                 x = ref[:, pl.ds(col, quarter)]
                 if n == 0:
                     x = x * jnp.asarray(HD**-0.5, BF)
                 if n == 1:
                     x = jnp.where(valid, x, jnp.zeros_like(x))
-                out[n, slot] = x
-
-
-def piece_rows(idx_ref):
-    c, _, a = coords(idx_ref)
+                return x
+
+            keep[n, slot] = part(a, r)
+            send[n, slot] = part(1 - a, r)
+            carry[0, n, slot] = part(carried, r)
+            carry[1, n, slot] = part(carried, 1 - r)
+
+
+def piece_rows(idx_ref, swapped):
+    c, r, a = coords(idx_ref)
+    last = (a ^ r) if swapped else a
     half = BLK // 2
     side = 2 - 2 * (c & 1)
     starts = []
-    for place, part in ((1, a), (1, 1 - a), (side, a), (side, 1 - a), (2 - side, a), (2 - side, 1 - a)):
+    for place, part in ((1, a), (1, 1 - a), (side, a), (side, 1 - a), (2 - side, last), (2 - side, 1 - last)):
         first = place * 2 * BLK + part * half
         starts.append([pl.multiple_of(first + core * BLK, half) for core in range(2)])
     return starts
 
 
+def piece_views(pieces):
+    return [*pieces[:-2], pieces[-2].at[0], pieces[-1].at[1]]
+
+
 def gather_audio(idx_ref, pieces, arrays, dst):
     half = BLK // 2
-    for ref, firsts in zip(pieces, piece_rows(idx_ref)):
+    for ref, firsts in zip(piece_views(pieces), piece_rows(idx_ref, True)):
         for core, first in enumerate(firsts):
             for n, k in enumerate(arrays):
                 dst[n, pl.ds(first, half), :] = ref[k, core]
@@ -83,7 +98,7 @@
 
 def scatter_audio(idx_ref, sources, pieces):
     half = BLK // 2
-    for ref, firsts in zip(pieces, piece_rows(idx_ref)):
+    for ref, firsts in zip(pieces, piece_rows(idx_ref, False)):
         for core, first in enumerate(firsts):
             for n, src in enumerate(sources):
                 ref[n, core] = src[n % 2, pl.ds(first, half), :]
@@ -170,11 +185,14 @@
     pieces, refs = refs[: 2 * count], refs[2 * count :]
     video, refs = ((refs[0], refs[1]), (refs[2], refs[3])), refs[4:]
     stat_ref, audio, bias = refs[-3:]
-    _, _, a = coords(idx_ref)
+    _, r, a = coords(idx_ref)
     half, quarter = BLK // 2, audio.shape[2]
+    if 2 in groups:
+        pieces = piece_views(pieces)
     group_bias(idx_ref, win_ref, groups, bias)
     for n in range(count):
-        for ref, part in ((pieces[2 * n], a), (pieces[2 * n + 1], 1 - a)):
+        first_part = (a ^ r) if groups[n] == 2 else a
+        for ref, part in ((pieces[2 * n], first_part), (pieces[2 * n + 1], 1 - first_part)):
             for core in range(2):
                 first = pl.multiple_of(n * PAIR + core * BLK + part * half, half)
                 for k in range(2):
@@ -381,6 +399,7 @@
         "Ax": perm(lambda v, a: (v ^ 2, 1 - a)),
         "B": perm(lambda v, a: (diagonal(v), a)),
         "Bx": perm(lambda v, a: (diagonal(v), 1 - a)),
+        "Bs": perm(lambda v, a: (diagonal(v), a ^ (v & 1))),
         "Q": perm(lambda v, a: (v - 4 if v & 2 else v + 4, a)),
         "Q2": perm(lambda v, a: (v + 4 if v & 2 else v - 4, a)),
     }
@@ -420,12 +439,27 @@
         audio = (q_a, g_a, k_a, v_a)
         audio_other = [move(x, "core") for x in audio]
         piece = shape((4, 2, half, quarter), BF)
-        keep, send = call(
-            pack_kernel, [smem] + [hbm] * 4 + [whole] * 4, [(whole, piece)] * 2, (audio_len, *[pltpu.with_memory_space_constraint(x, pltpu.HBM) for x in audio], *audio_other), grid=(),
-            scratch=(pltpu.VMEM((4, half, 2 * width), BF), pltpu.SemaphoreType.DMA((4,))),
-            est=cost(0, 0, 1200000),
-        )
-        pieces = [keep, move(send, "aud"), move(keep, "A"), move(send, "Ax"), move(keep, "B"), move(send, "Bx")]
+        stack, both = shape((4, half, 2 * width), BF), shape((2, 4, 2, half, quarter), BF)
+        (mine,) = call(
+            load_kernel,
+            [hbm] * 4,
+            [(whole, stack)],
+            [pltpu.with_memory_space_constraint(x, pltpu.HBM) for x in audio],
+            scratch=(pltpu.SemaphoreType.DMA((4,)),),
+            grid=(),
+            est=cost(0, 0, 800000),
+        )
+        keep, send, carry = call(
+            pack_kernel,
+            [smem] + [whole] * 5,
+            [(whole, piece)] * 2 + [(whole, both)],
+            (audio_len, mine, *audio_other),
+            grid=(),
+            est=cost(0, 0, 1600000),
+        )
+        pieces = [keep, move(send, "aud"), move(keep, "A"), move(send, "Ax")]
+        by_carry = move(carry, "Bs")
+        pieces += [by_carry, move(by_carry, "core")]
         k_f, v_f, q_f, g_f = [move(x, "core") for x in (k_v, v_v, q_v, g_v)]
 
         audio_scratch = pltpu.VMEM((2, KEYS, quarter), BF)

time: 88.9 us -> 81.2 us (0.913)
  waiting for transfers between devices: 22.1 us -> 17.3 us
  starting transfers between devices: 46.5 us -> 43.8 us
    ppermute x27, waiting for transfers between devices: 22.1 us -> 17.3 us  [move(): return lax.ppermute(x, ('vid', 'aud'), moves[name])]
    ppermute x27, starting transfers between devices: 46.5 us -> 43.8 us  [move(): return lax.ppermute(x, ('vid', 'aud'), moves[name])]
    pallas_call x8 -> x9, Pallas kernels: 18.9 us -> 18.7 us  [call(): pl.pallas_call(kernel, grid_spec=pltpu.PrefetchScalarGridSpec(num_scalar_...]
  transfers between devices with their start and end apart: 27 -> 27, of which waited for: 10 -> 4; matrix products, arithmetic and copies ran while one was open for 0% -> 0% of each run, Pallas kernels for 19% -> 20%
where the time goes in v6:
time: 81.2 us; the launch traced here: 80.8 us
  starting transfers between devices  43.8 us (54%)
  Pallas kernels  18.7 us (23%)
  waiting for transfers between devices  17.3 us (21%)
  between operations  0.89 us (1%)
    ppermute x27, starting transfers between devices, move(): return lax.ppermute(x, ('vid', 'aud'), moves[name])  43.8 us
    pallas_call x9, Pallas kernels, call(): pl.pallas_call(kernel, grid_spec=pltpu.PrefetchScalarGridSpec(num_scalar_...  18.7 us
    ppermute x27, waiting for transfers between devices, move(): return lax.ppermute(x, ('vid', 'aud'), moves[name])  17.3 us
  transfers between devices with their start and end apart: 27, of which 4 were waited for; matrix products, arithmetic and copies ran while one was open for 0% of the time, Pallas kernels for 20%

profile of v6, /device:TPU:129, one launch (start us, length us, event | category | flops | bytes accessed | tf_op | source)
XLA Modules:
  0.0 80.8 jit_solution(3587884072582817804)
XLA Ops:
  0.6 0.8 collective-permute-start
  1.4 0.1 collective-permute-start.2
  1.5 0.4 collective-permute-start.3
  1.9 0.1 collective-permute-start.1
  2.0 1.1 %shard_map.161.mine = bf16[4,32,1536]{2,1,0:T(8,128)(2,1)S(1)} custom-call(s32[1]{0:T(128)} %bitcast.idx_ref.refs_0_, bf16[32,1536]{1,0:T(8,128)(2,1)} %refs_0_.1, bf16[32,1536]{1,0:T(8,128)(2,1)} %refs_1_.4, bf16[32,1536]{1,0:T(8,128)(2,1)} %refs_2_.1, bf16[32,1536]{1,0:T(8,128)(2,1)} %refs_3_.1), custom_call_target="tpu_custom_call" | custom-call | bytes 800000 | tf_op jit(solution)/shard_map/pallas_call | solution.py:425
  3.1 0.0 copy-start
  3.1 0.0 copy-start.1
  3.1 0.0 collective-permute-done.refs_0_
  3.1 0.0 collective-permute-done.2.refs_2_
  3.2 0.3 collective-permute-done.1.refs_1_
  3.4 0.6 shard_map.162
  4.1 0.0 copy-start.3
  4.1 6.4 %collective-permute-start.7 = (bf16[2,4,2,32,384]{4,3,2,1,0:T(8,128)(2,1)S(1)}, bf16[2,4,2,32,384]{4,3,2,1,0:T(8,128)(2,1)S(1)}, u32[]{:S(2)}, u32[]{:S(2)}) collective-permute-start(bf16[2,4,2,32,384]{4,3,2,1,0:T(8,128)(2,1)S(1)} %get-tuple-element.39), channel_id=1, source_target_pairs={{4,8},{5,9},{6,11},{7,10},{8,4},{9,5},{10,7},{11,6},{12,16},{13,17... | collective-permute-start | bytes 1179656 | tf_op jit(solution)/shard_map/ppermute | solution.py:408
  10.5 0.1 collective-permute-start.6
  10.6 0.7 collective-permute-start.4
  11.3 2.5 %collective-permute-start.5 = (bf16[4,2,32,384]{3,2,1,0:T(8,128)(2,1)S(1)}, bf16[4,2,32,384]{3,2,1,0:T(8,128)(2,1)S(1)}, u32[]{:S(2)}, u32[]{:S(2)}) collective-permute-start(bf16[4,2,32,384]{3,2,1,0:T(8,128)(2,1)S(1)} %get-tuple-element.37.refs_0_.refs_2_), channel_id=1, source_target_pairs={{0,4},{1,5},{2,6},{3,7},{4,0},{5,1},{6,2},{7,3},{8,12},{9,13},{10,... | collective-permute-start | bytes 589832 | tf_op jit(solution)/shard_map/ppermute | solution.py:408
  13.8 0.0 collective-permute-start.11
  13.8 9.9 %collective-permute-done.6.refs_3_.refs_5_ = bf16[4,2,32,384]{3,2,1,0:T(8,128)(2,1)S(1)} collective-permute-done((bf16[4,2,32,384]{3,2,1,0:T(8,128)(2,1)S(1)}, bf16[4,2,32,384]{3,2,1,0:T(8,128)(2,1)S(1)}, u32[]{:S(2)}, u32[]{:S(2)}) %collective-permute-start.6) | collective-permute-done | bytes 196640 | tf_op jit(solution)/shard_map/ppermute | solution.py:408
  23.7 0.4 collective-permute-start.12
  24.1 0.2 collective-permute-start.8
  24.3 0.0 collective-permute-done.4.refs_1_.refs_3_
  24.3 0.4 collective-permute-start.9
  24.6 1.2 %collective-permute-start.10 = (bf16[256,768]{1,0:T(8,128)(2,1)}, bf16[256,768]{1,0:T(8,128)(2,1)}, u32[]{:S(2)}, u32[]{:S(2)}) collective-permute-start(bf16[256,768]{1,0:T(8,128)(2,1)} %refs_7_.2), channel_id=1, source_target_pairs={{0,2},{1,3},{2,0},{3,1},{4,6},{5,7},{6,4},{7,5},{8,10},{9,11},{10,... | collective-permute-start | bytes 1179656 | tf_op jit(solution)/shard_map/ppermute | solution.py:408
  25.8 0.1 copy.18.win_ref.refs_1_
  26.0 0.0 collective-permute-done.11.refs_8_.refs_6_.refs_10_
  26.0 2.5 %shard_map.164.refs_8_.refs_12_ = f32[3,8,256]{2,1,0:T(8,128)S(1)} custom-call(s32[1]{0:T(128)} %bitcast.idx_ref.refs_0_, s32[512,2]{1,0:T(8,128)S(1)} %copy.18.win_ref.refs_1_, bf16[4,2,32,384]{3,2,1,0:T(8,128)(2,1)S(1)} %get-tuple-element.37.refs_0_.refs_2_, bf16[4,2,32,384]{3,2,1,0:T(8,128)(2,1)S(1)} %collective-permute-done.4.refs_1_.refs_3_, ...), custom_call_target="tpu_custom_call" | custom-call | flops 201326592 | bytes 2000000 | tf_op jit(solution)/shard_map/pallas_call | solution.py:425
  28.5 2.2 %collective-permute-start.15 = (f32[3,8,256]{2,1,0:T(8,128)S(1)}, f32[3,8,256]{2,1,0:T(8,128)S(1)}, u32[]{:S(2)}, u32[]{:S(2)}) collective-permute-start(f32[3,8,256]{2,1,0:T(8,128)S(1)} %shard_map.164.refs_8_.refs_12_), channel_id=1, source_target_pairs={{0,8},{1,9},{2,10},{3,11},{8,16},{9,17},{10,18},{11,19},{12,4},{13... | collective-permute-start | bytes 73736 | tf_op jit(solution)/shard_map/ppermute | solution.py:408
  30.7 2.1 %collective-permute-start.13 = (f32[3,8,256]{2,1,0:T(8,128)S(1)}, f32[3,8,256]{2,1,0:T(8,128)S(1)}, u32[]{:S(2)}, u32[]{:S(2)}) collective-permute-start(f32[3,8,256]{2,1,0:T(8,128)S(1)} %shard_map.164.refs_8_.refs_12_), channel_id=1, source_target_pairs={{0,4},{1,5},{2,6},{3,7},{4,0},{5,1},{6,2},{7,3},{8,12},{9,13},{10,... | collective-permute-start | bytes 73736 | tf_op jit(solution)/shard_map/ppermute | solution.py:408
  32.8 0.0 collective-permute-done.8.refs_5_.refs_3_.refs_7_
  32.8 1.8 %shard_map.165.refs_13_ = f32[3,8,256]{2,1,0:T(8,128)S(1)} custom-call(s32[1]{0:T(128)} %bitcast.idx_ref.refs_0_, s32[512,2]{1,0:T(8,128)S(1)} %copy.18.win_ref.refs_1_, bf16[2,4,2,32,384]{4,3,2,1,0:T(8,128)(2,1)S(1)} %collective-permute-done.7.refs_4_.refs_2_.refs_6_, bf16[2,4,2,32,384]{4,3,2,1,0:T(8,128)(2,1)S(1)} %collective-permute-done.8.refs_5_.refs_3_.refs_7_, ...), custom_call_target="tpu_custom_call" | custom-call | flops 100663296 | bytes 2000000 | tf_op jit(solution)/shard_map/pallas_call | solution.py:425
  34.7 4.4 %collective-permute-start.16 = (f32[3,8,256]{2,1,0:T(8,128)S(1)}, f32[3,8,256]{2,1,0:T(8,128)S(1)}, u32[]{:S(2)}, u32[]{:S(2)}) collective-permute-start(f32[3,8,256]{2,1,0:T(8,128)S(1)} %shard_map.165.refs_13_), channel_id=1, source_target_pairs={{4,12},{5,13},{6,14},{7,15},{8,0},{9,1},{10,2},{11,3},{12,20},{13,... | collective-permute-start | bytes 73736 | tf_op jit(solution)/shard_map/ppermute | solution.py:408
  39.1 3.9 %collective-permute-start.14 = (f32[3,8,256]{2,1,0:T(8,128)S(1)}, f32[3,8,256]{2,1,0:T(8,128)S(1)}, u32[]{:S(2)}, u32[]{:S(2)}) collective-permute-start(f32[3,8,256]{2,1,0:T(8,128)S(1)} %shard_map.165.refs_13_), channel_id=1, source_target_pairs={{4,8},{5,9},{6,10},{7,11},{8,4},{9,5},{10,6},{11,7},{12,16},{13,17... | collective-permute-start | bytes 73736 | tf_op jit(solution)/shard_map/ppermute | solution.py:408
  43.1 5.0 %shard_map.163 = (bf16[256,384]{1,0:T(8,128)(2,1)S(1)}, bf16[256,384]{1,0:T(8,128)(2,1)S(1)}, bf16[256,384]{1,0:T(8,128)(2,1)S(1)}, bf16[256,384]{1,0:T(8,128)(2,1)S(1)}, bf16[2,384,384]{2,1,0:T(8,128)(2,1)S(1)}) custom-call(s32[1]{0:T(128)} %bitcast.idx_ref.refs_0_, s32[512,2]{1,0:T(8,128)S(1)} %copy.18.win_ref.refs_1_, s32[128]{0:T(128)S(1)} %copy-done.2, ...), custom_call_target="tpu_custom_call" | custom-call | flops 754974720 | bytes 5000000 | tf_op jit(solution)/shard_map/pallas_call | solution.py:425
  48.0 0.9 %collective-permute-start.17 = (bf16[256,384]{1,0:T(8,128)(2,1)S(1)}, bf16[256,384]{1,0:T(8,128)(2,1)S(1)}, u32[]{:S(2)}, u32[]{:S(2)}) collective-permute-start(bf16[256,384]{1,0:T(8,128)(2,1)S(1)} %get-tuple-element.45), channel_id=1, source_target_pairs={{0,2},{1,3},{2,0},{3,1},{4,6},{5,7},{6,4},{7,5},{8,10},{9,11},{10,... | collective-permute-start | bytes 589832 | tf_op jit(solution)/shard_map/ppermute | solution.py:408
  49.0 0.3 collective-permute-start.18
  49.3 4.2 %shard_map.166 = (bf16[256,384]{1,0:T(8,128)(2,1)S(1)}, bf16[256,384]{1,0:T(8,128)(2,1)S(1)}, bf16[256,384]{1,0:T(8,128)(2,1)S(1)}, bf16[256,384]{1,0:T(8,128)(2...) custom-call(s32[1]{0:T(128)} %bitcast.idx_ref.refs_0_, ...), custom_call_target="tpu_custom_call" | custom-call | flops 905969664 | bytes 5000000 | tf_op jit(solution)/shard_map/pallas_call | solution.py:425
  53.5 0.4 collective-permute-start.19
  53.9 0.2 collective-permute-start.20
  54.1 2.3 %collective-permute-start.21 = (bf16[4,2,32,384]{3,2,1,0:T(8,128)(2,1)S(1)}, bf16[4,2,32,384]{3,2,1,0:T(8,128)(2,1)S(1)}, u32[]{:S(2)}, u32[]{:S(2)}) collective-permute-start(bf16[4,2,32,384]{3,2,1,0:T(8,128)(2,1)S(1)} %get-tuple-element.51), channel_id=1, source_target_pairs={{0,1},{1,0},{2,3},{3,2},{4,5},{5,4},{6,7},{7,6},{8,9},{9,8},{10,11... | collective-permute-start | bytes 589832 | tf_op jit(solution)/shard_map/ppermute | solution.py:408
  56.4 0.9 %collective-permute-start.23 = (bf16[4,2,32,384]{3,2,1,0:T(8,128)(2,1)S(1)}, bf16[4,2,32,384]{3,2,1,0:T(8,128)(2,1)S(1)}, u32[]{:S(2)}, u32[]{:S(2)}) collective-permute-start(bf16[4,2,32,384]{3,2,1,0:T(8,128)(2,1)S(1)} %get-tuple-element.53), channel_id=1, source_target_pairs={{0,5},{1,4},{2,7},{3,6},{4,1},{5,0},{6,3},{7,2},{8,13},{9,12},{10,... | collective-permute-start | bytes 589832 | tf_op jit(solution)/shard_map/ppermute | solution.py:408
  57.3 5.6 %collective-permute-start.24 = (bf16[4,2,32,384]{3,2,1,0:T(8,128)(2,1)S(1)}, bf16[4,2,32,384]{3,2,1,0:T(8,128)(2,1)S(1)}, u32[]{:S(2)}, u32[]{:S(2)}) collective-permute-start(bf16[4,2,32,384]{3,2,1,0:T(8,128)(2,1)S(1)} %get-tuple-element.54), channel_id=1, source_target_pairs={{4,8},{5,9},{6,10},{7,11},{8,4},{9,5},{10,6},{11,7},{12,16},{13,17... | collective-permute-start | bytes 589832 | tf_op jit(solution)/shard_map/ppermute | solution.py:408
  62.9 5.1 %collective-permute-start.25 = (bf16[4,2,32,384]{3,2,1,0:T(8,128)(2,1)S(1)}, bf16[4,2,32,384]{3,2,1,0:T(8,128)(2,1)S(1)}, u32[]{:S(2)}, u32[]{:S(2)}) collective-permute-start(bf16[4,2,32,384]{3,2,1,0:T(8,128)(2,1)S(1)} %get-tuple-element.55), channel_id=1, source_target_pairs={{4,9},{5,8},{6,11},{7,10},{8,5},{9,4},{10,7},{11,6},{12,17},{13,16... | collective-permute-start | bytes 589832 | tf_op jit(solution)/shard_map/ppermute | solution.py:408
  68.0 1.3 %shard_map.167 = (bf16[256,768]{1,0:T(8,128)(2,1)}, bf16[256,768]{1,0:T(8,128)(2,1)}, bf16[256,768]{1,0:T(8,128)(2,1)}, bf16[256,768]{1,0:T(8,128)(2,1)}, s32[1]{0:T(128)}) custom-call(s32[1]{0:T(128)} %bitcast.idx_ref.refs_0_, bf16[256,384]{1,0:T(8,128)(2,1)S(1)} %get-tuple-element.40.refs_0_, bf16[256,384]{1,0:T(8,128)(2,1)S(1)} %get-tuple-element.41.refs_1_, ...), custom_call_target="tpu_custom_call" | custom-call | bytes 1600000 | tf_op jit(solution)/shard_map/pallas_call | solution.py:425
  69.3 6.0 %collective-permute-done.25.by_bx = bf16[4,2,32,384]{3,2,1,0:T(8,128)(2,1)S(1)} collective-permute-done((bf16[4,2,32,384]{3,2,1,0:T(8,128)(2,1)S(1)}, bf16[4,2,32,384]{3,2,1,0:T(8,128)(2,1)S(1)}, u32[]{:S(2)}, u32[]{:S(2)}) %collective-permute-start.25) | collective-permute-done | bytes 196640 | tf_op jit(solution)/shard_map/ppermute | solution.py:408
  75.3 1.3 %shard_map.168 = (bf16[4,2,32,384]{3,2,1,0:T(8,128)(2,1)S(1)}, bf16[4,2,32,384]{3,2,1,0:T(8,128)(2,1)S(1)}) custom-call(s32[1]{0:T(128)} %bitcast.idx_ref.refs_0_, s32[128]{0:T(128)S(1)} %copy-done.2, bf16[4,2,32,384]{3,2,1,0:T(8,128)(2,1)S(1)} %get-tuple-element.50.keep, bf16[4,2,32,384]{3,2,1,0:T(8,128)(2,1)S(1)} %collective-permute-done.21.by_aud, ...), custom_call_target="tpu_custom_call" | custom-call | flops 1000000 | bytes 1600000 | tf_op jit(solution)/shard_map/pallas_call | solution.py:425
  76.7 2.3 %collective-permute-start.26 = (bf16[4,2,32,384]{3,2,1,0:T(8,128)(2,1)S(1)}, bf16[4,2,32,384]{3,2,1,0:T(8,128)(2,1)S(1)}, u32[]{:S(2)}, u32[]{:S(2)}) collective-permute-start(bf16[4,2,32,384]{3,2,1,0:T(8,128)(2,1)S(1)} %get-tuple-element.58), channel_id=1, source_target_pairs={{0,2},{1,3},{2,0},{3,1},{4,6},{5,7},{6,4},{7,5},{8,10},{9,11},{10,... | collective-permute-start | bytes 589832 | tf_op jit(solution)/shard_map/ppermute | solution.py:408
  79.0 1.1 %collective-permute-done.26.other = bf16[4,2,32,384]{3,2,1,0:T(8,128)(2,1)S(1)} collective-permute-done((bf16[4,2,32,384]{3,2,1,0:T(8,128)(2,1)S(1)}, bf16[4,2,32,384]{3,2,1,0:T(8,128)(2,1)S(1)}, u32[]{:S(2)}, u32[]{:S(2)}) %collective-permute-start.26) | collective-permute-done | bytes 196640 | tf_op jit(solution)/shard_map/ppermute | solution.py:408
  80.1 0.8 shard_map.169
  (24 shorter events, 0.1 us)
Async XLA Ops:
  0.6 2.5 %collective-permute-start = (bf16[32,1536]{1,0:T(8,128)(2,1)}, bf16[32,1536]{1,0:T(8,128)(2,1)S(1)}, u32[]{:S(2)}, u32[]{:S(2)}) collective-permute-start(bf16[32,1536]{1,0:T(8,128)(2,1)} %refs_0_.1), channel_id=1, source_target_pairs={{0,2},{1,3},{2,0},{3,1},{4,6},{5,7},{6,4},{7,5},{8,10},{9,11},{10,... | collective-permute-start | bytes 294920 | tf_op jit(solution)/shard_map/ppermute | solution.py:408
  1.4 1.7 %collective-permute-start.2 = (bf16[32,1536]{1,0:T(8,128)(2,1)}, bf16[32,1536]{1,0:T(8,128)(2,1)S(1)}, u32[]{:S(2)}, u32[]{:S(2)}) collective-permute-start(bf16[32,1536]{1,0:T(8,128)(2,1)} %refs_2_.1), channel_id=1, source_target_pairs={{0,2},{1,3},{2,0},{3,1},{4,6},{5,7},{6,4},{7,5},{8,10},{9,11},{10,... | collective-permute-start | bytes 294920 | tf_op jit(solution)/shard_map/ppermute | solution.py:408
  1.5 1.7 %collective-permute-start.3 = (bf16[32,1536]{1,0:T(8,128)(2,1)}, bf16[32,1536]{1,0:T(8,128)(2,1)S(1)}, u32[]{:S(2)}, u32[]{:S(2)}) collective-permute-start(bf16[32,1536]{1,0:T(8,128)(2,1)} %refs_3_.1), channel_id=1, source_target_pairs={{0,2},{1,3},{2,0},{3,1},{4,6},{5,7},{6,4},{7,5},{8,10},{9,11},{10,... | collective-permute-start | bytes 294920 | tf_op jit(solution)/shard_map/ppermute | solution.py:408
  1.9 1.5 %collective-permute-start.1 = (bf16[32,1536]{1,0:T(8,128)(2,1)}, bf16[32,1536]{1,0:T(8,128)(2,1)S(1)}, u32[]{:S(2)}, u32[]{:S(2)}) collective-permute-start(bf16[32,1536]{1,0:T(8,128)(2,1)} %refs_1_.4), channel_id=1, source_target_pairs={{0,2},{1,3},{2,0},{3,1},{4,6},{5,7},{6,4},{7,5},{8,10},{9,11},{10,... | collective-permute-start | bytes 294920 | tf_op jit(solution)/shard_map/ppermute | solution.py:408
  2.0 1.4 %copy-start.2 = (s32[128]{0:T(128)S(1)}, s32[128]{0:T(128)}, u32[]{:S(2)}) copy-start(s32[128]{0:T(128)} %len_ref.5) | copy-start | bytes 1540
  3.1 10.7 %copy-start = (bf16[256,768]{1,0:T(8,128)(2,1)S(1)}, bf16[256,768]{1,0:T(8,128)(2,1)}, u32[]{:S(2)}) copy-start(bf16[256,768]{1,0:T(8,128)(2,1)} %refs_8_.1) | copy-start | bytes 1179652
  3.1 20.6 %copy-start.1 = (bf16[256,768]{1,0:T(8,128)(2,1)S(1)}, bf16[256,768]{1,0:T(8,128)(2,1)}, u32[]{:S(2)}) copy-start(bf16[256,768]{1,0:T(8,128)(2,1)} %refs_9_.1) | copy-start | bytes 1179652
  4.1 21.8 %copy-start.3 = (s32[512,2]{0,1:T(2,128)S(1)}, s32[512,2]{0,1:T(2,128)}, u32[]{:S(2)}) copy-start(s32[512,2]{0,1:T(2,128)} %param.18) | copy-start | bytes 12292
  4.1 20.0 %collective-permute-start.7 = (bf16[2,4,2,32,384]{4,3,2,1,0:T(8,128)(2,1)S(1)}, bf16[2,4,2,32,384]{4,3,2,1,0:T(8,128)(2,1)S(1)}, u32[]{:S(2)}, u32[]{:S(2)}) collective-permute-start(bf16[2,4,2,32,384]{4,3,2,1,0:T(8,128)(2,1)S(1)} %get-tuple-element.39), channel_id=1, source_target_pairs={{4,8},{5,9},{6,11},{7,10},{8,4},{9,5},{10,7},{11,6},{12,16},{13,17... | collective-permute-start | bytes 1179656 | tf_op jit(solution)/shard_map/ppermute | solution.py:408
  10.5 13.3 %collective-permute-start.6 = (bf16[4,2,32,384]{3,2,1,0:T(8,128)(2,1)S(1)}, bf16[4,2,32,384]{3,2,1,0:T(8,128)(2,1)S(1)}, u32[]{:S(2)}, u32[]{:S(2)}) collective-permute-start(bf16[4,2,32,384]{3,2,1,0:T(8,128)(2,1)S(1)} %get-tuple-element.38), channel_id=1, source_target_pairs={{0,5},{1,4},{2,7},{3,6},{4,1},{5,0},{6,3},{7,2},{8,13},{9,12},{10,... | collective-permute-start | bytes 589832 | tf_op jit(solution)/shard_map/ppermute | solution.py:408
  10.6 13.7 %collective-permute-start.4 = (bf16[4,2,32,384]{3,2,1,0:T(8,128)(2,1)S(1)}, bf16[4,2,32,384]{3,2,1,0:T(8,128)(2,1)S(1)}, u32[]{:S(2)}, u32[]{:S(2)}) collective-permute-start(bf16[4,2,32,384]{3,2,1,0:T(8,128)(2,1)S(1)} %get-tuple-element.38), channel_id=1, source_target_pairs={{0,1},{1,0},{2,3},{3,2},{4,5},{5,4},{6,7},{7,6},{8,9},{9,8},{10,11... | collective-permute-start | bytes 589832 | tf_op jit(solution)/shard_map/ppermute | solution.py:408
  11.3 13.3 %collective-permute-start.5 = (bf16[4,2,32,384]{3,2,1,0:T(8,128)(2,1)S(1)}, bf16[4,2,32,384]{3,2,1,0:T(8,128)(2,1)S(1)}, u32[]{:S(2)}, u32[]{:S(2)}) collective-permute-start(bf16[4,2,32,384]{3,2,1,0:T(8,128)(2,1)S(1)} %get-tuple-element.37.refs_0_.refs_2_), channel_id=1, source_target_pairs={{0,4},{1,5},{2,6},{3,7},{4,0},{5,1},{6,2},{7,3},{8,12},{9,13},{10,... | collective-permute-start | bytes 589832 | tf_op jit(solution)/shard_map/ppermute | solution.py:408
  13.8 12.2 %collective-permute-start.11 = (bf16[256,768]{1,0:T(8,128)(2,1)S(1)}, bf16[256,768]{1,0:T(8,128)(2,1)S(1)}, u32[]{:S(2)}, u32[]{:S(2)}) collective-permute-start(bf16[256,768]{1,0:T(8,128)(2,1)S(1)} %copy-done), channel_id=1, source_target_pairs={{0,2},{1,3},{2,0},{3,1},{4,6},{5,7},{6,4},{7,5},{8,10},{9,11},{10,... | collective-permute-start | bytes 1179656 | tf_op jit(solution)/shard_map/ppermute | solution.py:408
  23.7 2.2 %collective-permute-start.12 = (bf16[256,768]{1,0:T(8,128)(2,1)S(1)}, bf16[256,768]{1,0:T(8,128)(2,1)S(1)}, u32[]{:S(2)}, u32[]{:S(2)}) collective-permute-start(bf16[256,768]{1,0:T(8,128)(2,1)S(1)} %copy-done.1), channel_id=1, source_target_pairs={{0,2},{1,3},{2,0},{3,1},{4,6},{5,7},{6,4},{7,5},{8,10},{9,11},{10,... | collective-permute-start | bytes 1179656 | tf_op jit(solution)/shard_map/ppermute | solution.py:408
  24.1 8.7 %collective-permute-start.8 = (bf16[2,4,2,32,384]{4,3,2,1,0:T(8,128)(2,1)S(1)}, bf16[2,4,2,32,384]{4,3,2,1,0:T(8,128)(2,1)S(1)}, u32[]{:S(2)}, u32[]{:S(2)}) collective-permute-start(bf16[2,4,2,32,384]{4,3,2,1,0:T(8,128)(2,1)S(1)} %collective-permute-done.7.refs_4_.refs_2_.refs_6_), channel_id=1, source_target_pairs={{0,2},{1,3},{2,0},{3,1},{4,6},{5,7},{6,4},{7,5},{8,10},{9,11},{10,... | collective-permute-start | bytes 1179656 | tf_op jit(solution)/shard_map/ppermute | solution.py:408
  24.3 14.9 %collective-permute-start.9 = (bf16[256,768]{1,0:T(8,128)(2,1)}, bf16[256,768]{1,0:T(8,128)(2,1)}, u32[]{:S(2)}, u32[]{:S(2)}) collective-permute-start(bf16[256,768]{1,0:T(8,128)(2,1)} %refs_6_.2), channel_id=1, source_target_pairs={{0,2},{1,3},{2,0},{3,1},{4,6},{5,7},{6,4},{7,5},{8,10},{9,11},{10,... | collective-permute-start | bytes 1179656 | tf_op jit(solution)/shard_map/ppermute | solution.py:408
  24.6 18.4 %collective-permute-start.10 = (bf16[256,768]{1,0:T(8,128)(2,1)}, bf16[256,768]{1,0:T(8,128)(2,1)}, u32[]{:S(2)}, u32[]{:S(2)}) collective-permute-start(bf16[256,768]{1,0:T(8,128)(2,1)} %refs_7_.2), channel_id=1, source_target_pairs={{0,2},{1,3},{2,0},{3,1},{4,6},{5,7},{6,4},{7,5},{8,10},{9,11},{10,... | collective-permute-start | bytes 1179656 | tf_op jit(solution)/shard_map/ppermute | solution.py:408
  28.5 20.4 %collective-permute-start.15 = (f32[3,8,256]{2,1,0:T(8,128)S(1)}, f32[3,8,256]{2,1,0:T(8,128)S(1)}, u32[]{:S(2)}, u32[]{:S(2)}) collective-permute-start(f32[3,8,256]{2,1,0:T(8,128)S(1)} %shard_map.164.refs_8_.refs_12_), channel_id=1, source_target_pairs={{0,8},{1,9},{2,10},{3,11},{8,16},{9,17},{10,18},{11,19},{12,4},{13... | collective-permute-start | bytes 73736 | tf_op jit(solution)/shard_map/ppermute | solution.py:408
  30.7 18.5 %collective-permute-start.13 = (f32[3,8,256]{2,1,0:T(8,128)S(1)}, f32[3,8,256]{2,1,0:T(8,128)S(1)}, u32[]{:S(2)}, u32[]{:S(2)}) collective-permute-start(f32[3,8,256]{2,1,0:T(8,128)S(1)} %shard_map.164.refs_8_.refs_12_), channel_id=1, source_target_pairs={{0,4},{1,5},{2,6},{3,7},{4,0},{5,1},{6,2},{7,3},{8,12},{9,13},{10,... | collective-permute-start | bytes 73736 | tf_op jit(solution)/shard_map/ppermute | solution.py:408
  34.7 14.6 %collective-permute-start.16 = (f32[3,8,256]{2,1,0:T(8,128)S(1)}, f32[3,8,256]{2,1,0:T(8,128)S(1)}, u32[]{:S(2)}, u32[]{:S(2)}) collective-permute-start(f32[3,8,256]{2,1,0:T(8,128)S(1)} %shard_map.165.refs_13_), channel_id=1, source_target_pairs={{4,12},{5,13},{6,14},{7,15},{8,0},{9,1},{10,2},{11,3},{12,20},{13,... | collective-permute-start | bytes 73736 | tf_op jit(solution)/shard_map/ppermute | solution.py:408
  39.1 10.1 %collective-permute-start.14 = (f32[3,8,256]{2,1,0:T(8,128)S(1)}, f32[3,8,256]{2,1,0:T(8,128)S(1)}, u32[]{:S(2)}, u32[]{:S(2)}) collective-permute-start(f32[3,8,256]{2,1,0:T(8,128)S(1)} %shard_map.165.refs_13_), channel_id=1, source_target_pairs={{4,8},{5,9},{6,10},{7,11},{8,4},{9,5},{10,6},{11,7},{12,16},{13,17... | collective-permute-start | bytes 73736 | tf_op jit(solution)/shard_map/ppermute | solution.py:408
  48.0 8.4 %collective-permute-start.17 = (bf16[256,384]{1,0:T(8,128)(2,1)S(1)}, bf16[256,384]{1,0:T(8,128)(2,1)S(1)}, u32[]{:S(2)}, u32[]{:S(2)}) collective-permute-start(bf16[256,384]{1,0:T(8,128)(2,1)S(1)} %get-tuple-element.45), channel_id=1, source_target_pairs={{0,2},{1,3},{2,0},{3,1},{4,6},{5,7},{6,4},{7,5},{8,10},{9,11},{10,... | collective-permute-start | bytes 589832 | tf_op jit(solution)/shard_map/ppermute | solution.py:408
  49.0 7.5 %collective-permute-start.18 = (bf16[256,384]{1,0:T(8,128)(2,1)S(1)}, bf16[256,384]{1,0:T(8,128)(2,1)S(1)}, u32[]{:S(2)}, u32[]{:S(2)}) collective-permute-start(bf16[256,384]{1,0:T(8,128)(2,1)S(1)} %get-tuple-element.46), channel_id=1, source_target_pairs={{0,2},{1,3},{2,0},{3,1},{4,6},{5,7},{6,4},{7,5},{8,10},{9,11},{10,... | collective-permute-start | bytes 589832 | tf_op jit(solution)/shard_map/ppermute | solution.py:408
  53.5 3.9 %collective-permute-start.19 = (bf16[256,384]{1,0:T(8,128)(2,1)S(1)}, bf16[256,384]{1,0:T(8,128)(2,1)S(1)}, u32[]{:S(2)}, u32[]{:S(2)}) collective-permute-start(bf16[256,384]{1,0:T(8,128)(2,1)S(1)} %get-tuple-element.47), channel_id=1, source_target_pairs={{0,2},{1,3},{2,0},{3,1},{4,6},{5,7},{6,4},{7,5},{8,10},{9,11},{10,... | collective-permute-start | bytes 589832 | tf_op jit(solution)/shard_map/ppermute | solution.py:408
  53.9 9.0 %collective-permute-start.20 = (bf16[256,384]{1,0:T(8,128)(2,1)S(1)}, bf16[256,384]{1,0:T(8,128)(2,1)S(1)}, u32[]{:S(2)}, u32[]{:S(2)}) collective-permute-start(bf16[256,384]{1,0:T(8,128)(2,1)S(1)} %get-tuple-element.48), channel_id=1, source_target_pairs={{0,2},{1,3},{2,0},{3,1},{4,6},{5,7},{6,4},{7,5},{8,10},{9,11},{10,... | collective-permute-start | bytes 589832 | tf_op jit(solution)/shard_map/ppermute | solution.py:408
  54.1 15.2 %collective-permute-start.21 = (bf16[4,2,32,384]{3,2,1,0:T(8,128)(2,1)S(1)}, bf16[4,2,32,384]{3,2,1,0:T(8,128)(2,1)S(1)}, u32[]{:S(2)}, u32[]{:S(2)}) collective-permute-start(bf16[4,2,32,384]{3,2,1,0:T(8,128)(2,1)S(1)} %get-tuple-element.51), channel_id=1, source_target_pairs={{0,1},{1,0},{2,3},{3,2},{4,5},{5,4},{6,7},{7,6},{8,9},{9,8},{10,11... | collective-permute-start | bytes 589832 | tf_op jit(solution)/shard_map/ppermute | solution.py:408
  56.4 12.9 %collective-permute-start.22 = (bf16[4,2,32,384]{3,2,1,0:T(8,128)(2,1)S(1)}, bf16[4,2,32,384]{3,2,1,0:T(8,128)(2,1)S(1)}, u32[]{:S(2)}, u32[]{:S(2)}) collective-permute-start(bf16[4,2,32,384]{3,2,1,0:T(8,128)(2,1)S(1)} %get-tuple-element.52), channel_id=1, source_target_pairs={{0,4},{1,5},{2,6},{3,7},{4,0},{5,1},{6,2},{7,3},{8,12},{9,13},{10,... | collective-permute-start | bytes 589832 | tf_op jit(solution)/shard_map/ppermute | solution.py:408
  56.4 12.9 %collective-permute-start.23 = (bf16[4,2,32,384]{3,2,1,0:T(8,128)(2,1)S(1)}, bf16[4,2,32,384]{3,2,1,0:T(8,128)(2,1)S(1)}, u32[]{:S(2)}, u32[]{:S(2)}) collective-permute-start(bf16[4,2,32,384]{3,2,1,0:T(8,128)(2,1)S(1)} %get-tuple-element.53), channel_id=1, source_target_pairs={{0,5},{1,4},{2,7},{3,6},{4,1},{5,0},{6,3},{7,2},{8,13},{9,12},{10,... | collective-permute-start | bytes 589832 | tf_op jit(solution)/shard_map/ppermute | solution.py:408
  57.3 12.0 %collective-permute-start.24 = (bf16[4,2,32,384]{3,2,1,0:T(8,128)(2,1)S(1)}, bf16[4,2,32,384]{3,2,1,0:T(8,128)(2,1)S(1)}, u32[]{:S(2)}, u32[]{:S(2)}) collective-permute-start(bf16[4,2,32,384]{3,2,1,0:T(8,128)(2,1)S(1)} %get-tuple-element.54), channel_id=1, source_target_pairs={{4,8},{5,9},{6,10},{7,11},{8,4},{9,5},{10,6},{11,7},{12,16},{13,17... | collective-permute-start | bytes 589832 | tf_op jit(solution)/shard_map/ppermute | solution.py:408
  62.9 12.4 %collective-permute-start.25 = (bf16[4,2,32,384]{3,2,1,0:T(8,128)(2,1)S(1)}, bf16[4,2,32,384]{3,2,1,0:T(8,128)(2,1)S(1)}, u32[]{:S(2)}, u32[]{:S(2)}) collective-permute-start(bf16[4,2,32,384]{3,2,1,0:T(8,128)(2,1)S(1)} %get-tuple-element.55), channel_id=1, source_target_pairs={{4,9},{5,8},{6,11},{7,10},{8,5},{9,4},{10,7},{11,6},{12,17},{13,16... | collective-permute-start | bytes 589832 | tf_op jit(solution)/shard_map/ppermute | solution.py:408
  76.7 3.4 %collective-permute-start.26 = (bf16[4,2,32,384]{3,2,1,0:T(8,128)(2,1)S(1)}, bf16[4,2,32,384]{3,2,1,0:T(8,128)(2,1)S(1)}, u32[]{:S(2)}, u32[]{:S(2)}) collective-permute-start(bf16[4,2,32,384]{3,2,1,0:T(8,128)(2,1)S(1)} %get-tuple-element.58), channel_id=1, source_target_pairs={{0,2},{1,3},{2,0},{3,1},{4,6},{5,7},{6,4},{7,5},{8,10},{9,11},{10,... | collective-permute-start | bytes 589832 | tf_op jit(solution)/shard_map/ppermute | solution.py:408

commit v7 on v6

--- a/solution.py
+++ b/solution.py
@@ -1,3 +1,5 @@
+import functools
+
 import jax
 import jax.numpy as jnp
 from jax import lax
@@ -48,11 +50,10 @@
 
 
 def pack_kernel(idx_ref, len_ref, mine, *refs):
-    other, (keep, send, carry) = refs[:4], refs[4:]
+    other, (keep, send) = refs[:4], refs[4:]
     c, r, a = coords(idx_ref)
     half, quarter = keep.shape[2], keep.shape[3]
     row = lax.broadcasted_iota(jnp.int32, (half, quarter), 0) + a * half
-    carried = a ^ r
     for slot, arrays in ((r, [mine.at[n] for n in range(4)]), (1 - r, other)):
         valid = row < len_ref[2 * c + slot]
         for n, ref in enumerate(arrays):
@@ -68,29 +69,22 @@
 
             keep[n, slot] = part(a, r)
             send[n, slot] = part(1 - a, r)
-            carry[0, n, slot] = part(carried, r)
-            carry[1, n, slot] = part(carried, 1 - r)
-
-
-def piece_rows(idx_ref, swapped):
-    c, r, a = coords(idx_ref)
-    last = (a ^ r) if swapped else a
+
+
+def piece_rows(idx_ref):
+    c, _, a = coords(idx_ref)
     half = BLK // 2
     side = 2 - 2 * (c & 1)
     starts = []
-    for place, part in ((1, a), (1, 1 - a), (side, a), (side, 1 - a), (2 - side, last), (2 - side, 1 - last)):
+    for place, part in ((1, a), (1, 1 - a), (side, a), (side, 1 - a), (2 - side, a), (2 - side, 1 - a)):
         first = place * 2 * BLK + part * half
         starts.append([pl.multiple_of(first + core * BLK, half) for core in range(2)])
     return starts
 
 
-def piece_views(pieces):
-    return [*pieces[:-2], pieces[-2].at[0], pieces[-1].at[1]]
-
-
 def gather_audio(idx_ref, pieces, arrays, dst):
     half = BLK // 2
-    for ref, firsts in zip(piece_views(pieces), piece_rows(idx_ref, True)):
+    for ref, firsts in zip(pieces, piece_rows(idx_ref)):
         for core, first in enumerate(firsts):
             for n, k in enumerate(arrays):
                 dst[n, pl.ds(first, half), :] = ref[k, core]
@@ -98,7 +92,7 @@
 
 def scatter_audio(idx_ref, sources, pieces):
     half = BLK // 2
-    for ref, firsts in zip(pieces, piece_rows(idx_ref, False)):
+    for ref, firsts in zip(pieces, piece_rows(idx_ref)):
         for core, first in enumerate(firsts):
             for n, src in enumerate(sources):
                 ref[n, core] = src[n % 2, pl.ds(first, half), :]
@@ -180,19 +174,24 @@
         bias[i] = jnp.where((place >= lo) & (place < hi), 0.0, NEG)
 
 
+def pair_stats(x, y):
+    m = jnp.maximum(x[0:2], y[0:2])
+    wx, wy = jnp.exp(x[0:2] - m), jnp.exp(y[0:2] - m)
+    total = wx + wy
+    lse, delta = m + jnp.log(total), (wx * x[2:4] + wy * y[2:4]) / total
+    return jnp.concatenate([lse, delta, lse, delta], axis=0)
+
+
 def stats_kernel(groups, idx_ref, win_ref, *refs):
     count = len(groups)
     pieces, refs = refs[: 2 * count], refs[2 * count :]
     video, refs = ((refs[0], refs[1]), (refs[2], refs[3])), refs[4:]
     stat_ref, audio, bias = refs[-3:]
-    _, r, a = coords(idx_ref)
+    _, _, a = coords(idx_ref)
     half, quarter = BLK // 2, audio.shape[2]
-    if 2 in groups:
-        pieces = piece_views(pieces)
     group_bias(idx_ref, win_ref, groups, bias)
     for n in range(count):
-        first_part = (a ^ r) if groups[n] == 2 else a
-        for ref, part in ((pieces[2 * n], first_part), (pieces[2 * n + 1], 1 - first_part)):
+        for ref, part in ((pieces[2 * n], a), (pieces[2 * n + 1], 1 - a)):
             for core in range(2):
                 first = pl.multiple_of(n * PAIR + core * BLK + part * half, half)
                 for k in range(2):
@@ -202,27 +201,24 @@
     def _(h):
         cols, wide_cols = pair_cols(idx_ref, h, quarter)
         queries, cot = audio[0, :, cols], audio[1, :, cols]
+        work = []
+        for e in range(2):
+            s = [nt(head_part(k_ref[:, wide_cols], e), queries) + bias[i] for i, (k_ref, _) in enumerate(video)]
+            work.append((s, [nt(head_part(v_ref[:, wide_cols], e), cot) for _, v_ref in video]))
         lses, deltas = [], []
-        for e in range(2):
-            parts = []
-            for i, (k_ref, v_ref) in enumerate(video):
-                s = nt(head_part(k_ref[:, wide_cols], e), queries) + bias[i]
-                m = jnp.max(s, axis=0, keepdims=True)
-                ex = jnp.exp(s - m)
-                dp = nt(head_part(v_ref[:, wide_cols], e), cot)
-                parts.append((m, jnp.sum(ex, axis=0, keepdims=True), jnp.sum(ex * dp, axis=0, keepdims=True)))
-            m = jnp.maximum(parts[0][0], parts[1][0])
-            w0, w1 = jnp.exp(parts[0][0] - m), jnp.exp(parts[1][0] - m)
-            total = parts[0][1] * w0 + parts[1][1] * w1
+        for s, dp in work:
+            m = jnp.maximum(*[jnp.max(x, axis=0, keepdims=True) for x in s])
+            ex = [jnp.exp(x - m) for x in s]
+            total = sum(jnp.sum(x, axis=0, keepdims=True) for x in ex)
             lses.append(m + jnp.log(total))
-            deltas.append((parts[0][2] * w0 + parts[1][2] * w1) / total)
+            deltas.append(sum(jnp.sum(x * y, axis=0, keepdims=True) for x, y in zip(ex, dp)) / total)
         rows = jnp.concatenate(lses + deltas + lses + deltas, axis=0)
         if count == 1:
-            rows = jnp.concatenate([refs[0][h][:, :PAIR], rows], axis=1)
+            rows = jnp.concatenate([pair_stats(refs[0][h][:, :PAIR], refs[1][h][:, PAIR:]), rows], axis=1)
         stat_ref[h] = rows
 
 
-def merge_stats(idx_ref, chips, own_a, own_b, by_a, by_b, by_q, by_q2):
+def merge_stats(idx_ref, chips, own_a, own_b, by_a, by_b, by_q2):
     c, _, _ = coords(idx_ref)
     even = (c & 1) == 0
     has_b = jnp.where(even, c >= 2, c + 2 < chips)
@@ -236,11 +232,11 @@
     for group in (
         (part(own_a, 0), part(by_a, 1), part(by_b, 1, has_b)),
         (part(own_a, 1), part(by_a, 0), part(by_q2, 1, has_q2)),
-        (part(own_b, 1), part(by_b, 0, has_b), part(by_q, 1, has_b)),
+        (part(own_b, 1), part(by_b, 0, has_b)),
     ):
-        m = jnp.maximum(jnp.maximum(group[0][0], group[1][0]), group[2][0])
+        m = functools.reduce(jnp.maximum, [lse for lse, _ in group])
         ws = [jnp.exp(lse - m) for lse, _ in group]
-        total = ws[0] + ws[1] + ws[2]
+        total = sum(ws)
         merged.append((m + jnp.log(total), sum(wt * d for wt, (_, d) in zip(ws, group)) / total))
     return merged
 
@@ -293,10 +289,10 @@
 def av_kernel(chips, idx_ref, win_ref, *refs):
     pieces = refs[:6]
     video = ((refs[6], refs[7]), (refs[8], refs[9]))
-    stats, kv_grads = refs[10:16], refs[16]
-    outs = ((refs[17], refs[18]), (refs[19], refs[20]))
-    back = refs[21:27]
-    audio, bias, grads, rowstat, qo_grads = refs[27:]
+    stats, kv_grads = refs[10:15], refs[15]
+    outs = ((refs[16], refs[17]), (refs[18], refs[19]))
+    back = refs[20:26]
+    audio, bias, grads, rowstat, qo_grads = refs[26:]
     c, r, _ = coords(idx_ref)
     quarter = audio.shape[2]
     block_bias(idx_ref, win_ref, None, bias)
@@ -399,8 +395,6 @@
         "Ax": perm(lambda v, a: (v ^ 2, 1 - a)),
         "B": perm(lambda v, a: (diagonal(v), a)),
         "Bx": perm(lambda v, a: (diagonal(v), 1 - a)),
-        "Bs": perm(lambda v, a: (diagonal(v), a ^ (v & 1))),
-        "Q": perm(lambda v, a: (v - 4 if v & 2 else v + 4, a)),
         "Q2": perm(lambda v, a: (v + 4 if v & 2 else v - 4, a)),
     }
 
@@ -439,7 +433,7 @@
         audio = (q_a, g_a, k_a, v_a)
         audio_other = [move(x, "core") for x in audio]
         piece = shape((4, 2, half, quarter), BF)
-        stack, both = shape((4, half, 2 * width), BF), shape((2, 4, 2, half, quarter), BF)
+        stack = shape((4, half, 2 * width), BF)
         (mine,) = call(
             load_kernel,
             [hbm] * 4,
@@ -449,17 +443,16 @@
             grid=(),
             est=cost(0, 0, 800000),
         )
-        keep, send, carry = call(
+        keep, send = call(
             pack_kernel,
             [smem] + [whole] * 5,
-            [(whole, piece)] * 2 + [(whole, both)],
+            [(whole, piece)] * 2,
             (audio_len, mine, *audio_other),
             grid=(),
             est=cost(0, 0, 1600000),
         )
         pieces = [keep, move(send, "aud"), move(keep, "A"), move(send, "Ax")]
-        by_carry = move(carry, "Bs")
-        pieces += [by_carry, move(by_carry, "core")]
+        pieces += [move(keep, "B"), move(send, "Bx")]
         k_f, v_f, q_f, g_f = [move(x, "core") for x in (k_v, v_v, q_v, g_v)]
 
         audio_scratch = pltpu.VMEM((2, KEYS, quarter), BF)
@@ -482,8 +475,8 @@
             return found
 
         stats_a = find_stats((0, 1), ())
-        by_a, by_q = move(stats_a, "A"), move(stats_a, "Q")
-        stats_b = find_stats((2,), (stats_a,))
+        by_a = move(stats_a, "A")
+        stats_b = find_stats((2,), (stats_a, by_a))
         by_b, by_q2 = move(stats_b, "B"), move(stats_b, "Q2")
 
         full, part = shape((rows, width), BF), shape((rows, quarter), BF)
@@ -497,9 +490,9 @@
         )
         dk_own, dv_own, dk_far, dv_far, *back = call(
             lambda *refs: av_kernel(chips, *refs),
-            [win_spec] + [whole] * 17,
+            [win_spec] + [whole] * 16,
             [(whole, part)] * 4 + [(whole, piece)] * 6,
-            (window, *pieces, k_v, v_v, k_f, v_f, stats_a, stats_b, by_a, by_b, by_q, by_q2, kv_grads),
+            (window, *pieces, k_v, v_v, k_f, v_f, stats_a, stats_b, by_a, by_b, by_q2, kv_grads),
             scratch=(audio_scratch, bias_scratch, grad_scratch, grad_scratch, audio_scratch),
             est=cost(12 * HD * pairs, pairs, 5000000),
         )

time: 81.2 us -> 84 us (1.034)
  waiting for transfers between devices: 17.3 us -> 21.5 us
  starting transfers between devices: 43.8 us -> 42.3 us
    ppermute x27 -> x26, waiting for transfers between devices: 17.3 us -> 21.5 us  [move(): return lax.ppermute(x, ('vid', 'aud'), moves[name])]
    ppermute x27 -> x26, starting transfers between devices: 43.8 us -> 42.3 us  [move(): return lax.ppermute(x, ('vid', 'aud'), moves[name])]
  transfers between devices with their start and end apart: 27 -> 26, of which waited for: 4 -> 6; matrix products, arithmetic and copies ran while one was open for 0% -> 0% of each run, Pallas kernels for 20% -> 20%
where the time goes in v7:
time: 84 us; the launch traced here: 83.7 us
  starting transfers between devices  42.3 us (50%)
  waiting for transfers between devices  21.5 us (26%)
  Pallas kernels  18.9 us (22%)
  between operations  0.92 us (1%)
    ppermute x26, starting transfers between devices, move(): return lax.ppermute(x, ('vid', 'aud'), moves[name])  42.3 us
    ppermute x26, waiting for transfers between devices, move(): return lax.ppermute(x, ('vid', 'aud'), moves[name])  21.5 us
    pallas_call x9, Pallas kernels, call(): pl.pallas_call(kernel, grid_spec=pltpu.PrefetchScalarGridSpec(num_scalar_...  18.9 us
  transfers between devices with their start and end apart: 26, of which 6 were waited for; matrix products, arithmetic and copies ran while one was open for 0% of the time, Pallas kernels for 20%

profile of v7, /device:TPU:129, one launch (start us, length us, event | category | flops | bytes accessed | tf_op | source)
XLA Modules:
  0.0 83.7 jit_solution(4593669458143373992)
XLA Ops:
  0.6 0.8 collective-permute-start
  1.4 0.1 collective-permute-start.2
  1.5 0.4 collective-permute-start.3
  1.9 0.1 collective-permute-start.1
  2.0 0.4 collective-permute-start.11
  2.4 1.1 %shard_map.161.mine = bf16[4,32,1536]{2,1,0:T(8,128)(2,1)S(1)} custom-call(s32[1]{0:T(128)} %bitcast.idx_ref.refs_0_, bf16[32,1536]{1,0:T(8,128)(2,1)} %refs_0_.1, bf16[32,1536]{1,0:T(8,128)(2,1)} %refs_1_.4, bf16[32,1536]{1,0:T(8,128)(2,1)} %refs_2_.1, bf16[32,1536]{1,0:T(8,128)(2,1)} %refs_3_.1), custom_call_target="tpu_custom_call" | custom-call | bytes 800000 | tf_op jit(solution)/shard_map/pallas_call | solution.py:419
  3.6 0.0 copy-start.1
  3.6 0.0 copy-start
  3.6 0.0 collective-permute-done.refs_0_
  3.6 0.0 collective-permute-done.2.refs_2_
  3.6 0.0 collective-permute-done.1.refs_1_
  3.6 0.0 copy-start.4
  3.6 1.3 %shard_map.162 = (bf16[4,2,32,384]{3,2,1,0:T(8,128)(2,1)S(1)}, bf16[4,2,32,384]{3,2,1,0:T(8,128)(2,1)}) custom-call(s32[1]{0:T(128)} %bitcast.idx_ref.refs_0_, s32[128]{0:T(128)S(1)} %copy-done.3, bf16[4,32,1536]{2,1,0:T(8,128)(2,1)S(1)} %shard_map.161.mine, bf16[32,1536]{1,0:T(8,128)(2,1)S(1)} %collective-permute-done.refs_0_, ...), custom_call_target="tpu_custom_call" | custom-call | bytes 1600000 | tf_op jit(solution)/shard_map/pallas_call | solution.py:419
  4.9 2.5 %collective-permute-start.6 = (bf16[4,2,32,384]{3,2,1,0:T(8,128)(2,1)}, bf16[4,2,32,384]{3,2,1,0:T(8,128)(2,1)S(1)}, u32[]{:S(2)}, u32[]{:S(2)}) collective-permute-start(bf16[4,2,32,384]{3,2,1,0:T(8,128)(2,1)} %get-tuple-element.37), channel_id=1, source_target_pairs={{0,5},{1,4},{2,7},{3,6},{4,1},{5,0},{6,3},{7,2},{8,13},{9,12},{10,... | collective-permute-start | bytes 589832 | tf_op jit(solution)/shard_map/ppermute | solution.py:402
  7.4 0.5 collective-permute-start.4
  7.9 0.7 collective-permute-start.12
  8.6 0.3 collective-permute-start.5
  8.8 8.1 %collective-permute-done.6.refs_3_.refs_5_ = bf16[4,2,32,384]{3,2,1,0:T(8,128)(2,1)S(1)} collective-permute-done((bf16[4,2,32,384]{3,2,1,0:T(8,128)(2,1)}, bf16[4,2,32,384]{3,2,1,0:T(8,128)(2,1)S(1)}, u32[]{:S(2)}, u32[]{:S(2)}) %collective-permute-start.6) | collective-permute-done | bytes 196640 | tf_op jit(solution)/shard_map/ppermute | solution.py:402
  16.9 1.0 %collective-permute-start.9 = (bf16[256,768]{1,0:T(8,128)(2,1)S(1)}, bf16[256,768]{1,0:T(8,128)(2,1)}, u32[]{:S(2)}, u32[]{:S(2)}) collective-permute-start(bf16[256,768]{1,0:T(8,128)(2,1)S(1)} %copy-done.2), channel_id=1, source_target_pairs={{0,2},{1,3},{2,0},{3,1},{4,6},{5,7},{6,4},{7,5},{8,10},{9,11},{10,... | collective-permute-start | bytes 1179656 | tf_op jit(solution)/shard_map/ppermute | solution.py:402
  17.9 0.0 collective-permute-done.4.refs_1_.refs_3_
  17.9 0.1 collective-permute-start.10
  18.0 6.4 %collective-permute-start.8 = (bf16[4,2,32,384]{3,2,1,0:T(8,128)(2,1)}, bf16[4,2,32,384]{3,2,1,0:T(8,128)(2,1)S(1)}, u32[]{:S(2)}, u32[]{:S(2)}) collective-permute-start(bf16[4,2,32,384]{3,2,1,0:T(8,128)(2,1)} %get-tuple-element.37), channel_id=1, source_target_pairs={{4,9},{5,8},{6,11},{7,10},{8,5},{9,4},{10,7},{11,6},{12,17},{13,16... | collective-permute-start | bytes 589832 | tf_op jit(solution)/shard_map/ppermute | solution.py:402
  24.3 3.4 %collective-permute-start.7 = (bf16[4,2,32,384]{3,2,1,0:T(8,128)(2,1)S(1)}, bf16[4,2,32,384]{3,2,1,0:T(8,128)(2,1)S(1)}, u32[]{:S(2)}, u32[]{:S(2)}) collective-permute-start(bf16[4,2,32,384]{3,2,1,0:T(8,128)(2,1)S(1)} %get-tuple-element.36.refs_0_.refs_2_), channel_id=1, source_target_pairs={{4,8},{5,9},{6,10},{7,11},{8,4},{9,5},{10,6},{11,7},{12,16},{13,17... | collective-permute-start | bytes 589832 | tf_op jit(solution)/shard_map/ppermute | solution.py:402
  27.7 0.1 copy.18.win_ref.refs_1_
  27.9 2.4 %shard_map.164.refs_8_.refs_12_ = f32[3,8,256]{2,1,0:T(8,128)S(1)} custom-call(s32[1]{0:T(128)} %bitcast.idx_ref.refs_0_, s32[512,2]{1,0:T(8,128)S(1)} %copy.18.win_ref.refs_1_, bf16[4,2,32,384]{3,2,1,0:T(8,128)(2,1)S(1)} %get-tuple-element.36.refs_0_.refs_2_, bf16[4,2,32,384]{3,2,1,0:T(8,128)(2,1)S(1)} %collective-permute-done.4.refs_1_.refs_3_, ...), custom_call_target="tpu_custom_call" | custom-call | flops 201326592 | bytes 2000000 | tf_op jit(solution)/shard_map/pallas_call | solution.py:419
  30.3 0.1 collective-permute-start.13
  30.4 1.0 %collective-permute-done.8.refs_5_.refs_3_.refs_7_ = bf16[4,2,32,384]{3,2,1,0:T(8,128)(2,1)S(1)} collective-permute-done((bf16[4,2,32,384]{3,2,1,0:T(8,128)(2,1)}, bf16[4,2,32,384]{3,2,1,0:T(8,128)(2,1)S(1)}, u32[]{:S(2)}, u32[]{:S(2)}) %collective-permute-start.8) | collective-permute-done | bytes 196640 | tf_op jit(solution)/shard_map/ppermute | solution.py:402
  31.4 4.7 %collective-permute-done.7.refs_4_.refs_2_.refs_6_ = bf16[4,2,32,384]{3,2,1,0:T(8,128)(2,1)S(1)} collective-permute-done((bf16[4,2,32,384]{3,2,1,0:T(8,128)(2,1)S(1)}, bf16[4,2,32,384]{3,2,1,0:T(8,128)(2,1)S(1)}, u32[]{:S(2)}, u32[]{:S(2)}) %collective-permute-start.7) | collective-permute-done | bytes 196640 | tf_op jit(solution)/shard_map/ppermute | solution.py:402
  36.1 1.8 %shard_map.165.refs_13_ = f32[3,8,256]{2,1,0:T(8,128)S(1)} custom-call(s32[1]{0:T(128)} %bitcast.idx_ref.refs_0_, s32[512,2]{1,0:T(8,128)S(1)} %copy.18.win_ref.refs_1_, bf16[4,2,32,384]{3,2,1,0:T(8,128)(2,1)S(1)} %collective-permute-done.7.refs_4_.refs_2_.refs_6_, bf16[4,2,32,384]{3,2,1,0:T(8,128)(2,1)S(1)} %collective-permute-done.8.refs_5_.refs_3_.refs_7_, ...), custom_call_target="tpu_custom_call" | custom-call | flops 100663296 | bytes 2000000 | tf_op jit(solution)/shard_map/pallas_call | solution.py:419
  37.9 1.9 %collective-permute-start.15 = (f32[3,8,256]{2,1,0:T(8,128)S(1)}, f32[3,8,256]{2,1,0:T(8,128)S(1)}, u32[]{:S(2)}, u32[]{:S(2)}) collective-permute-start(f32[3,8,256]{2,1,0:T(8,128)S(1)} %shard_map.165.refs_13_), channel_id=1, source_target_pairs={{4,12},{5,13},{6,14},{7,15},{8,0},{9,1},{10,2},{11,3},{12,20},{13,... | collective-permute-start | bytes 73736 | tf_op jit(solution)/shard_map/ppermute | solution.py:402
  39.8 4.7 %collective-permute-start.14 = (f32[3,8,256]{2,1,0:T(8,128)S(1)}, f32[3,8,256]{2,1,0:T(8,128)S(1)}, u32[]{:S(2)}, u32[]{:S(2)}) collective-permute-start(f32[3,8,256]{2,1,0:T(8,128)S(1)} %shard_map.165.refs_13_), channel_id=1, source_target_pairs={{4,8},{5,9},{6,10},{7,11},{8,4},{9,5},{10,6},{11,7},{12,16},{13,17... | collective-permute-start | bytes 73736 | tf_op jit(solution)/shard_map/ppermute | solution.py:402
  44.5 4.8 %shard_map.163 = (bf16[256,384]{1,0:T(8,128)(2,1)S(1)}, bf16[256,384]{1,0:T(8,128)(2,1)S(1)}, bf16[256,384]{1,0:T(8,128)(2,1)S(1)}, bf16[256,384]{1,0:T(8,128)(2,1)S(1)}, bf16[2,384,384]{2,1,0:T(8,128)(2,1)S(1)}) custom-call(s32[1]{0:T(128)} %bitcast.idx_ref.refs_0_, s32[512,2]{1,0:T(8,128)S(1)} %copy.18.win_ref.refs_1_, s32[128]{0:T(128)S(1)} %copy-done.3, ...), custom_call_target="tpu_custom_call" | custom-call | flops 754974720 | bytes 5000000 | tf_op jit(solution)/shard_map/pallas_call | solution.py:419
  49.4 3.9 %collective-permute-start.16 = (bf16[256,384]{1,0:T(8,128)(2,1)S(1)}, bf16[256,384]{1,0:T(8,128)(2,1)S(1)}, u32[]{:S(2)}, u32[]{:S(2)}) collective-permute-start(bf16[256,384]{1,0:T(8,128)(2,1)S(1)} %get-tuple-element.43), channel_id=1, source_target_pairs={{0,2},{1,3},{2,0},{3,1},{4,6},{5,7},{6,4},{7,5},{8,10},{9,11},{10,... | collective-permute-start | bytes 589832 | tf_op jit(solution)/shard_map/ppermute | solution.py:402
  53.3 0.1 collective-permute-start.17
  53.4 4.2 %shard_map.166 = (bf16[256,384]{1,0:T(8,128)(2,1)S(1)}, bf16[256,384]{1,0:T(8,128)(2,1)S(1)}, bf16[256,384]{1,0:T(8,128)(2,1)S(1)}, bf16[256,384]{1,0:T(8,128)(2...) custom-call(s32[1]{0:T(128)} %bitcast.idx_ref.refs_0_, ...), custom_call_target="tpu_custom_call" | custom-call | flops 905969664 | bytes 5000000 | tf_op jit(solution)/shard_map/pallas_call | solution.py:419
  57.6 0.7 collective-permute-start.18
  58.3 0.1 collective-permute-start.19
  58.4 0.2 collective-permute-start.20
  58.6 3.0 %collective-permute-start.22 = (bf16[4,2,32,384]{3,2,1,0:T(8,128)(2,1)S(1)}, bf16[4,2,32,384]{3,2,1,0:T(8,128)(2,1)S(1)}, u32[]{:S(2)}, u32[]{:S(2)}) collective-permute-start(bf16[4,2,32,384]{3,2,1,0:T(8,128)(2,1)S(1)} %get-tuple-element.51), channel_id=1, source_target_pairs={{0,5},{1,4},{2,7},{3,6},{4,1},{5,0},{6,3},{7,2},{8,13},{9,12},{10,... | collective-permute-start | bytes 589832 | tf_op jit(solution)/shard_map/ppermute | solution.py:402
  61.6 4.2 %collective-permute-start.23 = (bf16[4,2,32,384]{3,2,1,0:T(8,128)(2,1)S(1)}, bf16[4,2,32,384]{3,2,1,0:T(8,128)(2,1)S(1)}, u32[]{:S(2)}, u32[]{:S(2)}) collective-permute-start(bf16[4,2,32,384]{3,2,1,0:T(8,128)(2,1)S(1)} %get-tuple-element.52), channel_id=1, source_target_pairs={{4,8},{5,9},{6,10},{7,11},{8,4},{9,5},{10,6},{11,7},{12,16},{13,17... | collective-permute-start | bytes 589832 | tf_op jit(solution)/shard_map/ppermute | solution.py:402
  65.8 4.4 %collective-permute-start.24 = (bf16[4,2,32,384]{3,2,1,0:T(8,128)(2,1)S(1)}, bf16[4,2,32,384]{3,2,1,0:T(8,128)(2,1)S(1)}, u32[]{:S(2)}, u32[]{:S(2)}) collective-permute-start(bf16[4,2,32,384]{3,2,1,0:T(8,128)(2,1)S(1)} %get-tuple-element.53), channel_id=1, source_target_pairs={{4,9},{5,8},{6,11},{7,10},{8,5},{9,4},{10,7},{11,6},{12,17},{13,16... | collective-permute-start | bytes 589832 | tf_op jit(solution)/shard_map/ppermute | solution.py:402
  70.2 1.3 %shard_map.167 = (bf16[256,768]{1,0:T(8,128)(2,1)}, bf16[256,768]{1,0:T(8,128)(2,1)}, bf16[256,768]{1,0:T(8,128)(2,1)}, bf16[256,768]{1,0:T(8,128)(2,1)}, s32[1]{0:T(128)}) custom-call(s32[1]{0:T(128)} %bitcast.idx_ref.refs_0_, bf16[256,384]{1,0:T(8,128)(2,1)S(1)} %get-tuple-element.38.refs_0_, bf16[256,384]{1,0:T(8,128)(2,1)S(1)} %get-tuple-element.39.refs_1_, ...), custom_call_target="tpu_custom_call" | custom-call | bytes 1600000 | tf_op jit(solution)/shard_map/pallas_call | solution.py:419
  71.5 1.4 %collective-permute-done.23.by_b = bf16[4,2,32,384]{3,2,1,0:T(8,128)(2,1)S(1)} collective-permute-done((bf16[4,2,32,384]{3,2,1,0:T(8,128)(2,1)S(1)}, bf16[4,2,32,384]{3,2,1,0:T(8,128)(2,1)S(1)}, u32[]{:S(2)}, u32[]{:S(2)}) %collective-permute-start.23) | collective-permute-done | bytes 196640 | tf_op jit(solution)/shard_map/ppermute | solution.py:402
  72.9 5.1 %collective-permute-done.24.by_bx = bf16[4,2,32,384]{3,2,1,0:T(8,128)(2,1)S(1)} collective-permute-done((bf16[4,2,32,384]{3,2,1,0:T(8,128)(2,1)S(1)}, bf16[4,2,32,384]{3,2,1,0:T(8,128)(2,1)S(1)}, u32[]{:S(2)}, u32[]{:S(2)}) %collective-permute-start.24) | collective-permute-done | bytes 196640 | tf_op jit(solution)/shard_map/ppermute | solution.py:402
  78.1 1.3 %shard_map.168 = (bf16[4,2,32,384]{3,2,1,0:T(8,128)(2,1)S(1)}, bf16[4,2,32,384]{3,2,1,0:T(8,128)(2,1)S(1)}) custom-call(s32[1]{0:T(128)} %bitcast.idx_ref.refs_0_, s32[128]{0:T(128)S(1)} %copy-done.3, bf16[4,2,32,384]{3,2,1,0:T(8,128)(2,1)S(1)} %get-tuple-element.48.keep, bf16[4,2,32,384]{3,2,1,0:T(8,128)(2,1)S(1)} %collective-permute-done.20.by_aud, ...), custom_call_target="tpu_custom_call" | custom-call | flops 1000000 | bytes 1600000 | tf_op jit(solution)/shard_map/pallas_call | solution.py:419
  79.4 2.5 %collective-permute-start.25 = (bf16[4,2,32,384]{3,2,1,0:T(8,128)(2,1)S(1)}, bf16[4,2,32,384]{3,2,1,0:T(8,128)(2,1)S(1)}, u32[]{:S(2)}, u32[]{:S(2)}) collective-permute-start(bf16[4,2,32,384]{3,2,1,0:T(8,128)(2,1)S(1)} %get-tuple-element.56), channel_id=1, source_target_pairs={{0,2},{1,3},{2,0},{3,1},{4,6},{5,7},{6,4},{7,5},{8,10},{9,11},{10,... | collective-permute-start | bytes 589832 | tf_op jit(solution)/shard_map/ppermute | solution.py:402
  81.9 1.1 %collective-permute-done.25.other = bf16[4,2,32,384]{3,2,1,0:T(8,128)(2,1)S(1)} collective-permute-done((bf16[4,2,32,384]{3,2,1,0:T(8,128)(2,1)S(1)}, bf16[4,2,32,384]{3,2,1,0:T(8,128)(2,1)S(1)}, u32[]{:S(2)}, u32[]{:S(2)}) %collective-permute-start.25) | collective-permute-done | bytes 196640 | tf_op jit(solution)/shard_map/ppermute | solution.py:402
  83.0 0.8 shard_map.169
  (24 shorter events, 0.1 us)
Async XLA Ops:
  0.6 2.9 %collective-permute-start = (bf16[32,1536]{1,0:T(8,128)(2,1)}, bf16[32,1536]{1,0:T(8,128)(2,1)S(1)}, u32[]{:S(2)}, u32[]{:S(2)}) collective-permute-start(bf16[32,1536]{1,0:T(8,128)(2,1)} %refs_0_.1), channel_id=1, source_target_pairs={{0,2},{1,3},{2,0},{3,1},{4,6},{5,7},{6,4},{7,5},{8,10},{9,11},{10,... | collective-permute-start | bytes 294920 | tf_op jit(solution)/shard_map/ppermute | solution.py:402
  1.4 2.2 %collective-permute-start.2 = (bf16[32,1536]{1,0:T(8,128)(2,1)}, bf16[32,1536]{1,0:T(8,128)(2,1)S(1)}, u32[]{:S(2)}, u32[]{:S(2)}) collective-permute-start(bf16[32,1536]{1,0:T(8,128)(2,1)} %refs_2_.1), channel_id=1, source_target_pairs={{0,2},{1,3},{2,0},{3,1},{4,6},{5,7},{6,4},{7,5},{8,10},{9,11},{10,... | collective-permute-start | bytes 294920 | tf_op jit(solution)/shard_map/ppermute | solution.py:402
  1.5 2.1 %collective-permute-start.3 = (bf16[32,1536]{1,0:T(8,128)(2,1)}, bf16[32,1536]{1,0:T(8,128)(2,1)S(1)}, u32[]{:S(2)}, u32[]{:S(2)}) collective-permute-start(bf16[32,1536]{1,0:T(8,128)(2,1)} %refs_3_.1), channel_id=1, source_target_pairs={{0,2},{1,3},{2,0},{3,1},{4,6},{5,7},{6,4},{7,5},{8,10},{9,11},{10,... | collective-permute-start | bytes 294920 | tf_op jit(solution)/shard_map/ppermute | solution.py:402
  1.9 1.7 %collective-permute-start.1 = (bf16[32,1536]{1,0:T(8,128)(2,1)}, bf16[32,1536]{1,0:T(8,128)(2,1)S(1)}, u32[]{:S(2)}, u32[]{:S(2)}) collective-permute-start(bf16[32,1536]{1,0:T(8,128)(2,1)} %refs_1_.4), channel_id=1, source_target_pairs={{0,2},{1,3},{2,0},{3,1},{4,6},{5,7},{6,4},{7,5},{8,10},{9,11},{10,... | collective-permute-start | bytes 294920 | tf_op jit(solution)/shard_map/ppermute | solution.py:402
  2.0 22.3 %collective-permute-start.11 = (bf16[256,768]{1,0:T(8,128)(2,1)}, bf16[256,768]{1,0:T(8,128)(2,1)S(1)}, u32[]{:S(2)}, u32[]{:S(2)}) collective-permute-start(bf16[256,768]{1,0:T(8,128)(2,1)} %refs_8_.1), channel_id=1, source_target_pairs={{0,2},{1,3},{2,0},{3,1},{4,6},{5,7},{6,4},{7,5},{8,10},{9,11},{10,... | collective-permute-start | bytes 1179656 | tf_op jit(solution)/shard_map/ppermute | solution.py:402
  2.4 1.2 %copy-start.3 = (s32[128]{0:T(128)S(1)}, s32[128]{0:T(128)}, u32[]{:S(2)}) copy-start(s32[128]{0:T(128)} %len_ref.5) | copy-start | bytes 1540
  2.4 14.5 %copy-start.2 = (bf16[256,768]{1,0:T(8,128)(2,1)S(1)}, bf16[256,768]{1,0:T(8,128)(2,1)}, u32[]{:S(2)}) copy-start(bf16[256,768]{1,0:T(8,128)(2,1)} %refs_6_.2) | copy-start | bytes 1179652
  3.6 4.4 %copy-start.1 = (bf16[256,768]{1,0:T(8,128)(2,1)S(1)}, bf16[256,768]{1,0:T(8,128)(2,1)}, u32[]{:S(2)}) copy-start(bf16[256,768]{1,0:T(8,128)(2,1)} %refs_9_.1) | copy-start | bytes 1179652
  3.6 24.3 %copy-start = (bf16[256,768]{1,0:T(8,128)(2,1)S(1)}, bf16[256,768]{1,0:T(8,128)(2,1)}, u32[]{:S(2)}) copy-start(bf16[256,768]{1,0:T(8,128)(2,1)} %refs_8_.1) | copy-start | bytes 1179652
  3.6 24.1 %copy-start.4 = (s32[512,2]{0,1:T(2,128)S(1)}, s32[512,2]{0,1:T(2,128)}, u32[]{:S(2)}) copy-start(s32[512,2]{0,1:T(2,128)} %param.18) | copy-start | bytes 12292
  4.9 12.0 %collective-permute-start.6 = (bf16[4,2,32,384]{3,2,1,0:T(8,128)(2,1)}, bf16[4,2,32,384]{3,2,1,0:T(8,128)(2,1)S(1)}, u32[]{:S(2)}, u32[]{:S(2)}) collective-permute-start(bf16[4,2,32,384]{3,2,1,0:T(8,128)(2,1)} %get-tuple-element.37), channel_id=1, source_target_pairs={{0,5},{1,4},{2,7},{3,6},{4,1},{5,0},{6,3},{7,2},{8,13},{9,12},{10,... | collective-permute-start | bytes 589832 | tf_op jit(solution)/shard_map/ppermute | solution.py:402
  7.4 10.5 %collective-permute-start.4 = (bf16[4,2,32,384]{3,2,1,0:T(8,128)(2,1)}, bf16[4,2,32,384]{3,2,1,0:T(8,128)(2,1)S(1)}, u32[]{:S(2)}, u32[]{:S(2)}) collective-permute-start(bf16[4,2,32,384]{3,2,1,0:T(8,128)(2,1)} %get-tuple-element.37), channel_id=1, source_target_pairs={{0,1},{1,0},{2,3},{3,2},{4,5},{5,4},{6,7},{7,6},{8,9},{9,8},{10,11... | collective-permute-start | bytes 589832 | tf_op jit(solution)/shard_map/ppermute | solution.py:402
  7.9 20.0 %collective-permute-start.12 = (bf16[256,768]{1,0:T(8,128)(2,1)S(1)}, bf16[256,768]{1,0:T(8,128)(2,1)S(1)}, u32[]{:S(2)}, u32[]{:S(2)}) collective-permute-start(bf16[256,768]{1,0:T(8,128)(2,1)S(1)} %copy-done.1), channel_id=1, source_target_pairs={{0,2},{1,3},{2,0},{3,1},{4,6},{5,7},{6,4},{7,5},{8,10},{9,11},{10,... | collective-permute-start | bytes 1179656 | tf_op jit(solution)/shard_map/ppermute | solution.py:402
  8.6 9.4 %collective-permute-start.5 = (bf16[4,2,32,384]{3,2,1,0:T(8,128)(2,1)S(1)}, bf16[4,2,32,384]{3,2,1,0:T(8,128)(2,1)S(1)}, u32[]{:S(2)}, u32[]{:S(2)}) collective-permute-start(bf16[4,2,32,384]{3,2,1,0:T(8,128)(2,1)S(1)} %get-tuple-element.36.refs_0_.refs_2_), channel_id=1, source_target_pairs={{0,4},{1,5},{2,6},{3,7},{4,0},{5,1},{6,2},{7,3},{8,12},{9,13},{10,... | collective-permute-start | bytes 589832 | tf_op jit(solution)/shard_map/ppermute | solution.py:402
  16.9 27.6 %collective-permute-start.9 = (bf16[256,768]{1,0:T(8,128)(2,1)S(1)}, bf16[256,768]{1,0:T(8,128)(2,1)}, u32[]{:S(2)}, u32[]{:S(2)}) collective-permute-start(bf16[256,768]{1,0:T(8,128)(2,1)S(1)} %copy-done.2), channel_id=1, source_target_pairs={{0,2},{1,3},{2,0},{3,1},{4,6},{5,7},{6,4},{7,5},{8,10},{9,11},{10,... | collective-permute-start | bytes 1179656 | tf_op jit(solution)/shard_map/ppermute | solution.py:402
  17.9 26.7 %collective-permute-start.10 = (bf16[256,768]{1,0:T(8,128)(2,1)}, bf16[256,768]{1,0:T(8,128)(2,1)}, u32[]{:S(2)}, u32[]{:S(2)}) collective-permute-start(bf16[256,768]{1,0:T(8,128)(2,1)} %refs_7_.2), channel_id=1, source_target_pairs={{0,2},{1,3},{2,0},{3,1},{4,6},{5,7},{6,4},{7,5},{8,10},{9,11},{10,... | collective-permute-start | bytes 1179656 | tf_op jit(solution)/shard_map/ppermute | solution.py:402
  18.0 13.5 %collective-permute-start.8 = (bf16[4,2,32,384]{3,2,1,0:T(8,128)(2,1)}, bf16[4,2,32,384]{3,2,1,0:T(8,128)(2,1)S(1)}, u32[]{:S(2)}, u32[]{:S(2)}) collective-permute-start(bf16[4,2,32,384]{3,2,1,0:T(8,128)(2,1)} %get-tuple-element.37), channel_id=1, source_target_pairs={{4,9},{5,8},{6,11},{7,10},{8,5},{9,4},{10,7},{11,6},{12,17},{13,16... | collective-permute-start | bytes 589832 | tf_op jit(solution)/shard_map/ppermute | solution.py:402
  24.3 11.8 %collective-permute-start.7 = (bf16[4,2,32,384]{3,2,1,0:T(8,128)(2,1)S(1)}, bf16[4,2,32,384]{3,2,1,0:T(8,128)(2,1)S(1)}, u32[]{:S(2)}, u32[]{:S(2)}) collective-permute-start(bf16[4,2,32,384]{3,2,1,0:T(8,128)(2,1)S(1)} %get-tuple-element.36.refs_0_.refs_2_), channel_id=1, source_target_pairs={{4,8},{5,9},{6,10},{7,11},{8,4},{9,5},{10,6},{11,7},{12,16},{13,17... | collective-permute-start | bytes 589832 | tf_op jit(solution)/shard_map/ppermute | solution.py:402
  30.3 5.8 %collective-permute-start.13 = (f32[3,8,256]{2,1,0:T(8,128)S(1)}, f32[3,8,256]{2,1,0:T(8,128)S(1)}, u32[]{:S(2)}, u32[]{:S(2)}) collective-permute-start(f32[3,8,256]{2,1,0:T(8,128)S(1)} %shard_map.164.refs_8_.refs_12_), channel_id=1, source_target_pairs={{0,4},{1,5},{2,6},{3,7},{4,0},{5,1},{6,2},{7,3},{8,12},{9,13},{10,... | collective-permute-start | bytes 73736 | tf_op jit(solution)/shard_map/ppermute | solution.py:402
  37.9 15.5 %collective-permute-start.15 = (f32[3,8,256]{2,1,0:T(8,128)S(1)}, f32[3,8,256]{2,1,0:T(8,128)S(1)}, u32[]{:S(2)}, u32[]{:S(2)}) collective-permute-start(f32[3,8,256]{2,1,0:T(8,128)S(1)} %shard_map.165.refs_13_), channel_id=1, source_target_pairs={{4,12},{5,13},{6,14},{7,15},{8,0},{9,1},{10,2},{11,3},{12,20},{13,... | collective-permute-start | bytes 73736 | tf_op jit(solution)/shard_map/ppermute | solution.py:402
  39.8 13.6 %collective-permute-start.14 = (f32[3,8,256]{2,1,0:T(8,128)S(1)}, f32[3,8,256]{2,1,0:T(8,128)S(1)}, u32[]{:S(2)}, u32[]{:S(2)}) collective-permute-start(f32[3,8,256]{2,1,0:T(8,128)S(1)} %shard_map.165.refs_13_), channel_id=1, source_target_pairs={{4,8},{5,9},{6,10},{7,11},{8,4},{9,5},{10,6},{11,7},{12,16},{13,17... | collective-permute-start | bytes 73736 | tf_op jit(solution)/shard_map/ppermute | solution.py:402
  49.4 9.2 %collective-permute-start.16 = (bf16[256,384]{1,0:T(8,128)(2,1)S(1)}, bf16[256,384]{1,0:T(8,128)(2,1)S(1)}, u32[]{:S(2)}, u32[]{:S(2)}) collective-permute-start(bf16[256,384]{1,0:T(8,128)(2,1)S(1)} %get-tuple-element.43), channel_id=1, source_target_pairs={{0,2},{1,3},{2,0},{3,1},{4,6},{5,7},{6,4},{7,5},{8,10},{9,11},{10,... | collective-permute-start | bytes 589832 | tf_op jit(solution)/shard_map/ppermute | solution.py:402
  53.3 5.3 %collective-permute-start.17 = (bf16[256,384]{1,0:T(8,128)(2,1)S(1)}, bf16[256,384]{1,0:T(8,128)(2,1)S(1)}, u32[]{:S(2)}, u32[]{:S(2)}) collective-permute-start(bf16[256,384]{1,0:T(8,128)(2,1)S(1)} %get-tuple-element.44), channel_id=1, source_target_pairs={{0,2},{1,3},{2,0},{3,1},{4,6},{5,7},{6,4},{7,5},{8,10},{9,11},{10,... | collective-permute-start | bytes 589832 | tf_op jit(solution)/shard_map/ppermute | solution.py:402
  57.6 4.0 %collective-permute-start.18 = (bf16[256,384]{1,0:T(8,128)(2,1)S(1)}, bf16[256,384]{1,0:T(8,128)(2,1)S(1)}, u32[]{:S(2)}, u32[]{:S(2)}) collective-permute-start(bf16[256,384]{1,0:T(8,128)(2,1)S(1)} %get-tuple-element.45), channel_id=1, source_target_pairs={{0,2},{1,3},{2,0},{3,1},{4,6},{5,7},{6,4},{7,5},{8,10},{9,11},{10,... | collective-permute-start | bytes 589832 | tf_op jit(solution)/shard_map/ppermute | solution.py:402
  58.3 7.6 %collective-permute-start.19 = (bf16[256,384]{1,0:T(8,128)(2,1)S(1)}, bf16[256,384]{1,0:T(8,128)(2,1)S(1)}, u32[]{:S(2)}, u32[]{:S(2)}) collective-permute-start(bf16[256,384]{1,0:T(8,128)(2,1)S(1)} %get-tuple-element.46), channel_id=1, source_target_pairs={{0,2},{1,3},{2,0},{3,1},{4,6},{5,7},{6,4},{7,5},{8,10},{9,11},{10,... | collective-permute-start | bytes 589832 | tf_op jit(solution)/shard_map/ppermute | solution.py:402
  58.4 13.1 %collective-permute-start.20 = (bf16[4,2,32,384]{3,2,1,0:T(8,128)(2,1)S(1)}, bf16[4,2,32,384]{3,2,1,0:T(8,128)(2,1)S(1)}, u32[]{:S(2)}, u32[]{:S(2)}) collective-permute-start(bf16[4,2,32,384]{3,2,1,0:T(8,128)(2,1)S(1)} %get-tuple-element.49), channel_id=1, source_target_pairs={{0,1},{1,0},{2,3},{3,2},{4,5},{5,4},{6,7},{7,6},{8,9},{9,8},{10,11... | collective-permute-start | bytes 589832 | tf_op jit(solution)/shard_map/ppermute | solution.py:402
  58.6 12.9 %collective-permute-start.21 = (bf16[4,2,32,384]{3,2,1,0:T(8,128)(2,1)S(1)}, bf16[4,2,32,384]{3,2,1,0:T(8,128)(2,1)S(1)}, u32[]{:S(2)}, u32[]{:S(2)}) collective-permute-start(bf16[4,2,32,384]{3,2,1,0:T(8,128)(2,1)S(1)} %get-tuple-element.50), channel_id=1, source_target_pairs={{0,4},{1,5},{2,6},{3,7},{4,0},{5,1},{6,2},{7,3},{8,12},{9,13},{10,... | collective-permute-start | bytes 589832 | tf_op jit(solution)/shard_map/ppermute | solution.py:402
  58.6 12.9 %collective-permute-start.22 = (bf16[4,2,32,384]{3,2,1,0:T(8,128)(2,1)S(1)}, bf16[4,2,32,384]{3,2,1,0:T(8,128)(2,1)S(1)}, u32[]{:S(2)}, u32[]{:S(2)}) collective-permute-start(bf16[4,2,32,384]{3,2,1,0:T(8,128)(2,1)S(1)} %get-tuple-element.51), channel_id=1, source_target_pairs={{0,5},{1,4},{2,7},{3,6},{4,1},{5,0},{6,3},{7,2},{8,13},{9,12},{10,... | collective-permute-start | bytes 589832 | tf_op jit(solution)/shard_map/ppermute | solution.py:402
  61.6 11.3 %collective-permute-start.23 = (bf16[4,2,32,384]{3,2,1,0:T(8,128)(2,1)S(1)}, bf16[4,2,32,384]{3,2,1,0:T(8,128)(2,1)S(1)}, u32[]{:S(2)}, u32[]{:S(2)}) collective-permute-start(bf16[4,2,32,384]{3,2,1,0:T(8,128)(2,1)S(1)} %get-tuple-element.52), channel_id=1, source_target_pairs={{4,8},{5,9},{6,10},{7,11},{8,4},{9,5},{10,6},{11,7},{12,16},{13,17... | collective-permute-start | bytes 589832 | tf_op jit(solution)/shard_map/ppermute | solution.py:402
  65.8 12.3 %collective-permute-start.24 = (bf16[4,2,32,384]{3,2,1,0:T(8,128)(2,1)S(1)}, bf16[4,2,32,384]{3,2,1,0:T(8,128)(2,1)S(1)}, u32[]{:S(2)}, u32[]{:S(2)}) collective-permute-start(bf16[4,2,32,384]{3,2,1,0:T(8,128)(2,1)S(1)} %get-tuple-element.53), channel_id=1, source_target_pairs={{4,9},{5,8},{6,11},{7,10},{8,5},{9,4},{10,7},{11,6},{12,17},{13,16... | collective-permute-start | bytes 589832 | tf_op jit(solution)/shard_map/ppermute | solution.py:402
  79.4 3.5 %collective-permute-start.25 = (bf16[4,2,32,384]{3,2,1,0:T(8,128)(2,1)S(1)}, bf16[4,2,32,384]{3,2,1,0:T(8,128)(2,1)S(1)}, u32[]{:S(2)}, u32[]{:S(2)}) collective-permute-start(bf16[4,2,32,384]{3,2,1,0:T(8,128)(2,1)S(1)} %get-tuple-element.56), channel_id=1, source_target_pairs={{0,2},{1,3},{2,0},{3,1},{4,6},{5,7},{6,4},{7,5},{8,10},{9,11},{10,... | collective-permute-start | bytes 589832 | tf_op jit(solution)/shard_map/ppermute | solution.py:402
